TPU v7x, 32 devices: a whole 2x2x4 slice. The times are simulated.
32 devices in a mesh: ctx: 4 (over y, x), fsdp: 8 (over z, core).
Axes of the slice: x: 2, y: 2, z: 4, core: 2. Of those that a mesh axis runs over, the one named last changes fastest.
Arguments:
- tokens: bfloat16 [8, 2560, 2048], P('fsdp', 'ctx'), may hold values from -6 to 6
- cotangent: bfloat16 [8, 2560, 2048], P('fsdp', 'ctx'), may hold values from -6 to 6
- block_table: int32 [8, 40], P('fsdp'), may hold values from 0 to 39, as said below
- ln_gain: bfloat16 [2048], replicated, may hold values from 0.5 to 1.5
- ln_bias: bfloat16 [2048], replicated, may hold values from -2 to 2
- w_qkv: bfloat16 [2048, 3, 2048], P('fsdp', None, 'ctx'), may hold values from -0.125 to 0.125
- b_qkv: bfloat16 [6144], replicated, may hold values from -2 to 2
- w_dense: bfloat16 [2048, 2048], P('ctx', 'fsdp'), may hold values from -0.5 to 0.5
- b_dense: bfloat16 [2048], replicated, may hold values from -2 to 2
- w_fc1: bfloat16 [2048, 8192], P('fsdp', 'ctx'), may hold values from -0.125 to 0.125
- b_fc1: bfloat16 [8192], replicated, may hold values from -2 to 2
- w_fc2: bfloat16 [8192, 2048], P('ctx', 'fsdp'), may hold values from -0.0625 to 0.0625
- b_fc2: bfloat16 [2048], replicated, may hold values from -2 to 2
Outputs:
- output: bfloat16 [8, 2560, 2048], P('fsdp', 'ctx')
- d_tokens: bfloat16 [8, 2560, 2048], P('fsdp', 'ctx')
- d_ln_gain: float32 [2048], replicated
- d_ln_bias: float32 [2048], replicated
- d_w_qkv: float32 [2048, 3, 2048], P('fsdp', None, 'ctx')
- d_b_qkv: float32 [6144], replicated
- d_w_dense: float32 [2048, 2048], P('ctx', 'fsdp')
- d_b_dense: float32 [2048], replicated
- d_w_fc1: float32 [2048, 8192], P('fsdp', 'ctx')
- d_b_fc1: float32 [8192], replicated
- d_w_fc2: float32 [8192, 2048], P('ctx', 'fsdp')
- d_b_fc2: float32 [2048], replicated
Inputs may be any that keep to these rules, and one draw needn't show every extreme that they name: `block_table`: each row lists each of the 40 blocks of its group exactly once.
All inputs are finite; a program needn't handle non-finite values.
Results may differ from a plain program's by a relative error of at most 0.015.
Values may be sent and summed in bfloat16 or wider, within the bound.
No kernel may reach another device: no remote copies, remote signals or barrier semaphores. Data moves between devices by JAX's collectives and lax.ppermute only.
A program may use at most 832 MiB of HBM per device.

v0:
```python
import math

import jax
import jax.numpy as jnp
from jax import lax
from jax.sharding import PartitionSpec as P

HEADS = 32
ROT = 32
PROMPT = 2048
CLEN = 256
BLK = 64


def layer_norm(values, gain, shift):
    average = jnp.mean(values, axis=-1, keepdims=True)
    centred = values - average
    variance = jnp.mean(centred * centred, axis=-1, keepdims=True)
    return centred * lax.rsqrt(variance + 1e-05) * gain + shift


def gelu_tanh(values):
    return (
        0.5
        * values
        * (
            1.0
            + jnp.tanh(math.sqrt(2.0 / math.pi) * (values + 0.044715 * values * values * values))
        )
    )


def segment_of(places):
    return jnp.where(places < PROMPT, 0, 1 + (places - PROMPT) // CLEN)


def position_of(places):
    return jnp.where(places < PROMPT, places, PROMPT + (places - PROMPT) % CLEN)


def visible(query_places, key_places):
    query_segment = segment_of(query_places)
    key_segment = segment_of(key_places)
    return (key_segment == 0) & (query_segment > 0) | (key_segment == query_segment) & (
        key_places <= query_places
    )


def frequencies():
    half_dims = ROT // 2
    return 10000.0 ** (-2.0 * jnp.arange(half_dims, dtype=jnp.float32) / ROT)


def rotate(values, angles, head_dim):
    row_count = values.shape[0]
    by_head = values.reshape(row_count, -1, head_dim)
    half_dims = angles.shape[1]
    cosine = jnp.cos(angles)[:, None, :]
    sine_part = jnp.sin(angles)[:, None, :]
    front = by_head[:, :, :half_dims]
    second = by_head[:, :, half_dims : 2 * half_dims]
    turned = jnp.concatenate(
        [
            front * cosine - second * sine_part,
            second * cosine + front * sine_part,
            by_head[:, :, 2 * half_dims :],
        ],
        axis=-1,
    )
    return turned.reshape(row_count, -1)


def product(left, right):
    return jnp.dot(left, right, preferred_element_type=jnp.float32)


def contract_rows(left, right):
    return lax.dot_general(
        left, right, (((0,), (0,)), ((), ())), preferred_element_type=jnp.float32
    )


def contract_cols(left, right):
    return lax.dot_general(
        left, right, (((1,), (1,)), ((), ())), preferred_element_type=jnp.float32
    )


def shards(
    tokens,
    cotangent,
    block_table,
    ln_gain,
    ln_bias,
    w_qkv,
    b_qkv,
    w_dense,
    b_dense,
    w_fc1,
    b_fc1,
    w_fc2,
    b_fc2,
):
    group_count, local_rows, width = tokens.shape
    head_dim = width // HEADS
    scale = 1.0 / math.sqrt(head_dim)
    ctx_count = lax.axis_size("ctx")
    ctx_index = lax.axis_index("ctx")
    group_rows = local_rows * ctx_count
    hidden_whole = b_fc1.shape[0]
    dense_each = width // ctx_count
    hidden_each = hidden_whole // ctx_count
    local_blocks = local_rows // BLK
    own_blocks = lax.dynamic_slice_in_dim(block_table, ctx_index * local_blocks, local_blocks, 1)
    offsets = jnp.arange(BLK, dtype=jnp.int32)
    own_place = (own_blocks[:, :, None] * BLK + offsets[None, None, :]).reshape(
        group_count, local_rows
    )
    key_place = (block_table[:, :, None] * BLK + offsets[None, None, :]).reshape(
        group_count, group_rows
    )
    flat_tokens = tokens.reshape(group_count * local_rows, width).astype(jnp.float32)
    grad_values = cotangent.reshape(group_count * local_rows, width).astype(jnp.float32)
    normed, norm_pull = jax.vjp(
        layer_norm, flat_tokens, ln_gain.astype(jnp.float32), ln_bias.astype(jnp.float32)
    )
    normed_low = normed.astype(jnp.bfloat16)
    qkv_weight, fc1_weight, dense_weight, fc2_weight = (
        lax.all_gather(w_qkv, "ctx", axis=2, tiled=True),
        lax.all_gather(w_fc1, "ctx", axis=1, tiled=True),
        lax.all_gather(w_dense, "ctx", axis=0, tiled=True),
        lax.all_gather(w_fc2, "ctx", axis=0, tiled=True),
    )
    grad_rows = cotangent.reshape(-1, width)
    row_count = normed_low.shape[0]
    query_rows = row_count // group_count
    qkv_cols = qkv_weight.shape[2]
    head_total = qkv_cols // head_dim
    pieces = (
        lax.all_gather(qkv_weight, "fsdp", axis=0, tiled=True),
        lax.all_gather(fc1_weight, "fsdp", axis=0, tiled=True),
    )
    piece_rows = pieces[0].shape[0]
    columns = normed_low
    projected = product(columns, pieces[0].reshape(piece_rows, -1))
    expanded = product(columns, pieces[1])
    qkv_bias = b_qkv.reshape(3, width).reshape(-1)
    projected = projected + qkv_bias.astype(jnp.float32)
    expanded = expanded + b_fc1.astype(jnp.float32)
    angles = (
        position_of(own_place.reshape(row_count)).astype(jnp.float32)[:, None]
        * frequencies()[None, :]
    )

    def turn(pair_values):
        return rotate(pair_values, angles, head_dim)

    turned, turn_pull = jax.vjp(turn, projected[:, : 2 * qkv_cols])
    query_low = turned[:, :qkv_cols].astype(jnp.bfloat16).reshape(group_count, query_rows, qkv_cols)
    key_low = turned[:, qkv_cols:].astype(jnp.bfloat16).reshape(group_count, query_rows, qkv_cols)
    value_low = (
        projected[:, 2 * qkv_cols :].astype(jnp.bfloat16).reshape(group_count, query_rows, qkv_cols)
    )
    key_all, value_all = (
        lax.all_gather(key_low, "ctx", axis=1, tiled=True),
        lax.all_gather(value_low, "ctx", axis=1, tiled=True),
    )
    heads_each = min(8, head_total)
    block_count = query_rows // query_rows

    def split_heads(values):
        shaped = values.reshape(
            values.shape[0], values.shape[1], head_total // heads_each, heads_each, head_dim
        )
        return jnp.moveaxis(shaped, 2, 0)

    def join_heads(values):
        moved = jnp.moveaxis(values, 0, 2)
        return moved.reshape(moved.shape[0], moved.shape[1], qkv_cols)

    def split_rows(values):
        shaped = values.reshape((values.shape[0], block_count, query_rows) + values.shape[2:])
        return jnp.moveaxis(shaped, 1, 0)

    def join_rows(values):
        moved = jnp.moveaxis(values, 0, 1)
        return moved.reshape((moved.shape[0], query_rows) + moved.shape[3:])

    place_blocks = split_rows(own_place)

    def scores_of(query_part, key_part, place_part):
        allowed = visible(place_part[:, :, None], key_place[:, None, :])
        raw = (
            jnp.einsum("gqhe,gkhe->ghqk", query_part, key_part, preferred_element_type=jnp.float32)
            * scale
        )
        return (jnp.where(allowed[:, None], raw, -1e30), allowed)

    def forward_heads(operands):
        query_part, key_part, value_part = operands

        def forward_one_block(items):
            query_block, place_block = items
            scores, allowed = scores_of(query_block, key_part, place_block)
            top_score = jnp.max(scores, axis=-1, keepdims=True)
            summed_exp = jnp.sum(jnp.exp(scores - top_score), axis=-1, keepdims=True)
            log_total = top_score + jnp.log(summed_exp)
            weights = jnp.where(allowed[:, None], jnp.exp(scores - log_total), 0.0)
            mixed = jnp.einsum(
                "ghqk,gkhe->gqhe",
                weights.astype(jnp.bfloat16),
                value_part,
                preferred_element_type=jnp.float32,
            )
            return (mixed, log_total)

        mixed, log_total = lax.map(forward_one_block, (split_rows(query_part), place_blocks))
        return (join_rows(mixed), log_total)

    attended, log_totals = lax.map(
        forward_heads, (split_heads(query_low), split_heads(key_all), split_heads(value_all))
    )
    attended_low = join_heads(attended).reshape(row_count, qkv_cols).astype(jnp.bfloat16)
    activated, gelu_pull = jax.vjp(gelu_tanh, expanded)
    activated_low = activated.astype(jnp.bfloat16)
    pieces = (
        lax.all_gather(dense_weight, "fsdp", axis=1, tiled=True),
        lax.all_gather(fc2_weight, "fsdp", axis=1, tiled=True),
    )
    part_sum = product(attended_low, pieces[0]) + product(activated_low, pieces[1])
    summed = part_sum
    result = flat_tokens + summed + b_dense.astype(jnp.float32) + b_fc2.astype(jnp.float32)
    output = result.astype(jnp.bfloat16).reshape(group_count, local_rows, width)
    out_bias_grad = jnp.sum(grad_values, axis=0)
    out_each = dense_each + hidden_each

    def out_block(index):
        attended_part = lax.dynamic_slice_in_dim(attended_low, index * dense_each, dense_each, 1)
        activated_part = lax.dynamic_slice_in_dim(
            activated_low, index * hidden_each, hidden_each, 1
        )
        return jnp.concatenate(
            [contract_rows(attended_part, grad_rows), contract_rows(activated_part, grad_rows)],
            axis=0,
        )

    blocks = lax.map(
        out_block, jnp.arange(out_each * lax.axis_size("ctx") // out_each, dtype=jnp.int32)
    )
    out_local = lax.psum_scatter(
        blocks.reshape(out_each * lax.axis_size("ctx"), width).astype(jnp.bfloat16),
        "ctx",
        scatter_dimension=0,
        tiled=True,
    )
    pieces = (
        lax.all_gather(dense_weight, "fsdp", axis=1, tiled=True),
        lax.all_gather(fc2_weight, "fsdp", axis=1, tiled=True),
    )
    columns = grad_rows
    attended_grad = contract_cols(columns, pieces[0])
    activated_grad = contract_cols(columns, pieces[1])
    attended_grad_low = attended_grad.astype(jnp.bfloat16).reshape(
        group_count, query_rows, qkv_cols
    )
    expanded_grad = gelu_pull(activated_grad)[0].astype(jnp.bfloat16)

    def backward_heads(operands):
        query_part, key_part, value_part, grad_part, log_total = operands

        def backward_one_block(carry, items):
            query_block, grad_block, place_block, log_block = items
            scores, allowed = scores_of(query_block, key_part, place_block)
            weights = jnp.where(allowed[:, None], jnp.exp(scores - log_block), 0.0)
            weight_grad = jnp.einsum(
                "gqhe,gkhe->ghqk", grad_block, value_part, preferred_element_type=jnp.float32
            )
            inner = jnp.sum(weights * weight_grad, axis=-1, keepdims=True)
            score_grad = (weights * (weight_grad - inner)).astype(jnp.bfloat16)
            query_grad = (
                jnp.einsum(
                    "ghqk,gkhe->gqhe", score_grad, key_part, preferred_element_type=jnp.float32
                )
                * scale
            )
            key_grad = (
                carry[0]
                + jnp.einsum(
                    "ghqk,gqhe->gkhe", score_grad, query_block, preferred_element_type=jnp.float32
                )
                * scale
            )
            value_grad = carry[1] + jnp.einsum(
                "ghqk,gqhe->gkhe",
                weights.astype(jnp.bfloat16),
                grad_block,
                preferred_element_type=jnp.float32,
            )
            return ((key_grad, value_grad), query_grad)

        zero_grad = jnp.zeros(key_part.shape, jnp.float32)
        sums, query_grad = lax.scan(
            backward_one_block,
            (zero_grad, zero_grad),
            (split_rows(query_part), split_rows(grad_part), place_blocks, log_total),
        )
        return (join_rows(query_grad), sums[0], sums[1])

    query_grads, key_grads, value_grads = lax.map(
        backward_heads,
        (
            split_heads(query_low),
            split_heads(key_all),
            split_heads(value_all),
            split_heads(attended_grad_low),
            log_totals,
        ),
    )
    key_full = join_heads(key_grads)
    value_full = join_heads(value_grads)
    key_mine, value_mine = (
        lax.psum_scatter(
            key_full.astype(jnp.bfloat16), "ctx", scatter_dimension=1, tiled=True
        ).astype(jnp.float32),
        lax.psum_scatter(
            value_full.astype(jnp.bfloat16), "ctx", scatter_dimension=1, tiled=True
        ).astype(jnp.float32),
    )
    pair_grad = jnp.concatenate(
        [
            join_heads(query_grads).reshape(row_count, qkv_cols),
            key_mine.reshape(row_count, qkv_cols),
        ],
        axis=1,
    )
    turned_back = turn_pull(pair_grad)[0]
    projected_grad = jnp.concatenate(
        [turned_back, value_mine.reshape(row_count, qkv_cols)], axis=1
    ).astype(jnp.bfloat16)
    grad_by_part = projected_grad.reshape(row_count, 3, qkv_cols)

    def in_block(index):
        qkv_part = lax.dynamic_slice_in_dim(
            grad_by_part, index * dense_each, dense_each, 2
        ).reshape(row_count, 3 * dense_each)
        hidden_part = lax.dynamic_slice_in_dim(expanded_grad, index * hidden_each, hidden_each, 1)
        return jnp.concatenate(
            [contract_rows(normed_low, qkv_part), contract_rows(normed_low, hidden_part)], axis=1
        )

    span_rows = width * lax.axis_size("ctx")
    blocks = lax.map(in_block, jnp.arange(span_rows // width, dtype=jnp.int32))
    in_local = lax.psum_scatter(
        blocks.reshape(span_rows, -1).astype(jnp.bfloat16), "ctx", scatter_dimension=0, tiled=True
    )
    qkv_bias_part = jnp.sum(projected_grad.astype(jnp.float32), axis=0).reshape(3, qkv_cols)
    qkv_bias_grad = qkv_bias_part.reshape(-1)
    fc1_bias_part = jnp.sum(expanded_grad.astype(jnp.float32), axis=0)
    pieces = (
        lax.all_gather(qkv_weight, "fsdp", axis=0, tiled=True),
        lax.all_gather(fc1_weight, "fsdp", axis=0, tiled=True),
    )
    piece_rows = pieces[0].shape[0]
    part_sum = contract_cols(projected_grad, pieces[0].reshape(piece_rows, -1)) + contract_cols(
        expanded_grad, pieces[1]
    )
    out_share, in_share = (
        lax.psum_scatter(out_local, "fsdp", scatter_dimension=1, tiled=True).astype(jnp.float32),
        lax.psum_scatter(in_local, "fsdp", scatter_dimension=0, tiled=True).astype(jnp.float32),
    )
    d_w_dense = out_share[:dense_each]
    d_w_fc2 = out_share[dense_each:]
    d_w_qkv = in_share[:, : 3 * dense_each].reshape(-1, 3, dense_each)
    d_w_fc1 = in_share[:, 3 * dense_each :]
    token_grad_norm, gain_grad, shift_grad = norm_pull(part_sum)
    d_tokens = (
        (grad_values + token_grad_norm).astype(jnp.bfloat16).reshape(group_count, local_rows, width)
    )
    gain_sum, shift_sum, qkv_bias_sum, out_bias_sum, fc1_bias_sum = lax.psum(
        (gain_grad, shift_grad, qkv_bias_grad, out_bias_grad, fc1_bias_part), ("ctx", "fsdp")
    )
    return (
        output,
        d_tokens,
        gain_sum,
        shift_sum,
        d_w_qkv,
        qkv_bias_sum,
        d_w_dense,
        out_bias_sum,
        d_w_fc1,
        fc1_bias_sum,
        d_w_fc2,
        out_bias_sum,
    )


def solution(mesh):
    in_specs = (
        P("fsdp", "ctx", None),
        P("fsdp", "ctx", None),
        P("fsdp", None),
        P(),
        P(),
        P("fsdp", None, "ctx"),
        P(),
        P("ctx", "fsdp"),
        P(),
        P("fsdp", "ctx"),
        P(),
        P("ctx", "fsdp"),
        P(),
    )
    out_specs = (
        P("fsdp", "ctx", None),
        P("fsdp", "ctx", None),
        P(),
        P(),
        P("fsdp", None, "ctx"),
        P(),
        P("ctx", "fsdp"),
        P(),
        P("fsdp", "ctx"),
        P(),
        P("ctx", "fsdp"),
        P(),
    )
    return jax.shard_map(shards, mesh=mesh, in_specs=in_specs, out_specs=out_specs, check_vma=False)
```

profile of v0, /device:TPU:0, one launch (start us, length us, event | category | flops | bytes accessed | tf_op | source)
XLA Modules:
  0.0 3172.5 jit_solution(17487051022101723926)
XLA Ops:
  10.5 46.7 %all-gather.13.cloned.1.call-done = bf16[256,3,2048]{0,2,1:T(8,128)(2,1)} async-done(((bf16[256,3,512]{0,2,1:T(8,128)(2,1)}), bf16[256,3,2048]{0,2,1:T(8,128)(2,1)}) %all-gather.13.cloned.1.call-update) | async-done | bytes 3145744 | tf_op jit(solution)/shard_map/all_gather | solution.py:129
  87.7 220.7 %all-gather.15.cloned.1.call-done = bf16[2048,3,2048]{0,2,1:T(8,128)(2,1)} async-done(((bf16[256,3,2048]{0,2,1:T(8,128)(2,1)}), bf16[2048,3,2048]{0,2,1:T(8,128)(2,1)}) %all-gather.15.cloned.1.call-update) | async-done | bytes 25165840 | tf_op jit(solution)/shard_map/all_gather | solution.py:140
  369.6 46.2 %all-gather.25.cloned.1.call-done = bf16[8192,256]{1,0:T(8,128)(2,1)} async-done(((bf16[2048,256]{1,0:T(8,128)(2,1)}), bf16[8192,256]{1,0:T(8,128)(2,1)}) %all-gather.25.cloned.1.call-update) | async-done | bytes 4194320 | tf_op jit(solution)/shard_map/all_gather | solution.py:132
  416.3 83.4 %all-gather.19.cloned.1.call-done = bf16[2048,2048]{1,0:T(8,128)(2,1)} async-done(((bf16[2048,256]{1,0:T(8,128)(2,1)}), bf16[2048,2048]{1,0:T(8,128)(2,1)}) %all-gather.19.cloned.1.call-update) | async-done | bytes 8388624 | tf_op jit(solution)/shard_map/all_gather | solution.py:227
  512.0 93.4 %all-gather.29.cloned.1.call-done = bf16[2560,2048]{1,0:T(8,128)(2,1)} async-done(((bf16[640,2048]{1,0:T(8,128)(2,1)}), bf16[2560,2048]{1,0:T(8,128)(2,1)}) %all-gather.29.cloned.1.call-update) | async-done | bytes 10485776 | tf_op jit(solution)/shard_map/all_gather | solution.py:166
  619.7 92.8 %all-gather.31.cloned.1.call-done = bf16[2560,2048]{0,1:T(8,128)(2,1)} async-done(((bf16[640,2048]{0,1:T(8,128)(2,1)}), bf16[2560,2048]{0,1:T(8,128)(2,1)}) %all-gather.31.cloned.1.call-update) | async-done | bytes 10485776 | tf_op jit(solution)/shard_map/all_gather | solution.py:165
  712.4 278.3 %while.71 = (s32[]{:T(128)}, bf16[4,1,640,8,64]{2,4,3,1,0:T(8,128)(2,1)}, f32[4,1,1,8,640,1]{4,3,5,2,1,0:T(8,128)S(1)}, bf16[4,1,2560,8,64]{2,4,3,1,0:T(8,128)(2...) while((s32[]{:T(128)}, ...), condition=%wide.region_5.6_spmd.clone.clone, body=%wide.region_2.5_spmd.clone.sunk.clone | while | flops 3520983552 | bytes 171326496 | solution.py:220
  990.7 649.2 %while.72 = (s32[]{:T(128)}, f32[4,1,640,8,64]{2,4,3,1,0:T(8,128)}, bf16[4,1,2560,8,64]{2,4,3,1,0:T(8,128)(2,1)}, bf16[4,1,2560,8,64]{2,4,3,1,0:T(8,128)(2,1)}, ...) while((s32[]{:T(128)}, f32[4,1,640,8,64]{2,4,3,1,0:T(8,128)}, ...), condition=%wide.region_8.9_spmd.clone.clone, body=%wide.region_6.8_spmd.clone.sunk.clone | while | flops 8529572352 | bytes 418994240 | solution.py:309
  1020.2 45.3 %multiply_reduce_fusion.3 = (f32[8,640]{1,0:T(8,128)S(1)}, f32[8,640,2560]{2,1,0:T(8,128)}) fusion(f32[8,640,2560]{2,1,0:T(8,128)} %fusion.238, f32[8,640]{1,0:T(8,128)S(1)} %dynamic-slice_bitcast_fusion.3, bf16[4,1,2560,8,64]{2,4,3,1,0:T(8,128)(2,1)} %get-tuple-element.1049, s32[]{:T(128)} %get-tuple-element.1034, ...), kind=kOutput, calls=%fused_computation.66.clone.1.clone | convolution fusion | flops 1756359680 | bytes 109814784 | tf_op jit(solution)/shard_map/while/body/eval_jaxpr/while/body/eval_jaxpr/gqhe,gkhe->ghqk/dot_general | solution.py:194
  1065.6 42.1 %multiply_convert_fusion.4 = bf16[8,640,2560]{2,1,0:T(8,128)(2,1)} fusion(f32[8,640,2560]{2,1,0:T(8,128)} %get-tuple-element.985, f32[8,640,2560]{2,1,0:T(8,128)} %fusion.238, f32[8,640]{1,0:T(8,128)S(1)} %get-tuple-element.986), kind=kLoop, calls=%fused_computation.65.clone.1.clone | loop fusion | flops 39321600 | bytes 131092480 | tf_op jit(solution)/shard_map/while/body/eval_jaxpr/while/body/eval_jaxpr/convert_element_type | solution.py:279
  1182.8 44.9 %multiply_reduce_fusion.3 = (f32[8,640]{1,0:T(8,128)S(1)}, f32[8,640,2560]{2,1,0:T(8,128)}) fusion(f32[8,640,2560]{2,1,0:T(8,128)} %fusion.238, f32[8,640]{1,0:T(8,128)S(1)} %dynamic-slice_bitcast_fusion.3, bf16[4,1,2560,8,64]{2,4,3,1,0:T(8,128)(2,1)} %get-tuple-element.1049, s32[]{:T(128)} %get-tuple-element.1034, ...), kind=kOutput, calls=%fused_computation.66.clone.1.clone | convolution fusion | flops 1756359680 | bytes 109814784 | tf_op jit(solution)/shard_map/while/body/eval_jaxpr/while/body/eval_jaxpr/gqhe,gkhe->ghqk/dot_general | solution.py:194
  1227.7 42.2 %multiply_convert_fusion.4 = bf16[8,640,2560]{2,1,0:T(8,128)(2,1)} fusion(f32[8,640,2560]{2,1,0:T(8,128)} %get-tuple-element.985, f32[8,640,2560]{2,1,0:T(8,128)} %fusion.238, f32[8,640]{1,0:T(8,128)S(1)} %get-tuple-element.986), kind=kLoop, calls=%fused_computation.65.clone.1.clone | loop fusion | flops 39321600 | bytes 131092480 | tf_op jit(solution)/shard_map/while/body/eval_jaxpr/while/body/eval_jaxpr/convert_element_type | solution.py:279
  1344.2 44.8 %multiply_reduce_fusion.3 = (f32[8,640]{1,0:T(8,128)S(1)}, f32[8,640,2560]{2,1,0:T(8,128)}) fusion(f32[8,640,2560]{2,1,0:T(8,128)} %fusion.238, f32[8,640]{1,0:T(8,128)S(1)} %dynamic-slice_bitcast_fusion.3, bf16[4,1,2560,8,64]{2,4,3,1,0:T(8,128)(2,1)} %get-tuple-element.1049, s32[]{:T(128)} %get-tuple-element.1034, ...), kind=kOutput, calls=%fused_computation.66.clone.1.clone | convolution fusion | flops 1756359680 | bytes 109814784 | tf_op jit(solution)/shard_map/while/body/eval_jaxpr/while/body/eval_jaxpr/gqhe,gkhe->ghqk/dot_general | solution.py:194
  1389.0 41.6 %multiply_convert_fusion.4 = bf16[8,640,2560]{2,1,0:T(8,128)(2,1)} fusion(f32[8,640,2560]{2,1,0:T(8,128)} %get-tuple-element.985, f32[8,640,2560]{2,1,0:T(8,128)} %fusion.238, f32[8,640]{1,0:T(8,128)S(1)} %get-tuple-element.986), kind=kLoop, calls=%fused_computation.65.clone.1.clone | loop fusion | flops 39321600 | bytes 131092480 | tf_op jit(solution)/shard_map/while/body/eval_jaxpr/while/body/eval_jaxpr/convert_element_type | solution.py:279
  1504.3 44.7 %multiply_reduce_fusion.3 = (f32[8,640]{1,0:T(8,128)S(1)}, f32[8,640,2560]{2,1,0:T(8,128)}) fusion(f32[8,640,2560]{2,1,0:T(8,128)} %fusion.238, f32[8,640]{1,0:T(8,128)S(1)} %dynamic-slice_bitcast_fusion.3, bf16[4,1,2560,8,64]{2,4,3,1,0:T(8,128)(2,1)} %get-tuple-element.1049, s32[]{:T(128)} %get-tuple-element.1034, ...), kind=kOutput, calls=%fused_computation.66.clone.1.clone | convolution fusion | flops 1756359680 | bytes 109814784 | tf_op jit(solution)/shard_map/while/body/eval_jaxpr/while/body/eval_jaxpr/gqhe,gkhe->ghqk/dot_general | solution.py:194
  1639.9 42.3 %copy.60 = bf16[1,2560,2048]{2,0,1:T(2,128)(2,1)} copy(bf16[1,2560,2048]{1,2,0:T(8,128)(2,1)} %bitcast.366) | data formatting | bytes 20971520
  1698.5 42.9 %copy.62 = bf16[1,2560,2048]{2,0,1:T(2,128)(2,1)} copy(bf16[1,2560,2048]{1,2,0:T(8,128)(2,1)} %bitcast.367) | data formatting | bytes 20971520
  1796.7 110.1 %while.70 = (s32[]{:T(128)}, bf16[4,2560,2048]{2,1,0:T(8,128)(2,1)}, s32[4]{0:T(128)S(1)}, bf16[640,2048]{0,1:T(8,128)(2,1)}, bf16[640,2048]{1,0:T(8,128)(2,1)S(...) while((s32[]{:T(128)}, bf16[4,2560,2048]{2,1,0:T(8,128)(2,1)}, s32[4]{0:T(128)S(1)}, ...), condition=%wide.region_24.25_spmd.clone, body=%wide.region_23.24_spmd.sunk.clone | while | flops 6731857920 | bytes 39977668 | solution.py:247
  1906.9 45.1 %convert_reduce_fusion = (f32[8192]{0:T(1024)}, bf16[640,8192]{1,0:T(8,128)(2,1)}) fusion(bf16[8192,2048]{1,0:T(8,128)(2,1)} %all-gather.27.cloned.1.call-done, bf16[1,640,2048]{2,1,0:T(8,128)(2,1)S(1)} %bitcast.373, f32[640,8192]{1,0:T(8,128)} %get-tuple-element.675, f32[8192]{0:T(1024)S(1)} %convert_element_type.176), kind=kOutput, calls=%fused_computation.132 | convolution fusion | flops 21616386048 | bytes 67698688 | tf_op jit(solution)/shard_map/dot_general | solution.py:84
  2017.2 148.8 %while.69 = (s32[]{:T(128)}, bf16[4,2048,3584]{1,2,0:T(8,128)(2,1)}, s32[4]{0:T(128)S(1)}, bf16[640,3,2048]{0,2,1:T(8,128)(2,1)}, bf16[640,2048]{1,0:T(8,128)(2,...) while((s32[]{:T(128)}, bf16[4,2048,3584]{1,2,0:T(8,128)(2,1)}, s32[4]{0:T(128)S(1)}, ...), condition=%wide.region_18.19_spmd.clone, body=%wide.region_17.18_spmd.sunk.clone | while | flops 9424601088 | bytes 93455112 | solution.py:352
  2273.6 490.2 %reduce-scatter.13.cloned.1.call-done = bf16[2048,3584]{0,1:T(8,128)(2,1)} async-done(((bf16[8192,3584]{0,1:T(8,128)(2,1)}), bf16[2048,3584]{0,1:T(8,128)(2,1)}) %reduce-scatter.13.cloned.1.call-update) | async-done | bytes 14680080 | tf_op jit(solution)/shard_map/reduce_scatter | solution.py:353
  2800.9 92.6 %all-reduce.7.cloned.1.call-done = (f32[2048]{0:T(1024)}, f32[2048]{0:T(1024)}, f32[6144]{0:T(1024)}, f32[2048]{0:T(1024)}, f32[8192]{0:T(1024)}) async-done(((f32[2048]{0:T(1024)}, f32[2048]{0:T(1024)}, f32[6144]{0:T(1024)}, f32[2048]{0:T(1024)}, f32[8192]{0:T(1024)}), (f32[2048]{0:T(1024)}, f32[2048]{0:T(1024)}, f32[6144]{0:T(1024)}, f32[2048]{0:T(1024)}, f32[8192]{0:T(1024)})) %all-reduce.7.cloned.1.call-update) | async-done | bytes 81936 | tf_op jit(solution)/shard_map/psum | solution.py:379
  2893.5 113.0 %reduce-scatter.17.cloned.1.call-done = bf16[2560,256]{1,0:T(8,128)(2,1)} async-done(((bf16[2560,2048]{1,0:T(8,128)(2,1)}), bf16[2560,256]{1,0:T(8,128)(2,1)}) %reduce-scatter.17.cloned.1.call-update) | async-done | bytes 1310736 | tf_op jit(solution)/shard_map/reduce_scatter | solution.py:368
  3011.0 145.1 %reduce-scatter.15.cloned.1.call-done = bf16[256,3584]{0,1:T(8,128)(2,1)} async-done(((bf16[2048,3584]{0,1:T(8,128)(2,1)}), bf16[256,3584]{0,1:T(8,128)(2,1)}) %reduce-scatter.15.cloned.1.call-update) | async-done | bytes 1835024 | tf_op jit(solution)/shard_map/reduce_scatter | solution.py:369
  (381 shorter events, 1286.1 us)
Async XLA Ops:
  7.2 78.6 %copy-start.34 = (bf16[2048]{0:T(1024)(128)(2,1)S(1)}, bf16[2048]{0:T(1024)(128)(2,1)}, u32[]{:S(2)}) copy-start(bf16[2048]{0:T(1024)(128)(2,1)} %param.25) | copy-start | bytes 12292
  7.2 78.6 %copy-start.30 = (bf16[6144]{0:T(1024)(128)(2,1)S(1)}, bf16[6144]{0:T(1024)(128)(2,1)}, u32[]{:S(2)}) copy-start(bf16[6144]{0:T(1024)(128)(2,1)} %param.27) | copy-start | bytes 36868
  7.2 78.6 %copy-start = (bf16[1,640,2048]{2,1,0:T(8,128)(2,1)S(1)}, bf16[1,640,2048]{2,1,0:T(8,128)(2,1)}, u32[]{:S(2)}) copy-start(bf16[1,640,2048]{2,1,0:T(8,128)(2,1)} %param.21) | copy-start | bytes 7864324
  7.2 50.0 %all-gather.13.cloned.1.call-start = ((), (), s32[]{:S(2)}) async-start(), calls=%async_computation.6 | async-start | bytes 3932160 | tf_op jit(solution)/shard_map/all_gather | solution.py:129
  9.7 76.0 %all-gather.17.cloned.1.call-start = ((), (), s32[]{:S(2)}) async-start(), calls=%async_computation.8 | async-start | bytes 1310720 | tf_op jit(solution)/shard_map/all_gather | solution.py:131
  10.5 298.0 %all-gather.15.cloned.1.call-start = ((), (), s32[]{:S(2)}) async-start(), calls=%async_computation.7 | async-start | bytes 28311552 | tf_op jit(solution)/shard_map/all_gather | solution.py:140
  57.2 309.8 %all-gather.21.cloned.1.call-start = ((), (), s32[]{:S(2)}) async-start(), calls=%async_computation.10 | async-start | bytes 5242880 | tf_op jit(solution)/shard_map/all_gather | solution.py:130
  57.8 358.0 %all-gather.25.cloned.1.call-start = ((), (), s32[]{:S(2)}) async-start(), calls=%async_computation.12 | async-start | bytes 5242880 | tf_op jit(solution)/shard_map/all_gather | solution.py:132
  58.4 441.4 %all-gather.19.cloned.1.call-start = ((), (), s32[]{:S(2)}) async-start(), calls=%async_computation.9 | async-start | bytes 9437184 | tf_op jit(solution)/shard_map/all_gather | solution.py:227
  85.7 519.8 %all-gather.29.cloned.1.call-start = ((), (), s32[]{:S(2)}) async-start(), calls=%async_computation.17 | async-start | bytes 13107200 | tf_op jit(solution)/shard_map/all_gather | solution.py:166
  85.8 245.3 %copy-start.13 = (f32[2048]{0:T(1024)}, f32[2048]{0:T(1024)S(1)}, u32[]{:S(2)}) copy-start(f32[2048]{0:T(1024)S(1)} %convert_element_type.166) | copy-start | bytes 24580
  85.8 245.3 %copy-start.24 = (f32[2048]{0:T(1024)}, f32[2048]{0:T(1024)S(1)}, u32[]{:S(2)}) copy-start(f32[2048]{0:T(1024)S(1)} %convert_element_type.167) | copy-start | bytes 24580
  86.3 244.8 %copy-start.16 = (f32[640]{0:T(1024)}, f32[640]{0:T(1024)S(1)}, u32[]{:S(2)}) copy-start(f32[640]{0:T(1024)S(1)} %broadcast_multiply_fusion) | copy-start | bytes 7684
  87.7 243.4 %copy-start.19 = (f32[640]{0:T(1024)}, f32[640]{0:T(1024)S(1)}, u32[]{:S(2)}) copy-start(f32[640]{0:T(1024)S(1)} %fusion.130) | copy-start | bytes 7684
  335.5 376.9 %all-gather.31.cloned.1.call-start = ((), (), s32[]{:S(2)}) async-start(), calls=%async_computation.18 | async-start | bytes 13107200 | tf_op jit(solution)/shard_map/all_gather | solution.py:165
  367.0 1395.3 %all-gather.23.cloned.1.call-start = ((), (), s32[]{:S(2)}) async-start(), calls=%async_computation.11 | async-start | bytes 37748736 | tf_op jit(solution)/shard_map/all_gather | solution.py:141
  367.7 1539.2 %all-gather.27.cloned.1.call-start = ((), (), s32[]{:S(2)}) async-start(), calls=%async_computation.13 | async-start | bytes 37748736 | tf_op jit(solution)/shard_map/all_gather | solution.py:228
  415.8 1536.2 %reduce-scatter.19.cloned.1.call-start = ((), (), s32[]{:S(2)}) async-start(), calls=%async_computation.19 | async-start | bytes 13107200
  1698.5 272.9 %reduce-scatter.21.cloned.1.call-start = ((), (), s32[]{:S(2)}) async-start(), calls=%async_computation.20 | async-start | bytes 13107200
  1758.0 515.1 %reduce-scatter.23.cloned.1.call-start = ((), (), s32[]{:S(2)}) async-start(), calls=%async_computation.21 | async-start | bytes 52428800
  1906.8 856.9 %reduce-scatter.13.cloned.1.call-start = ((), (), s32[]{:S(2)}) async-start(), calls=%async_computation.14 | async-start | bytes 73400320 | tf_op jit(solution)/shard_map/reduce_scatter | solution.py:353
  2206.6 687.0 %all-reduce.7.cloned.1.call-start = ((), (), s32[]{:S(2)}) async-start(), calls=%async_computation.22 | async-start | bytes 163840 | tf_op jit(solution)/shard_map/psum | solution.py:379
  2273.0 733.5 %reduce-scatter.17.cloned.1.call-start = ((), (), s32[]{:S(2)}) async-start(), calls=%async_computation.16 | async-start | bytes 11796480 | tf_op jit(solution)/shard_map/reduce_scatter | solution.py:368
  2273.6 882.5 %reduce-scatter.15.cloned.1.call-start = ((), (), s32[]{:S(2)}) async-start(), calls=%async_computation.15 | async-start | bytes 16515072 | tf_op jit(solution)/shard_map/reduce_scatter | solution.py:369
  (46 other events, 544.7 us)
Sparse Core Ops, SparseCore 0:
  10.5 46.6 all-gather.12
  59.0 26.6 all-gather.16
  87.3 221.1 all-gather.14
  310.2 51.2 all-gather.20
  363.1 52.6 all-gather.24
  417.2 82.4 all-gather.18
  502.2 103.2 all-gather.28
  607.3 105.0 all-gather.30
  714.0 288.6 all-gather.22
  1004.1 288.6 all-gather.26
  1698.6 104.0 reduce-scatter.18
  1805.6 103.5 reduce-scatter.20
  1912.3 356.3 reduce-scatter.22
  2271.9 491.8 reduce-scatter.12
  2771.2 122.2 all-reduce.6
  2895.7 110.7 reduce-scatter.16
  3008.6 147.3 reduce-scatter.14
where the time goes:
time: 3190 us; the launch traced here: 3170 us
  waiting for transfers between devices  1450 us (45%)
  matrix products  980 us (31%)
  other arithmetic  435 us (14%)
  local copies, waits for them, and re-layouts  276 us (9%)
    reduce_scatter x1, waiting for transfers between devices, shards(): lax.psum_scatter(blocks.reshape(span_rows, -1).astype(jnp.bfloat16), 'ctx...  490 us
    dot_general x8, matrix products, scores_of(): jnp.einsum('gqhe,gkhe->ghqk', query_part, key_part, preferred_element_typ...  274 us
    all_gather x1, waiting for transfers between devices, shards(): lax.all_gather(qkv_weight, 'fsdp', axis=0, tiled=True)  221 us
    convert_element_type x4, other arithmetic, backward_one_block(): score_grad = (weights * (weight_grad - inner)).astype(jnp.bfloat16)  168 us
    unnamed x99, local copies, waits for them, and re-layouts  165 us
    reduce_scatter x1, waiting for transfers between devices, shards(): lax.psum_scatter(in_local, 'fsdp', scatter_dimension=0, tiled=True)  145 us
    dot_general x16, matrix products, contract_rows(): lax.dot_general(left, right, (((0,), (0,)), ((), ())), preferred_element_...  122 us
    reduce_scatter x1, waiting for transfers between devices, shards(): lax.psum_scatter(out_local, 'fsdp', scatter_dimension=1, tiled=True)  113 us
  transfers between devices with their start and end apart: 17, of which 11 were waited for; matrix products, arithmetic and copies ran while one was open for 53% of the time, Pallas kernels for 0%

commit v1 on v0

v1 whole, which is shorter than its diff:
```python
import functools
import math

import jax
import jax.numpy as jnp
from jax import lax
from jax.experimental import pallas as pl
from jax.experimental.pallas import tpu as pltpu
from jax.sharding import PartitionSpec as P

HEADS = 32
ROT = 32
PROMPT = 2048
CLEN = 256
BLK = 64
CHUNK = 256
LANES = 128
NT = (((1,), (1,)), ((), ()))
NN = (((1,), (0,)), ((), ()))
TN = (((0,), (0,)), ((), ()))
LOW = jnp.bfloat16
WIDE = jnp.float32


def dot(left, right, dims):
    return lax.dot_general(left, right, dims, preferred_element_type=WIDE)


def attention_kernel(where_ref, *refs, chunk, chunks, full_chunks, blk, pairs, scale):
    per = chunk // blk
    q_in, k_in, v_in, g_in = (refs[n * per : (n + 1) * per] for n in range(4))
    cos_ref, up_ref, down_ref, att_hbm, grad_hbm = refs[4 * per : 4 * per + 5]
    (
        keys,
        values,
        keys_t,
        values_t,
        probs,
        key_sum,
        value_sum,
        att_stage,
        query_stage,
        key_stage,
        value_stage,
        row_sem,
        col_sem,
    ) = refs[4 * per + 5 :]
    pair, i = pl.program_id(0), pl.program_id(1)
    step = pair * chunks + i
    slot = lax.rem(step, 2)
    last = chunks - 1
    half = LANES // 2
    first = lax.broadcasted_iota(jnp.int32, (1, LANES), 1) < half
    width = pairs * LANES

    def columns(part):
        return pl.ds(pl.multiple_of(part * width + pair * LANES, LANES), LANES)

    def row_copies(which, at):
        stage, target = ((att_stage, att_hbm), (query_stage, grad_hbm))[which]
        return [
            pltpu.make_async_copy(
                stage.at[at, pl.ds(r * blk, blk)],
                target.at[where_ref[i * per + r], :, columns(0)],
                row_sem.at[at, which, r],
            )
            for r in range(per)
        ]

    def col_copies(n):
        block = where_ref[n]
        rows = pl.ds(pl.multiple_of(n * blk, blk), blk)
        return (
            pltpu.make_async_copy(
                key_stage.at[rows], grad_hbm.at[block, :, columns(1)], col_sem.at[0, n]
            ),
            pltpu.make_async_copy(
                value_stage.at[rows], grad_hbm.at[block, :, columns(2)], col_sem.at[1, n]
            ),
        )

    def wait_cols():
        @pl.loop(0, chunks * per)
        def _(n):
            for copy in col_copies(n):
                copy.wait()

    def load(parts):
        return jnp.concatenate([part[0] for part in parts], axis=0)

    def tables(n):
        rows = pl.ds(pl.multiple_of(n * chunk, chunk), chunk)
        return cos_ref[rows], up_ref[rows], down_ref[rows]

    quarter = ROT // 2

    def turn(x, tab):
        return (
            x * tab[0]
            + pltpu.roll(x, quarter, 1) * tab[1]
            + pltpu.roll(x, LANES - quarter, 1) * tab[2]
        )

    def turn_back(x, tab):
        return (
            x * tab[0]
            - pltpu.roll(x, quarter, 1) * tab[1]
            - pltpu.roll(x, LANES - quarter, 1) * tab[2]
        )

    @pl.when(step >= 2)
    def _():
        for which in range(2):
            for copy in row_copies(which, slot):
                copy.wait()

    tab = tables(i)
    query = (turn(load(q_in).astype(WIDE), tab) * scale).astype(LOW)
    key_new = turn(load(k_in).astype(WIDE), tab)
    value_new = load(v_in)
    grad = load(g_in)
    keys[i] = key_new.astype(LOW)
    values[i] = value_new
    keys_t[i] = key_new.T.astype(LOW)
    values_t[i] = value_new.astype(WIDE).T.astype(LOW)
    key_sum[i] = jnp.zeros((chunk, LANES), WIDE)
    value_sum[i] = jnp.zeros((chunk, LANES), WIDE)
    nothing = jnp.zeros_like(query)
    query_of = (jnp.where(first, query, nothing), jnp.where(first, nothing, query))
    grad_of = (jnp.where(first, grad, nothing), jnp.where(first, nothing, grad))
    before = jnp.minimum(i, full_chunks)
    count = before + 1
    key_row = lax.broadcasted_iota(jnp.int32, (chunk, chunk), 0)
    query_col = lax.broadcasted_iota(jnp.int32, (chunk, chunk), 1)

    def fold(values_in, how):
        return how(values_in.reshape(chunk // 8, 8, chunk), axis=0)

    def chunk_of(t):
        return jnp.where(t < before, t, i)

    def score(t, carry):
        j = chunk_of(t)
        key = keys[j]
        out = []
        for h in range(2):
            raw = dot(key, query_of[h], NT)
            raw = jnp.where(key_row <= query_col + (i - j) * chunk, raw, -1e30)
            probs[h, t] = raw
            out.append(jnp.maximum(carry[h], fold(raw, jnp.max)))
        return tuple(out)

    low_start = jnp.full((8, chunk), -1e30, WIDE)
    top = lax.fori_loop(0, count, score, (low_start, low_start))
    top = [jnp.max(x, axis=0, keepdims=True) for x in top]

    def mix(t, carry):
        j = chunk_of(t)
        out = []
        for h in range(2):
            weight = jnp.exp(probs[h, t] - top[h])
            probs[h, t] = weight
            out.append(carry[2 * h] + fold(weight, jnp.sum))
            out.append(
                carry[2 * h + 1]
                + dot(values_t[j, h * half : (h + 1) * half, :], weight.astype(LOW), NN)
            )
        return tuple(out)

    zero_row = jnp.zeros((8, chunk), WIDE)
    zero_mix = jnp.zeros((half, chunk), WIDE)
    mixed = lax.fori_loop(0, count, mix, (zero_row, zero_mix, zero_row, zero_mix))
    inverse = [1.0 / jnp.sum(mixed[2 * h], axis=0, keepdims=True) for h in range(2)]
    attended = jnp.concatenate([mixed[2 * h + 1] * inverse[h] for h in range(2)], axis=0)
    shared = grad.astype(WIDE).T * attended
    inner = [jnp.sum(shared[h * half : (h + 1) * half], axis=0, keepdims=True) for h in range(2)]
    att_stage[slot] = attended.T.astype(LOW)
    for copy in row_copies(0, slot):
        copy.start()

    def back(t, carry):
        j = chunk_of(t)
        value = values[j]
        weights, grads, out = [], [], []
        for h in range(2):
            weight = probs[h, t] * inverse[h]
            weight_grad = dot(value, grad_of[h], NT)
            score_grad = (weight * (weight_grad - inner[h])).astype(LOW)
            out.append(carry[h] + dot(keys_t[j, h * half : (h + 1) * half, :], score_grad, NN))
            weights.append(weight.astype(LOW))
            grads.append(score_grad)
        value_sum[j] += dot(weights[0], grad_of[0], NN) + dot(weights[1], grad_of[1], NN)
        key_sum[j] += dot(grads[0], query_of[0], NN) + dot(grads[1], query_of[1], NN)
        return tuple(out)

    query_grad = lax.fori_loop(0, count, back, (zero_mix, zero_mix))
    query_stage[slot] = turn_back(jnp.concatenate(query_grad, axis=0).T * scale, tab).astype(LOW)
    for copy in row_copies(1, slot):
        copy.start()

    @pl.when(i == last)
    def _():
        @pl.when(pair > 0)
        def _():
            wait_cols()

        @pl.loop(0, chunks)
        def _(n):
            rows = pl.ds(pl.multiple_of(n * chunk, chunk), chunk)
            key_stage[rows] = turn_back(key_sum[n], tables(n)).astype(LOW)
            value_stage[rows] = value_sum[n].astype(LOW)

        @pl.loop(0, chunks * per)
        def _(n):
            for copy in col_copies(n):
                copy.start()

    @pl.when(step == pairs * chunks - 1)
    def _():
        for at in range(2):
            for which in range(2):
                for copy in row_copies(which, at):
                    copy.wait()
        wait_cols()


def attention(qkv, grad, where, tabs, head_dim):
    rows, width = grad.shape
    chunk, blk = CHUNK, BLK
    per, chunks, pairs, blocks = chunk // blk, rows // chunk, width // LANES, rows // blk
    qkv_blocks = qkv.reshape(blocks, blk, 3 * width)
    grad_blocks = grad.reshape(blocks, blk, width)

    def spec(part, r):
        return pl.BlockSpec(
            (1, blk, LANES), lambda p, i, at: (at[i * per + r], 0, part * pairs + p)
        )

    in_specs = [spec(part, r) for part in range(3) for r in range(per)]
    in_specs += [spec(0, r) for r in range(per)]
    in_specs += [pl.BlockSpec((rows, LANES), lambda p, i, at: (0, 0))] * 3
    operands = [qkv_blocks] * (3 * per) + [grad_blocks] * per + list(tabs)
    kernel = functools.partial(
        attention_kernel,
        chunk=chunk,
        chunks=chunks,
        full_chunks=PROMPT // chunk,
        blk=blk,
        pairs=pairs,
        scale=1.0 / math.sqrt(head_dim),
    )
    low_scratch = pltpu.VMEM((chunks, chunk, LANES), LOW)
    low_turned = pltpu.VMEM((chunks, LANES, chunk), LOW)
    wide_scratch = pltpu.VMEM((chunks, chunk, LANES), WIDE)
    attended, grads = pl.pallas_call(
        kernel,
        out_shape=(
            jax.ShapeDtypeStruct((blocks, blk, width), LOW),
            jax.ShapeDtypeStruct((blocks, blk, 3 * width), LOW),
        ),
        grid_spec=pltpu.PrefetchScalarGridSpec(
            num_scalar_prefetch=1,
            grid=(pairs, chunks),
            in_specs=in_specs,
            out_specs=[pl.BlockSpec(memory_space=pl.ANY)] * 2,
            scratch_shapes=[
                low_scratch,
                low_scratch,
                low_turned,
                low_turned,
                pltpu.VMEM((2, PROMPT // chunk + 1, chunk, chunk), WIDE),
                wide_scratch,
                wide_scratch,
                pltpu.VMEM((2, chunk, LANES), LOW),
                pltpu.VMEM((2, chunk, LANES), LOW),
                pltpu.VMEM((rows, LANES), LOW),
                pltpu.VMEM((rows, LANES), LOW),
                pltpu.SemaphoreType.DMA((2, 2, per)),
                pltpu.SemaphoreType.DMA((2, blocks)),
            ],
        ),
        compiler_params=pltpu.CompilerParams(
            dimension_semantics=("arbitrary", "arbitrary"), vmem_limit_bytes=56 << 20
        ),
        cost_estimate=pl.CostEstimate(
            flops=6 * rows * rows * width, bytes_accessed=16 * rows * width, transcendentals=0
        ),
        name="attention",
    )(where, *operands)
    return attended.reshape(rows, width), grads.reshape(rows, 3 * width)


def ring_of(count):
    order = list(range(count // 2)) + list(range(count - 1, count // 2 - 1, -1))
    ahead = [(order[n], order[(n + 1) % count]) for n in range(count)]
    return order, ahead, [(b, a) for a, b in ahead]


def ring_gather(own, axis):
    count = lax.axis_size(axis)
    _, ahead, behind = ring_of(count)
    pieces, half = [own], own.shape[0] // 2
    from_behind = from_ahead = own
    for _ in range(count // 2 - 1):
        from_behind = lax.ppermute(from_behind, axis, ahead)
        from_ahead = lax.ppermute(from_ahead, axis, behind)
        pieces += [from_behind, from_ahead]
    pieces.append(lax.ppermute(from_behind[:half], axis, ahead))
    pieces.append(lax.ppermute(from_ahead[half:], axis, behind))
    return jnp.concatenate(pieces, axis=0)


def ring_rank(offset, count):
    ranks = [0] * count
    for s in range(1, count // 2):
        ranks[s], ranks[count - s] = 2 * s, 2 * s - 1
    ranks[count // 2] = count - 1
    return jnp.asarray(ranks, jnp.int32)[offset]


def ring_reduce(parts, axis):
    count = lax.axis_size(axis)
    _, ahead, behind = ring_of(count)
    rows = parts.shape[0] // count
    half = rows // 2

    def part(rank):
        return parts[rank * rows : (rank + 1) * rows]

    def plus(a, b):
        return (a.astype(WIDE) + b.astype(WIDE)).astype(LOW)

    far = part(count - 1)
    up, down = lax.ppermute(far[:half], axis, ahead), lax.ppermute(far[half:], axis, behind)
    own = part(0).astype(WIDE)
    if count == 2:
        return own + jnp.concatenate([up, down], axis=0).astype(WIDE)
    for s in range(count // 2 - 1, 0, -1):
        to_ahead, to_behind = part(2 * s), part(2 * s - 1)
        if s == count // 2 - 1:
            up = [
                lax.ppermute(plus(to_ahead[:half], up), axis, ahead),
                lax.ppermute(to_ahead[half:], axis, ahead),
            ]
            down = [
                lax.ppermute(to_behind[:half], axis, behind),
                lax.ppermute(plus(to_behind[half:], down), axis, behind),
            ]
            up, down = jnp.concatenate(up, axis=0), jnp.concatenate(down, axis=0)
        else:
            up = lax.ppermute(plus(to_ahead, up), axis, ahead)
            down = lax.ppermute(plus(to_behind, down), axis, behind)
    return own + up.astype(WIDE) + down.astype(WIDE)


def gelu_tanh(values):
    return (
        0.5
        * values
        * (
            1.0
            + jnp.tanh(math.sqrt(2.0 / math.pi) * (values + 0.044715 * values * values * values))
        )
    )


def rope_tables(rows):
    place = jnp.arange(rows, dtype=jnp.int32)
    pos = jnp.where(place < PROMPT, place, PROMPT + (place - PROMPT) % CLEN)
    half = ROT // 2
    freq = 10000.0 ** (-2.0 * jnp.arange(half, dtype=WIDE) / ROT)
    angle = pos.astype(WIDE)[:, None] * freq[None, :]
    cosine, sine = jnp.cos(angle), jnp.sin(angle)
    zero, one = jnp.zeros_like(cosine), jnp.ones_like(cosine)
    tabs = ((cosine, cosine, one, one), (zero, sine, zero, zero), (-sine, zero, zero, zero))
    return [jnp.concatenate(tab * (LANES // (4 * half)), axis=1) for tab in tabs]


def shards(
    tokens,
    cotangent,
    block_table,
    ln_gain,
    ln_bias,
    w_qkv,
    b_qkv,
    w_dense,
    b_dense,
    w_fc1,
    b_fc1,
    w_fc2,
    b_fc2,
):
    _, local_rows, width = tokens.shape
    head_dim = width // HEADS
    count = lax.axis_size("ctx")
    me = lax.axis_index("ctx")
    rows = local_rows * count
    local_blocks = local_rows // BLK
    each = w_dense.shape[0]
    hidden = w_fc2.shape[0]
    gain, shift = ln_gain.astype(WIDE), ln_bias.astype(WIDE)

    order, _, _ = ring_of(count)
    places = [0] * count
    for n, device in enumerate(order):
        places[device] = n
    places = jnp.asarray(places, jnp.int32)
    slots = jnp.arange(rows // BLK, dtype=jnp.int32)
    offset = (places[slots // local_blocks] - places[me]) % count
    held_at = ring_rank(offset, count) * local_blocks + slots % local_blocks
    hit = block_table[0][None, :] == slots[:, None]
    where = jnp.sum(jnp.where(hit, held_at[None, :], 0), axis=1).astype(jnp.int32)

    own_tokens = tokens[0].astype(WIDE)
    own_grad = cotangent[0]
    average = jnp.mean(own_tokens, axis=-1, keepdims=True)
    centred = own_tokens - average
    rstd = lax.rsqrt(jnp.mean(centred * centred, axis=-1, keepdims=True) + 1e-05)
    xhat = centred * rstd
    normed_own = (xhat * gain + shift).astype(LOW)

    normed = ring_gather(normed_own, "ctx")
    grads = ring_gather(own_grad, "ctx")

    def gather_rows(shard):
        return lax.all_gather(shard, "fsdp", axis=0, tiled=True)

    qkv_weight = gather_rows(w_qkv.reshape(w_qkv.shape[0], 3 * each))
    fc1_weight = gather_rows(w_fc1)
    dense_turned = gather_rows(w_dense.T)
    fc2_turned = gather_rows(w_fc2.T)

    qkv_bias = lax.dynamic_slice_in_dim(b_qkv.reshape(3, width), me * each, each, 1)
    fc1_bias = lax.dynamic_slice_in_dim(b_fc1, me * hidden, hidden, 0)

    qkv = (dot(normed, qkv_weight, NN) + qkv_bias.reshape(-1).astype(WIDE)).astype(LOW)
    expanded = dot(normed, fc1_weight, NN) + fc1_bias.astype(WIDE)
    activated, gelu_pull = jax.vjp(gelu_tanh, expanded)
    activated = activated.astype(LOW)

    attended_grad = dot(grads, dense_turned, NN).astype(LOW)
    attended, qkv_grad = attention(qkv, attended_grad, where, rope_tables(rows), head_dim)

    out_part = dot(attended, dense_turned, NT) + dot(activated, fc2_turned, NT)
    out_sum = ring_reduce(out_part.astype(LOW), "ctx")
    output = own_tokens + out_sum + b_dense.astype(WIDE) + b_fc2.astype(WIDE)

    expanded_grad = gelu_pull(dot(grads, fc2_turned, NN))[0].astype(LOW)

    def scatter_rows(whole):
        return lax.psum_scatter(
            whole.astype(LOW), "fsdp", scatter_dimension=0, tiled=True
        ).astype(WIDE)

    d_fc2 = scatter_rows(dot(grads, activated, TN)).T
    d_dense = scatter_rows(dot(grads, attended, TN)).T
    d_fc1 = scatter_rows(dot(normed, expanded_grad, TN))
    d_qkv = scatter_rows(dot(normed, qkv_grad, TN))

    normed_grad_part = dot(qkv_grad, qkv_weight, NT) + dot(expanded_grad, fc1_weight, NT)
    normed_grad = ring_reduce(normed_grad_part.astype(LOW), "ctx")

    scaled = normed_grad * gain
    d_tokens = own_grad.astype(WIDE) + rstd * (
        scaled
        - jnp.mean(scaled, axis=-1, keepdims=True)
        - xhat * jnp.mean(scaled * xhat, axis=-1, keepdims=True)
    )

    qkv_bias_part = jnp.sum(qkv_grad.astype(WIDE), axis=0).reshape(3, each)
    fc1_bias_part = jnp.sum(expanded_grad.astype(WIDE), axis=0)
    qkv_bias_wide = lax.dynamic_update_slice_in_dim(
        jnp.zeros((3, width), WIDE), qkv_bias_part, me * each, 1
    ).reshape(-1)
    fc1_bias_wide = lax.dynamic_update_slice_in_dim(
        jnp.zeros((b_fc1.shape[0],), WIDE), fc1_bias_part, me * hidden, 0
    )
    small = jnp.concatenate(
        [
            jnp.sum(normed_grad * xhat, axis=0),
            jnp.sum(normed_grad, axis=0),
            qkv_bias_wide,
            jnp.sum(own_grad.astype(WIDE), axis=0),
            fc1_bias_wide,
        ]
    )
    small = lax.psum(small, ("ctx", "fsdp"))
    cuts = [width, 2 * width, 5 * width, 6 * width]
    d_gain, d_shift, d_b_qkv, d_b_out, d_b_fc1 = jnp.split(small, cuts)
    return (
        output.astype(LOW)[None],
        d_tokens.astype(LOW)[None],
        d_gain,
        d_shift,
        d_qkv.reshape(-1, 3, each),
        d_b_qkv,
        d_dense,
        d_b_out,
        d_fc1,
        d_b_fc1,
        d_fc2,
        d_b_out,
    )


def solution(mesh):
    in_specs = (
        P("fsdp", "ctx", None),
        P("fsdp", "ctx", None),
        P("fsdp", None),
        P(),
        P(),
        P("fsdp", None, "ctx"),
        P(),
        P("ctx", "fsdp"),
        P(),
        P("fsdp", "ctx"),
        P(),
        P("ctx", "fsdp"),
        P(),
    )
    out_specs = (
        P("fsdp", "ctx", None),
        P("fsdp", "ctx", None),
        P(),
        P(),
        P("fsdp", None, "ctx"),
        P(),
        P("ctx", "fsdp"),
        P(),
        P("fsdp", "ctx"),
        P(),
        P("ctx", "fsdp"),
        P(),
    )
    return jax.shard_map(shards, mesh=mesh, in_specs=in_specs, out_specs=out_specs, check_vma=False)
```

time: 3190 us -> 1270 us (0.40)
  waiting for transfers between devices: 1450 us -> 507 us
  matrix products: 980 us -> 300 us
  other arithmetic: 435 us -> 50.4 us
  Pallas kernels: 0 us -> 305 us
  local copies, waits for them, and re-layouts: 276 us -> 65.1 us
    dot_general x52 -> x12, matrix products: 980 us -> 300 us  [dot(): return lax.dot_general(left, right, dims, preferred_element_type=WIDE)]
    all_gather x10 -> x4, waiting for transfers between devices: 611 us -> 0.01 us  [gather_rows(): return lax.all_gather(shard, 'fsdp', axis=0, tiled=True)]
    reduce_scatter x3 -> x4, waiting for transfers between devices: 748 us -> 244 us  [scatter_rows(): lax.psum_scatter(whole.astype(LOW), 'fsdp', scatter_dimension=0, tiled=True)]
    pallas_call x0 -> x1, Pallas kernels: none -> 305 us  [attention(): pl.pallas_call(kernel, out_shape=(jax.ShapeDtypeStruct((blocks, blk, widt...]
    ppermute x0 -> x20, waiting for transfers between devices: none -> 226 us  [the longest x2 80.7 us: ring_gather(): from_behind = lax.ppermute(from_behind, axis, ahead)]
    convert_element_type x12 -> x10, other arithmetic: 170 us -> 14.3 us  [the longest x2 8.77 us: plus(): return (a.astype(WIDE) + b.astype(WIDE)).astype(LOW)]
    unnamed x99 -> x60, local copies, waits for them, and re-layouts: 165 us -> 31.1 us
    dynamic_update_slice x12 -> x0, other arithmetic: 114 us -> none  [the longest x4 66.6 us: shards(): blocks = lax.map(in_block, jnp.arange(span_rows // width, dtype=jnp.int32))]
  transfers between devices with their start and end apart: 17 -> 29, of which waited for: 11 -> 16; matrix products, arithmetic and copies ran while one was open for 53% -> 26% of each run, Pallas kernels for 0% -> 24%
where the time goes in v1:
time: 1270 us
  waiting for transfers between devices  507 us (40%)
  Pallas kernels  305 us (24%)
  matrix products  300 us (24%)
  local copies, waits for them, and re-layouts  65.1 us (5%)
  other arithmetic  50.4 us (4%)
  starting transfers between devices  22.6 us (2%)
  between operations  14.5 us (1%)
    pallas_call x1, Pallas kernels, attention(): pl.pallas_call(kernel, out_shape=(jax.ShapeDtypeStruct((blocks, blk, widt...  305 us
    dot_general x12, matrix products, dot(): return lax.dot_general(left, right, dims, preferred_element_type=WIDE)  300 us
    reduce_scatter x4, waiting for transfers between devices, scatter_rows(): lax.psum_scatter(whole.astype(LOW), 'fsdp', scatter_dimension=0, tiled=True)  244 us
    ppermute x2, waiting for transfers between devices, ring_gather(): from_behind = lax.ppermute(from_behind, axis, ahead)  80.7 us
    ppermute x2, waiting for transfers between devices, ring_reduce(): lax.ppermute(to_ahead[half:], axis, ahead)  46 us
    ppermute x2, waiting for transfers between devices, ring_reduce(): lax.ppermute(plus(to_ahead[:half], up), axis, ahead)  38.7 us
    psum x1, waiting for transfers between devices, shards(): small = lax.psum(small, ('ctx', 'fsdp'))  35.2 us
    ppermute x2, waiting for transfers between devices, ring_gather(): pieces.append(lax.ppermute(from_behind[:half], axis, ahead))  31.9 us
  transfers between devices with their start and end apart: 29, of which 16 were waited for; matrix products, arithmetic and copies ran while one was open for 26% of the time, Pallas kernels for 24%

profile of v1, /device:TPU:0, one launch (start us, length us, event | category | flops | bytes accessed | tf_op | source)
XLA Modules:
  0.0 1265.4 jit_solution(16068964146180990744)
XLA Ops:
  37.4 40.9 %collective-permute-done = bf16[640,2048]{1,0:T(8,128)(2,1)} collective-permute-done((bf16[640,2048]{1,0:T(8,128)(2,1)}, bf16[640,2048]{1,0:T(8,128)(2,1)}, u32[]{:S(2)}, u32[]{:S(2)}) %collective-permute-start) | collective-permute-done | bytes 2621472 | tf_op jit(solution)/shard_map/ppermute | solution.py:305
  94.6 39.9 %collective-permute-done.4 = bf16[640,2048]{1,0:T(8,128)(2,1)} collective-permute-done((bf16[640,2048]{1,0:T(8,128)(2,1)}, bf16[640,2048]{1,0:T(8,128)(2,1)}, u32[]{:S(2)}, u32[]{:S(2)}) %collective-permute-start.4) | collective-permute-done | bytes 2621472 | tf_op jit(solution)/shard_map/ppermute | solution.py:305
  166.4 23.3 %collective-permute-done.6 = bf16[320,2048]{1,0:T(8,128)(2,1)S(1)} collective-permute-done((bf16[320,2048]{1,0:T(8,128)(2,1)S(1)}, bf16[320,2048]{1,0:T(8,128)(2,1)S(1)}, u32[]{:S(2)}, u32[]{:S(2)}) %collective-permute-start.6) | collective-permute-done | bytes 1310752 | tf_op jit(solution)/shard_map/ppermute | solution.py:308
  192.3 11.5 convolution_convert_fusion.3
  203.8 22.5 %add_convert_fusion.2 = bf16[2560,1536]{1,0:T(8,128)(2,1)} fusion(bf16[2560,2048]{1,0:T(8,128)(2,1)} %constant_dynamic-update-slice_fusion, bf16[2048,1536]{0,1:T(8,128)(2,1)} %all-gather.5.cloned.1.call-done, f32[1536]{0:T(1024)S(1)} %reshape.231), kind=kOutput, calls=%fused_computation.15 | convolution fusion | flops 16113991680 | bytes 24647680 | tf_op jit(solution)/shard_map/dot_general | solution.py:26
  226.3 305.1 %attention.1 = (bf16[40,64,512]{2,1,0:T(8,128)(2,1)}, bf16[40,64,1536]{2,1,0:T(8,128)(2,1)}) custom-call(s32[40]{0:T(128)} %select_reduce_fusion.where_ref, bf16[40,64,1536]{2,1,0:T(8,128)(2,1)} %bitcast.95, bf16[40,64,1536]{2,1,0:T(8,128)(2,1)} %bitcast.96, bf16[40,64,1536]{2,1,0:T(8,128)(2,1)} %bitcast.97, bf16[40,64,1536]{2,1,0:T(8,128)(2,1)} %bitcast.98, ...), custom_call_target="tpu_custom_call" | custom-call | flops 20132659200 | bytes 20971520 | tf_op jit(solution)/shard_map/attention/pallas_call | solution.py:255
  531.4 12.0 fusion.42
  543.5 20.1 %fusion.44 = f32[2560,2048]{1,0:T(8,128)} fusion(bf16[2560,1536]{1,0:T(8,128)(2,1)S(1)} %bitcast.112, bf16[2048,1536]{0,1:T(8,128)(2,1)S(1)} %bitcast.118), kind=kOutput, calls=%fused_computation.118 | convolution fusion | flops 16106127360 | bytes 35127296 | tf_op jit(solution)/shard_map/dot_general | solution.py:26
  563.6 28.8 %fusion.43 = f32[2560,2048]{1,0:T(8,128)} fusion(bf16[2560,2048]{1,0:T(8,128)(2,1)} %constant_dynamic-update-slice_fusion, bf16[2048,2048]{1,0:T(8,128)(2,1)} %all-gather.9.cloned.1.call-done), kind=kOutput, calls=%fused_computation.117 | convolution fusion | flops 21474836480 | bytes 39845888 | tf_op jit(solution)/shard_map/dot_general | solution.py:26
  592.4 47.6 %convert_reduce_fusion = (f32[2048]{0:T(1024)S(1)}, bf16[2560,2048]{1,0:T(8,128)(2,1)}) fusion(f32[2560,2048]{1,0:T(8,128)} %fusion.43, f32[2048]{0:T(1024)S(1)} %copy-done.14, bf16[2560,2048]{1,0:T(8,128)(2,1)} %constant_dynamic-update-slice_fusion.5, bf16[2048,2048]{0,1:T(8,128)(2,1)} %all-gather.11.cloned.1.call-done), kind=kOutput, calls=%fused_computation.10 | convolution fusion | flops 21616392192 | bytes 50348032 | tf_op jit(solution)/shard_map/dot_general | solution.py:26
  639.9 30.8 %add_convert_fusion = bf16[2560,2048]{1,0:T(8,128)(2,1)} fusion(f32[2560,2048]{1,0:T(8,128)} %fusion.44, bf16[2560,2048]{1,0:T(8,128)(2,1)} %get-tuple-element.69, bf16[2048,2048]{1,0:T(8,128)(2,1)} %all-gather.9.cloned.1.call-done), kind=kOutput, calls=%fused_computation.11 | convolution fusion | flops 21485322240 | bytes 50331648 | tf_op jit(solution)/shard_map/dot_general | solution.py:26
  677.3 34.0 %add_convert_fusion.1 = bf16[2560,2048]{1,0:T(8,128)(2,1)} fusion(f32[2560,2048]{1,0:T(8,128)} %fusion.42, bf16[2048,2048]{0,1:T(8,128)(2,1)} %all-gather.11.cloned.1.call-done, f32[2560,2048]{1,0:T(8,128)} %fusion.43, f32[2048]{0:T(1024)S(1)} %copy-done.14), kind=kOutput, calls=%fused_computation.12 | convolution fusion | flops 21537751040 | bytes 60825600 | tf_op jit(solution)/shard_map/dot_general | solution.py:26
  765.0 24.0 %collective-permute-done.16 = bf16[320,2048]{1,0:T(8,128)(2,1)} collective-permute-done((bf16[320,2048]{1,0:T(8,128)(2,1)}, bf16[320,2048]{1,0:T(8,128)(2,1)}, u32[]{:S(2)}, u32[]{:S(2)}) %collective-permute-start.16) | collective-permute-done | bytes 1310752 | tf_op jit(solution)/shard_map/ppermute | solution.py:343
  791.0 26.1 %collective-permute-done.15 = bf16[320,2048]{1,0:T(8,128)(2,1)} collective-permute-done((bf16[320,2048]{1,0:T(8,128)(2,1)}, bf16[320,2048]{1,0:T(8,128)(2,1)}, u32[]{:S(2)}, u32[]{:S(2)}) %collective-permute-start.15) | collective-permute-done | bytes 1310752 | tf_op jit(solution)/shard_map/ppermute | solution.py:342
  823.1 22.0 %collective-permute-done.10 = bf16[320,2048]{1,0:T(8,128)(2,1)S(1)} collective-permute-done((bf16[320,2048]{1,0:T(8,128)(2,1)}, bf16[320,2048]{1,0:T(8,128)(2,1)S(1)}, u32[]{:S(2)}, u32[]{:S(2)}) %collective-permute-start.10) | collective-permute-done | bytes 1310752 | tf_op jit(solution)/shard_map/ppermute | solution.py:343
  845.1 12.8 %collective-permute-done.13 = bf16[320,2048]{1,0:T(8,128)(2,1)S(1)} collective-permute-done((bf16[320,2048]{1,0:T(8,128)(2,1)S(1)}, bf16[320,2048]{1,0:T(8,128)(2,1)S(1)}, u32[]{:S(2)}, u32[]{:S(2)}) %collective-permute-start.13) | collective-permute-done | bytes 1310752 | tf_op jit(solution)/shard_map/ppermute | solution.py:347
  857.9 12.6 collective-permute-done.9
  880.9 22.4 %convolution_convert_fusion = bf16[2048,1536]{1,0:T(8,128)(2,1)} fusion(bf16[2560,2048]{1,0:T(8,128)(2,1)} %constant_dynamic-update-slice_fusion, bf16[2560,1536]{1,0:T(8,128)(2,1)} %bitcast.111), kind=kOutput, calls=%fused_computation.16 | convolution fusion | flops 16109273088 | bytes 24641536 | tf_op jit(solution)/shard_map/dot_general | solution.py:26
  903.5 30.5 %convolution_convert_fusion.1 = bf16[2048,2048]{1,0:T(8,128)(2,1)} fusion(bf16[2560,2048]{1,0:T(8,128)(2,1)} %constant_dynamic-update-slice_fusion.5, f32[2560,2048]{1,0:T(8,128)} %fusion.43, f32[2048]{0:T(1024)S(1)} %copy-done.14), kind=kOutput, calls=%fused_computation.17 | convolution fusion | flops 21531459584 | bytes 39854080 | tf_op jit(solution)/shard_map/dot_general | solution.py:26
  934.3 28.9 %convolution_convert_fusion.2 = bf16[2048,2048]{1,0:T(8,128)(2,1)} fusion(bf16[2560,2048]{1,0:T(8,128)(2,1)} %constant_dynamic-update-slice_fusion, bf16[2560,2048]{1,0:T(8,128)(2,1)} %get-tuple-element.69), kind=kOutput, calls=%fused_computation.18 | convolution fusion | flops 21479030784 | bytes 29360128 | tf_op jit(solution)/shard_map/dot_general | solution.py:26
  965.3 35.2 %all-reduce.2.cloned.1.call-done = f32[20480]{0:T(1024)} async-done(((f32[20480]{0:T(1024)}), f32[20480]{0:T(1024)}) %all-reduce.2.cloned.1.call-update) | async-done | bytes 81936 | tf_op jit(solution)/shard_map/psum | solution.py:488
  1004.6 70.0 %reduce-scatter.5.cloned.1.call-done = bf16[256,1536]{1,0:T(8,128)(2,1)} async-done(((bf16[2048,1536]{1,0:T(8,128)(2,1)}), bf16[256,1536]{1,0:T(8,128)(2,1)}) %reduce-scatter.5.cloned.1.call-update) | async-done | bytes 786448 | tf_op jit(solution)/shard_map/reduce_scatter | solution.py:452
  1077.7 87.2 %reduce-scatter.11.cloned.1.call-done = bf16[256,2048]{1,0:T(8,128)(2,1)} async-done(((bf16[2048,2048]{1,0:T(8,128)(2,1)}), bf16[256,2048]{1,0:T(8,128)(2,1)}) %reduce-scatter.11.cloned.1.call-update) | async-done | bytes 1048592 | tf_op jit(solution)/shard_map/reduce_scatter | solution.py:452
  1168.2 87.0 %reduce-scatter.9.cloned.1.call-done = bf16[256,2048]{1,0:T(8,128)(2,1)} async-done(((bf16[2048,2048]{1,0:T(8,128)(2,1)}), bf16[256,2048]{1,0:T(8,128)(2,1)}) %reduce-scatter.9.cloned.1.call-update) | async-done | bytes 1048592 | tf_op jit(solution)/shard_map/reduce_scatter | solution.py:452
  (171 shorter events, 175.6 us)
Async XLA Ops:
  7.2 185.2 %all-gather.7.cloned.1.call-start = ((), (), s32[]{:S(2)}) async-start(), calls=%async_computation.5 | async-start | bytes 2359296 | tf_op jit(solution)/shard_map/all_gather | solution.py:427
  7.9 195.9 %all-gather.5.cloned.1.call-start = ((), (), s32[]{:S(2)}) async-start(), calls=%async_computation.4 | async-start | bytes 7077888 | tf_op jit(solution)/shard_map/all_gather | solution.py:427
  10.3 553.3 %all-gather.9.cloned.1.call-start = ((), (), s32[]{:S(2)}) async-start(), calls=%async_computation.6 | async-start | bytes 9437184 | tf_op jit(solution)/shard_map/all_gather | solution.py:427
  11.0 581.3 %all-gather.11.cloned.1.call-start = ((), (), s32[]{:S(2)}) async-start(), calls=%async_computation.7 | async-start | bytes 9437184 | tf_op jit(solution)/shard_map/all_gather | solution.py:427
  17.3 61.0 %collective-permute-start = (bf16[640,2048]{1,0:T(8,128)(2,1)}, bf16[640,2048]{1,0:T(8,128)(2,1)}, u32[]{:S(2)}, u32[]{:S(2)}) collective-permute-start(bf16[640,2048]{1,0:T(8,128)(2,1)} %get-tuple-element.72), channel_id=1, source_target_pairs={{0,8},{8,24},{24,16},{16,0},{1,9},{9,25},{25,17},{17,1},{2,10},{10... | collective-permute-start | bytes 7864328 | tf_op jit(solution)/shard_map/ppermute | solution.py:305
  20.2 72.7 %collective-permute-start.1 = (bf16[640,2048]{1,0:T(8,128)(2,1)}, bf16[640,2048]{1,0:T(8,128)(2,1)}, u32[]{:S(2)}, u32[]{:S(2)}) collective-permute-start(bf16[640,2048]{1,0:T(8,128)(2,1)} %get-tuple-element.72), channel_id=1, source_target_pairs={{8,0},{24,8},{16,24},{0,16},{9,1},{25,9},{17,25},{1,17},{10,2},{26... | collective-permute-start | bytes 7864328 | tf_op jit(solution)/shard_map/ppermute | solution.py:306
  20.3 114.1 %collective-permute-start.4 = (bf16[640,2048]{1,0:T(8,128)(2,1)}, bf16[640,2048]{1,0:T(8,128)(2,1)}, u32[]{:S(2)}, u32[]{:S(2)}) collective-permute-start(bf16[640,2048]{1,0:T(8,128)(2,1)} %bitcast.6), channel_id=1, source_target_pairs={{0,8},{8,24},{24,16},{16,0},{1,9},{9,25},{25,17},{17,1},{2,10},{10... | collective-permute-start | bytes 7864328 | tf_op jit(solution)/shard_map/ppermute | solution.py:305
  22.3 115.8 %collective-permute-start.5 = (bf16[640,2048]{1,0:T(8,128)(2,1)}, bf16[640,2048]{1,0:T(8,128)(2,1)}, u32[]{:S(2)}, u32[]{:S(2)}) collective-permute-start(bf16[640,2048]{1,0:T(8,128)(2,1)} %bitcast.6), channel_id=1, source_target_pairs={{8,0},{24,8},{16,24},{0,16},{9,1},{25,9},{17,25},{1,17},{10,2},{26... | collective-permute-start | bytes 7864328 | tf_op jit(solution)/shard_map/ppermute | solution.py:306
  22.4 940.9 %reduce-scatter.7.cloned.1.call-start = ((), (), s32[]{:S(2)}) async-start(), calls=%async_computation.10 | async-start | bytes 2359296 | tf_op jit(solution)/shard_map/reduce_scatter | solution.py:452
  80.8 81.7 %collective-permute-start.2 = (bf16[320,2048]{1,0:T(8,128)(2,1)}, bf16[320,2048]{1,0:T(8,128)(2,1)}, u32[]{:S(2)}, u32[]{:S(2)}) collective-permute-start(bf16[320,2048]{1,0:T(8,128)(2,1)} %slice.100), channel_id=1, source_target_pairs={{0,8},{8,24},{24,16},{16,0},{1,9},{9,25},{25,17},{17,1},{2,10},{10... | collective-permute-start | bytes 3932168 | tf_op jit(solution)/shard_map/ppermute | solution.py:308
  94.5 70.7 %collective-permute-start.3 = (bf16[320,2048]{1,0:T(8,128)(2,1)S(1)}, bf16[320,2048]{1,0:T(8,128)(2,1)S(1)}, u32[]{:S(2)}, u32[]{:S(2)}) collective-permute-start(bf16[320,2048]{1,0:T(8,128)(2,1)S(1)} %slice.101), channel_id=1, source_target_pairs={{8,0},{24,8},{16,24},{0,16},{9,1},{25,9},{17,25},{1,17},{10,2},{26... | collective-permute-start | bytes 3932168 | tf_op jit(solution)/shard_map/ppermute | solution.py:309
  675.3 55.8 %collective-permute-start.14 = (bf16[320,2048]{1,0:T(8,128)(2,1)}, bf16[320,2048]{1,0:T(8,128)(2,1)}, u32[]{:S(2)}, u32[]{:S(2)}) collective-permute-start(bf16[320,2048]{1,0:T(8,128)(2,1)} %get-tuple-element.75), channel_id=1, source_target_pairs={{0,8},{8,24},{24,16},{16,0},{1,9},{9,25},{25,17},{17,1},{2,10},{10... | collective-permute-start | bytes 3932168 | tf_op jit(solution)/shard_map/ppermute | solution.py:334
  676.8 54.7 %collective-permute-start.18 = (bf16[320,2048]{1,0:T(8,128)(2,1)S(1)}, bf16[320,2048]{1,0:T(8,128)(2,1)}, u32[]{:S(2)}, u32[]{:S(2)}) collective-permute-start(bf16[320,2048]{1,0:T(8,128)(2,1)S(1)} %get-tuple-element.76), channel_id=1, source_target_pairs={{8,0},{24,8},{16,24},{0,16},{9,1},{25,9},{17,25},{1,17},{10,2},{26... | collective-permute-start | bytes 3932168 | tf_op jit(solution)/shard_map/ppermute | solution.py:334
  729.4 271.1 %all-reduce.2.cloned.1.call-start = ((), (), s32[]{:S(2)}) async-start(), calls=%async_computation.8 | async-start | bytes 163840 | tf_op jit(solution)/shard_map/psum | solution.py:488
  729.5 59.6 %collective-permute-start.16 = (bf16[320,2048]{1,0:T(8,128)(2,1)}, bf16[320,2048]{1,0:T(8,128)(2,1)}, u32[]{:S(2)}, u32[]{:S(2)}) collective-permute-start(bf16[320,2048]{1,0:T(8,128)(2,1)} %get-tuple-element.78), channel_id=1, source_target_pairs={{0,8},{8,24},{24,16},{16,0},{1,9},{9,25},{25,17},{17,1},{2,10},{10... | collective-permute-start | bytes 3932168 | tf_op jit(solution)/shard_map/ppermute | solution.py:343
  731.0 59.5 %collective-permute-start.17 = (bf16[320,2048]{1,0:T(8,128)(2,1)}, bf16[320,2048]{1,0:T(8,128)(2,1)}, u32[]{:S(2)}, u32[]{:S(2)}) collective-permute-start(bf16[320,2048]{1,0:T(8,128)(2,1)} %get-tuple-element.77), channel_id=1, source_target_pairs={{8,0},{24,8},{16,24},{0,16},{9,1},{25,9},{17,25},{1,17},{10,2},{26... | collective-permute-start | bytes 3932168 | tf_op jit(solution)/shard_map/ppermute | solution.py:346
  736.8 80.3 %collective-permute-start.15 = (bf16[320,2048]{1,0:T(8,128)(2,1)}, bf16[320,2048]{1,0:T(8,128)(2,1)}, u32[]{:S(2)}, u32[]{:S(2)}) collective-permute-start(bf16[320,2048]{1,0:T(8,128)(2,1)} %get-tuple-element.73), channel_id=1, source_target_pairs={{0,8},{8,24},{24,16},{16,0},{1,9},{9,25},{25,17},{17,1},{2,10},{10... | collective-permute-start | bytes 3932168 | tf_op jit(solution)/shard_map/ppermute | solution.py:342
  747.9 69.7 %collective-permute-start.19 = (bf16[320,2048]{1,0:T(8,128)(2,1)}, bf16[320,2048]{1,0:T(8,128)(2,1)}, u32[]{:S(2)}, u32[]{:S(2)}) collective-permute-start(bf16[320,2048]{1,0:T(8,128)(2,1)} %get-tuple-element.74), channel_id=1, source_target_pairs={{8,0},{24,8},{16,24},{0,16},{9,1},{25,9},{17,25},{1,17},{10,2},{26... | collective-permute-start | bytes 3932168 | tf_op jit(solution)/shard_map/ppermute | solution.py:347
  760.9 84.2 %collective-permute-start.10 = (bf16[320,2048]{1,0:T(8,128)(2,1)}, bf16[320,2048]{1,0:T(8,128)(2,1)S(1)}, u32[]{:S(2)}, u32[]{:S(2)}) collective-permute-start(bf16[320,2048]{1,0:T(8,128)(2,1)} %get-tuple-element.81), channel_id=1, source_target_pairs={{0,8},{8,24},{24,16},{16,0},{1,9},{9,25},{25,17},{17,1},{2,10},{10... | collective-permute-start | bytes 3932168 | tf_op jit(solution)/shard_map/ppermute | solution.py:343
  789.0 56.1 %collective-permute-start.11 = (bf16[320,2048]{1,0:T(8,128)(2,1)S(1)}, bf16[320,2048]{1,0:T(8,128)(2,1)S(1)}, u32[]{:S(2)}, u32[]{:S(2)}) collective-permute-start(bf16[320,2048]{1,0:T(8,128)(2,1)S(1)} %copy-done.4), channel_id=1, source_target_pairs={{8,0},{24,8},{16,24},{0,16},{9,1},{25,9},{17,25},{1,17},{10,2},{26... | collective-permute-start | bytes 3932168 | tf_op jit(solution)/shard_map/ppermute | solution.py:346
  790.6 67.3 %collective-permute-start.13 = (bf16[320,2048]{1,0:T(8,128)(2,1)S(1)}, bf16[320,2048]{1,0:T(8,128)(2,1)S(1)}, u32[]{:S(2)}, u32[]{:S(2)}) collective-permute-start(bf16[320,2048]{1,0:T(8,128)(2,1)S(1)} %get-tuple-element.83), channel_id=1, source_target_pairs={{8,0},{24,8},{16,24},{0,16},{9,1},{25,9},{17,25},{1,17},{10,2},{26... | collective-permute-start | bytes 3932168 | tf_op jit(solution)/shard_map/ppermute | solution.py:347
  880.8 193.8 %reduce-scatter.5.cloned.1.call-start = ((), (), s32[]{:S(2)}) async-start(), calls=%async_computation.9 | async-start | bytes 7077888 | tf_op jit(solution)/shard_map/reduce_scatter | solution.py:452
  903.2 261.6 %reduce-scatter.11.cloned.1.call-start = ((), (), s32[]{:S(2)}) async-start(), calls=%async_computation.12 | async-start | bytes 9437184 | tf_op jit(solution)/shard_map/reduce_scatter | solution.py:452
  934.0 321.1 %reduce-scatter.9.cloned.1.call-start = ((), (), s32[]{:S(2)}) async-start(), calls=%async_computation.11 | async-start | bytes 9437184 | tf_op jit(solution)/shard_map/reduce_scatter | solution.py:452
  (27 other events, 1557.4 us)
Sparse Core Ops, SparseCore 0:
  9.6 33.5 all-gather.6
  44.8 64.2 all-gather.4
  110.6 80.2 all-gather.8
  192.4 81.0 all-gather.10
  729.5 36.8 reduce-scatter.6
  880.9 119.5 all-reduce.1
  1002.8 71.7 reduce-scatter.4
  1076.9 87.9 reduce-scatter.10
  1167.2 87.9 reduce-scatter.8

commit v2 on v1

v2 whole, which is shorter than its diff:
```python
import functools
import math

import jax
import jax.numpy as jnp
from jax import lax
from jax.experimental import pallas as pl
from jax.experimental.pallas import tpu as pltpu
from jax.sharding import PartitionSpec as P

HEADS = 32
ROT = 32
PROMPT = 2048
CLEN = 256
BLK = 64
CHUNK = 256
LANES = 128
NT = (((1,), (1,)), ((), ()))
NN = (((1,), (0,)), ((), ()))
TN = (((0,), (0,)), ((), ()))
LOW = jnp.bfloat16
WIDE = jnp.float32
LITTLE = pl.CostEstimate(flops=1000000, bytes_accessed=1000000, transcendentals=0)


def dot(left, right, dims):
    return lax.dot_general(left, right, dims, preferred_element_type=WIDE)


def attention_kernel(where_ref, *refs, chunk, chunks, full_chunks, blk, group, scale):
    per = chunk // blk
    q_in, k_in, v_in, g_in = (refs[n * per : (n + 1) * per] for n in range(4))
    cos_ref, up_ref, down_ref, att_hbm, grad_hbm = refs[4 * per : 4 * per + 5]
    (
        keys,
        values,
        values_t,
        probs,
        key_sum,
        value_sum,
        top_ref,
        total_ref,
        mix_ref,
        back_ref,
        att_stage,
        query_stage,
        key_stage,
        value_stage,
        row_sem,
        col_sem,
    ) = refs[4 * per + 5 :]
    i = pl.program_id(0)
    slot = lax.rem(i, 2)
    half = LANES // 2
    lanes = group * LANES
    heads = 2 * group
    first = lax.broadcasted_iota(jnp.int32, (1, LANES), 1) < half

    def columns(part):
        return pl.ds(part * lanes, lanes)

    def row_copies(which, at):
        stage, target = ((att_stage, att_hbm), (query_stage, grad_hbm))[which]
        return [
            pltpu.make_async_copy(
                stage.at[at, pl.ds(r * blk, blk)],
                target.at[where_ref[i * per + r], :, columns(0)],
                row_sem.at[at, which, r],
            )
            for r in range(per)
        ]

    def col_copies(n):
        block = where_ref[n]
        rows = pl.ds(pl.multiple_of(n * blk, blk), blk)
        return (
            pltpu.make_async_copy(
                key_stage.at[rows], grad_hbm.at[block, :, columns(1)], col_sem.at[0, n]
            ),
            pltpu.make_async_copy(
                value_stage.at[rows], grad_hbm.at[block, :, columns(2)], col_sem.at[1, n]
            ),
        )

    def load(parts):
        return jnp.concatenate([part[0] for part in parts], axis=0)

    def tables(rows):
        return cos_ref[rows], up_ref[rows], down_ref[rows]

    quarter = ROT // 2

    def turned(x, tab, sign):
        return jnp.concatenate(
            [
                y * tab[0]
                + sign
                * (pltpu.roll(y, quarter, 1) * tab[1] + pltpu.roll(y, LANES - quarter, 1) * tab[2])
                for y in (x[:, n * LANES : (n + 1) * LANES] for n in range(group))
            ],
            axis=1,
        )

    def one_head(x, h):
        pair = x[:, (h // 2) * LANES : (h // 2 + 1) * LANES]
        nothing = jnp.zeros_like(pair)
        return jnp.where(first, pair, nothing) if h % 2 == 0 else jnp.where(first, nothing, pair)

    @pl.when(i >= 2)
    def _():
        for which in range(2):
            for copy in row_copies(which, slot):
                copy.wait()

    here = pl.ds(pl.multiple_of(i * chunk, chunk), chunk)
    tab = tables(here)
    query = (turned(load(q_in).astype(WIDE), tab, 1.0) * scale).astype(LOW)
    key_new = turned(load(k_in).astype(WIDE), tab, 1.0)
    value_new = load(v_in)
    grad = load(g_in)
    keys[here] = key_new.astype(LOW)
    values[here] = value_new
    values_t[:, here] = value_new.astype(WIDE).T.astype(LOW)
    key_sum[here] = jnp.zeros((chunk, lanes), WIDE)
    value_sum[here] = jnp.zeros((chunk, lanes), WIDE)
    top_ref[...] = jnp.full(top_ref.shape, -1e30, WIDE)
    total_ref[...] = jnp.zeros(total_ref.shape, WIDE)
    mix_ref[...] = jnp.zeros(mix_ref.shape, WIDE)
    back_ref[...] = jnp.zeros(back_ref.shape, WIDE)
    query_of = [one_head(query, h) for h in range(heads)]
    grad_of = [one_head(grad, h) for h in range(heads)]
    query_pair = [
        jnp.concatenate(query_of[2 * n : 2 * n + 2], axis=0) for n in range(group)
    ]
    grad_pair = [jnp.concatenate(grad_of[2 * n : 2 * n + 2], axis=0) for n in range(group)]
    before = jnp.minimum(i, full_chunks)
    doubles = before // 2
    odd = before - 2 * doubles

    def fold(x, how):
        return how(x.reshape(x.shape[0] // 8, 8, chunk), axis=0)

    def pair_lanes(n):
        return slice(n * LANES, (n + 1) * LANES)

    def head_rows(h):
        return slice(h * half, (h + 1) * half)

    def sweep(tile):
        def double(t, carry):
            start = pl.multiple_of(t * 2 * chunk, 2 * chunk)
            tile(start, start, 2 * chunk, False)
            return carry

        lax.fori_loop(0, doubles, double, 0)
        held = pl.multiple_of(doubles * 2 * chunk, chunk)

        @pl.when(odd == 1)
        def _():
            tile(held, held, 2 * chunk, True)

        @pl.when(odd == 0)
        def _():
            tile(pl.multiple_of(i * chunk, chunk), held, chunk, True)

    def score(start, held, size, masked):
        rows, to = pl.ds(start, size), pl.ds(held, size)
        if masked:
            key_row = lax.broadcasted_iota(jnp.int32, (size, chunk), 0) + start
            query_col = lax.broadcasted_iota(jnp.int32, (size, chunk), 1) + i * chunk
            seen = key_row <= query_col
        for h in range(heads):
            raw = dot(keys[rows, pair_lanes(h // 2)], query_of[h], NT)
            if masked:
                raw = jnp.where(seen, raw, -1e30)
            probs[h, to] = raw
            top_ref[h] = jnp.maximum(top_ref[h], fold(raw, jnp.max))

    sweep(score)
    top = [jnp.max(top_ref[h], axis=0, keepdims=True) for h in range(heads)]

    def mix(start, held, size, masked):
        rows, to = pl.ds(start, size), pl.ds(held, size)
        for h in range(heads):
            weight = jnp.exp(probs[h, to] - top[h])
            probs[h, to] = weight
            total_ref[h] += fold(weight, jnp.sum)
            mix_ref[head_rows(h)] += dot(values_t[head_rows(h), rows], weight.astype(LOW), NN)

    sweep(mix)
    inverse = [1.0 / jnp.sum(total_ref[h], axis=0, keepdims=True) for h in range(heads)]
    attended = jnp.concatenate(
        [mix_ref[head_rows(h)] * inverse[h] for h in range(heads)], axis=0
    )
    shared = grad.astype(WIDE).T * attended
    inner = [jnp.sum(shared[head_rows(h)], axis=0, keepdims=True) for h in range(heads)]
    att_stage[slot] = attended.T.astype(LOW)
    for copy in row_copies(0, slot):
        copy.start()

    def back(start, held, size, masked):
        rows, to = pl.ds(start, size), pl.ds(held, size)
        for n in range(group):
            value = values[rows, pair_lanes(n)]
            weights, grads = [], []
            for h in (2 * n, 2 * n + 1):
                weight = probs[h, to] * inverse[h]
                weight_grad = dot(value, grad_of[h], NT)
                score_grad = (weight * (weight_grad - inner[h])).astype(LOW)
                weights.append(weight.astype(LOW))
                grads.append(score_grad)
            value_sum[rows, pair_lanes(n)] += dot(
                jnp.concatenate(weights, axis=1), grad_pair[n], NN
            )
            key = keys[rows, pair_lanes(n)]
            back_ref[:, pair_lanes(n)] += dot(
                jnp.concatenate(grads, axis=0),
                jnp.concatenate([one_head(key, h) for h in range(2)], axis=0),
                TN,
            )
            key_sum[rows, pair_lanes(n)] += dot(
                jnp.concatenate(grads, axis=1), query_pair[n], NN
            )

    sweep(back)
    query_stage[slot] = turned(back_ref[...] * scale, tab, -1.0).astype(LOW)
    for copy in row_copies(1, slot):
        copy.start()

    @pl.when(i == chunks - 1)
    def _():
        @pl.loop(0, chunks)
        def _(n):
            rows = pl.ds(pl.multiple_of(n * chunk, chunk), chunk)
            key_stage[rows] = turned(key_sum[rows], tables(rows), -1.0).astype(LOW)
            value_stage[rows] = value_sum[rows].astype(LOW)
            for r in range(per):
                for copy in col_copies(n * per + r):
                    copy.start()

        for at in range(2):
            for which in range(2):
                for copy in row_copies(which, at):
                    copy.wait()

        @pl.loop(0, chunks * per)
        def _(n):
            for copy in col_copies(n):
                copy.wait()


def attention(qkv, grad, where, tabs, lanes, which, head_dim):
    rows = grad.shape[0]
    chunk, blk = CHUNK, BLK
    per, chunks, blocks = chunk // blk, rows // chunk, rows // blk
    group = lanes // LANES
    heads = 2 * group
    qkv_blocks = qkv.reshape(blocks, blk, qkv.shape[1])
    grad_blocks = grad.reshape(blocks, blk, grad.shape[1])

    def spec(column, r):
        return pl.BlockSpec((1, blk, lanes), lambda i, at: (at[i * per + r], 0, column))

    in_specs = [spec(3 * which + part, r) for part in range(3) for r in range(per)]
    in_specs += [spec(which, r) for r in range(per)]
    in_specs += [pl.BlockSpec((rows, LANES), lambda i, at: (0, 0), pipeline_mode=pl.Buffered(1))] * 3
    operands = [qkv_blocks] * (3 * per) + [grad_blocks] * per + list(tabs)
    kernel = functools.partial(
        attention_kernel,
        chunk=chunk,
        chunks=chunks,
        full_chunks=PROMPT // chunk,
        blk=blk,
        group=group,
        scale=1.0 / math.sqrt(head_dim),
    )
    attended, grads = pl.pallas_call(
        kernel,
        out_shape=(
            jax.ShapeDtypeStruct((blocks, blk, lanes), LOW),
            jax.ShapeDtypeStruct((blocks, blk, 3 * lanes), LOW),
        ),
        grid_spec=pltpu.PrefetchScalarGridSpec(
            num_scalar_prefetch=1,
            grid=(chunks,),
            in_specs=in_specs,
            out_specs=[pl.BlockSpec(memory_space=pl.ANY)] * 2,
            scratch_shapes=[
                pltpu.VMEM((rows, lanes), LOW),
                pltpu.VMEM((rows, lanes), LOW),
                pltpu.VMEM((lanes, rows), LOW),
                pltpu.VMEM((heads, PROMPT + chunk, chunk), WIDE),
                pltpu.VMEM((rows, lanes), WIDE),
                pltpu.VMEM((rows, lanes), WIDE),
                pltpu.VMEM((heads, 8, chunk), WIDE),
                pltpu.VMEM((heads, 8, chunk), WIDE),
                pltpu.VMEM((lanes, chunk), WIDE),
                pltpu.VMEM((chunk, lanes), WIDE),
                pltpu.VMEM((2, chunk, lanes), LOW),
                pltpu.VMEM((2, chunk, lanes), LOW),
                pltpu.VMEM((rows, lanes), LOW),
                pltpu.VMEM((rows, lanes), LOW),
                pltpu.SemaphoreType.DMA((2, 2, per)),
                pltpu.SemaphoreType.DMA((2, blocks)),
            ],
        ),
        compiler_params=pltpu.CompilerParams(
            dimension_semantics=("arbitrary",), vmem_limit_bytes=56 << 20
        ),
        cost_estimate=LITTLE,
        name="attention",
    )(where, *operands)
    return attended.reshape(rows, lanes), grads.reshape(rows, 3 * lanes)


def after(value, *others):
    return lax.optimization_barrier((value,) + others)[0]


def ring_of(count):
    order = list(range(count // 2)) + list(range(count - 1, count // 2 - 1, -1))
    ahead = [(order[n], order[(n + 1) % count]) for n in range(count)]
    return order, ahead, [(b, a) for a, b in ahead]


def rank_of(offset, count):
    offset %= count
    if offset == 0 or 2 * offset == count:
        return max(2 * offset - 1, 0)
    return 2 * offset if 2 * offset < count else 2 * (count - offset) - 1


def ring_pieces(own, axis, gate=()):
    count = lax.axis_size(axis)
    _, ahead, behind = ring_of(count)
    pieces, half = [own], own.shape[0] // 2
    from_behind = from_ahead = own
    for _ in range(count // 2 - 1):
        from_behind = lax.ppermute(from_behind, axis, ahead)
        from_ahead = lax.ppermute(from_ahead, axis, behind)
        pieces += [from_behind, from_ahead]
    from_behind, from_ahead = after(from_behind[:half], *gate), after(from_ahead[half:], *gate)
    far = [lax.ppermute(from_behind, axis, ahead), lax.ppermute(from_ahead, axis, behind)]
    return pieces + far


def ring_reduce(part, own, axis):
    count = lax.axis_size(axis)
    _, ahead, behind = ring_of(count)
    far = part(count - 1)
    half = far.shape[0] // 2

    def plus(a, b):
        return (a.astype(WIDE) + b.astype(WIDE)).astype(LOW)

    up, down = lax.ppermute(far[:half], axis, ahead), lax.ppermute(far[half:], axis, behind)
    far = early = (up, down)
    if count == 2:
        return own(early).astype(WIDE) + jnp.concatenate(early, axis=0).astype(WIDE), early, early
    for s in range(count // 2 - 1, 0, -1):
        to_ahead, to_behind = part(2 * s), part(2 * s - 1)
        if s == count // 2 - 1:
            free_up = lax.ppermute(to_ahead[half:], axis, ahead)
            free_down = lax.ppermute(to_behind[:half], axis, behind)
            early += (free_up, free_down)
            up = lax.ppermute(plus(to_ahead[:half], up), axis, ahead)
            down = lax.ppermute(plus(to_behind[half:], down), axis, behind)
            late = (up, down)
            up = jnp.concatenate([up, free_up], axis=0)
            down = jnp.concatenate([free_down, down], axis=0)
        else:
            up = lax.ppermute(plus(to_ahead, up), axis, ahead)
            down = lax.ppermute(plus(to_behind, down), axis, behind)
            late = (up, down)
    return own(far).astype(WIDE) + up.astype(WIDE) + down.astype(WIDE), early, late


def ring_exchange(part, axis):
    count = lax.axis_size(axis)
    order, _, _ = ring_of(count)
    got = [None] * count
    got[0] = part(0)
    for offset in range(1, count):
        hops = [(order[n], order[(n + offset) % count]) for n in range(count)]
        got[rank_of(-offset, count)] = lax.ppermute(part(rank_of(offset, count)), axis, hops)
    return got


def sum_everywhere(values, axes):
    for axis in axes:
        count, span = lax.axis_size(axis), 1
        while span < count:
            pairs = [(n, n ^ span) for n in range(count)]
            values = values + lax.ppermute(values, axis, pairs)
            span *= 2
    return values


def gelu_and_slope(h):
    inner_scale = math.sqrt(2.0 / math.pi)
    square = h * h
    t = jnp.tanh(h * (inner_scale + (inner_scale * 0.044715) * square))
    half = 0.5 * h
    rise = 0.5 + 0.5 * t
    bend = inner_scale + (3.0 * inner_scale * 0.044715) * square
    return (h * rise).astype(LOW), (rise + (half - half * t * t) * bend).astype(LOW)


def expand_kernel(x_ref, w_ref, b_ref, act_ref, slope_ref, *, cols):
    x = x_ref[...]
    for n in range(w_ref.shape[1] // cols):
        at = slice(n * cols, (n + 1) * cols)
        act, slope = gelu_and_slope(dot(x, w_ref[:, at], NN) + b_ref[:, at])
        act_ref[:, at] = act
        slope_ref[:, at] = slope


def expand(x, w, b):
    rows, width = x.shape
    hidden = w.shape[1]
    tile = 320
    out = jax.ShapeDtypeStruct((rows, hidden), LOW)
    return pl.pallas_call(
        functools.partial(expand_kernel, cols=min(512, hidden)),
        out_shape=(out, out),
        grid=(rows // tile,),
        in_specs=[
            pl.BlockSpec((tile, width), lambda i: (i, 0)),
            pl.BlockSpec((width, hidden), lambda i: (0, 0), pipeline_mode=pl.Buffered(1)),
            pl.BlockSpec((1, hidden), lambda i: (0, 0)),
        ],
        out_specs=[pl.BlockSpec((tile, hidden), lambda i: (i, 0))] * 2,
        compiler_params=pltpu.CompilerParams(
            dimension_semantics=("arbitrary",), vmem_limit_bytes=48 << 20
        ),
        cost_estimate=LITTLE,
        name="expand",
    )(x, w, b.astype(WIDE)[None])


def input_grad_kernel(*refs, terms):
    grads, weights = refs[:terms], refs[terms : 2 * terms]
    normed_ref, out_ref, sums_ref = refs[2 * terms :]
    total = sum(dot(g[...], w[...], NT) for g, w in zip(grads, weights))
    out_ref[...] = total.astype(LOW)
    sums_ref[0:1] = jnp.sum(total, axis=0, keepdims=True)
    sums_ref[1:2] = jnp.sum(total * normed_ref[...].astype(WIDE), axis=0, keepdims=True)


def input_grad(grads, weights, normed, rank, rows):
    width = normed.shape[1]
    cols = 512
    keep = pl.Buffered(1)
    in_specs = [
        pl.BlockSpec((rows, g.shape[1]), lambda i: (rank, 0), pipeline_mode=keep) for g in grads
    ]
    in_specs += [
        pl.BlockSpec((cols, g.shape[1]), lambda i, at=at: (i, at))
        for g, (_, at) in zip(grads, weights)
    ]
    in_specs.append(pl.BlockSpec((rows, cols), lambda i: (rank, i)))
    return pl.pallas_call(
        functools.partial(input_grad_kernel, terms=len(grads)),
        out_shape=(
            jax.ShapeDtypeStruct((rows, width), LOW),
            jax.ShapeDtypeStruct((2, width), WIDE),
        ),
        grid=(width // cols,),
        in_specs=in_specs,
        out_specs=[
            pl.BlockSpec((rows, cols), lambda i: (0, i)),
            pl.BlockSpec((2, cols), lambda i: (0, i)),
        ],
        compiler_params=pltpu.CompilerParams(
            dimension_semantics=("arbitrary",), vmem_limit_bytes=48 << 20
        ),
        cost_estimate=LITTLE,
        name="input_grad",
    )(*grads, *[w for w, _ in weights], normed)


def pair_grad_kernel(x_ref, y_ref, a_ref, b_ref, out_ref):
    split = a_ref.shape[1]
    out_ref[:, :split] = dot(x_ref[...], a_ref[...], TN).astype(LOW)
    out_ref[:, split:] = dot(y_ref[...], b_ref[...], TN).astype(LOW)


def pair_grad(x, y, a, b):
    rows, width = x.shape
    columns = a.shape[1] + b.shape[1]
    tile = 512
    keep = pl.Buffered(1)
    return pl.pallas_call(
        pair_grad_kernel,
        out_shape=jax.ShapeDtypeStruct((width, columns), LOW),
        grid=(width // tile,),
        in_specs=[
            pl.BlockSpec((rows, tile), lambda i: (0, i)),
            pl.BlockSpec((rows, tile), lambda i: (0, i)),
            pl.BlockSpec(a.shape, lambda i: (0, 0), pipeline_mode=keep),
            pl.BlockSpec(b.shape, lambda i: (0, 0), pipeline_mode=keep),
        ],
        out_specs=pl.BlockSpec((tile, columns), lambda i: (i, 0)),
        compiler_params=pltpu.CompilerParams(
            dimension_semantics=("arbitrary",), vmem_limit_bytes=48 << 20
        ),
        cost_estimate=LITTLE,
        name="pair_grad",
    )(x, y, a, b)


def rope_tables(rows):
    place = jnp.arange(rows, dtype=jnp.int32)
    pos = jnp.where(place < PROMPT, place, PROMPT + (place - PROMPT) % CLEN)
    half = ROT // 2
    freq = 10000.0 ** (-2.0 * jnp.arange(half, dtype=WIDE) / ROT)
    angle = pos.astype(WIDE)[:, None] * freq[None, :]
    cosine, sine = jnp.cos(angle), jnp.sin(angle)
    zero, one = jnp.zeros_like(cosine), jnp.ones_like(cosine)
    tabs = ((cosine, cosine, one, one), (zero, sine, zero, zero), (-sine, zero, zero, zero))
    return [jnp.concatenate(tab * (LANES // (4 * half)), axis=1) for tab in tabs]


def shards(
    tokens,
    cotangent,
    block_table,
    ln_gain,
    ln_bias,
    w_qkv,
    b_qkv,
    w_dense,
    b_dense,
    w_fc1,
    b_fc1,
    w_fc2,
    b_fc2,
):
    _, local_rows, width = tokens.shape
    head_dim = width // HEADS
    count = lax.axis_size("ctx")
    me = lax.axis_index("ctx")
    rows = local_rows * count
    local_blocks = local_rows // BLK
    each = w_dense.shape[0]
    hidden = w_fc2.shape[0]
    gain, shift = ln_gain.astype(WIDE), ln_bias.astype(WIDE)

    def of_rank(whole, rank):
        return whole[rank * local_rows : (rank + 1) * local_rows]

    order, _, _ = ring_of(count)
    places = [0] * count
    for n, device in enumerate(order):
        places[device] = n
    places = jnp.asarray(places, jnp.int32)
    ranks = jnp.asarray([rank_of(n, count) for n in range(count)], jnp.int32)
    slots = jnp.arange(rows // BLK, dtype=jnp.int32)
    offset = (places[slots // local_blocks] - places[me]) % count
    held_at = ranks[offset] * local_blocks + slots % local_blocks
    hit = block_table[0][None, :] == slots[:, None]
    where = jnp.sum(jnp.where(hit, held_at[None, :], 0), axis=1).astype(jnp.int32)

    own_tokens = tokens[0].astype(WIDE)
    own_grad = cotangent[0]
    average = jnp.mean(own_tokens, axis=-1, keepdims=True)
    centred = own_tokens - average
    rstd = lax.rsqrt(jnp.mean(centred * centred, axis=-1, keepdims=True) + 1e-05)
    xhat = centred * rstd
    normed_own = (xhat * gain + shift).astype(LOW)

    def gather_rows(shard):
        return lax.all_gather(shard, "fsdp", axis=0, tiled=True)

    def scatter_rows(whole):
        return lax.psum_scatter(whole, "fsdp", scatter_dimension=0, tiled=True)

    lanes = 2 * LANES if each % (2 * LANES) == 0 else LANES
    groups = each // lanes

    def by_group(values):
        cut = values.reshape(-1, 3, groups, lanes)
        return jnp.swapaxes(cut, 1, 2).reshape(-1, 3 * each)

    normed_pieces = ring_pieces(normed_own, "ctx")
    normed = jnp.concatenate(normed_pieces, axis=0)
    attention_shard = jnp.concatenate([by_group(w_qkv), w_dense.T], axis=1)
    fc1_weight = gather_rows(w_fc1)
    attention_weight = gather_rows(after(attention_shard, *normed_pieces[1:-2]))
    fc2_turned = gather_rows(after(w_fc2.T, *normed_pieces[-2:]))
    qkv_weight, dense_turned = attention_weight[:, : 3 * each], attention_weight[:, 3 * each :]

    fc1_bias = lax.dynamic_slice_in_dim(b_fc1, me * hidden, hidden, 0)
    qkv_bias = lax.dynamic_slice_in_dim(b_qkv.reshape(3, width), me * each, each, 1)
    activated, slope = expand(normed, fc1_weight, fc1_bias)

    sent_grad = after(own_grad, *normed_pieces[-2:])
    grad_pieces = ring_pieces(sent_grad, "ctx", gate=(activated,))
    grads = jnp.concatenate(grad_pieces, axis=0)

    qkv = dot(after(normed, activated), qkv_weight, NN)
    qkv = (qkv + by_group(qkv_bias)[0].astype(WIDE)).astype(LOW)
    attended_grad = dot(after(grads, qkv), dense_turned, NN).astype(LOW)
    d_fc2_part = dot(after(grads, attended_grad), activated, TN).astype(LOW)
    d_fc2 = scatter_rows(d_fc2_part)

    dense_pieces = ring_pieces(dense_turned, "ctx")
    dense_whole = jnp.concatenate(
        dense_pieces[:-2] + [jnp.concatenate(dense_pieces[-2:], axis=0)], axis=1
    )

    def feed_forward(gate, later):
        act = after(activated, *gate)
        ff_part = dot(act, fc2_turned, NT).astype(LOW)
        ff_sum, early, late = ring_reduce(
            lambda rank: of_rank(ff_part, rank), lambda _: of_rank(ff_part, 0), "ctx"
        )
        gated = after(grads, ff_part, *later)
        expanded_grad = (dot(gated, fc2_turned, NN) * slope.astype(WIDE)).astype(LOW)
        d_fc1_part = dot(after(normed, expanded_grad, *early), expanded_grad, TN).astype(LOW)
        return ff_sum, late, expanded_grad, d_fc1_part, scatter_rows(d_fc1_part)

    tabs = rope_tables(rows)
    attended, qkv_grads, d_attention, swapped = [], [], [], []
    ordered = (d_fc2_part,)
    for which in range(groups):
        if which == groups - 1:
            gate = (d_part,) + tuple(dense_pieces) if which else ()
            ff_sum, ff_late, expanded_grad, d_fc1_part, d_fc1 = feed_forward(
                gate, (d_fc2,) if which else ()
            )
            ordered = (d_fc1_part,) + ff_late + tuple(d_attention)
        got, got_grads = attention(
            after(qkv, *ordered), attended_grad, where, tabs, lanes, which, head_dim
        )
        attended.append(got)
        qkv_grads.append(got_grads)
        if which < groups - 1:
            swapped.append(ring_exchange(lambda rank, got=got: of_rank(got, rank), "ctx"))
            d_part = pair_grad(normed, grads, got_grads, got)
            ordered = (d_part,)
            d_attention.append(scatter_rows(d_part))

    weights = [(attention_weight, which) for which in range(groups)] + [(fc1_weight, 0)]
    parts, sums = [None] * count, 0.0
    early_swaps = [piece for pieces in swapped for piece in pieces]
    turn = after(expanded_grad, *early_swaps, *attended)

    def input_part(rank, turn):
        return input_grad(qkv_grads + [turn], weights, normed, rank, local_rows)

    for rank in range(count - 1, 0, -1):
        parts[rank], part_sums = input_part(rank, turn)
        sums = sums + part_sums
        turn = after(turn, parts[rank])

    own_sums = []

    def own_part(arrived):
        gated = after(normed, parts[1], d_fc1, *arrived)
        d_part = pair_grad(gated, grads, qkv_grads[-1], attended[-1])
        d_attention.append(scatter_rows(d_part))
        got = after(attended[-1], *arrived)
        swapped.append(ring_exchange(lambda rank: of_rank(got, rank), "ctx"))
        part, part_sums = input_part(0, after(turn, d_part))
        own_sums.append(part_sums)
        return part

    normed_grad, _, _ = ring_reduce(lambda rank: parts[rank], own_part, "ctx")
    sums = sums + own_sums[0]

    d_qkv = jnp.concatenate(
        [part[:, : 3 * lanes].reshape(-1, 3, lanes) for part in d_attention], axis=2
    ).astype(WIDE)
    d_dense = jnp.concatenate([part[:, 3 * lanes :].T for part in d_attention], axis=0)

    attended_own = jnp.concatenate(
        [swapped[which][rank] for rank in range(count) for which in range(groups)], axis=1
    )
    out_sum = ff_sum + dot(attended_own, dense_whole, NT)
    output = own_tokens + out_sum + b_dense.astype(WIDE) + b_fc2.astype(WIDE)

    scaled = normed_grad * gain
    d_tokens = own_grad.astype(WIDE) + rstd * (
        scaled
        - jnp.mean(scaled, axis=-1, keepdims=True)
        - xhat * jnp.mean(scaled * xhat, axis=-1, keepdims=True)
    )

    qkv_bias_part = jnp.concatenate(
        [jnp.sum(part.astype(WIDE), axis=0).reshape(3, lanes) for part in qkv_grads], axis=1
    )
    fc1_bias_part = jnp.sum(expanded_grad.astype(WIDE), axis=0)
    qkv_bias_wide = lax.dynamic_update_slice_in_dim(
        jnp.zeros((3, width), WIDE), qkv_bias_part, me * each, 1
    ).reshape(-1)
    fc1_bias_wide = lax.dynamic_update_slice_in_dim(
        jnp.zeros((b_fc1.shape[0],), WIDE), fc1_bias_part, me * hidden, 0
    )
    small = sum_everywhere(
        jnp.concatenate(
            [
                sums.reshape(-1),
                qkv_bias_wide,
                jnp.sum(sent_grad.astype(WIDE), axis=0),
                fc1_bias_wide,
            ]
        ),
        ("fsdp", "ctx"),
    )
    d_shift, with_normed, d_b_qkv, d_b_out, d_b_fc1 = jnp.split(
        small, [width, 2 * width, 5 * width, 6 * width]
    )
    d_gain = (with_normed - shift * d_shift) / gain
    return (
        output.astype(LOW)[None],
        d_tokens.astype(LOW)[None],
        d_gain,
        d_shift,
        d_qkv,
        d_b_qkv,
        d_dense.astype(WIDE),
        d_b_out,
        d_fc1.astype(WIDE),
        d_b_fc1,
        d_fc2.T.astype(WIDE),
        d_b_out,
    )


def solution(mesh):
    in_specs = (
        P("fsdp", "ctx", None),
        P("fsdp", "ctx", None),
        P("fsdp", None),
        P(),
        P(),
        P("fsdp", None, "ctx"),
        P(),
        P("ctx", "fsdp"),
        P(),
        P("fsdp", "ctx"),
        P(),
        P("ctx", "fsdp"),
        P(),
    )
    out_specs = (
        P("fsdp", "ctx", None),
        P("fsdp", "ctx", None),
        P(),
        P(),
        P("fsdp", None, "ctx"),
        P(),
        P("ctx", "fsdp"),
        P(),
        P("fsdp", "ctx"),
        P(),
        P("ctx", "fsdp"),
        P(),
    )
    return jax.shard_map(shards, mesh=mesh, in_specs=in_specs, out_specs=out_specs, check_vma=False)
```

time: 1270 us -> 920 us (0.72)
  waiting for transfers between devices: 507 us -> 258 us
  matrix products: 300 us -> 160 us
  local copies, waits for them, and re-layouts: 65.1 us -> 92.6 us
  starting transfers between devices: 22.6 us -> 41.3 us
  Pallas kernels: 305 us -> 292 us
    reduce_scatter x4, waiting for transfers between devices: 244 us -> 0.01 us  [scatter_rows(): return lax.psum_scatter(whole, 'fsdp', scatter_dimension=0, tiled=True)]
    dot_general x12 -> x7, matrix products: 300 us -> 160 us  [dot(): return lax.dot_general(left, right, dims, preferred_element_type=WIDE)]
    psum x1 -> x0, waiting for transfers between devices: 35.2 us -> none  [shards(): small = lax.psum(small, ('ctx', 'fsdp'))]
    ppermute x16 -> x31, waiting for transfers between devices: 210 us -> 235 us  [the longest x3 90.3 us: ring_pieces(): from_ahead = lax.ppermute(from_ahead, axis, behind)]
    ppermute x16 -> x31, starting transfers between devices: 17.7 us -> 36 us  [the longest x5 7.43 us: sum_everywhere(): values = values + lax.ppermute(values, axis, pairs)]
    unnamed x60 -> x116, local copies, waits for them, and re-layouts: 31.1 us -> 45.6 us
    pallas_call x1 -> x9, Pallas kernels: 305 us -> 292 us  [the longest x2 164 us: attention(): pl.pallas_call(kernel, out_shape=(jax.ShapeDtypeStruct((blocks, blk, lane...]
  transfers between devices with their start and end apart: 29 -> 42, of which waited for: 16 -> 14; matrix products, arithmetic and copies ran while one was open for 26% -> 31% of each run, Pallas kernels for 24% -> 30%
where the time goes in v2:
time: 920 us; the launch traced here: 912 us
  Pallas kernels  292 us (32%)
  waiting for transfers between devices  258 us (28%)
  matrix products  160 us (17%)
  local copies, waits for them, and re-layouts  92.6 us (10%)
  other arithmetic  53.4 us (6%)
  starting transfers between devices  41.3 us (4%)
  between operations  15.1 us (2%)
    pallas_call x2, Pallas kernels, attention(): pl.pallas_call(kernel, out_shape=(jax.ShapeDtypeStruct((blocks, blk, lane...  164 us
    dot_general x7, matrix products, dot(): return lax.dot_general(left, right, dims, preferred_element_type=WIDE)  160 us
    ppermute x3, waiting for transfers between devices, ring_pieces(): from_ahead = lax.ppermute(from_ahead, axis, behind)  90.3 us
    pallas_call x4, Pallas kernels, input_grad(): pl.pallas_call(functools.partial(input_grad_kernel, terms=len(grads)), ou...  58.6 us
    unnamed x116, local copies, waits for them, and re-layouts  45.6 us
    ppermute x3, waiting for transfers between devices, ring_pieces(): from_behind = lax.ppermute(from_behind, axis, ahead)  44.9 us
    pallas_call x1, Pallas kernels, expand(): pl.pallas_call(functools.partial(expand_kernel, cols=min(512, hidden)), o...  38.7 us
    pallas_call x2, Pallas kernels, pair_grad(): pl.pallas_call(pair_grad_kernel, out_shape=jax.ShapeDtypeStruct((width, c...  30.4 us
  transfers between devices with their start and end apart: 42, of which 14 were waited for; matrix products, arithmetic and copies ran while one was open for 31% of the time, Pallas kernels for 30%

profile of v2, /device:TPU:0, one launch (start us, length us, event | category | flops | bytes accessed | tf_op | source)
XLA Modules:
  0.0 911.9 jit_solution(6909783577781758496)
XLA Ops:
  26.5 49.3 %collective-permute-done.1 = bf16[640,2048]{1,0:T(8,128)(2,1)S(1)} collective-permute-done((bf16[640,2048]{1,0:T(8,128)(2,1)}, bf16[640,2048]{1,0:T(8,128)(2,1)S(1)}, u32[]{:S(2)}, u32[]{:S(2)}) %collective-permute-start.1) | collective-permute-done | bytes 2621472 | tf_op jit(solution)/shard_map/ppermute | solution.py:340
  82.8 26.5 %collective-permute-done.3 = bf16[320,2048]{1,0:T(8,128)(2,1)} collective-permute-done((bf16[320,2048]{1,0:T(8,128)(2,1)S(1)}, bf16[320,2048]{1,0:T(8,128)(2,1)}, u32[]{:S(2)}, u32[]{:S(2)}) %collective-permute-start.3) | collective-permute-done | bytes 1310752 | tf_op jit(solution)/shard_map/ppermute | solution.py:343
  125.4 43.3 %collective-permute-done.4 = bf16[640,2048]{1,0:T(8,128)(2,1)} collective-permute-done((bf16[640,2048]{1,0:T(8,128)(2,1)S(1)}, bf16[640,2048]{1,0:T(8,128)(2,1)}, u32[]{:S(2)}, u32[]{:S(2)}) %collective-permute-start.4) | collective-permute-done | bytes 2621472 | tf_op jit(solution)/shard_map/ppermute | solution.py:339
  171.3 38.7 %expand.1 = (bf16[2560,2048]{1,0:T(8,128)(2,1)}, bf16[2560,2048]{1,0:T(8,128)(2,1)}) custom-call(bf16[2560,2048]{1,0:T(8,128)(2,1)} %constant_dynamic-update-slice_fusion.x_ref.refs_6_, bf16[2048,2048]{1,0:T(8,128)(2,1)} %all-gather.4.cloned.1.call-done.w_ref.refs_5_, f32[1,2048]{1,0:T(1,128)S(1)} %bitcast.112), custom_call_target="tpu_custom_call" | custom-call | flops 1000000 | bytes 1000000 | tf_op jit(solution)/shard_map/expand/pallas_call | solution.py:423
  223.7 14.4 %collective-permute-done.6 = bf16[320,2048]{1,0:T(8,128)(2,1)} collective-permute-done((bf16[320,2048]{1,0:T(8,128)(2,1)}, bf16[320,2048]{1,0:T(8,128)(2,1)}, u32[]{:S(2)}, u32[]{:S(2)}) %collective-permute-start.6) | collective-permute-done | bytes 1310752 | tf_op jit(solution)/shard_map/ppermute | solution.py:343
  243.9 22.3 %add_convert_fusion = bf16[2560,1536]{1,0:T(8,128)(2,1)} fusion(bf16[2560,2048]{1,0:T(8,128)(2,1)} %constant_dynamic-update-slice_fusion.x_ref.refs_6_, f32[1536]{0:T(1024)S(1)} %reshape.262, bf16[2048,2048]{1,0:T(8,128)(2,1)} %all-gather.6.cloned.1.call-done.refs_3_.refs_4_), kind=kOutput, calls=%fused_computation.2 | convolution fusion | flops 16113991680 | bytes 24647680 | tf_op jit(solution)/shard_map/dot_general | solution.py:27
  266.2 10.0 %convolution_convert_fusion.3 = bf16[2560,512]{1,0:T(8,128)(2,1)} fusion(bf16[2560,2048]{1,0:T(8,128)(2,1)} %constant_dynamic-update-slice_fusion.5.y_ref, bf16[2048,2048]{1,0:T(8,128)(2,1)} %all-gather.6.cloned.1.call-done.refs_3_.refs_4_), kind=kOutput, calls=%fused_computation.41 | convolution fusion | flops 5370019840 | bytes 15204352 | tf_op jit(solution)/shard_map/dot_general | solution.py:27
  276.2 28.8 %convolution_convert_fusion.2 = bf16[2048,2048]{1,0:T(8,128)(2,1)} fusion(bf16[2560,2048]{1,0:T(8,128)(2,1)} %constant_dynamic-update-slice_fusion.5.y_ref, bf16[2560,2048]{1,0:T(8,128)(2,1)} %get-tuple-element.57), kind=kOutput, calls=%fused_computation.17 | convolution fusion | flops 21479030784 | bytes 29360128 | tf_op jit(solution)/shard_map/dot_general | solution.py:27
  309.5 41.0 %collective-permute-done.9 = bf16[2048,512]{1,0:T(8,128)(2,1)} collective-permute-done((bf16[2048,512]{1,0:T(8,128)(2,1)S(1)}, bf16[2048,512]{1,0:T(8,128)(2,1)}, u32[]{:S(2)}, u32[]{:S(2)}) %collective-permute-start.9) | collective-permute-done | bytes 2097184 | tf_op jit(solution)/shard_map/ppermute | solution.py:340
  379.6 81.9 %attention.2 = (bf16[40,64,256]{2,1,0:T(8,128)(2,1)}, bf16[40,64,768]{2,1,0:T(8,128)(2,1)}) custom-call(s32[40]{0:T(128)} %select_reduce_fusion.where_ref, bf16[40,64,1536]{2,1,0:T(8,128)(2,1)} %bitcast.113, bf16[40,64,1536]{2,1,0:T(8,128)(2,1)} %bitcast.114, bf16[40,64,1536]{2,1,0:T(8,128)(2,1)} %bitcast.115, bf16[40,64,1536]{2,1,0:T(8,128)(2,1)} %bitcast.116, ...), custom_call_target="tpu_custom_call" | custom-call | flops 1000000 | bytes 1000000 | tf_op jit(solution)/shard_map/attention/pallas_call | solution.py:277
  465.0 15.2 %pair_grad.2 = bf16[2048,1024]{1,0:T(8,128)(2,1)} custom-call(bf16[2560,2048]{1,0:T(8,128)(2,1)} %constant_dynamic-update-slice_fusion.x_ref.refs_6_, bf16[2560,2048]{1,0:T(8,128)(2,1)} %constant_dynamic-update-slice_fusion.5.y_ref, bf16[2560,768]{1,0:T(8,128)(2,1)S(1)} %bitcast.103, bf16[2560,256]{1,0:T(8,128)(2,1)S(1)} %bitcast.111), custom_call_target="tpu_custom_call" | custom-call | flops 1000000 | bytes 1000000 | tf_op jit(solution)/shard_map/pair_grad/pallas_call | solution.py:493
  480.4 26.5 %convolution_convert_fusion = bf16[2560,2048]{1,0:T(8,128)(2,1)S(1)} fusion(bf16[2560,2048]{1,0:T(8,128)(2,1)} %get-tuple-element.57, bf16[2048,2048]{0,1:T(8,128)(2,1)} %all-gather.8.cloned.1.call-done), kind=kOutput, calls=%fused_computation.3 | convolution fusion | flops 21480079360 | bytes 29360128 | tf_op jit(solution)/shard_map/dot_general | solution.py:27
  515.8 29.2 %convert_reduce_fusion = (f32[2048]{0:T(1024)S(1)}, bf16[2560,2048]{1,0:T(8,128)(2,1)}) fusion(bf16[2560,2048]{1,0:T(8,128)(2,1)} %get-tuple-element.60, bf16[2560,2048]{1,0:T(8,128)(2,1)} %constant_dynamic-update-slice_fusion.5.y_ref, bf16[2048,2048]{0,1:T(8,128)(2,1)} %all-gather.8.cloned.1.call-done), kind=kOutput, calls=%fused_computation | convolution fusion | flops 21501048832 | bytes 39854080 | tf_op jit(solution)/shard_map/dot_general | solution.py:27
  545.0 20.2 %collective-permute-done.16 = bf16[320,2048]{1,0:T(8,128)(2,1)} collective-permute-done((bf16[320,2048]{1,0:T(8,128)(2,1)}, bf16[320,2048]{1,0:T(8,128)(2,1)}, u32[]{:S(2)}, u32[]{:S(2)}) %collective-permute-start.16) | collective-permute-done | bytes 1310752 | tf_op jit(solution)/shard_map/ppermute | solution.py:356
  566.9 28.8 %convolution_convert_fusion.1 = bf16[2048,2048]{1,0:T(8,128)(2,1)} fusion(bf16[2560,2048]{1,0:T(8,128)(2,1)} %constant_dynamic-update-slice_fusion.x_ref.refs_6_, bf16[2560,2048]{1,0:T(8,128)(2,1)} %get-tuple-element.74.refs_2_), kind=kOutput, calls=%fused_computation.16 | convolution fusion | flops 21479030784 | bytes 29360128 | tf_op jit(solution)/shard_map/dot_general | solution.py:27
  605.8 24.3 %collective-permute-done.17 = bf16[320,2048]{1,0:T(8,128)(2,1)S(1)} collective-permute-done((bf16[320,2048]{1,0:T(8,128)(2,1)S(1)}, bf16[320,2048]{1,0:T(8,128)(2,1)S(1)}, u32[]{:S(2)}, u32[]{:S(2)}) %collective-permute-start.17) | collective-permute-done | bytes 1310752 | tf_op jit(solution)/shard_map/ppermute | solution.py:367
  631.2 81.9 %attention.3 = (bf16[40,64,256]{2,1,0:T(8,128)(2,1)}, bf16[40,64,768]{2,1,0:T(8,128)(2,1)}) custom-call(s32[40]{0:T(128)} %select_reduce_fusion.where_ref, bf16[40,64,1536]{2,1,0:T(8,128)(2,1)} %bitcast.125, bf16[40,64,1536]{2,1,0:T(8,128)(2,1)} %bitcast.126, bf16[40,64,1536]{2,1,0:T(8,128)(2,1)} %bitcast.127, bf16[40,64,1536]{2,1,0:T(8,128)(2,1)} %bitcast.128, ...), custom_call_target="tpu_custom_call" | custom-call | flops 1000000 | bytes 1000000 | tf_op jit(solution)/shard_map/attention/pallas_call | solution.py:277
  713.9 14.7 %input_grad.4 = (bf16[640,2048]{1,0:T(8,128)(2,1)S(1)}, f32[2,2048]{1,0:T(2,128)S(1)}) custom-call(bf16[2560,768]{1,0:T(8,128)(2,1)} %bitcast.99, bf16[2560,768]{1,0:T(8,128)(2,1)} %bitcast.104, bf16[2560,2048]{1,0:T(8,128)(2,1)} %get-tuple-element.74.refs_2_, bf16[2048,2048]{1,0:T(8,128)(2,1)} %all-gather.6.cloned.1.call-done.refs_3_.refs_4_, ...), custom_call_target="tpu_custom_call" | custom-call | flops 1000000 | bytes 1000000 | tf_op jit(solution)/shard_map/input_grad/pallas_call | solution.py:462
  736.1 14.5 %input_grad.5 = (bf16[640,2048]{1,0:T(8,128)(2,1)S(1)}, f32[2,2048]{1,0:T(2,128)S(1)}) custom-call(bf16[2560,768]{1,0:T(8,128)(2,1)} %bitcast.100, bf16[2560,768]{1,0:T(8,128)(2,1)} %bitcast.105, bf16[2560,2048]{1,0:T(8,128)(2,1)} %get-tuple-element.74.refs_2_, bf16[2048,2048]{1,0:T(8,128)(2,1)} %all-gather.6.cloned.1.call-done.refs_3_.refs_4_, ...), custom_call_target="tpu_custom_call" | custom-call | flops 1000000 | bytes 1000000 | tf_op jit(solution)/shard_map/input_grad/pallas_call | solution.py:462
  752.2 14.6 %input_grad.6 = (bf16[640,2048]{1,0:T(8,128)(2,1)S(1)}, f32[2,2048]{1,0:T(2,128)S(1)}) custom-call(bf16[2560,768]{1,0:T(8,128)(2,1)} %bitcast.101, bf16[2560,768]{1,0:T(8,128)(2,1)} %bitcast.106, bf16[2560,2048]{1,0:T(8,128)(2,1)} %get-tuple-element.74.refs_2_, bf16[2048,2048]{1,0:T(8,128)(2,1)} %all-gather.6.cloned.1.call-done.refs_3_.refs_4_, ...), custom_call_target="tpu_custom_call" | custom-call | flops 1000000 | bytes 1000000 | tf_op jit(solution)/shard_map/input_grad/pallas_call | solution.py:462
  770.5 15.2 %pair_grad.3 = bf16[2048,1024]{1,0:T(8,128)(2,1)} custom-call(bf16[2560,2048]{1,0:T(8,128)(2,1)} %constant_dynamic-update-slice_fusion.x_ref.refs_6_, bf16[2560,2048]{1,0:T(8,128)(2,1)} %constant_dynamic-update-slice_fusion.5.y_ref, bf16[2560,768]{1,0:T(8,128)(2,1)S(1)} %bitcast.108, bf16[2560,256]{1,0:T(8,128)(2,1)S(1)} %bitcast.109), custom_call_target="tpu_custom_call" | custom-call | flops 1000000 | bytes 1000000 | tf_op jit(solution)/shard_map/pair_grad/pallas_call | solution.py:493
  807.9 28.3 %collective-permute-done.23 = bf16[640,256]{1,0:T(8,128)(2,1)S(1)} collective-permute-done((bf16[640,256]{1,0:T(8,128)(2,1)S(1)}, bf16[640,256]{1,0:T(8,128)(2,1)S(1)}, u32[]{:S(2)}, u32[]{:S(2)}) %collective-permute-start.23) | collective-permute-done | bytes 327712 | tf_op jit(solution)/shard_map/ppermute | solution.py:385
  841.6 14.7 %input_grad.7 = (bf16[640,2048]{1,0:T(8,128)(2,1)S(1)}, f32[2,2048]{1,0:T(2,128)S(1)}) custom-call(bf16[2560,768]{1,0:T(8,128)(2,1)} %bitcast.102, bf16[2560,768]{1,0:T(8,128)(2,1)} %bitcast.107, bf16[2560,2048]{1,0:T(8,128)(2,1)} %get-tuple-element.74.refs_2_, bf16[2048,2048]{1,0:T(8,128)(2,1)} %all-gather.6.cloned.1.call-done.refs_3_.refs_4_, ...), custom_call_target="tpu_custom_call" | custom-call | flops 1000000 | bytes 1000000 | tf_op jit(solution)/shard_map/input_grad/pallas_call | solution.py:462
  858.4 14.4 %fusion.29 = bf16[1,640,2048]{2,1,0:T(8,128)(2,1)} fusion(bf16[1,640,2048]{2,1,0:T(8,128)(2,1)} %param.15, bf16[2560,2048]{1,0:T(8,128)(2,1)} %copy-done.20, bf16[320,2048]{1,0:T(8,128)(2,1)} %collective-permute-done.14, bf16[320,2048]{1,0:T(8,128)(2,1)} %collective-permute-done.13, bf16[320,2048]{1,0:T(8,128)(2,1)} %copy-done.45, ...), kind=kOutput, calls=%fused_computation.42 | convolution fusion | flops 5432934400 | bytes 24133632 | tf_op jit(solution)/shard_map/dot_general | solution.py:27
  (282 shorter events, 198.0 us)
Async XLA Ops:
  7.2 164.1 %all-gather.4.cloned.1.call-start = ((), (), s32[]{:S(2)}) async-start(), calls=%async_computation.4 | async-start | bytes 9437184 | tf_op jit(solution)/shard_map/all_gather | solution.py:573
  7.9 236.0 %all-gather.6.cloned.1.call-start = ((), (), s32[]{:S(2)}) async-start(), calls=%async_computation.5 | async-start | bytes 9437184 | tf_op jit(solution)/shard_map/all_gather | solution.py:573
  15.8 60.0 %collective-permute-start.1 = (bf16[640,2048]{1,0:T(8,128)(2,1)}, bf16[640,2048]{1,0:T(8,128)(2,1)S(1)}, u32[]{:S(2)}, u32[]{:S(2)}) collective-permute-start(bf16[640,2048]{1,0:T(8,128)(2,1)} %get-tuple-element.145), channel_id=1, source_target_pairs={{8,0},{24,8},{16,24},{0,16},{9,1},{25,9},{17,25},{1,17},{10,2},{26... | collective-permute-start | bytes 7864328 | tf_op jit(solution)/shard_map/ppermute | solution.py:340
  18.8 58.6 %collective-permute-start = (bf16[640,2048]{1,0:T(8,128)(2,1)}, bf16[640,2048]{1,0:T(8,128)(2,1)}, u32[]{:S(2)}, u32[]{:S(2)}) collective-permute-start(bf16[640,2048]{1,0:T(8,128)(2,1)} %get-tuple-element.145), channel_id=1, source_target_pairs={{0,8},{8,24},{24,16},{16,0},{1,9},{9,25},{25,17},{17,1},{2,10},{10... | collective-permute-start | bytes 7864328 | tf_op jit(solution)/shard_map/ppermute | solution.py:339
  77.5 403.0 %all-gather.8.cloned.1.call-start = ((), (), s32[]{:S(2)}) async-start(), calls=%async_computation.6 | async-start | bytes 9437184 | tf_op jit(solution)/shard_map/all_gather | solution.py:573
  111.9 403.9 %reduce-scatter.5.cloned.1.call-start = ((), (), s32[]{:S(2)}) async-start(), calls=%async_computation.7 | async-start | bytes 9437184 | tf_op jit(solution)/shard_map/reduce_scatter | solution.py:576
  112.0 56.8 %collective-permute-start.4 = (bf16[640,2048]{1,0:T(8,128)(2,1)S(1)}, bf16[640,2048]{1,0:T(8,128)(2,1)}, u32[]{:S(2)}, u32[]{:S(2)}) collective-permute-start(bf16[640,2048]{1,0:T(8,128)(2,1)S(1)} %bitcast.145), channel_id=1, source_target_pairs={{0,8},{8,24},{24,16},{16,0},{1,9},{9,25},{25,17},{17,1},{2,10},{10... | collective-permute-start | bytes 7864328 | tf_op jit(solution)/shard_map/ppermute | solution.py:339
  112.6 98.2 %collective-permute-start.5 = (bf16[640,2048]{1,0:T(8,128)(2,1)S(1)}, bf16[640,2048]{1,0:T(8,128)(2,1)}, u32[]{:S(2)}, u32[]{:S(2)}) collective-permute-start(bf16[640,2048]{1,0:T(8,128)(2,1)S(1)} %bitcast.146), channel_id=1, source_target_pairs={{8,0},{24,8},{16,24},{0,16},{9,1},{25,9},{17,25},{1,17},{10,2},{26... | collective-permute-start | bytes 7864328 | tf_op jit(solution)/shard_map/ppermute | solution.py:340
  305.0 326.1 %reduce-scatter.7.cloned.1.call-start = ((), (), s32[]{:S(2)}) async-start(), calls=%async_computation.8 | async-start | bytes 4718592 | tf_op jit(solution)/shard_map/reduce_scatter | solution.py:576
  306.8 43.7 %collective-permute-start.9 = (bf16[2048,512]{1,0:T(8,128)(2,1)S(1)}, bf16[2048,512]{1,0:T(8,128)(2,1)}, u32[]{:S(2)}, u32[]{:S(2)}) collective-permute-start(bf16[2048,512]{1,0:T(8,128)(2,1)S(1)} %slice.172), channel_id=1, source_target_pairs={{8,0},{24,8},{16,24},{0,16},{9,1},{25,9},{17,25},{1,17},{10,2},{26... | collective-permute-start | bytes 6291464 | tf_op jit(solution)/shard_map/ppermute | solution.py:340
  308.0 45.8 %collective-permute-start.8 = (bf16[2048,512]{1,0:T(8,128)(2,1)S(1)}, bf16[2048,512]{1,0:T(8,128)(2,1)}, u32[]{:S(2)}, u32[]{:S(2)}) collective-permute-start(bf16[2048,512]{1,0:T(8,128)(2,1)S(1)} %slice.172), channel_id=1, source_target_pairs={{0,8},{8,24},{24,16},{16,0},{1,9},{9,25},{25,17},{17,1},{2,10},{10... | collective-permute-start | bytes 6291464 | tf_op jit(solution)/shard_map/ppermute | solution.py:339
  352.8 127.6 %collective-permute-start.11 = (bf16[1024,512]{1,0:T(8,128)(2,1)}, bf16[1024,512]{1,0:T(8,128)(2,1)}, u32[]{:S(2)}, u32[]{:S(2)}) collective-permute-start(bf16[1024,512]{1,0:T(8,128)(2,1)} %slice.174), channel_id=1, source_target_pairs={{8,0},{24,8},{16,24},{0,16},{9,1},{25,9},{17,25},{1,17},{10,2},{26... | collective-permute-start | bytes 3145736 | tf_op jit(solution)/shard_map/ppermute | solution.py:343
  356.1 124.3 %collective-permute-start.10 = (bf16[1024,512]{1,0:T(8,128)(2,1)}, bf16[1024,512]{1,0:T(8,128)(2,1)}, u32[]{:S(2)}, u32[]{:S(2)}) collective-permute-start(bf16[1024,512]{1,0:T(8,128)(2,1)} %slice.173), channel_id=1, source_target_pairs={{0,8},{8,24},{24,16},{16,0},{1,9},{9,25},{25,17},{17,1},{2,10},{10... | collective-permute-start | bytes 3145736 | tf_op jit(solution)/shard_map/ppermute | solution.py:343
  480.2 288.2 %reduce-scatter.9.cloned.1.call-start = ((), (), s32[]{:S(2)}) async-start(), calls=%async_computation.9 | async-start | bytes 9437184 | tf_op jit(solution)/shard_map/reduce_scatter | solution.py:576
  512.8 52.4 %collective-permute-start.16 = (bf16[320,2048]{1,0:T(8,128)(2,1)}, bf16[320,2048]{1,0:T(8,128)(2,1)}, u32[]{:S(2)}, u32[]{:S(2)}) collective-permute-start(bf16[320,2048]{1,0:T(8,128)(2,1)} %get-tuple-element.147), channel_id=1, source_target_pairs={{8,0},{24,8},{16,24},{0,16},{9,1},{25,9},{17,25},{1,17},{10,2},{26... | collective-permute-start | bytes 3932168 | tf_op jit(solution)/shard_map/ppermute | solution.py:356
  514.2 51.0 %collective-permute-start.14 = (bf16[320,2048]{1,0:T(8,128)(2,1)S(1)}, bf16[320,2048]{1,0:T(8,128)(2,1)}, u32[]{:S(2)}, u32[]{:S(2)}) collective-permute-start(bf16[320,2048]{1,0:T(8,128)(2,1)S(1)} %get-tuple-element.148), channel_id=1, source_target_pairs={{0,8},{8,24},{24,16},{16,0},{1,9},{9,25},{25,17},{17,1},{2,10},{10... | collective-permute-start | bytes 3932168 | tf_op jit(solution)/shard_map/ppermute | solution.py:363
  514.8 52.1 %collective-permute-start.12 = (bf16[320,2048]{1,0:T(8,128)(2,1)S(1)}, bf16[320,2048]{1,0:T(8,128)(2,1)}, u32[]{:S(2)}, u32[]{:S(2)}) collective-permute-start(bf16[320,2048]{1,0:T(8,128)(2,1)S(1)} %get-tuple-element.149), channel_id=1, source_target_pairs={{0,8},{8,24},{24,16},{16,0},{1,9},{9,25},{25,17},{17,1},{2,10},{10... | collective-permute-start | bytes 3932168 | tf_op jit(solution)/shard_map/ppermute | solution.py:356
  595.7 303.6 %reduce-scatter.11.cloned.1.call-start = ((), (), s32[]{:S(2)}) async-start(), calls=%async_computation.10 | async-start | bytes 4718592 | tf_op jit(solution)/shard_map/reduce_scatter | solution.py:576
  602.5 110.6 %collective-permute-start.19 = (bf16[640,256]{1,0:T(8,128)(2,1)}, bf16[640,256]{1,0:T(8,128)(2,1)S(1)}, u32[]{:S(2)}, u32[]{:S(2)}) collective-permute-start(bf16[640,256]{1,0:T(8,128)(2,1)} %bitcast.22), channel_id=1, source_target_pairs={{0,16},{8,0},{24,8},{16,24},{1,17},{9,1},{25,9},{17,25},{2,18},{10... | collective-permute-start | bytes 983048 | tf_op jit(solution)/shard_map/ppermute | solution.py:385
  602.8 110.3 %collective-permute-start.20 = (bf16[640,256]{1,0:T(8,128)(2,1)}, bf16[640,256]{1,0:T(8,128)(2,1)S(1)}, u32[]{:S(2)}, u32[]{:S(2)}) collective-permute-start(bf16[640,256]{1,0:T(8,128)(2,1)} %bitcast.23), channel_id=1, source_target_pairs={{0,24},{8,16},{24,0},{16,8},{1,25},{9,17},{25,1},{17,9},{2,26},{10... | collective-permute-start | bytes 983048 | tf_op jit(solution)/shard_map/ppermute | solution.py:385
  604.5 108.6 %collective-permute-start.18 = (bf16[640,256]{1,0:T(8,128)(2,1)S(1)}, bf16[640,256]{1,0:T(8,128)(2,1)S(1)}, u32[]{:S(2)}, u32[]{:S(2)}) collective-permute-start(bf16[640,256]{1,0:T(8,128)(2,1)S(1)} %bitcast.156), channel_id=1, source_target_pairs={{0,8},{8,24},{24,16},{16,0},{1,9},{9,25},{25,17},{17,1},{2,10},{10... | collective-permute-start | bytes 983048 | tf_op jit(solution)/shard_map/ppermute | solution.py:385
  795.0 80.5 %collective-permute-start.27 = (bf16[320,2048]{1,0:T(8,128)(2,1)}, bf16[320,2048]{1,0:T(8,128)(2,1)}, u32[]{:S(2)}, u32[]{:S(2)}) collective-permute-start(bf16[320,2048]{1,0:T(8,128)(2,1)} %slice.150), channel_id=1, source_target_pairs={{0,8},{8,24},{24,16},{16,0},{1,9},{9,25},{25,17},{17,1},{2,10},{10... | collective-permute-start | bytes 3932168 | tf_op jit(solution)/shard_map/ppermute | solution.py:363
  795.8 79.8 %collective-permute-start.28 = (bf16[320,2048]{1,0:T(8,128)(2,1)}, bf16[320,2048]{1,0:T(8,128)(2,1)}, u32[]{:S(2)}, u32[]{:S(2)}) collective-permute-start(bf16[320,2048]{1,0:T(8,128)(2,1)} %slice.151), channel_id=1, source_target_pairs={{8,0},{24,8},{16,24},{0,16},{9,1},{25,9},{17,25},{1,17},{10,2},{26... | collective-permute-start | bytes 3932168 | tf_op jit(solution)/shard_map/ppermute | solution.py:364
  798.1 58.3 %collective-permute-start.25 = (bf16[640,256]{1,0:T(8,128)(2,1)S(1)}, bf16[640,256]{1,0:T(8,128)(2,1)S(1)}, u32[]{:S(2)}, u32[]{:S(2)}) collective-permute-start(bf16[640,256]{1,0:T(8,128)(2,1)S(1)} %get-tuple-element.154), channel_id=1, source_target_pairs={{0,24},{8,16},{24,0},{16,8},{1,25},{9,17},{25,1},{17,9},{2,26},{10... | collective-permute-start | bytes 983048 | tf_op jit(solution)/shard_map/ppermute | solution.py:385
  (67 other events, 945.1 us)
Sparse Core Ops, SparseCore 0:
  9.6 84.7 all-gather.3
  96.6 80.5 all-gather.5
  178.8 81.0 all-gather.7
  305.1 90.6 reduce-scatter.4
  480.3 50.5 reduce-scatter.6
  595.8 88.4 reduce-scatter.8
  785.8 48.5 reduce-scatter.10

commit v3 on v2

--- a/solution.py
+++ b/solution.py
@@ -314,7 +314,7 @@
 
 
 def after(value, *others):
-    return lax.optimization_barrier((value,) + others)[0]
+    return lax.optimization_barrier((value,) + others)[0] if others else value
 
 
 def ring_of(count):
@@ -339,12 +339,16 @@
         from_behind = lax.ppermute(from_behind, axis, ahead)
         from_ahead = lax.ppermute(from_ahead, axis, behind)
         pieces += [from_behind, from_ahead]
-    from_behind, from_ahead = after(from_behind[:half], *gate), after(from_ahead[half:], *gate)
-    far = [lax.ppermute(from_behind, axis, ahead), lax.ppermute(from_ahead, axis, behind)]
+    if gate:
+        from_behind, from_ahead = after(from_behind, *gate), after(from_ahead, *gate)
+    far = [
+        lax.ppermute(from_behind[:half], axis, ahead),
+        lax.ppermute(from_ahead[half:], axis, behind),
+    ]
     return pieces + far
 
 
-def ring_reduce(part, own, axis):
+def ring_reduce(part, own, axis, staged=False):
     count = lax.axis_size(axis)
     _, ahead, behind = ring_of(count)
     far = part(count - 1)
@@ -354,25 +358,28 @@
         return (a.astype(WIDE) + b.astype(WIDE)).astype(LOW)
 
     up, down = lax.ppermute(far[:half], axis, ahead), lax.ppermute(far[half:], axis, behind)
-    far = early = (up, down)
+    first = second = last = (up, down)
     if count == 2:
-        return own(early).astype(WIDE) + jnp.concatenate(early, axis=0).astype(WIDE), early, early
+        mine = own(first, second).astype(WIDE)
+        return mine + jnp.concatenate(first, axis=0).astype(WIDE), first, second, last
     for s in range(count // 2 - 1, 0, -1):
         to_ahead, to_behind = part(2 * s), part(2 * s - 1)
         if s == count // 2 - 1:
-            free_up = lax.ppermute(to_ahead[half:], axis, ahead)
-            free_down = lax.ppermute(to_behind[:half], axis, behind)
-            early += (free_up, free_down)
             up = lax.ppermute(plus(to_ahead[:half], up), axis, ahead)
             down = lax.ppermute(plus(to_behind[half:], down), axis, behind)
-            late = (up, down)
+            second = (up, down)
+            gate = second if staged else ()
+            free_up = lax.ppermute(after(to_ahead[half:], *gate), axis, ahead)
+            free_down = lax.ppermute(after(to_behind[:half], *gate), axis, behind)
+            last = (free_up, free_down)
             up = jnp.concatenate([up, free_up], axis=0)
             down = jnp.concatenate([free_down, down], axis=0)
         else:
             up = lax.ppermute(plus(to_ahead, up), axis, ahead)
             down = lax.ppermute(plus(to_behind, down), axis, behind)
-            late = (up, down)
-    return own(far).astype(WIDE) + up.astype(WIDE) + down.astype(WIDE), early, late
+            last = (up, down)
+    total = own(first, second).astype(WIDE) + up.astype(WIDE) + down.astype(WIDE)
+    return total, first, second, last
 
 
 def ring_exchange(part, axis):
@@ -433,7 +440,11 @@
         compiler_params=pltpu.CompilerParams(
             dimension_semantics=("arbitrary",), vmem_limit_bytes=48 << 20
         ),
-        cost_estimate=LITTLE,
+        cost_estimate=pl.CostEstimate(
+            flops=2 * rows * width * hidden,
+            bytes_accessed=2 * (rows * width + width * hidden + 2 * rows * hidden),
+            transcendentals=rows * hidden,
+        ),
         name="expand",
     )(x, w, b.astype(WIDE)[None])
 
@@ -586,8 +597,8 @@
     normed = jnp.concatenate(normed_pieces, axis=0)
     attention_shard = jnp.concatenate([by_group(w_qkv), w_dense.T], axis=1)
     fc1_weight = gather_rows(w_fc1)
-    attention_weight = gather_rows(after(attention_shard, *normed_pieces[1:-2]))
-    fc2_turned = gather_rows(after(w_fc2.T, *normed_pieces[-2:]))
+    fc2_turned = gather_rows(after(w_fc2.T, *normed_pieces[1:-2]))
+    attention_weight = gather_rows(after(attention_shard, *normed_pieces[-2:]))
     qkv_weight, dense_turned = attention_weight[:, : 3 * each], attention_weight[:, 3 * each :]
 
     fc1_bias = lax.dynamic_slice_in_dim(b_fc1, me * hidden, hidden, 0)
@@ -596,40 +607,32 @@
 
     sent_grad = after(own_grad, *normed_pieces[-2:])
     grad_pieces = ring_pieces(sent_grad, "ctx", gate=(activated,))
-    grads = jnp.concatenate(grad_pieces, axis=0)
-
-    qkv = dot(after(normed, activated), qkv_weight, NN)
+    ff_part = dot(activated, fc2_turned, NT).astype(LOW)
+    grads = jnp.concatenate([after(piece, ff_part) for piece in grad_pieces], axis=0)
+    ff_sum, first, second, last = ring_reduce(
+        lambda rank: of_rank(ff_part, rank), lambda *_: of_rank(ff_part, 0), "ctx", staged=True
+    )
+
+    gated = after(grads, ff_part)
+    expanded_grad = (dot(gated, fc2_turned, NN) * slope.astype(WIDE)).astype(LOW)
+    d_fc2_part = dot(after(grads, expanded_grad, *first), activated, TN).astype(LOW)
+    d_fc2 = scatter_rows(d_fc2_part)
+    qkv = dot(after(normed, d_fc2_part), qkv_weight, NN)
     qkv = (qkv + by_group(qkv_bias)[0].astype(WIDE)).astype(LOW)
     attended_grad = dot(after(grads, qkv), dense_turned, NN).astype(LOW)
-    d_fc2_part = dot(after(grads, attended_grad), activated, TN).astype(LOW)
-    d_fc2 = scatter_rows(d_fc2_part)
-
-    dense_pieces = ring_pieces(dense_turned, "ctx")
+    gated = after(normed, attended_grad, *second)
+    d_fc1_part = dot(gated, expanded_grad, TN).astype(LOW)
+    d_fc1 = scatter_rows(d_fc1_part)
+
+    dense_pieces = ring_pieces(after(dense_turned, *second), "ctx")
     dense_whole = jnp.concatenate(
         dense_pieces[:-2] + [jnp.concatenate(dense_pieces[-2:], axis=0)], axis=1
     )
 
-    def feed_forward(gate, later):
-        act = after(activated, *gate)
-        ff_part = dot(act, fc2_turned, NT).astype(LOW)
-        ff_sum, early, late = ring_reduce(
-            lambda rank: of_rank(ff_part, rank), lambda _: of_rank(ff_part, 0), "ctx"
-        )
-        gated = after(grads, ff_part, *later)
-        expanded_grad = (dot(gated, fc2_turned, NN) * slope.astype(WIDE)).astype(LOW)
-        d_fc1_part = dot(after(normed, expanded_grad, *early), expanded_grad, TN).astype(LOW)
-        return ff_sum, late, expanded_grad, d_fc1_part, scatter_rows(d_fc1_part)
-
     tabs = rope_tables(rows)
     attended, qkv_grads, d_attention, swapped = [], [], [], []
-    ordered = (d_fc2_part,)
+    ordered = (d_fc1_part,)
     for which in range(groups):
-        if which == groups - 1:
-            gate = (d_part,) + tuple(dense_pieces) if which else ()
-            ff_sum, ff_late, expanded_grad, d_fc1_part, d_fc1 = feed_forward(
-                gate, (d_fc2,) if which else ()
-            )
-            ordered = (d_fc1_part,) + ff_late + tuple(d_attention)
         got, got_grads = attention(
             after(qkv, *ordered), attended_grad, where, tabs, lanes, which, head_dim
         )
@@ -637,36 +640,40 @@
         qkv_grads.append(got_grads)
         if which < groups - 1:
             swapped.append(ring_exchange(lambda rank, got=got: of_rank(got, rank), "ctx"))
-            d_part = pair_grad(normed, grads, got_grads, got)
+            gated = after(normed, d_fc2, *last, *dense_pieces[1:-2]) if which == 0 else normed
+            d_part = pair_grad(gated, grads, got_grads, got)
             ordered = (d_part,)
             d_attention.append(scatter_rows(d_part))
 
     weights = [(attention_weight, which) for which in range(groups)] + [(fc1_weight, 0)]
     parts, sums = [None] * count, 0.0
     early_swaps = [piece for pieces in swapped for piece in pieces]
-    turn = after(expanded_grad, *early_swaps, *attended)
+    turn = after(expanded_grad, d_fc1, *dense_pieces[-2:], *early_swaps, *attended)
+    swapped.append(ring_exchange(lambda rank: of_rank(attended[-1], rank), "ctx"))
 
     def input_part(rank, turn):
         return input_grad(qkv_grads + [turn], weights, normed, rank, local_rows)
 
     for rank in range(count - 1, 0, -1):
+        if rank == 1:
+            turn = after(turn, *swapped[-1])
         parts[rank], part_sums = input_part(rank, turn)
         sums = sums + part_sums
         turn = after(turn, parts[rank])
+        if rank == count - 1:
+            gated = after(normed, parts[rank], *d_attention)
+            d_part = pair_grad(gated, grads, qkv_grads[-1], attended[-1])
+            d_attention.append(scatter_rows(d_part))
+            turn = after(turn, d_part)
 
     own_sums = []
 
-    def own_part(arrived):
-        gated = after(normed, parts[1], d_fc1, *arrived)
-        d_part = pair_grad(gated, grads, qkv_grads[-1], attended[-1])
-        d_attention.append(scatter_rows(d_part))
-        got = after(attended[-1], *arrived)
-        swapped.append(ring_exchange(lambda rank: of_rank(got, rank), "ctx"))
-        part, part_sums = input_part(0, after(turn, d_part))
+    def own_part(first, second):
+        part, part_sums = input_part(0, after(turn, *first))
         own_sums.append(part_sums)
         return part
 
-    normed_grad, _, _ = ring_reduce(lambda rank: parts[rank], own_part, "ctx")
+    normed_grad, *_ = ring_reduce(lambda rank: parts[rank], own_part, "ctx")
     sums = sums + own_sums[0]
 
     d_qkv = jnp.concatenate(

time: 920 us -> 795 us (0.86)
  waiting for transfers between devices: 258 us -> 129 us
    ppermute x3, waiting for transfers between devices: 90.3 us -> 1.44 us  [ring_pieces(): from_ahead = lax.ppermute(from_ahead, axis, behind)]
    ppermute x5, waiting for transfers between devices: 3.06 us -> 38.2 us  [sum_everywhere(): values = values + lax.ppermute(values, axis, pairs)]
    ppermute x6, waiting for transfers between devices: 28.3 us -> 0.02 us  [ring_exchange(): lax.ppermute(part(rank_of(offset, count)), axis, hops)]
    ppermute x2, waiting for transfers between devices: 24.3 us -> 0.01 us  [ring_reduce(): down = lax.ppermute(plus(to_behind[half:], down), axis, behind)]
    ppermute x10, waiting for transfers between devices: 44.3 us -> 22.8 us  [the longest x3 20.5 us: ring_pieces(): lax.ppermute(from_behind[:half], axis, ahead)]
    ppermute x3, waiting for transfers between devices: 44.9 us -> 65.8 us  [ring_pieces(): from_behind = lax.ppermute(from_behind, axis, ahead)]
    ppermute x2, waiting for transfers between devices: 20.2 us -> 0.01 us  [ring_reduce(): lax.ppermute(far[half:], axis, behind)]
    unnamed x116 -> x95, local copies, waits for them, and re-layouts: 45.6 us -> 49.2 us
  transfers between devices with their start and end apart: 42 -> 42, of which waited for: 14 -> 8; matrix products, arithmetic and copies ran while one was open for 31% -> 37% of each run, Pallas kernels for 30% -> 37%
where the time goes in v3:
time: 795 us; the launch traced here: 788 us
  Pallas kernels  291 us (37%)
  matrix products  161 us (20%)
  waiting for transfers between devices  129 us (16%)
  local copies, waits for them, and re-layouts  95.2 us (12%)
  other arithmetic  55.5 us (7%)
  starting transfers between devices  39.8 us (5%)
  between operations  15 us (2%)
    pallas_call x2, Pallas kernels, attention(): pl.pallas_call(kernel, out_shape=(jax.ShapeDtypeStruct((blocks, blk, lane...  164 us
    dot_general x7, matrix products, dot(): return lax.dot_general(left, right, dims, preferred_element_type=WIDE)  161 us
    ppermute x3, waiting for transfers between devices, ring_pieces(): from_behind = lax.ppermute(from_behind, axis, ahead)  65.8 us
    pallas_call x4, Pallas kernels, input_grad(): pl.pallas_call(functools.partial(input_grad_kernel, terms=len(grads)), ou...  58.5 us
    unnamed x95, local copies, waits for them, and re-layouts  49.2 us
    pallas_call x1, Pallas kernels, expand(): pl.pallas_call(functools.partial(expand_kernel, cols=min(512, hidden)), o...  38.7 us
    ppermute x5, waiting for transfers between devices, sum_everywhere(): values = values + lax.ppermute(values, axis, pairs)  38.2 us
    pallas_call x2, Pallas kernels, pair_grad(): pl.pallas_call(pair_grad_kernel, out_shape=jax.ShapeDtypeStruct((width, c...  30.4 us
  transfers between devices with their start and end apart: 42, of which 8 were waited for; matrix products, arithmetic and copies ran while one was open for 37% of the time, Pallas kernels for 37%

profile of v3, /device:TPU:0, one launch (start us, length us, event | category | flops | bytes accessed | tf_op | source)
XLA Modules:
  0.0 787.5 jit_solution(6875492598914753272)
XLA Ops:
  17.9 56.8 %collective-permute-done = bf16[640,2048]{1,0:T(8,128)(2,1)S(1)} collective-permute-done((bf16[640,2048]{1,0:T(8,128)(2,1)S(1)}, bf16[640,2048]{1,0:T(8,128)(2,1)S(1)}, u32[]{:S(2)}, u32[]{:S(2)}) %collective-permute-start) | collective-permute-done | bytes 2621472 | tf_op jit(solution)/shard_map/ppermute | solution.py:339
  89.7 20.5 %collective-permute-done.2 = bf16[320,2048]{1,0:T(8,128)(2,1)} collective-permute-done((bf16[320,2048]{1,0:T(8,128)(2,1)}, bf16[320,2048]{1,0:T(8,128)(2,1)}, u32[]{:S(2)}, u32[]{:S(2)}) %collective-permute-start.2) | collective-permute-done | bytes 1310752 | tf_op jit(solution)/shard_map/ppermute | solution.py:345
  121.5 38.7 %expand.1 = (bf16[2560,2048]{1,0:T(8,128)(2,1)}, bf16[2560,2048]{1,0:T(8,128)(2,1)}) custom-call(bf16[2560,2048]{1,0:T(8,128)(2,1)} %constant_dynamic-update-slice_fusion.x_ref.refs_6_, bf16[2048,2048]{1,0:T(8,128)(2,1)} %all-gather.4.cloned.1.call-done.w_ref.refs_5_, f32[1,2048]{1,0:T(1,128)S(1)} %bitcast.115), custom_call_target="tpu_custom_call" | custom-call | flops 21474836480 | bytes 39845888 | tf_op jit(solution)/shard_map/expand/pallas_call | solution.py:430
  160.2 9.0 %collective-permute-done.10 = bf16[640,2048]{1,0:T(8,128)(2,1)} collective-permute-done((bf16[640,2048]{1,0:T(8,128)(2,1)S(1)}, bf16[640,2048]{1,0:T(8,128)(2,1)}, u32[]{:S(2)}, u32[]{:S(2)}) %collective-permute-start.10) | collective-permute-done | bytes 2621472 | tf_op jit(solution)/shard_map/ppermute | solution.py:339
  177.1 26.5 %convolution_convert_fusion = bf16[2560,2048]{1,0:T(8,128)(2,1)S(1)} fusion(bf16[2560,2048]{1,0:T(8,128)(2,1)} %get-tuple-element.55, bf16[2048,2048]{0,1:T(8,128)(2,1)} %all-gather.6.cloned.1.call-done), kind=kOutput, calls=%fused_computation.3 | convolution fusion | flops 21480079360 | bytes 29360128 | tf_op jit(solution)/shard_map/dot_general | solution.py:27
  224.3 29.1 %convert_reduce_fusion = (f32[2048]{0:T(1024)S(1)}, bf16[2560,2048]{1,0:T(8,128)(2,1)}) fusion(bf16[2560,2048]{1,0:T(8,128)(2,1)} %get-tuple-element.68, bf16[2560,2048]{1,0:T(8,128)(2,1)} %constant_dynamic-update-slice_fusion.5.y_ref, bf16[2048,2048]{0,1:T(8,128)(2,1)} %all-gather.6.cloned.1.call-done), kind=kOutput, calls=%fused_computation | convolution fusion | flops 21501048832 | bytes 39854080 | tf_op jit(solution)/shard_map/dot_general | solution.py:27
  255.5 29.0 %convolution_convert_fusion.2 = bf16[2048,2048]{1,0:T(8,128)(2,1)} fusion(bf16[2560,2048]{1,0:T(8,128)(2,1)} %constant_dynamic-update-slice_fusion.5.y_ref, bf16[2560,2048]{1,0:T(8,128)(2,1)} %get-tuple-element.55), kind=kOutput, calls=%fused_computation.17 | convolution fusion | flops 21479030784 | bytes 29360128 | tf_op jit(solution)/shard_map/dot_general | solution.py:27
  292.6 22.2 %add_convert_fusion = bf16[2560,1536]{1,0:T(8,128)(2,1)} fusion(bf16[2560,2048]{1,0:T(8,128)(2,1)} %constant_dynamic-update-slice_fusion.x_ref.refs_6_, f32[1536]{0:T(1024)S(1)} %reshape.266, bf16[2048,2048]{1,0:T(8,128)(2,1)} %all-gather.8.cloned.1.call-done.refs_3_.refs_4_), kind=kOutput, calls=%fused_computation.2 | convolution fusion | flops 16113991680 | bytes 24647680 | tf_op jit(solution)/shard_map/dot_general | solution.py:27
  314.9 10.0 %convolution_convert_fusion.3 = bf16[2560,512]{1,0:T(8,128)(2,1)} fusion(bf16[2560,2048]{1,0:T(8,128)(2,1)} %constant_dynamic-update-slice_fusion.5.y_ref, bf16[2048,2048]{1,0:T(8,128)(2,1)} %all-gather.8.cloned.1.call-done.refs_3_.refs_4_), kind=kOutput, calls=%fused_computation.41 | convolution fusion | flops 5370019840 | bytes 15204352 | tf_op jit(solution)/shard_map/dot_general | solution.py:27
  324.9 29.9 %convolution_convert_fusion.1 = bf16[2048,2048]{1,0:T(8,128)(2,1)} fusion(bf16[2560,2048]{1,0:T(8,128)(2,1)} %constant_dynamic-update-slice_fusion.x_ref.refs_6_, bf16[2560,2048]{1,0:T(8,128)(2,1)} %get-tuple-element.92.refs_2_), kind=kOutput, calls=%fused_computation.16 | convolution fusion | flops 21479030784 | bytes 29360128 | tf_op jit(solution)/shard_map/dot_general | solution.py:27
  362.7 6.4 fusion.31
  385.0 81.9 %attention.2 = (bf16[40,64,256]{2,1,0:T(8,128)(2,1)}, bf16[40,64,768]{2,1,0:T(8,128)(2,1)}) custom-call(s32[40]{0:T(128)} %select_reduce_fusion.where_ref, bf16[40,64,1536]{2,1,0:T(8,128)(2,1)} %bitcast.116, bf16[40,64,1536]{2,1,0:T(8,128)(2,1)} %bitcast.117, bf16[40,64,1536]{2,1,0:T(8,128)(2,1)} %bitcast.118, bf16[40,64,1536]{2,1,0:T(8,128)(2,1)} %bitcast.119, ...), custom_call_target="tpu_custom_call" | custom-call | flops 1000000 | bytes 1000000 | tf_op jit(solution)/shard_map/attention/pallas_call | solution.py:277
  470.4 15.2 %pair_grad.2 = bf16[2048,1024]{1,0:T(8,128)(2,1)} custom-call(bf16[2560,2048]{1,0:T(8,128)(2,1)} %constant_dynamic-update-slice_fusion.x_ref.refs_6_, bf16[2560,2048]{1,0:T(8,128)(2,1)} %constant_dynamic-update-slice_fusion.5.y_ref, bf16[2560,768]{1,0:T(8,128)(2,1)S(1)} %bitcast.107, bf16[2560,256]{1,0:T(8,128)(2,1)S(1)} %bitcast.114), custom_call_target="tpu_custom_call" | custom-call | flops 1000000 | bytes 1000000 | tf_op jit(solution)/shard_map/pair_grad/pallas_call | solution.py:504
  500.8 81.9 %attention.3 = (bf16[40,64,256]{2,1,0:T(8,128)(2,1)}, bf16[40,64,768]{2,1,0:T(8,128)(2,1)}) custom-call(s32[40]{0:T(128)} %select_reduce_fusion.where_ref, bf16[40,64,1536]{2,1,0:T(8,128)(2,1)} %bitcast.128, bf16[40,64,1536]{2,1,0:T(8,128)(2,1)} %bitcast.129, bf16[40,64,1536]{2,1,0:T(8,128)(2,1)} %bitcast.130, bf16[40,64,1536]{2,1,0:T(8,128)(2,1)} %bitcast.131, ...), custom_call_target="tpu_custom_call" | custom-call | flops 1000000 | bytes 1000000 | tf_op jit(solution)/shard_map/attention/pallas_call | solution.py:277
  589.5 14.6 %input_grad.4 = (bf16[640,2048]{1,0:T(8,128)(2,1)S(1)}, f32[2,2048]{1,0:T(2,128)S(1)}) custom-call(bf16[2560,768]{1,0:T(8,128)(2,1)} %bitcast.103, bf16[2560,768]{1,0:T(8,128)(2,1)} %bitcast.108, bf16[2560,2048]{1,0:T(8,128)(2,1)} %get-tuple-element.92.refs_2_, bf16[2048,2048]{1,0:T(8,128)(2,1)} %all-gather.8.cloned.1.call-done.refs_3_.refs_4_, ...), custom_call_target="tpu_custom_call" | custom-call | flops 1000000 | bytes 1000000 | tf_op jit(solution)/shard_map/input_grad/pallas_call | solution.py:473
  610.0 15.3 %pair_grad.3 = bf16[2048,1024]{1,0:T(8,128)(2,1)} custom-call(bf16[2560,2048]{1,0:T(8,128)(2,1)} %constant_dynamic-update-slice_fusion.x_ref.refs_6_, bf16[2560,2048]{1,0:T(8,128)(2,1)} %constant_dynamic-update-slice_fusion.5.y_ref, bf16[2560,768]{1,0:T(8,128)(2,1)S(1)} %bitcast.112, bf16[2560,256]{1,0:T(8,128)(2,1)S(1)} %bitcast.113), custom_call_target="tpu_custom_call" | custom-call | flops 1000000 | bytes 1000000 | tf_op jit(solution)/shard_map/pair_grad/pallas_call | solution.py:504
  638.3 14.7 %input_grad.5 = (bf16[640,2048]{1,0:T(8,128)(2,1)S(1)}, f32[2,2048]{1,0:T(2,128)S(1)}) custom-call(bf16[2560,768]{1,0:T(8,128)(2,1)} %bitcast.104, bf16[2560,768]{1,0:T(8,128)(2,1)} %bitcast.109, bf16[2560,2048]{1,0:T(8,128)(2,1)} %get-tuple-element.92.refs_2_, bf16[2048,2048]{1,0:T(8,128)(2,1)} %all-gather.8.cloned.1.call-done.refs_3_.refs_4_, ...), custom_call_target="tpu_custom_call" | custom-call | flops 1000000 | bytes 1000000 | tf_op jit(solution)/shard_map/input_grad/pallas_call | solution.py:473
  653.0 14.7 %input_grad.6 = (bf16[640,2048]{1,0:T(8,128)(2,1)S(1)}, f32[2,2048]{1,0:T(2,128)S(1)}) custom-call(bf16[2560,768]{1,0:T(8,128)(2,1)} %bitcast.105, bf16[2560,768]{1,0:T(8,128)(2,1)} %bitcast.110, bf16[2560,2048]{1,0:T(8,128)(2,1)} %get-tuple-element.92.refs_2_, bf16[2048,2048]{1,0:T(8,128)(2,1)} %all-gather.8.cloned.1.call-done.refs_3_.refs_4_, ...), custom_call_target="tpu_custom_call" | custom-call | flops 1000000 | bytes 1000000 | tf_op jit(solution)/shard_map/input_grad/pallas_call | solution.py:473
  667.7 14.6 %input_grad.7 = (bf16[640,2048]{1,0:T(8,128)(2,1)S(1)}, f32[2,2048]{1,0:T(2,128)S(1)}) custom-call(bf16[2560,768]{1,0:T(8,128)(2,1)} %bitcast.106, bf16[2560,768]{1,0:T(8,128)(2,1)} %bitcast.111, bf16[2560,2048]{1,0:T(8,128)(2,1)} %get-tuple-element.92.refs_2_, bf16[2048,2048]{1,0:T(8,128)(2,1)} %all-gather.8.cloned.1.call-done.refs_3_.refs_4_, ...), custom_call_target="tpu_custom_call" | custom-call | flops 1000000 | bytes 1000000 | tf_op jit(solution)/shard_map/input_grad/pallas_call | solution.py:473
  702.3 14.4 %fusion.29 = bf16[1,640,2048]{2,1,0:T(8,128)(2,1)} fusion(bf16[1,640,2048]{2,1,0:T(8,128)(2,1)} %param.15, bf16[2560,2048]{1,0:T(8,128)(2,1)} %copy-done.15, bf16[320,2048]{1,0:T(8,128)(2,1)} %collective-permute-done.8, bf16[320,2048]{1,0:T(8,128)(2,1)} %copy-done.33, bf16[320,2048]{1,0:T(8,128)(2,1)} %copy-done.34, ...), kind=kOutput, calls=%fused_computation.42 | convolution fusion | flops 5432934400 | bytes 24133632 | tf_op jit(solution)/shard_map/dot_general | solution.py:27
  719.6 33.6 %collective-permute-done.33 = f32[20480]{0:T(1024)S(1)} collective-permute-done((f32[20480]{0:T(1024)S(1)}, f32[20480]{0:T(1024)S(1)}, u32[]{:S(2)}, u32[]{:S(2)}) %collective-permute-start.33) | collective-permute-done | bytes 81952 | tf_op jit(solution)/shard_map/ppermute | solution.py:401
  754.1 4.5 collective-permute-done.34
  762.2 4.6 fusion.47
  767.0 8.9 %fusion.30 = bf16[1,640,2048]{2,1,0:T(8,128)(2,1)} fusion(bf16[1,640,2048]{2,1,0:T(8,128)(2,1)S(1)} %copy-done.7, f32[640]{0:T(1024)S(1)} %get-tuple-element.186, f32[640]{0:T(1024)S(1)} %get-tuple-element.187, f32[640]{0:T(1024)S(1)} %copy-done.28, f32[640]{0:T(1024)S(1)} %copy-done.26, bf16[1,640,2048]{2,1,0:T(8,128)(2,1)S(1)} %copy-done.10, ...), kind=kLoop, calls=%fused_computation.43 | loop fusion | flops 28835840 | bytes 15747072 | tf_op jit(solution)/shard_map/broadcast_in_dim | solution.py:724
  (261 shorter events, 175.7 us)
Async XLA Ops:
  7.2 114.3 %all-gather.4.cloned.1.call-start = ((), (), s32[]{:S(2)}) async-start(), calls=%async_computation.4 | async-start | bytes 9437184 | tf_op jit(solution)/shard_map/all_gather | solution.py:584
  7.9 169.1 %all-gather.6.cloned.1.call-start = ((), (), s32[]{:S(2)}) async-start(), calls=%async_computation.5 | async-start | bytes 9437184 | tf_op jit(solution)/shard_map/all_gather | solution.py:584
  14.9 59.8 %collective-permute-start = (bf16[640,2048]{1,0:T(8,128)(2,1)S(1)}, bf16[640,2048]{1,0:T(8,128)(2,1)S(1)}, u32[]{:S(2)}, u32[]{:S(2)}) collective-permute-start(bf16[640,2048]{1,0:T(8,128)(2,1)S(1)} %get-tuple-element.163), channel_id=1, source_target_pairs={{0,8},{8,24},{24,16},{16,0},{1,9},{9,25},{25,17},{17,1},{2,10},{10... | collective-permute-start | bytes 7864328 | tf_op jit(solution)/shard_map/ppermute | solution.py:339
  76.3 216.4 %all-gather.8.cloned.1.call-start = ((), (), s32[]{:S(2)}) async-start(), calls=%async_computation.6 | async-start | bytes 9437184 | tf_op jit(solution)/shard_map/all_gather | solution.py:584
  116.4 350.6 %reduce-scatter.5.cloned.1.call-start = ((), (), s32[]{:S(2)}) async-start(), calls=%async_computation.7 | async-start | bytes 9437184 | tf_op jit(solution)/shard_map/reduce_scatter | solution.py:587
  284.5 305.0 %reduce-scatter.7.cloned.1.call-start = ((), (), s32[]{:S(2)}) async-start(), calls=%async_computation.8 | async-start | bytes 9437184 | tf_op jit(solution)/shard_map/reduce_scatter | solution.py:587
  354.9 253.1 %reduce-scatter.9.cloned.1.call-start = ((), (), s32[]{:S(2)}) async-start(), calls=%async_computation.9 | async-start | bytes 4718592 | tf_op jit(solution)/shard_map/reduce_scatter | solution.py:587
  358.0 109.0 %collective-permute-start.14 = (bf16[2048,512]{1,0:T(8,128)(2,1)}, bf16[2048,512]{1,0:T(8,128)(2,1)}, u32[]{:S(2)}, u32[]{:S(2)}) collective-permute-start(bf16[2048,512]{1,0:T(8,128)(2,1)} %slice.193), channel_id=1, source_target_pairs={{0,8},{8,24},{24,16},{16,0},{1,9},{9,25},{25,17},{17,1},{2,10},{10... | collective-permute-start | bytes 6291464 | tf_op jit(solution)/shard_map/ppermute | solution.py:339
  359.4 107.5 %collective-permute-start.15 = (bf16[2048,512]{1,0:T(8,128)(2,1)}, bf16[2048,512]{1,0:T(8,128)(2,1)}, u32[]{:S(2)}, u32[]{:S(2)}) collective-permute-start(bf16[2048,512]{1,0:T(8,128)(2,1)} %slice.193), channel_id=1, source_target_pairs={{8,0},{24,8},{16,24},{0,16},{9,1},{25,9},{17,25},{1,17},{10,2},{26... | collective-permute-start | bytes 6291464 | tf_op jit(solution)/shard_map/ppermute | solution.py:340
  360.6 106.3 %collective-permute-start.9 = (bf16[320,2048]{1,0:T(8,128)(2,1)}, bf16[320,2048]{1,0:T(8,128)(2,1)}, u32[]{:S(2)}, u32[]{:S(2)}) collective-permute-start(bf16[320,2048]{1,0:T(8,128)(2,1)} %get-tuple-element.58), channel_id=1, source_target_pairs={{8,0},{24,8},{16,24},{0,16},{9,1},{25,9},{17,25},{1,17},{10,2},{26... | collective-permute-start | bytes 3932168 | tf_op jit(solution)/shard_map/ppermute | solution.py:373
  362.1 104.8 %collective-permute-start.8 = (bf16[320,2048]{1,0:T(8,128)(2,1)}, bf16[320,2048]{1,0:T(8,128)(2,1)}, u32[]{:S(2)}, u32[]{:S(2)}) collective-permute-start(bf16[320,2048]{1,0:T(8,128)(2,1)} %get-tuple-element.57), channel_id=1, source_target_pairs={{0,8},{8,24},{24,16},{16,0},{1,9},{9,25},{25,17},{17,1},{2,10},{10... | collective-permute-start | bytes 3932168 | tf_op jit(solution)/shard_map/ppermute | solution.py:372
  485.6 290.3 %reduce-scatter.11.cloned.1.call-start = ((), (), s32[]{:S(2)}) async-start(), calls=%async_computation.10 | async-start | bytes 4718592 | tf_op jit(solution)/shard_map/reduce_scatter | solution.py:587
  489.5 99.9 %collective-permute-start.22 = (bf16[1024,512]{1,0:T(8,128)(2,1)S(1)}, bf16[1024,512]{1,0:T(8,128)(2,1)}, u32[]{:S(2)}, u32[]{:S(2)}) collective-permute-start(bf16[1024,512]{1,0:T(8,128)(2,1)S(1)} %slice.194), channel_id=1, source_target_pairs={{0,8},{8,24},{24,16},{16,0},{1,9},{9,25},{25,17},{17,1},{2,10},{10... | collective-permute-start | bytes 3145736 | tf_op jit(solution)/shard_map/ppermute | solution.py:345
  493.5 96.0 %collective-permute-start.23 = (bf16[1024,512]{1,0:T(8,128)(2,1)}, bf16[1024,512]{1,0:T(8,128)(2,1)}, u32[]{:S(2)}, u32[]{:S(2)}) collective-permute-start(bf16[1024,512]{1,0:T(8,128)(2,1)} %slice.195), channel_id=1, source_target_pairs={{8,0},{24,8},{16,24},{0,16},{9,1},{25,9},{17,25},{1,17},{10,2},{26... | collective-permute-start | bytes 3145736 | tf_op jit(solution)/shard_map/ppermute | solution.py:346
  495.0 91.6 %collective-permute-start.16 = (bf16[640,256]{1,0:T(8,128)(2,1)}, bf16[640,256]{1,0:T(8,128)(2,1)}, u32[]{:S(2)}, u32[]{:S(2)}) collective-permute-start(bf16[640,256]{1,0:T(8,128)(2,1)} %bitcast.20), channel_id=1, source_target_pairs={{0,8},{8,24},{24,16},{16,0},{1,9},{9,25},{25,17},{17,1},{2,10},{10... | collective-permute-start | bytes 983048 | tf_op jit(solution)/shard_map/ppermute | solution.py:392
  496.4 91.1 %collective-permute-start.18 = (bf16[640,256]{1,0:T(8,128)(2,1)S(1)}, bf16[640,256]{1,0:T(8,128)(2,1)}, u32[]{:S(2)}, u32[]{:S(2)}) collective-permute-start(bf16[640,256]{1,0:T(8,128)(2,1)S(1)} %bitcast.161), channel_id=1, source_target_pairs={{0,16},{8,0},{24,8},{16,24},{1,17},{9,1},{25,9},{17,25},{2,18},{10... | collective-permute-start | bytes 983048 | tf_op jit(solution)/shard_map/ppermute | solution.py:392
  497.0 91.8 %collective-permute-start.20 = (bf16[640,256]{1,0:T(8,128)(2,1)S(1)}, bf16[640,256]{1,0:T(8,128)(2,1)}, u32[]{:S(2)}, u32[]{:S(2)}) collective-permute-start(bf16[640,256]{1,0:T(8,128)(2,1)S(1)} %bitcast.160), channel_id=1, source_target_pairs={{0,24},{8,16},{24,0},{16,8},{1,25},{9,17},{25,1},{17,9},{2,26},{10... | collective-permute-start | bytes 983048 | tf_op jit(solution)/shard_map/ppermute | solution.py:392
  588.8 64.2 %collective-permute-start.21 = (bf16[640,256]{1,0:T(8,128)(2,1)}, bf16[640,256]{1,0:T(8,128)(2,1)}, u32[]{:S(2)}, u32[]{:S(2)}) collective-permute-start(bf16[640,256]{1,0:T(8,128)(2,1)} %bitcast.25), channel_id=1, source_target_pairs={{0,24},{8,16},{24,0},{16,8},{1,25},{9,17},{25,1},{17,9},{2,26},{10... | collective-permute-start | bytes 983048 | tf_op jit(solution)/shard_map/ppermute | solution.py:392
  605.9 61.8 %collective-permute-start.24 = (bf16[320,2048]{1,0:T(8,128)(2,1)}, bf16[320,2048]{1,0:T(8,128)(2,1)}, u32[]{:S(2)}, u32[]{:S(2)}) collective-permute-start(bf16[320,2048]{1,0:T(8,128)(2,1)} %get-tuple-element.170), channel_id=1, source_target_pairs={{0,8},{8,24},{24,16},{16,0},{1,9},{9,25},{25,17},{17,1},{2,10},{10... | collective-permute-start | bytes 3932168 | tf_op jit(solution)/shard_map/ppermute | solution.py:360
  607.3 60.4 %collective-permute-start.25 = (bf16[320,2048]{1,0:T(8,128)(2,1)}, bf16[320,2048]{1,0:T(8,128)(2,1)}, u32[]{:S(2)}, u32[]{:S(2)}) collective-permute-start(bf16[320,2048]{1,0:T(8,128)(2,1)} %get-tuple-element.171), channel_id=1, source_target_pairs={{8,0},{24,8},{16,24},{0,16},{9,1},{25,9},{17,25},{1,17},{10,2},{26... | collective-permute-start | bytes 3932168 | tf_op jit(solution)/shard_map/ppermute | solution.py:360
  691.0 71.2 %collective-permute-start.26 = (bf16[320,2048]{1,0:T(8,128)(2,1)}, bf16[320,2048]{1,0:T(8,128)(2,1)}, u32[]{:S(2)}, u32[]{:S(2)}) collective-permute-start(bf16[320,2048]{1,0:T(8,128)(2,1)} %add_convert_fusion.2), channel_id=1, source_target_pairs={{0,8},{8,24},{24,16},{16,0},{1,9},{9,25},{25,17},{17,1},{2,10},{10... | collective-permute-start | bytes 3932168 | tf_op jit(solution)/shard_map/ppermute | solution.py:368
  692.5 69.6 %collective-permute-start.28 = (bf16[320,2048]{1,0:T(8,128)(2,1)}, bf16[320,2048]{1,0:T(8,128)(2,1)}, u32[]{:S(2)}, u32[]{:S(2)}) collective-permute-start(bf16[320,2048]{1,0:T(8,128)(2,1)} %slice.167), channel_id=1, source_target_pairs={{8,0},{24,8},{16,24},{0,16},{9,1},{25,9},{17,25},{1,17},{10,2},{26... | collective-permute-start | bytes 3932168 | tf_op jit(solution)/shard_map/ppermute | solution.py:373
  698.7 63.4 %collective-permute-start.29 = (bf16[320,2048]{1,0:T(8,128)(2,1)}, bf16[320,2048]{1,0:T(8,128)(2,1)}, u32[]{:S(2)}, u32[]{:S(2)}) collective-permute-start(bf16[320,2048]{1,0:T(8,128)(2,1)} %add_convert_fusion.1), channel_id=1, source_target_pairs={{8,0},{24,8},{16,24},{0,16},{9,1},{25,9},{17,25},{1,17},{10,2},{26... | collective-permute-start | bytes 3932168 | tf_op jit(solution)/shard_map/ppermute | solution.py:369
  699.7 62.4 %collective-permute-start.27 = (bf16[320,2048]{1,0:T(8,128)(2,1)}, bf16[320,2048]{1,0:T(8,128)(2,1)}, u32[]{:S(2)}, u32[]{:S(2)}) collective-permute-start(bf16[320,2048]{1,0:T(8,128)(2,1)} %slice.166), channel_id=1, source_target_pairs={{0,8},{8,24},{24,16},{16,0},{1,9},{9,25},{25,17},{17,1},{2,10},{10... | collective-permute-start | bytes 3932168 | tf_op jit(solution)/shard_map/ppermute | solution.py:372
  (56 other events, 1029.6 us)
Sparse Core Ops, SparseCore 0:
  9.6 84.7 all-gather.3
  96.0 81.0 all-gather.5
  178.7 80.2 all-gather.7
  284.6 89.6 reduce-scatter.4
  376.5 87.9 reduce-scatter.6
  485.7 50.6 reduce-scatter.8
  625.4 50.5 reduce-scatter.10

commit v4 on v3

--- a/solution.py
+++ b/solution.py
@@ -348,7 +348,7 @@
     return pieces + far
 
 
-def ring_reduce(part, own, axis, staged=False):
+def ring_reduce(part, axis, cuts=1, staged=False):
     count = lax.axis_size(axis)
     _, ahead, behind = ring_of(count)
     far = part(count - 1)
@@ -358,28 +358,41 @@
         return (a.astype(WIDE) + b.astype(WIDE)).astype(LOW)
 
     up, down = lax.ppermute(far[:half], axis, ahead), lax.ppermute(far[half:], axis, behind)
-    first = second = last = (up, down)
+    hops = [(up, down)]
     if count == 2:
-        mine = own(first, second).astype(WIDE)
-        return mine + jnp.concatenate(first, axis=0).astype(WIDE), first, second, last
-    for s in range(count // 2 - 1, 0, -1):
-        to_ahead, to_behind = part(2 * s), part(2 * s - 1)
-        if s == count // 2 - 1:
-            up = lax.ppermute(plus(to_ahead[:half], up), axis, ahead)
-            down = lax.ppermute(plus(to_behind[half:], down), axis, behind)
-            second = (up, down)
-            gate = second if staged else ()
-            free_up = lax.ppermute(after(to_ahead[half:], *gate), axis, ahead)
-            free_down = lax.ppermute(after(to_behind[:half], *gate), axis, behind)
-            last = (free_up, free_down)
-            up = jnp.concatenate([up, free_up], axis=0)
-            down = jnp.concatenate([free_down, down], axis=0)
-        else:
-            up = lax.ppermute(plus(to_ahead, up), axis, ahead)
-            down = lax.ppermute(plus(to_behind, down), axis, behind)
-            last = (up, down)
-    total = own(first, second).astype(WIDE) + up.astype(WIDE) + down.astype(WIDE)
-    return total, first, second, last
+        return [(0, up), (half, down)], hops
+    cut = half // cuts
+    to_ahead, to_behind = part(count - 2), part(count - 3)
+    got_up, got_down = {}, {}
+
+    def loose():
+        for n in range(cuts):
+            at = half + n * cut
+            gate = hops[-1] if staged else ()
+            got_up[at] = lax.ppermute(after(to_ahead[at : at + cut], *gate), axis, ahead)
+            at = n * cut
+            got_down[at] = lax.ppermute(after(to_behind[at : at + cut], *gate), axis, behind)
+            hops.append((got_up[half + at], got_down[at]))
+
+    def summed():
+        for n in range(cuts):
+            at, span = n * cut, slice(n * cut, (n + 1) * cut)
+            got_up[at] = lax.ppermute(plus(to_ahead[span], up[span]), axis, ahead)
+            there = slice(half + at, half + at + cut)
+            got_down[half + at] = lax.ppermute(plus(to_behind[there], down[span]), axis, behind)
+            hops.append((got_up[at], got_down[half + at]))
+
+    for send in (summed, loose) if staged else (loose, summed):
+        send()
+    if count == 4:
+        return sorted(got_up.items()) + sorted(got_down.items()), hops
+    up = jnp.concatenate([piece for _, piece in sorted(got_up.items())], axis=0)
+    down = jnp.concatenate([piece for _, piece in sorted(got_down.items())], axis=0)
+    for s in range(count // 2 - 2, 0, -1):
+        up = lax.ppermute(plus(part(2 * s), up), axis, ahead)
+        down = lax.ppermute(plus(part(2 * s - 1), down), axis, behind)
+        hops.append((up, down))
+    return [(0, up), (0, down)], hops
 
 
 def ring_exchange(part, axis):
@@ -449,45 +462,147 @@
     )(x, w, b.astype(WIDE)[None])
 
 
-def input_grad_kernel(*refs, terms):
-    grads, weights = refs[:terms], refs[terms : 2 * terms]
-    normed_ref, out_ref, sums_ref = refs[2 * terms :]
-    total = sum(dot(g[...], w[...], NT) for g, w in zip(grads, weights))
-    out_ref[...] = total.astype(LOW)
-    sums_ref[0:1] = jnp.sum(total, axis=0, keepdims=True)
-    sums_ref[1:2] = jnp.sum(total * normed_ref[...].astype(WIDE), axis=0, keepdims=True)
-
-
-def input_grad(grads, weights, normed, rank, rows):
+def input_grad_kernel(*refs, terms, ranks):
+    grads, weights = refs[: terms * ranks], refs[terms * ranks : terms * ranks + terms]
+    rest = refs[terms * (ranks + 1) :]
+    normed_refs, out_refs, sums_ref = rest[:ranks], rest[ranks : 2 * ranks], rest[2 * ranks]
+    plain = weighted = 0.0
+    for n in range(ranks):
+        mine = grads[n * terms : (n + 1) * terms]
+        total = sum(dot(g[...], w[...], NT) for g, w in zip(mine, weights))
+        out_refs[n][...] = total.astype(LOW)
+        plain += jnp.sum(total, axis=0, keepdims=True)
+        weighted += jnp.sum(total * normed_refs[n][...].astype(WIDE), axis=0, keepdims=True)
+    sums_ref[0:1] = plain
+    sums_ref[1:2] = weighted
+
+
+def input_grad(grads, weights, normed, ranks, rows):
     width = normed.shape[1]
     cols = 512
     keep = pl.Buffered(1)
     in_specs = [
-        pl.BlockSpec((rows, g.shape[1]), lambda i: (rank, 0), pipeline_mode=keep) for g in grads
+        pl.BlockSpec((rows, g.shape[1]), lambda i, rank=rank: (rank, 0), pipeline_mode=keep)
+        for rank in ranks
+        for g in grads
     ]
     in_specs += [
         pl.BlockSpec((cols, g.shape[1]), lambda i, at=at: (i, at))
         for g, (_, at) in zip(grads, weights)
     ]
-    in_specs.append(pl.BlockSpec((rows, cols), lambda i: (rank, i)))
-    return pl.pallas_call(
-        functools.partial(input_grad_kernel, terms=len(grads)),
-        out_shape=(
-            jax.ShapeDtypeStruct((rows, width), LOW),
-            jax.ShapeDtypeStruct((2, width), WIDE),
-        ),
+    in_specs += [pl.BlockSpec((rows, cols), lambda i, rank=rank: (rank, i)) for rank in ranks]
+    *parts, sums = pl.pallas_call(
+        functools.partial(input_grad_kernel, terms=len(grads), ranks=len(ranks)),
+        out_shape=[jax.ShapeDtypeStruct((rows, width), LOW)] * len(ranks)
+        + [jax.ShapeDtypeStruct((2, width), WIDE)],
         grid=(width // cols,),
         in_specs=in_specs,
-        out_specs=[
-            pl.BlockSpec((rows, cols), lambda i: (0, i)),
-            pl.BlockSpec((2, cols), lambda i: (0, i)),
-        ],
+        out_specs=[pl.BlockSpec((rows, cols), lambda i: (0, i))] * len(ranks)
+        + [pl.BlockSpec((2, cols), lambda i: (0, i))],
+        compiler_params=pltpu.CompilerParams(
+            dimension_semantics=("arbitrary",), vmem_limit_bytes=56 << 20
+        ),
+        cost_estimate=LITTLE,
+        name="input_grad",
+    )(*grads * len(ranks), *[w for w, _ in weights], *[normed] * len(ranks))
+    return parts, sums
+
+
+def place_kernel(*refs, starts, count, groups):
+    pieces = refs[: count * groups]
+    dense = refs[count * groups : count * groups + count + 1]
+    rest = refs[count * (groups + 1) + 1 :]
+    token_ref, bias_ref, own_ref = rest[:3]
+    terms, out_ref, acc = rest[3:-2], rest[-2], rest[-1]
+    acc[...] = token_ref[...].astype(WIDE) + bias_ref[...] + own_ref[...].astype(WIDE)
+    for start, term in zip(starts, terms):
+        acc[start : start + term.shape[0]] += term[...].astype(WIDE)
+    lanes = pieces[0].shape[1]
+    steps = pl.num_programs(0)
+    low_half = pl.program_id(0) * 2 < steps
+    far = jnp.where(low_half, dense[count - 1][...], dense[count][...])
+    total = acc[...]
+    for rank in range(count):
+        weight = dense[rank][...] if rank < count - 1 else far
+        for n in range(groups):
+            part = weight[:, n * lanes : (n + 1) * lanes]
+            total += dot(pieces[rank * groups + n][...], part, NT)
+    out_ref[...] = total.astype(LOW)
+
+
+def place_output(pieces, dense_pieces, tokens, bias, own, terms, count, groups):
+    rows, width = tokens.shape
+    cols = 512
+    half = width // cols // 2
+    whole = lambda a: pl.BlockSpec(a.shape, lambda i: (0, 0), pipeline_mode=pl.Buffered(1))
+    in_specs = [whole(piece) for piece in pieces]
+    depth = dense_pieces[0].shape[1]
+    in_specs += [pl.BlockSpec((cols, depth), lambda i: (i, 0)) for _ in range(count - 1)]
+    in_specs.append(pl.BlockSpec((cols, depth), lambda i: (jnp.minimum(i, half - 1), 0)))
+    in_specs.append(pl.BlockSpec((cols, depth), lambda i: (jnp.maximum(i - half, 0), 0)))
+    by_column = lambda n: pl.BlockSpec((n, cols), lambda i: (0, i))
+    in_specs += [by_column(rows), by_column(1), by_column(rows)]
+    in_specs += [by_column(term.shape[0]) for _, term in terms]
+    return pl.pallas_call(
+        functools.partial(
+            place_kernel, starts=tuple(start for start, _ in terms), count=count, groups=groups
+        ),
+        out_shape=jax.ShapeDtypeStruct((rows, width), LOW),
+        grid=(width // cols,),
+        in_specs=in_specs,
+        out_specs=by_column(rows),
+        scratch_shapes=[pltpu.VMEM((rows, cols), WIDE)],
         compiler_params=pltpu.CompilerParams(
             dimension_semantics=("arbitrary",), vmem_limit_bytes=48 << 20
         ),
         cost_estimate=LITTLE,
-        name="input_grad",
-    )(*grads, *[w for w, _ in weights], normed)
+        name="place_output",
+    )(*pieces, *dense_pieces, tokens, bias, own, *[term for _, term in terms])
+
+
+def token_grad_kernel(token_ref, grad_ref, own_ref, gain_ref, *refs, starts, tile):
+    terms, out_ref, total = refs[:-2], refs[-2], refs[-1]
+    first = pl.program_id(0) * tile
+    total[...] = own_ref[...].astype(WIDE)
+    for start, term in zip(starts, terms):
+        size = min(tile, term.shape[0])
+        for at in range(0, term.shape[0], size):
+
+            @pl.when(first == (start + at) // tile * tile)
+            def _(start=start, term=term, at=at, size=size):
+                to = (start + at) % tile
+                total[to : to + size] += term[at : at + size].astype(WIDE)
+
+    x = token_ref[...].astype(WIDE)
+    centred = x - jnp.mean(x, axis=-1, keepdims=True)
+    rstd = lax.rsqrt(jnp.mean(centred * centred, axis=-1, keepdims=True) + 1e-05)
+    xhat = centred * rstd
+    scaled = total[...] * gain_ref[...]
+    mean = jnp.mean(scaled, axis=-1, keepdims=True)
+    along = jnp.mean(scaled * xhat, axis=-1, keepdims=True)
+    out_ref[...] = (grad_ref[...].astype(WIDE) + rstd * (scaled - mean - xhat * along)).astype(LOW)
+
+
+def token_grad(tokens, grad, own, gain, terms, tile):
+    rows, width = tokens.shape
+    by_row = pl.BlockSpec((tile, width), lambda i: (i, 0))
+    whole = lambda a: pl.BlockSpec(a.shape, lambda i: (0, 0), pipeline_mode=pl.Buffered(1))
+    return pl.pallas_call(
+        functools.partial(
+            token_grad_kernel, starts=tuple(start for start, _ in terms), tile=tile
+        ),
+        out_shape=jax.ShapeDtypeStruct((rows, width), LOW),
+        grid=(rows // tile,),
+        in_specs=[by_row, by_row, by_row, pl.BlockSpec((1, width), lambda i: (0, 0))]
+        + [whole(term) for _, term in terms],
+        out_specs=by_row,
+        scratch_shapes=[pltpu.VMEM((tile, width), WIDE)],
+        compiler_params=pltpu.CompilerParams(
+            dimension_semantics=("arbitrary",), vmem_limit_bytes=48 << 20
+        ),
+        cost_estimate=LITTLE,
+        name="token_grad",
+    )(tokens, grad, own, gain[None], *[term for _, term in terms])
 
 
 def pair_grad_kernel(x_ref, y_ref, a_ref, b_ref, out_ref):
@@ -601,6 +716,9 @@
     attention_weight = gather_rows(after(attention_shard, *normed_pieces[-2:]))
     qkv_weight, dense_turned = attention_weight[:, : 3 * each], attention_weight[:, 3 * each :]
 
+    tabs = rope_tables(rows)
+    normed = after(normed, where, *tabs)
+
     fc1_bias = lax.dynamic_slice_in_dim(b_fc1, me * hidden, hidden, 0)
     qkv_bias = lax.dynamic_slice_in_dim(b_qkv.reshape(3, width), me * each, each, 1)
     activated, slope = expand(normed, fc1_weight, fc1_bias)
@@ -609,9 +727,8 @@
     grad_pieces = ring_pieces(sent_grad, "ctx", gate=(activated,))
     ff_part = dot(activated, fc2_turned, NT).astype(LOW)
     grads = jnp.concatenate([after(piece, ff_part) for piece in grad_pieces], axis=0)
-    ff_sum, first, second, last = ring_reduce(
-        lambda rank: of_rank(ff_part, rank), lambda *_: of_rank(ff_part, 0), "ctx", staged=True
-    )
+    ff_terms, ff_hops = ring_reduce(lambda rank: of_rank(ff_part, rank), "ctx", staged=True)
+    first, second, last = ff_hops[0], ff_hops[min(1, len(ff_hops) - 1)], ff_hops[-1]
 
     gated = after(grads, ff_part)
     expanded_grad = (dot(gated, fc2_turned, NN) * slope.astype(WIDE)).astype(LOW)
@@ -625,11 +742,7 @@
     d_fc1 = scatter_rows(d_fc1_part)
 
     dense_pieces = ring_pieces(after(dense_turned, *second), "ctx")
-    dense_whole = jnp.concatenate(
-        dense_pieces[:-2] + [jnp.concatenate(dense_pieces[-2:], axis=0)], axis=1
-    )
-
-    tabs = rope_tables(rows)
+
     attended, qkv_grads, d_attention, swapped = [], [], [], []
     ordered = (d_fc1_part,)
     for which in range(groups):
@@ -646,53 +759,47 @@
             d_attention.append(scatter_rows(d_part))
 
     weights = [(attention_weight, which) for which in range(groups)] + [(fc1_weight, 0)]
-    parts, sums = [None] * count, 0.0
     early_swaps = [piece for pieces in swapped for piece in pieces]
     turn = after(expanded_grad, d_fc1, *dense_pieces[-2:], *early_swaps, *attended)
     swapped.append(ring_exchange(lambda rank: of_rank(attended[-1], rank), "ctx"))
-
-    def input_part(rank, turn):
-        return input_grad(qkv_grads + [turn], weights, normed, rank, local_rows)
-
-    for rank in range(count - 1, 0, -1):
-        if rank == 1:
-            turn = after(turn, *swapped[-1])
-        parts[rank], part_sums = input_part(rank, turn)
-        sums = sums + part_sums
-        turn = after(turn, parts[rank])
-        if rank == count - 1:
-            gated = after(normed, parts[rank], *d_attention)
-            d_part = pair_grad(gated, grads, qkv_grads[-1], attended[-1])
-            d_attention.append(scatter_rows(d_part))
-            turn = after(turn, d_part)
-
-    own_sums = []
-
-    def own_part(first, second):
-        part, part_sums = input_part(0, after(turn, *first))
-        own_sums.append(part_sums)
-        return part
-
-    normed_grad, *_ = ring_reduce(lambda rank: parts[rank], own_part, "ctx")
-    sums = sums + own_sums[0]
+    far_part, far_sums = input_grad(qkv_grads + [turn], weights, normed, [count - 1], local_rows)
+    middle = list(range(count - 2, 0, -1))
+    middle_sums, parts = 0.0, {count - 1: far_part[0]}
+    turn = after(turn, *far_part)
+    for n in range(0, len(middle), 2):
+        some, some_sums = input_grad(
+            qkv_grads + [turn], weights, normed, middle[n : n + 2], local_rows
+        )
+        turn = after(turn, *some)
+        middle_sums = middle_sums + some_sums
+        parts.update(zip(middle[n : n + 2], some))
+
+    grad_terms, hops = ring_reduce(lambda rank: parts[rank], "ctx", cuts=2)
+    covers = hops[1:] if len(hops) == 5 else [()] * 4
+    gated = after(normed, turn, *hops[0], *swapped[-1], *d_attention)
+    d_part = pair_grad(gated, grads, qkv_grads[-1], attended[-1])
+    d_attention.append(scatter_rows(d_part))
+    own_part, own_sums = input_grad(
+        qkv_grads + [after(turn, d_part, *covers[0])], weights, normed, [0], local_rows
+    )
+    attended_own = [swapped[which][rank] for rank in range(count) for which in range(groups)]
+    output = place_output(
+        attended_own,
+        dense_pieces,
+        after(tokens[0], *own_part, *covers[1]),
+        (b_dense.astype(WIDE) + b_fc2.astype(WIDE))[None],
+        ff_part,
+        ff_terms,
+        count,
+        groups,
+    )
+    sums = after(far_sums + middle_sums + own_sums, output, *covers[2])
+    d_tokens = token_grad(tokens[0], own_grad, own_part[0], gain, grad_terms, local_rows // 4)
 
     d_qkv = jnp.concatenate(
         [part[:, : 3 * lanes].reshape(-1, 3, lanes) for part in d_attention], axis=2
     ).astype(WIDE)
     d_dense = jnp.concatenate([part[:, 3 * lanes :].T for part in d_attention], axis=0)
-
-    attended_own = jnp.concatenate(
-        [swapped[which][rank] for rank in range(count) for which in range(groups)], axis=1
-    )
-    out_sum = ff_sum + dot(attended_own, dense_whole, NT)
-    output = own_tokens + out_sum + b_dense.astype(WIDE) + b_fc2.astype(WIDE)
-
-    scaled = normed_grad * gain
-    d_tokens = own_grad.astype(WIDE) + rstd * (
-        scaled
-        - jnp.mean(scaled, axis=-1, keepdims=True)
-        - xhat * jnp.mean(scaled * xhat, axis=-1, keepdims=True)
-    )
 
     qkv_bias_part = jnp.concatenate(
         [jnp.sum(part.astype(WIDE), axis=0).reshape(3, lanes) for part in qkv_grads], axis=1
@@ -713,15 +820,16 @@
                 fc1_bias_wide,
             ]
         ),
-        ("fsdp", "ctx"),
-    )
+        ("fsdp",),
+    )
+    small = sum_everywhere(after(small, *covers[3]), ("ctx",))
     d_shift, with_normed, d_b_qkv, d_b_out, d_b_fc1 = jnp.split(
         small, [width, 2 * width, 5 * width, 6 * width]
     )
     d_gain = (with_normed - shift * d_shift) / gain
     return (
-        output.astype(LOW)[None],
-        d_tokens.astype(LOW)[None],
+        output[None],
+        d_tokens[None],
         d_gain,
         d_shift,
         d_qkv,

time: 795 us -> 763 us (0.960)
  Pallas kernels: 291 us -> 310 us
  matrix products: 161 us -> 143 us
  waiting for transfers between devices: 129 us -> 115 us
  other arithmetic: 55.5 us -> 42.8 us
  local copies, waits for them, and re-layouts: 95.2 us -> 85.7 us
    ppermute x5, waiting for transfers between devices: 38.2 us -> 10.3 us  [sum_everywhere(): values = values + lax.ppermute(values, axis, pairs)]
    ppermute x8 -> x12, waiting for transfers between devices: 0.02 us -> 26.8 us  [the longest x3 21 us: summed(): got_up[at] = lax.ppermute(plus(to_ahead[span], up[span]), axis, ahead)]
    ppermute x3, waiting for transfers between devices: 20.5 us -> 0.01 us  [ring_pieces(): lax.ppermute(from_behind[:half], axis, ahead)]
    pallas_call x4 -> x5, Pallas kernels: 58.5 us -> 76.8 us  [the longest x3 57.3 us: input_grad(): pl.pallas_call(functools.partial(input_grad_kernel, terms=len(grads), ran...]
    dot_general x7 -> x6, matrix products: 161 us -> 143 us  [dot(): return lax.dot_general(left, right, dims, preferred_element_type=WIDE)]
    broadcast_in_dim x1 -> x0, other arithmetic: 8.86 us -> none  [shards(): d_tokens.astype(LOW)[None]]
    unnamed x95 -> x138, local copies, waits for them, and re-layouts: 49.2 us -> 42.9 us
  transfers between devices with their start and end apart: 42 -> 46, of which waited for: 8 -> 15; matrix products, arithmetic and copies ran while one was open for 37% -> 33% of each run, Pallas kernels for 37% -> 39%
where the time goes in v4:
time: 763 us; the launch traced here: 754 us
  Pallas kernels  310 us (41%)
  matrix products  143 us (19%)
  waiting for transfers between devices  115 us (15%)
  local copies, waits for them, and re-layouts  85.7 us (11%)
  other arithmetic  42.8 us (6%)
  starting transfers between devices  42.2 us (6%)
  between operations  15.2 us (2%)
    pallas_call x2, Pallas kernels, attention(): pl.pallas_call(kernel, out_shape=(jax.ShapeDtypeStruct((blocks, blk, lane...  164 us
    dot_general x6, matrix products, dot(): return lax.dot_general(left, right, dims, preferred_element_type=WIDE)  143 us
    ppermute x3, waiting for transfers between devices, ring_pieces(): from_behind = lax.ppermute(from_behind, axis, ahead)  66.8 us
    pallas_call x3, Pallas kernels, input_grad(): pl.pallas_call(functools.partial(input_grad_kernel, terms=len(grads), ran...  57.3 us
    unnamed x138, local copies, waits for them, and re-layouts  42.9 us
    pallas_call x1, Pallas kernels, expand(): pl.pallas_call(functools.partial(expand_kernel, cols=min(512, hidden)), o...  38.8 us
    pallas_call x2, Pallas kernels, pair_grad(): pl.pallas_call(pair_grad_kernel, out_shape=jax.ShapeDtypeStruct((width, c...  30.3 us
    ppermute x3, waiting for transfers between devices, summed(): got_up[at] = lax.ppermute(plus(to_ahead[span], up[span]), axis, ahead)  21 us
  transfers between devices with their start and end apart: 46, of which 15 were waited for; matrix products, arithmetic and copies ran while one was open for 33% of the time, Pallas kernels for 39%

profile of v4, /device:TPU:0, one launch (start us, length us, event | category | flops | bytes accessed | tf_op | source)
XLA Modules:
  0.0 753.8 jit_solution(12367321044883789450)
XLA Ops:
  17.9 56.9 %collective-permute-done = bf16[640,2048]{1,0:T(8,128)(2,1)S(1)} collective-permute-done((bf16[640,2048]{1,0:T(8,128)(2,1)S(1)}, bf16[640,2048]{1,0:T(8,128)(2,1)S(1)}, u32[]{:S(2)}, u32[]{:S(2)}) %collective-permute-start) | collective-permute-done | bytes 2621472 | tf_op jit(solution)/shard_map/ppermute | solution.py:339
  82.9 6.2 fusion.7
  121.7 38.8 %expand.1 = (bf16[2560,2048]{1,0:T(8,128)(2,1)}, bf16[2560,2048]{1,0:T(8,128)(2,1)}) custom-call(bf16[2560,2048]{1,0:T(8,128)(2,1)} %constant_dynamic-update-slice_fusion.x_ref.refs_6_.refs_9_.refs_10_, bf16[2048,2048]{1,0:T(8,128)(2,1)} %all-gather.4.cloned.1.call-done.w_ref.refs_5_.refs_8_, f32[1,2048]{1,0:T(1,128)S(1)} %bitcast.78), custom_call_target="tpu_custom_call" | custom-call | flops 21474836480 | bytes 39845888 | tf_op jit(solution)/shard_map/expand/pallas_call | solution.py:443
  160.4 10.0 %collective-permute-done.4 = bf16[640,2048]{1,0:T(8,128)(2,1)} collective-permute-done((bf16[640,2048]{1,0:T(8,128)(2,1)S(1)}, bf16[640,2048]{1,0:T(8,128)(2,1)}, u32[]{:S(2)}, u32[]{:S(2)}) %collective-permute-start.4) | collective-permute-done | bytes 2621472 | tf_op jit(solution)/shard_map/ppermute | solution.py:339
  177.9 26.5 %convolution_convert_fusion.refs_15_ = bf16[2560,2048]{1,0:T(8,128)(2,1)S(1)} fusion(bf16[2560,2048]{1,0:T(8,128)(2,1)} %get-tuple-element.57, bf16[2048,2048]{0,1:T(8,128)(2,1)} %all-gather.6.cloned.1.call-done), kind=kOutput, calls=%fused_computation.3 | convolution fusion | flops 21480079360 | bytes 29360128 | tf_op jit(solution)/shard_map/dot_general | solution.py:27
  207.8 4.7 constant_dynamic-update-slice_fusion.8
  224.8 29.7 %convert_reduce_fusion = (f32[2048]{0:T(1024)}, bf16[2560,2048]{1,0:T(8,128)(2,1)}) fusion(bf16[2560,2048]{1,0:T(8,128)(2,1)} %get-tuple-element.67, bf16[2560,2048]{1,0:T(8,128)(2,1)} %constant_dynamic-update-slice_fusion.5.y_ref, bf16[2048,2048]{0,1:T(8,128)(2,1)} %all-gather.6.cloned.1.call-done), kind=kOutput, calls=%fused_computation | convolution fusion | flops 21501048832 | bytes 39854080 | tf_op jit(solution)/shard_map/dot_general | solution.py:27
  255.6 28.9 %convolution_convert_fusion.2 = bf16[2048,2048]{1,0:T(8,128)(2,1)} fusion(bf16[2560,2048]{1,0:T(8,128)(2,1)} %constant_dynamic-update-slice_fusion.5.y_ref, bf16[2560,2048]{1,0:T(8,128)(2,1)} %get-tuple-element.57), kind=kOutput, calls=%fused_computation.7 | convolution fusion | flops 21479030784 | bytes 29360128 | tf_op jit(solution)/shard_map/dot_general | solution.py:27
  285.3 22.4 %add_convert_fusion = bf16[2560,1536]{1,0:T(8,128)(2,1)} fusion(bf16[2560,2048]{1,0:T(8,128)(2,1)} %constant_dynamic-update-slice_fusion.x_ref.refs_6_.refs_9_.refs_10_, f32[1536]{0:T(1024)S(1)} %reshape.255, bf16[2048,2048]{1,0:T(8,128)(2,1)} %all-gather.8.cloned.1.call-done.refs_3_.refs_4_.refs_6_.refs_7_), kind=kOutput, calls=%fused_computation.2 | convolution fusion | flops 16113991680 | bytes 24647680 | tf_op jit(solution)/shard_map/dot_general | solution.py:27
  312.6 10.4 %convolution_convert_fusion.3 = bf16[2560,512]{1,0:T(8,128)(2,1)} fusion(bf16[2560,2048]{1,0:T(8,128)(2,1)} %constant_dynamic-update-slice_fusion.5.y_ref, bf16[2048,2048]{1,0:T(8,128)(2,1)} %all-gather.8.cloned.1.call-done.refs_3_.refs_4_.refs_6_.refs_7_), kind=kOutput, calls=%fused_computation.18 | convolution fusion | flops 5370019840 | bytes 15204352 | tf_op jit(solution)/shard_map/dot_general | solution.py:27
  323.0 16.4 %collective-permute-done.10.refs_16_ = bf16[320,2048]{1,0:T(8,128)(2,1)S(1)} collective-permute-done((bf16[320,2048]{1,0:T(8,128)(2,1)S(1)}, bf16[320,2048]{1,0:T(8,128)(2,1)S(1)}, u32[]{:S(2)}, u32[]{:S(2)}) %collective-permute-start.10) | collective-permute-done | bytes 1310752 | tf_op jit(solution)/shard_map/ppermute | solution.py:380
  340.8 25.4 %convolution_convert_fusion.1 = bf16[2048,2048]{1,0:T(8,128)(2,1)} fusion(bf16[2560,2048]{1,0:T(8,128)(2,1)S(1)} %bitcast.104, bf16[2560,2048]{1,0:T(8,128)(2,1)S(1)} %bitcast.114), kind=kOutput, calls=%fused_computation.6 | convolution fusion | flops 21479030784 | bytes 29360128 | tf_op jit(solution)/shard_map/dot_general | solution.py:27
  372.4 81.9 %attention.2 = (bf16[40,64,256]{2,1,0:T(8,128)(2,1)}, bf16[40,64,768]{2,1,0:T(8,128)(2,1)}) custom-call(s32[40]{0:T(128)} %select_reduce_fusion.where_ref, bf16[40,64,1536]{2,1,0:T(8,128)(2,1)} %bitcast.79, bf16[40,64,1536]{2,1,0:T(8,128)(2,1)} %bitcast.80, bf16[40,64,1536]{2,1,0:T(8,128)(2,1)} %bitcast.81, bf16[40,64,1536]{2,1,0:T(8,128)(2,1)} %bitcast.82, ...), custom_call_target="tpu_custom_call" | custom-call | flops 1000000 | bytes 1000000 | tf_op jit(solution)/shard_map/attention/pallas_call | solution.py:277
  460.2 15.2 %pair_grad.2 = bf16[2048,1024]{1,0:T(8,128)(2,1)} custom-call(bf16[2560,2048]{1,0:T(8,128)(2,1)} %constant_dynamic-update-slice_fusion.x_ref.refs_6_.refs_9_.refs_10_, bf16[2560,2048]{1,0:T(8,128)(2,1)} %constant_dynamic-update-slice_fusion.5.y_ref, bf16[2560,768]{1,0:T(8,128)(2,1)S(1)} %bitcast.66, bf16[2560,256]{1,0:T(8,128)(2,1)S(1)} %bitcast.73), custom_call_target="tpu_custom_call" | custom-call | flops 1000000 | bytes 1000000 | tf_op jit(solution)/shard_map/pair_grad/pallas_call | solution.py:619
  484.9 81.9 %attention.3 = (bf16[40,64,256]{2,1,0:T(8,128)(2,1)}, bf16[40,64,768]{2,1,0:T(8,128)(2,1)}) custom-call(s32[40]{0:T(128)} %select_reduce_fusion.where_ref, bf16[40,64,1536]{2,1,0:T(8,128)(2,1)} %bitcast.91, bf16[40,64,1536]{2,1,0:T(8,128)(2,1)} %bitcast.92, bf16[40,64,1536]{2,1,0:T(8,128)(2,1)} %bitcast.93, bf16[40,64,1536]{2,1,0:T(8,128)(2,1)} %bitcast.94, ...), custom_call_target="tpu_custom_call" | custom-call | flops 1000000 | bytes 1000000 | tf_op jit(solution)/shard_map/attention/pallas_call | solution.py:277
  569.4 15.2 %input_grad.3 = (bf16[640,2048]{1,0:T(8,128)(2,1)}, f32[2,2048]{1,0:T(2,128)}) custom-call(bf16[2560,768]{1,0:T(8,128)(2,1)} %bitcast.62, bf16[2560,768]{1,0:T(8,128)(2,1)} %bitcast.67, bf16[2560,2048]{1,0:T(8,128)(2,1)} %get-tuple-element.90.refs_2_.refs_5_, bf16[2048,2048]{1,0:T(8,128)(2,1)} %all-gather.8.cloned.1.call-done.refs_3_.refs_4_.refs_6_.refs_7_, ...), custom_call_target="tpu_custom_call" | custom-call | flops 1000000 | bytes 1000000 | tf_op jit(solution)/shard_map/input_grad/pallas_call | solution.py:494
  592.0 26.5 %input_grad.4 = (bf16[640,2048]{1,0:T(8,128)(2,1)}, bf16[640,2048]{1,0:T(8,128)(2,1)}, f32[2,2048]{1,0:T(2,128)}) custom-call(bf16[2560,768]{1,0:T(8,128)(2,1)} %bitcast.63, bf16[2560,768]{1,0:T(8,128)(2,1)} %bitcast.68, bf16[2560,2048]{1,0:T(8,128)(2,1)} %get-tuple-element.90.refs_2_.refs_5_, bf16[2560,768]{1,0:T(8,128)(2,1)} %bitcast.64, ...), custom_call_target="tpu_custom_call" | custom-call | flops 1000000 | bytes 1000000 | tf_op jit(solution)/shard_map/input_grad/pallas_call | solution.py:494
  618.5 4.8 collective-permute-done.17.refs_3_
  629.8 15.2 %pair_grad.3 = bf16[2048,1024]{1,0:T(8,128)(2,1)} custom-call(bf16[2560,2048]{1,0:T(8,128)(2,1)} %constant_dynamic-update-slice_fusion.x_ref.refs_6_.refs_9_.refs_10_, bf16[2560,2048]{1,0:T(8,128)(2,1)} %constant_dynamic-update-slice_fusion.5.y_ref, bf16[2560,768]{1,0:T(8,128)(2,1)S(1)} %bitcast.71, bf16[2560,256]{1,0:T(8,128)(2,1)S(1)} %bitcast.72), custom_call_target="tpu_custom_call" | custom-call | flops 1000000 | bytes 1000000 | tf_op jit(solution)/shard_map/pair_grad/pallas_call | solution.py:619
  666.2 5.0 collective-permute-done.26.refs_2_
  674.4 15.6 %input_grad.5 = (bf16[640,2048]{1,0:T(8,128)(2,1)}, f32[2,2048]{1,0:T(2,128)}) custom-call(bf16[2560,768]{1,0:T(8,128)(2,1)} %bitcast.65, bf16[2560,768]{1,0:T(8,128)(2,1)} %bitcast.70, bf16[2560,2048]{1,0:T(8,128)(2,1)} %get-tuple-element.90.refs_2_.refs_5_, bf16[2048,2048]{1,0:T(8,128)(2,1)} %all-gather.8.cloned.1.call-done.refs_3_.refs_4_.refs_6_.refs_7_, ...), custom_call_target="tpu_custom_call" | custom-call | flops 1000000 | bytes 1000000 | tf_op jit(solution)/shard_map/input_grad/pallas_call | solution.py:494
  690.1 10.7 %place_output.1 = bf16[640,2048]{1,0:T(8,128)(2,1)} custom-call(bf16[640,256]{1,0:T(8,128)(2,1)S(1)} %bitcast.74, bf16[640,256]{1,0:T(8,128)(2,1)S(1)} %bitcast.75, bf16[640,256]{1,0:T(8,128)(2,1)S(1)} %collective-permute-done.16.refs_2_, bf16[640,256]{1,0:T(8,128)(2,1)S(1)} %copy-done.15, bf16[640,256]{1,0:T(8,128)(2,1)S(1)} %copy-done.11, ...), custom_call_target="tpu_custom_call" | custom-call | flops 1000000 | bytes 1000000 | tf_op jit(solution)/shard_map/place_output/pallas_call | solution.py:546
  707.8 5.8 collective-permute-done.36
  728.6 8.8 %token_grad.1 = bf16[640,2048]{1,0:T(8,128)(2,1)} custom-call(bf16[640,2048]{1,0:T(8,128)(2,1)} %bitcast.116, bf16[640,2048]{1,0:T(8,128)(2,1)} %bitcast.118, bf16[640,2048]{1,0:T(8,128)(2,1)} %get-tuple-element.91.own_ref, f32[1,2048]{1,0:T(1,128)S(1)} %bitcast.76, bf16[160,2048]{1,0:T(8,128)(2,1)} %collective-permute-done.30.refs_0_, ...), custom_call_target="tpu_custom_call" | custom-call | flops 1000000 | bytes 1000000 | tf_op jit(solution)/shard_map/token_grad/pallas_call | solution.py:590
  (308 shorter events, 175.7 us)
Async XLA Ops:
  7.2 114.5 %all-gather.4.cloned.1.call-start = ((), (), s32[]{:S(2)}) async-start(), calls=%async_computation.4 | async-start | bytes 9437184 | tf_op jit(solution)/shard_map/all_gather | solution.py:699
  7.9 170.0 %all-gather.6.cloned.1.call-start = ((), (), s32[]{:S(2)}) async-start(), calls=%async_computation.5 | async-start | bytes 9437184 | tf_op jit(solution)/shard_map/all_gather | solution.py:699
  14.9 59.8 %collective-permute-start = (bf16[640,2048]{1,0:T(8,128)(2,1)S(1)}, bf16[640,2048]{1,0:T(8,128)(2,1)S(1)}, u32[]{:S(2)}, u32[]{:S(2)}) collective-permute-start(bf16[640,2048]{1,0:T(8,128)(2,1)S(1)} %get-tuple-element.161), channel_id=1, source_target_pairs={{0,8},{8,24},{24,16},{16,0},{1,9},{9,25},{25,17},{17,1},{2,10},{10... | collective-permute-start | bytes 7864328 | tf_op jit(solution)/shard_map/ppermute | solution.py:339
  17.8 58.3 %collective-permute-start.1 = (bf16[640,2048]{1,0:T(8,128)(2,1)S(1)}, bf16[640,2048]{1,0:T(8,128)(2,1)S(1)}, u32[]{:S(2)}, u32[]{:S(2)}) collective-permute-start(bf16[640,2048]{1,0:T(8,128)(2,1)S(1)} %get-tuple-element.161), channel_id=1, source_target_pairs={{8,0},{24,8},{16,24},{0,16},{9,1},{25,9},{17,25},{1,17},{10,2},{26... | collective-permute-start | bytes 7864328 | tf_op jit(solution)/shard_map/ppermute | solution.py:340
  76.2 209.0 %all-gather.8.cloned.1.call-start = ((), (), s32[]{:S(2)}) async-start(), calls=%async_computation.6 | async-start | bytes 9437184 | tf_op jit(solution)/shard_map/all_gather | solution.py:699
  112.7 57.7 %collective-permute-start.4 = (bf16[640,2048]{1,0:T(8,128)(2,1)S(1)}, bf16[640,2048]{1,0:T(8,128)(2,1)}, u32[]{:S(2)}, u32[]{:S(2)}) collective-permute-start(bf16[640,2048]{1,0:T(8,128)(2,1)S(1)} %bitcast.119), channel_id=1, source_target_pairs={{0,8},{8,24},{24,16},{16,0},{1,9},{9,25},{25,17},{17,1},{2,10},{10... | collective-permute-start | bytes 7864328 | tf_op jit(solution)/shard_map/ppermute | solution.py:339
  114.4 59.9 %collective-permute-start.5 = (bf16[640,2048]{1,0:T(8,128)(2,1)S(1)}, bf16[640,2048]{1,0:T(8,128)(2,1)}, u32[]{:S(2)}, u32[]{:S(2)}) collective-permute-start(bf16[640,2048]{1,0:T(8,128)(2,1)S(1)} %bitcast.120), channel_id=1, source_target_pairs={{8,0},{24,8},{16,24},{0,16},{9,1},{25,9},{17,25},{1,17},{10,2},{26... | collective-permute-start | bytes 7864328 | tf_op jit(solution)/shard_map/ppermute | solution.py:340
  121.6 335.1 %reduce-scatter.5.cloned.1.call-start = ((), (), s32[]{:S(2)}) async-start(), calls=%async_computation.7 | async-start | bytes 9437184 | tf_op jit(solution)/shard_map/reduce_scatter | solution.py:702
  284.5 284.9 %reduce-scatter.7.cloned.1.call-start = ((), (), s32[]{:S(2)}) async-start(), calls=%async_computation.8 | async-start | bytes 9437184 | tf_op jit(solution)/shard_map/reduce_scatter | solution.py:702
  366.3 261.4 %reduce-scatter.9.cloned.1.call-start = ((), (), s32[]{:S(2)}) async-start(), calls=%async_computation.9 | async-start | bytes 4718592 | tf_op jit(solution)/shard_map/reduce_scatter | solution.py:702
  368.1 86.2 %collective-permute-start.14 = (bf16[2048,512]{1,0:T(8,128)(2,1)S(1)}, bf16[2048,512]{1,0:T(8,128)(2,1)S(1)}, u32[]{:S(2)}, u32[]{:S(2)}) collective-permute-start(bf16[2048,512]{1,0:T(8,128)(2,1)S(1)} %slice.216.refs_8_), channel_id=1, source_target_pairs={{0,8},{8,24},{24,16},{16,0},{1,9},{9,25},{25,17},{17,1},{2,10},{10... | collective-permute-start | bytes 6291464 | tf_op jit(solution)/shard_map/ppermute | solution.py:339
  369.6 87.1 %collective-permute-start.15 = (bf16[2048,512]{1,0:T(8,128)(2,1)S(1)}, bf16[2048,512]{1,0:T(8,128)(2,1)}, u32[]{:S(2)}, u32[]{:S(2)}) collective-permute-start(bf16[2048,512]{1,0:T(8,128)(2,1)S(1)} %slice.216.refs_8_), channel_id=1, source_target_pairs={{8,0},{24,8},{16,24},{0,16},{9,1},{25,9},{17,25},{1,17},{10,2},{26... | collective-permute-start | bytes 6291464 | tf_op jit(solution)/shard_map/ppermute | solution.py:340
  370.2 84.1 %collective-permute-start.12 = (bf16[320,2048]{1,0:T(8,128)(2,1)}, bf16[320,2048]{1,0:T(8,128)(2,1)S(1)}, u32[]{:S(2)}, u32[]{:S(2)}) collective-permute-start(bf16[320,2048]{1,0:T(8,128)(2,1)} %get-tuple-element.75), channel_id=1, source_target_pairs={{0,8},{8,24},{24,16},{16,0},{1,9},{9,25},{25,17},{17,1},{2,10},{10... | collective-permute-start | bytes 3932168 | tf_op jit(solution)/shard_map/ppermute | solution.py:372
  371.6 82.7 %collective-permute-start.13 = (bf16[320,2048]{1,0:T(8,128)(2,1)S(1)}, bf16[320,2048]{1,0:T(8,128)(2,1)S(1)}, u32[]{:S(2)}, u32[]{:S(2)}) collective-permute-start(bf16[320,2048]{1,0:T(8,128)(2,1)S(1)} %get-tuple-element.76), channel_id=1, source_target_pairs={{8,0},{24,8},{16,24},{0,16},{9,1},{25,9},{17,25},{1,17},{10,2},{26... | collective-permute-start | bytes 3932168 | tf_op jit(solution)/shard_map/ppermute | solution.py:374
  475.4 264.8 %reduce-scatter.11.cloned.1.call-start = ((), (), s32[]{:S(2)}) async-start(), calls=%async_computation.10 | async-start | bytes 4718592 | tf_op jit(solution)/shard_map/reduce_scatter | solution.py:702
  476.8 91.5 %collective-permute-start.22 = (bf16[1024,512]{1,0:T(8,128)(2,1)S(1)}, bf16[1024,512]{1,0:T(8,128)(2,1)S(1)}, u32[]{:S(2)}, u32[]{:S(2)}) collective-permute-start(bf16[1024,512]{1,0:T(8,128)(2,1)S(1)} %slice.221), channel_id=1, source_target_pairs={{0,8},{8,24},{24,16},{16,0},{1,9},{9,25},{25,17},{17,1},{2,10},{10... | collective-permute-start | bytes 3145736 | tf_op jit(solution)/shard_map/ppermute | solution.py:345
  479.7 88.7 %collective-permute-start.23 = (bf16[1024,512]{1,0:T(8,128)(2,1)S(1)}, bf16[1024,512]{1,0:T(8,128)(2,1)S(1)}, u32[]{:S(2)}, u32[]{:S(2)}) collective-permute-start(bf16[1024,512]{1,0:T(8,128)(2,1)S(1)} %slice.222), channel_id=1, source_target_pairs={{8,0},{24,8},{16,24},{0,16},{9,1},{25,9},{17,25},{1,17},{10,2},{26... | collective-permute-start | bytes 3145736 | tf_op jit(solution)/shard_map/ppermute | solution.py:346
  480.4 86.5 %collective-permute-start.16 = (bf16[640,256]{1,0:T(8,128)(2,1)S(1)}, bf16[640,256]{1,0:T(8,128)(2,1)S(1)}, u32[]{:S(2)}, u32[]{:S(2)}) collective-permute-start(bf16[640,256]{1,0:T(8,128)(2,1)S(1)} %bitcast.132), channel_id=1, source_target_pairs={{0,8},{8,24},{24,16},{16,0},{1,9},{9,25},{25,17},{17,1},{2,10},{10... | collective-permute-start | bytes 983048 | tf_op jit(solution)/shard_map/ppermute | solution.py:405
  481.9 85.0 %collective-permute-start.18 = (bf16[640,256]{1,0:T(8,128)(2,1)S(1)}, bf16[640,256]{1,0:T(8,128)(2,1)S(1)}, u32[]{:S(2)}, u32[]{:S(2)}) collective-permute-start(bf16[640,256]{1,0:T(8,128)(2,1)S(1)} %bitcast.131), channel_id=1, source_target_pairs={{0,16},{8,0},{24,8},{16,24},{1,17},{9,1},{25,9},{17,25},{2,18},{10... | collective-permute-start | bytes 983048 | tf_op jit(solution)/shard_map/ppermute | solution.py:405
  482.8 84.8 %collective-permute-start.20 = (bf16[640,256]{1,0:T(8,128)(2,1)S(1)}, bf16[640,256]{1,0:T(8,128)(2,1)S(1)}, u32[]{:S(2)}, u32[]{:S(2)}) collective-permute-start(bf16[640,256]{1,0:T(8,128)(2,1)S(1)} %bitcast.130), channel_id=1, source_target_pairs={{0,24},{8,16},{24,0},{16,8},{1,25},{9,17},{25,1},{17,9},{2,26},{10... | collective-permute-start | bytes 983048 | tf_op jit(solution)/shard_map/ppermute | solution.py:405
  586.8 40.9 %collective-permute-start.24 = (bf16[320,2048]{1,0:T(8,128)(2,1)S(1)}, bf16[320,2048]{1,0:T(8,128)(2,1)}, u32[]{:S(2)}, u32[]{:S(2)}) collective-permute-start(bf16[320,2048]{1,0:T(8,128)(2,1)S(1)} %get-tuple-element.177), channel_id=1, source_target_pairs={{0,8},{8,24},{24,16},{16,0},{1,9},{9,25},{25,17},{17,1},{2,10},{10... | collective-permute-start | bytes 3932168 | tf_op jit(solution)/shard_map/ppermute | solution.py:360
  587.4 40.3 %collective-permute-start.25 = (bf16[320,2048]{1,0:T(8,128)(2,1)S(1)}, bf16[320,2048]{1,0:T(8,128)(2,1)}, u32[]{:S(2)}, u32[]{:S(2)}) collective-permute-start(bf16[320,2048]{1,0:T(8,128)(2,1)S(1)} %get-tuple-element.176), channel_id=1, source_target_pairs={{8,0},{24,8},{16,24},{0,16},{9,1},{25,9},{17,25},{1,17},{10,2},{26... | collective-permute-start | bytes 3932168 | tf_op jit(solution)/shard_map/ppermute | solution.py:360
  591.2 35.7 %collective-permute-start.21 = (bf16[640,256]{1,0:T(8,128)(2,1)S(1)}, bf16[640,256]{1,0:T(8,128)(2,1)S(1)}, u32[]{:S(2)}, u32[]{:S(2)}) collective-permute-start(bf16[640,256]{1,0:T(8,128)(2,1)S(1)} %bitcast.133), channel_id=1, source_target_pairs={{0,24},{8,16},{24,0},{16,8},{1,25},{9,17},{25,1},{17,9},{2,26},{10... | collective-permute-start | bytes 983048 | tf_op jit(solution)/shard_map/ppermute | solution.py:405
  661.6 39.3 %collective-permute-start.30 = (bf16[160,2048]{1,0:T(8,128)(2,1)}, bf16[160,2048]{1,0:T(8,128)(2,1)}, u32[]{:S(2)}, u32[]{:S(2)}) collective-permute-start(bf16[160,2048]{1,0:T(8,128)(2,1)} %get-tuple-element.171), channel_id=1, source_target_pairs={{0,8},{8,24},{24,16},{16,0},{1,9},{9,25},{25,17},{17,1},{2,10},{10... | collective-permute-start | bytes 1966088 | tf_op jit(solution)/shard_map/ppermute | solution.py:380
  (84 other events, 1160.6 us)
Sparse Core Ops, SparseCore 0:
  9.6 84.7 all-gather.3
  96.0 81.0 all-gather.5
  178.7 80.2 all-gather.7
  284.6 90.5 reduce-scatter.4
  377.4 87.9 reduce-scatter.6
  475.5 48.5 reduce-scatter.8
  645.1 47.5 reduce-scatter.10

commit v5 on v4

--- a/solution.py
+++ b/solution.py
@@ -21,6 +21,7 @@
 LOW = jnp.bfloat16
 WIDE = jnp.float32
 LITTLE = pl.CostEstimate(flops=1000000, bytes_accessed=1000000, transcendentals=0)
+MUCH = pl.CostEstimate(flops=100000000000, bytes_accessed=1000000, transcendentals=0)
 
 
 def dot(left, right, dims):
@@ -147,12 +148,18 @@
         return slice(h * half, (h + 1) * half)
 
     def sweep(tile):
-        def double(t, carry):
-            start = pl.multiple_of(t * 2 * chunk, 2 * chunk)
+        def quad(t, carry):
+            start = pl.multiple_of(t * 4 * chunk, 4 * chunk)
+            tile(start, start, 4 * chunk, False)
+            return carry
+
+        lax.fori_loop(0, doubles // 2, quad, 0)
+
+        @pl.when(doubles % 2 == 1)
+        def _():
+            start = pl.multiple_of((doubles - 1) * 2 * chunk, 2 * chunk)
             tile(start, start, 2 * chunk, False)
-            return carry
-
-        lax.fori_loop(0, doubles, double, 0)
+
         held = pl.multiple_of(doubles * 2 * chunk, chunk)
 
         @pl.when(odd == 1)
@@ -348,7 +355,7 @@
     return pieces + far
 
 
-def ring_reduce(part, axis, cuts=1, staged=False):
+def ring_reduce(part, axis, cuts=1, chained=False):
     count = lax.axis_size(axis)
     _, ahead, behind = ring_of(count)
     far = part(count - 1)
@@ -361,29 +368,18 @@
     hops = [(up, down)]
     if count == 2:
         return [(0, up), (half, down)], hops
-    cut = half // cuts
     to_ahead, to_behind = part(count - 2), part(count - 3)
     got_up, got_down = {}, {}
 
-    def loose():
-        for n in range(cuts):
-            at = half + n * cut
-            gate = hops[-1] if staged else ()
-            got_up[at] = lax.ppermute(after(to_ahead[at : at + cut], *gate), axis, ahead)
-            at = n * cut
-            got_down[at] = lax.ppermute(after(to_behind[at : at + cut], *gate), axis, behind)
-            hops.append((got_up[half + at], got_down[at]))
-
-    def summed():
-        for n in range(cuts):
-            at, span = n * cut, slice(n * cut, (n + 1) * cut)
-            got_up[at] = lax.ppermute(plus(to_ahead[span], up[span]), axis, ahead)
-            there = slice(half + at, half + at + cut)
-            got_down[half + at] = lax.ppermute(plus(to_behind[there], down[span]), axis, behind)
-            hops.append((got_up[at], got_down[half + at]))
-
-    for send in (summed, loose) if staged else (loose, summed):
-        send()
+    got_up[0] = lax.ppermute(plus(to_ahead[:half], up), axis, ahead)
+    got_down[half] = lax.ppermute(plus(to_behind[half:], down), axis, behind)
+    hops.append((got_up[0], got_down[half]))
+    for at in range(0, half, half // cuts):
+        span, there = slice(at, at + half // cuts), slice(half + at, half + at + half // cuts)
+        gate = hops[-1] if chained else ()
+        got_up[half + at] = lax.ppermute(after(to_ahead[there], *gate), axis, ahead)
+        got_down[at] = lax.ppermute(after(to_behind[span], *gate), axis, behind)
+        hops.append((got_up[half + at], got_down[at]))
     if count == 4:
         return sorted(got_up.items()) + sorted(got_down.items()), hops
     up = jnp.concatenate([piece for _, piece in sorted(got_up.items())], axis=0)
@@ -500,7 +496,7 @@
         out_specs=[pl.BlockSpec((rows, cols), lambda i: (0, i))] * len(ranks)
         + [pl.BlockSpec((2, cols), lambda i: (0, i))],
         compiler_params=pltpu.CompilerParams(
-            dimension_semantics=("arbitrary",), vmem_limit_bytes=56 << 20
+            dimension_semantics=("arbitrary",), vmem_limit_bytes=58 << 20
         ),
         cost_estimate=LITTLE,
         name="input_grad",
@@ -555,7 +551,7 @@
         compiler_params=pltpu.CompilerParams(
             dimension_semantics=("arbitrary",), vmem_limit_bytes=48 << 20
         ),
-        cost_estimate=LITTLE,
+        cost_estimate=MUCH,
         name="place_output",
     )(*pieces, *dense_pieces, tokens, bias, own, *[term for _, term in terms])
 
@@ -600,7 +596,7 @@
         compiler_params=pltpu.CompilerParams(
             dimension_semantics=("arbitrary",), vmem_limit_bytes=48 << 20
         ),
-        cost_estimate=LITTLE,
+        cost_estimate=MUCH,
         name="token_grad",
     )(tokens, grad, own, gain[None], *[term for _, term in terms])
 
@@ -628,7 +624,7 @@
         ],
         out_specs=pl.BlockSpec((tile, columns), lambda i: (i, 0)),
         compiler_params=pltpu.CompilerParams(
-            dimension_semantics=("arbitrary",), vmem_limit_bytes=48 << 20
+            dimension_semantics=("arbitrary",), vmem_limit_bytes=58 << 20
         ),
         cost_estimate=LITTLE,
         name="pair_grad",
@@ -717,7 +713,8 @@
     qkv_weight, dense_turned = attention_weight[:, : 3 * each], attention_weight[:, 3 * each :]
 
     tabs = rope_tables(rows)
-    normed = after(normed, where, *tabs)
+    own_grad_sum = jnp.sum(own_grad.astype(WIDE), axis=0)
+    normed = after(normed, where, own_grad_sum, *tabs)
 
     fc1_bias = lax.dynamic_slice_in_dim(b_fc1, me * hidden, hidden, 0)
     qkv_bias = lax.dynamic_slice_in_dim(b_qkv.reshape(3, width), me * each, each, 1)
@@ -727,7 +724,7 @@
     grad_pieces = ring_pieces(sent_grad, "ctx", gate=(activated,))
     ff_part = dot(activated, fc2_turned, NT).astype(LOW)
     grads = jnp.concatenate([after(piece, ff_part) for piece in grad_pieces], axis=0)
-    ff_terms, ff_hops = ring_reduce(lambda rank: of_rank(ff_part, rank), "ctx", staged=True)
+    ff_terms, ff_hops = ring_reduce(lambda rank: of_rank(ff_part, rank), "ctx", chained=True)
     first, second, last = ff_hops[0], ff_hops[min(1, len(ff_hops) - 1)], ff_hops[-1]
 
     gated = after(grads, ff_part)
@@ -736,8 +733,8 @@
     d_fc2 = scatter_rows(d_fc2_part)
     qkv = dot(after(normed, d_fc2_part), qkv_weight, NN)
     qkv = (qkv + by_group(qkv_bias)[0].astype(WIDE)).astype(LOW)
-    attended_grad = dot(after(grads, qkv), dense_turned, NN).astype(LOW)
-    gated = after(normed, attended_grad, *second)
+    attended_grad = dot(after(grads, qkv, *second), dense_turned, NN).astype(LOW)
+    gated = after(normed, attended_grad)
     d_fc1_part = dot(gated, expanded_grad, TN).astype(LOW)
     d_fc1 = scatter_rows(d_fc1_part)
 
@@ -775,31 +772,32 @@
         parts.update(zip(middle[n : n + 2], some))
 
     grad_terms, hops = ring_reduce(lambda rank: parts[rank], "ctx", cuts=2)
-    covers = hops[1:] if len(hops) == 5 else [()] * 4
+    covers = hops[1:] if len(hops) == 4 else [()] * 3
     gated = after(normed, turn, *hops[0], *swapped[-1], *d_attention)
     d_part = pair_grad(gated, grads, qkv_grads[-1], attended[-1])
     d_attention.append(scatter_rows(d_part))
     own_part, own_sums = input_grad(
-        qkv_grads + [after(turn, d_part, *covers[0])], weights, normed, [0], local_rows
+        qkv_grads + [after(turn, d_part)], weights, normed, [0], local_rows
     )
     attended_own = [swapped[which][rank] for rank in range(count) for which in range(groups)]
     output = place_output(
         attended_own,
         dense_pieces,
-        after(tokens[0], *own_part, *covers[1]),
+        after(tokens[0], *own_part, *covers[0]),
         (b_dense.astype(WIDE) + b_fc2.astype(WIDE))[None],
         ff_part,
         ff_terms,
         count,
         groups,
     )
-    sums = after(far_sums + middle_sums + own_sums, output, *covers[2])
+    sums = after(far_sums + middle_sums + own_sums, output, *covers[1])
     d_tokens = token_grad(tokens[0], own_grad, own_part[0], gain, grad_terms, local_rows // 4)
 
     d_qkv = jnp.concatenate(
         [part[:, : 3 * lanes].reshape(-1, 3, lanes) for part in d_attention], axis=2
     ).astype(WIDE)
     d_dense = jnp.concatenate([part[:, 3 * lanes :].T for part in d_attention], axis=0)
+    d_fc1, d_fc2 = d_fc1.astype(WIDE), d_fc2.T.astype(WIDE)
 
     qkv_bias_part = jnp.concatenate(
         [jnp.sum(part.astype(WIDE), axis=0).reshape(3, lanes) for part in qkv_grads], axis=1
@@ -816,13 +814,13 @@
             [
                 sums.reshape(-1),
                 qkv_bias_wide,
-                jnp.sum(sent_grad.astype(WIDE), axis=0),
+                own_grad_sum,
                 fc1_bias_wide,
             ]
         ),
         ("fsdp",),
     )
-    small = sum_everywhere(after(small, *covers[3]), ("ctx",))
+    small = sum_everywhere(after(small, d_fc1, d_fc2, *covers[2]), ("ctx",))
     d_shift, with_normed, d_b_qkv, d_b_out, d_b_fc1 = jnp.split(
         small, [width, 2 * width, 5 * width, 6 * width]
     )
@@ -836,9 +834,9 @@
         d_b_qkv,
         d_dense.astype(WIDE),
         d_b_out,
-        d_fc1.astype(WIDE),
+        d_fc1,
         d_b_fc1,
-        d_fc2.T.astype(WIDE),
+        d_fc2,
         d_b_out,
     )
 

time: 763 us -> 755 us (0.990)
    reduce_scatter x4, waiting for transfers between devices: 0.01 us -> 30 us  [scatter_rows(): return lax.psum_scatter(whole, 'fsdp', scatter_dimension=0, tiled=True)]
    ppermute x12 -> x10, waiting for transfers between devices: 26.8 us -> 2.91 us  [the longest x3 0.86 us: ring_reduce(): got_down[at] = lax.ppermute(after(to_behind[span], *gate), axis, behind)]
    pallas_call x2, Pallas kernels: 164 us -> 156 us  [attention(): pl.pallas_call(kernel, out_shape=(jax.ShapeDtypeStruct((blocks, blk, lane...]
    unnamed x138 -> x112, local copies, waits for them, and re-layouts: 42.9 us -> 42.1 us
  transfers between devices with their start and end apart: 46 -> 44, of which waited for: 15 -> 12; matrix products, arithmetic and copies ran while one was open for 33% -> 34% of each run, Pallas kernels for 39% -> 41%
where the time goes in v5:
time: 755 us; the launch traced here: 748 us
  Pallas kernels  307 us (41%)
  matrix products  148 us (20%)
  waiting for transfers between devices  110 us (15%)
  local copies, waits for them, and re-layouts  87.2 us (12%)
  starting transfers between devices  42.7 us (6%)
  other arithmetic  38.9 us (5%)
  between operations  15.2 us (2%)
    pallas_call x2, Pallas kernels, attention(): pl.pallas_call(kernel, out_shape=(jax.ShapeDtypeStruct((blocks, blk, lane...  156 us
    dot_general x6, matrix products, dot(): return lax.dot_general(left, right, dims, preferred_element_type=WIDE)  148 us
    ppermute x3, waiting for transfers between devices, ring_pieces(): from_behind = lax.ppermute(from_behind, axis, ahead)  63.3 us
    pallas_call x3, Pallas kernels, input_grad(): pl.pallas_call(functools.partial(input_grad_kernel, terms=len(grads), ran...  57.3 us
    unnamed x112, local copies, waits for them, and re-layouts  42.1 us
    pallas_call x1, Pallas kernels, expand(): pl.pallas_call(functools.partial(expand_kernel, cols=min(512, hidden)), o...  38.8 us
    pallas_call x2, Pallas kernels, pair_grad(): pl.pallas_call(pair_grad_kernel, out_shape=jax.ShapeDtypeStruct((width, c...  34.3 us
    reduce_scatter x4, waiting for transfers between devices, scatter_rows(): return lax.psum_scatter(whole, 'fsdp', scatter_dimension=0, tiled=True)  30 us
  transfers between devices with their start and end apart: 44, of which 12 were waited for; matrix products, arithmetic and copies ran while one was open for 34% of the time, Pallas kernels for 41%

profile of v5, /device:TPU:0, one launch (start us, length us, event | category | flops | bytes accessed | tf_op | source)
XLA Modules:
  0.0 747.9 jit_solution(15913454939767114829)
XLA Ops:
  17.9 57.0 %collective-permute-done = bf16[640,2048]{1,0:T(8,128)(2,1)} collective-permute-done((bf16[640,2048]{1,0:T(8,128)(2,1)S(1)}, bf16[640,2048]{1,0:T(8,128)(2,1)}, u32[]{:S(2)}, u32[]{:S(2)}) %collective-permute-start) | collective-permute-done | bytes 2621472 | tf_op jit(solution)/shard_map/ppermute | solution.py:346
  77.7 6.2 fusion.7
  99.3 4.6 concatenate.36.refs_17_
  116.1 3.8 collective-permute-done.3
  131.1 38.8 %expand.1 = (bf16[2560,2048]{1,0:T(8,128)(2,1)}, bf16[2560,2048]{1,0:T(8,128)(2,1)}) custom-call(bf16[2560,2048]{1,0:T(8,128)(2,1)} %constant_dynamic-update-slice_fusion.x_ref.refs_6_.refs_9_.refs_10_, bf16[2048,2048]{1,0:T(8,128)(2,1)} %all-gather.4.cloned.1.call-done.w_ref.refs_5_.refs_8_, f32[1,2048]{1,0:T(1,128)S(1)} %bitcast.67), custom_call_target="tpu_custom_call" | custom-call | flops 21474836480 | bytes 39845888 | tf_op jit(solution)/shard_map/expand/pallas_call | solution.py:439
  169.9 6.3 collective-permute-done.4
  183.3 27.8 %convolution_convert_fusion.refs_15_ = bf16[2560,2048]{1,0:T(8,128)(2,1)S(1)} fusion(bf16[2560,2048]{1,0:T(8,128)(2,1)} %get-tuple-element.57, bf16[2048,2048]{0,1:T(8,128)(2,1)} %all-gather.6.cloned.1.call-done), kind=kOutput, calls=%fused_computation.3 | convolution fusion | flops 21480079360 | bytes 29360128 | tf_op jit(solution)/shard_map/dot_general | solution.py:28
  212.9 5.6 constant_dynamic-update-slice_fusion.8
  231.1 29.7 %convert_reduce_fusion = (f32[2048]{0:T(1024)}, bf16[2560,2048]{1,0:T(8,128)(2,1)}) fusion(bf16[2560,2048]{1,0:T(8,128)(2,1)} %get-tuple-element.67, bf16[2560,2048]{1,0:T(8,128)(2,1)} %constant_dynamic-update-slice_fusion.5.y_ref, bf16[2048,2048]{0,1:T(8,128)(2,1)} %all-gather.6.cloned.1.call-done), kind=kOutput, calls=%fused_computation | convolution fusion | flops 21501048832 | bytes 39854080 | tf_op jit(solution)/shard_map/dot_general | solution.py:28
  261.8 28.9 %convolution_convert_fusion.2 = bf16[2048,2048]{1,0:T(8,128)(2,1)} fusion(bf16[2560,2048]{1,0:T(8,128)(2,1)} %constant_dynamic-update-slice_fusion.5.y_ref, bf16[2560,2048]{1,0:T(8,128)(2,1)} %get-tuple-element.57), kind=kOutput, calls=%fused_computation.7 | convolution fusion | flops 21479030784 | bytes 29360128 | tf_op jit(solution)/shard_map/dot_general | solution.py:28
  291.4 4.7 add_convert_fusion.3
  298.4 22.3 %add_convert_fusion = bf16[2560,1536]{1,0:T(8,128)(2,1)} fusion(bf16[2560,2048]{1,0:T(8,128)(2,1)} %constant_dynamic-update-slice_fusion.x_ref.refs_6_.refs_9_.refs_10_, f32[1536]{0:T(1024)S(1)} %reshape.255, bf16[2048,2048]{1,0:T(8,128)(2,1)} %all-gather.8.cloned.1.call-done.refs_3_.refs_4_.refs_6_.refs_7_), kind=kOutput, calls=%fused_computation.2 | convolution fusion | flops 16113991680 | bytes 24647680 | tf_op jit(solution)/shard_map/dot_general | solution.py:28
  322.0 10.1 %convolution_convert_fusion.3 = bf16[2560,512]{1,0:T(8,128)(2,1)} fusion(bf16[2560,2048]{1,0:T(8,128)(2,1)} %constant_dynamic-update-slice_fusion.5.y_ref, bf16[2048,2048]{1,0:T(8,128)(2,1)} %all-gather.8.cloned.1.call-done.refs_3_.refs_4_.refs_6_.refs_7_), kind=kOutput, calls=%fused_computation.18 | convolution fusion | flops 5370019840 | bytes 15204352 | tf_op jit(solution)/shard_map/dot_general | solution.py:28
  332.0 28.9 %convolution_convert_fusion.1 = bf16[2048,2048]{1,0:T(8,128)(2,1)} fusion(bf16[2560,2048]{1,0:T(8,128)(2,1)} %constant_dynamic-update-slice_fusion.x_ref.refs_6_.refs_9_.refs_10_, bf16[2560,2048]{1,0:T(8,128)(2,1)} %get-tuple-element.90.refs_2_.refs_5_), kind=kOutput, calls=%fused_computation.6 | convolution fusion | flops 21479030784 | bytes 29360128 | tf_op jit(solution)/shard_map/dot_general | solution.py:28
  367.4 78.0 %attention.2 = (bf16[40,64,256]{2,1,0:T(8,128)(2,1)}, bf16[40,64,768]{2,1,0:T(8,128)(2,1)}) custom-call(s32[40]{0:T(128)} %select_reduce_fusion.where_ref, bf16[40,64,1536]{2,1,0:T(8,128)(2,1)} %bitcast.68, bf16[40,64,1536]{2,1,0:T(8,128)(2,1)} %bitcast.69, bf16[40,64,1536]{2,1,0:T(8,128)(2,1)} %bitcast.70, bf16[40,64,1536]{2,1,0:T(8,128)(2,1)} %bitcast.71, ...), custom_call_target="tpu_custom_call" | custom-call | flops 1000000 | bytes 1000000 | tf_op jit(solution)/shard_map/attention/pallas_call | solution.py:284
  446.7 17.1 %pair_grad.2 = bf16[2048,1024]{1,0:T(8,128)(2,1)} custom-call(bf16[2560,2048]{1,0:T(8,128)(2,1)} %constant_dynamic-update-slice_fusion.x_ref.refs_6_.refs_9_.refs_10_, bf16[2560,2048]{1,0:T(8,128)(2,1)} %constant_dynamic-update-slice_fusion.5.y_ref, bf16[2560,768]{1,0:T(8,128)(2,1)} %bitcast.100, bf16[2560,256]{1,0:T(8,128)(2,1)} %bitcast.117), custom_call_target="tpu_custom_call" | custom-call | flops 1000000 | bytes 1000000 | tf_op jit(solution)/shard_map/pair_grad/pallas_call | solution.py:615
  472.1 78.0 %attention.3 = (bf16[40,64,256]{2,1,0:T(8,128)(2,1)}, bf16[40,64,768]{2,1,0:T(8,128)(2,1)}) custom-call(s32[40]{0:T(128)} %select_reduce_fusion.where_ref, bf16[40,64,1536]{2,1,0:T(8,128)(2,1)} %bitcast.80, bf16[40,64,1536]{2,1,0:T(8,128)(2,1)} %bitcast.81, bf16[40,64,1536]{2,1,0:T(8,128)(2,1)} %bitcast.82, bf16[40,64,1536]{2,1,0:T(8,128)(2,1)} %bitcast.83, ...), custom_call_target="tpu_custom_call" | custom-call | flops 1000000 | bytes 1000000 | tf_op jit(solution)/shard_map/attention/pallas_call | solution.py:284
  554.4 15.5 %input_grad.3 = (bf16[640,2048]{1,0:T(8,128)(2,1)}, f32[2,2048]{1,0:T(2,128)}) custom-call(bf16[2560,768]{1,0:T(8,128)(2,1)} %bitcast.101, bf16[2560,768]{1,0:T(8,128)(2,1)} %bitcast.105, bf16[2560,2048]{1,0:T(8,128)(2,1)} %get-tuple-element.90.refs_2_.refs_5_, bf16[2048,2048]{1,0:T(8,128)(2,1)} %all-gather.8.cloned.1.call-done.refs_3_.refs_4_.refs_6_.refs_7_, ...), custom_call_target="tpu_custom_call" | custom-call | flops 1000000 | bytes 1000000 | tf_op jit(solution)/shard_map/input_grad/pallas_call | solution.py:490
  581.0 26.5 %input_grad.4 = (bf16[640,2048]{1,0:T(8,128)(2,1)}, bf16[640,2048]{1,0:T(8,128)(2,1)}, f32[2,2048]{1,0:T(2,128)}) custom-call(bf16[2560,768]{1,0:T(8,128)(2,1)} %bitcast.102, bf16[2560,768]{1,0:T(8,128)(2,1)} %bitcast.106, bf16[2560,2048]{1,0:T(8,128)(2,1)} %get-tuple-element.90.refs_2_.refs_5_, bf16[2560,768]{1,0:T(8,128)(2,1)} %bitcast.103, ...), custom_call_target="tpu_custom_call" | custom-call | flops 1000000 | bytes 1000000 | tf_op jit(solution)/shard_map/input_grad/pallas_call | solution.py:490
  622.9 17.1 %pair_grad.3 = bf16[2048,1024]{1,0:T(8,128)(2,1)} custom-call(bf16[2560,2048]{1,0:T(8,128)(2,1)} %constant_dynamic-update-slice_fusion.x_ref.refs_6_.refs_9_.refs_10_, bf16[2560,2048]{1,0:T(8,128)(2,1)} %constant_dynamic-update-slice_fusion.5.y_ref, bf16[2560,768]{1,0:T(8,128)(2,1)} %bitcast.108, bf16[2560,256]{1,0:T(8,128)(2,1)} %bitcast.116), custom_call_target="tpu_custom_call" | custom-call | flops 1000000 | bytes 1000000 | tf_op jit(solution)/shard_map/pair_grad/pallas_call | solution.py:615
  640.0 15.4 %input_grad.5 = (bf16[640,2048]{1,0:T(8,128)(2,1)}, f32[2,2048]{1,0:T(2,128)}) custom-call(bf16[2560,768]{1,0:T(8,128)(2,1)} %bitcast.104, bf16[2560,768]{1,0:T(8,128)(2,1)} %bitcast.109, bf16[2560,2048]{1,0:T(8,128)(2,1)} %get-tuple-element.90.refs_2_.refs_5_, bf16[2048,2048]{1,0:T(8,128)(2,1)} %all-gather.8.cloned.1.call-done.refs_3_.refs_4_.refs_6_.refs_7_, ...), custom_call_target="tpu_custom_call" | custom-call | flops 1000000 | bytes 1000000 | tf_op jit(solution)/shard_map/input_grad/pallas_call | solution.py:490
  659.6 11.0 %place_output.1 = bf16[640,2048]{1,0:T(8,128)(2,1)} custom-call(bf16[640,256]{1,0:T(8,128)(2,1)S(1)} %bitcast.63, bf16[640,256]{1,0:T(8,128)(2,1)S(1)} %bitcast.64, bf16[640,256]{1,0:T(8,128)(2,1)S(1)} %copy-done.9, bf16[640,256]{1,0:T(8,128)(2,1)} %collective-permute-done.17.refs_3_, bf16[640,256]{1,0:T(8,128)(2,1)S(1)} %copy-done.11, ...), custom_call_target="tpu_custom_call" | custom-call | flops 99999997952 | bytes 1000000 | tf_op jit(solution)/shard_map/place_output/pallas_call | solution.py:542
  689.5 9.2 %token_grad.1 = bf16[640,2048]{1,0:T(8,128)(2,1)} custom-call(bf16[640,2048]{1,0:T(8,128)(2,1)} %bitcast.111, bf16[640,2048]{1,0:T(8,128)(2,1)} %bitcast.112, bf16[640,2048]{1,0:T(8,128)(2,1)} %get-tuple-element.91.own_ref, f32[1,2048]{1,0:T(1,128)S(1)} %bitcast.65, bf16[320,2048]{1,0:T(8,128)(2,1)S(1)} %collective-permute-done.26.refs_0_, ...), custom_call_target="tpu_custom_call" | custom-call | flops 99999997952 | bytes 1000000 | tf_op jit(solution)/shard_map/token_grad/pallas_call | solution.py:586
  705.1 30.0 %reduce-scatter.11.cloned.1.call-done = bf16[256,1024]{1,0:T(8,128)(2,1)} async-done(((bf16[2048,1024]{1,0:T(8,128)(2,1)}), bf16[256,1024]{1,0:T(8,128)(2,1)}) %reduce-scatter.11.cloned.1.call-update) | async-done | bytes 524304 | tf_op jit(solution)/shard_map/reduce_scatter | solution.py:698
  (276 shorter events, 160.3 us)
Async XLA Ops:
  7.2 123.9 %all-gather.4.cloned.1.call-start = ((), (), s32[]{:S(2)}) async-start(), calls=%async_computation.4 | async-start | bytes 9437184 | tf_op jit(solution)/shard_map/all_gather | solution.py:695
  7.9 175.4 %all-gather.6.cloned.1.call-start = ((), (), s32[]{:S(2)}) async-start(), calls=%async_computation.5 | async-start | bytes 9437184 | tf_op jit(solution)/shard_map/all_gather | solution.py:695
  14.9 59.9 %collective-permute-start = (bf16[640,2048]{1,0:T(8,128)(2,1)S(1)}, bf16[640,2048]{1,0:T(8,128)(2,1)}, u32[]{:S(2)}, u32[]{:S(2)}) collective-permute-start(bf16[640,2048]{1,0:T(8,128)(2,1)S(1)} %get-tuple-element.161), channel_id=1, source_target_pairs={{0,8},{8,24},{24,16},{16,0},{1,9},{9,25},{25,17},{17,1},{2,10},{10... | collective-permute-start | bytes 7864328 | tf_op jit(solution)/shard_map/ppermute | solution.py:346
  17.8 58.4 %collective-permute-start.1 = (bf16[640,2048]{1,0:T(8,128)(2,1)S(1)}, bf16[640,2048]{1,0:T(8,128)(2,1)}, u32[]{:S(2)}, u32[]{:S(2)}) collective-permute-start(bf16[640,2048]{1,0:T(8,128)(2,1)S(1)} %get-tuple-element.161), channel_id=1, source_target_pairs={{8,0},{24,8},{16,24},{0,16},{9,1},{25,9},{17,25},{1,17},{10,2},{26... | collective-permute-start | bytes 7864328 | tf_op jit(solution)/shard_map/ppermute | solution.py:347
  76.3 222.1 %all-gather.8.cloned.1.call-start = ((), (), s32[]{:S(2)}) async-start(), calls=%async_computation.6 | async-start | bytes 9437184 | tf_op jit(solution)/shard_map/all_gather | solution.py:695
  119.9 56.3 %collective-permute-start.4 = (bf16[640,2048]{1,0:T(8,128)(2,1)S(1)}, bf16[640,2048]{1,0:T(8,128)(2,1)}, u32[]{:S(2)}, u32[]{:S(2)}) collective-permute-start(bf16[640,2048]{1,0:T(8,128)(2,1)S(1)} %bitcast.113), channel_id=1, source_target_pairs={{0,8},{8,24},{24,16},{16,0},{1,9},{9,25},{25,17},{17,1},{2,10},{10... | collective-permute-start | bytes 7864328 | tf_op jit(solution)/shard_map/ppermute | solution.py:346
  120.5 59.0 %collective-permute-start.5 = (bf16[640,2048]{1,0:T(8,128)(2,1)S(1)}, bf16[640,2048]{1,0:T(8,128)(2,1)}, u32[]{:S(2)}, u32[]{:S(2)}) collective-permute-start(bf16[640,2048]{1,0:T(8,128)(2,1)S(1)} %bitcast.114), channel_id=1, source_target_pairs={{8,0},{24,8},{16,24},{0,16},{9,1},{25,9},{17,25},{1,17},{10,2},{26... | collective-permute-start | bytes 7864328 | tf_op jit(solution)/shard_map/ppermute | solution.py:347
  130.6 316.1 %reduce-scatter.5.cloned.1.call-start = ((), (), s32[]{:S(2)}) async-start(), calls=%async_computation.7 | async-start | bytes 9437184 | tf_op jit(solution)/shard_map/reduce_scatter | solution.py:698
  290.7 263.7 %reduce-scatter.7.cloned.1.call-start = ((), (), s32[]{:S(2)}) async-start(), calls=%async_computation.8 | async-start | bytes 9437184 | tf_op jit(solution)/shard_map/reduce_scatter | solution.py:698
  361.0 261.9 %reduce-scatter.9.cloned.1.call-start = ((), (), s32[]{:S(2)}) async-start(), calls=%async_computation.9 | async-start | bytes 4718592 | tf_op jit(solution)/shard_map/reduce_scatter | solution.py:698
  362.9 82.5 %collective-permute-start.14 = (bf16[2048,512]{1,0:T(8,128)(2,1)S(1)}, bf16[2048,512]{1,0:T(8,128)(2,1)S(1)}, u32[]{:S(2)}, u32[]{:S(2)}) collective-permute-start(bf16[2048,512]{1,0:T(8,128)(2,1)S(1)} %slice.194.refs_8_), channel_id=1, source_target_pairs={{0,8},{8,24},{24,16},{16,0},{1,9},{9,25},{25,17},{17,1},{2,10},{10... | collective-permute-start | bytes 6291464 | tf_op jit(solution)/shard_map/ppermute | solution.py:346
  364.2 82.5 %collective-permute-start.15 = (bf16[2048,512]{1,0:T(8,128)(2,1)S(1)}, bf16[2048,512]{1,0:T(8,128)(2,1)}, u32[]{:S(2)}, u32[]{:S(2)}) collective-permute-start(bf16[2048,512]{1,0:T(8,128)(2,1)S(1)} %slice.194.refs_8_), channel_id=1, source_target_pairs={{8,0},{24,8},{16,24},{0,16},{9,1},{25,9},{17,25},{1,17},{10,2},{26... | collective-permute-start | bytes 6291464 | tf_op jit(solution)/shard_map/ppermute | solution.py:347
  365.0 80.4 %collective-permute-start.12 = (bf16[320,2048]{1,0:T(8,128)(2,1)S(1)}, bf16[320,2048]{1,0:T(8,128)(2,1)}, u32[]{:S(2)}, u32[]{:S(2)}) collective-permute-start(bf16[320,2048]{1,0:T(8,128)(2,1)S(1)} %copy-done.26), channel_id=1, source_target_pairs={{0,8},{8,24},{24,16},{16,0},{1,9},{9,25},{25,17},{17,1},{2,10},{10... | collective-permute-start | bytes 3932168 | tf_op jit(solution)/shard_map/ppermute | solution.py:380
  366.2 79.1 %collective-permute-start.13 = (bf16[320,2048]{1,0:T(8,128)(2,1)S(1)}, bf16[320,2048]{1,0:T(8,128)(2,1)}, u32[]{:S(2)}, u32[]{:S(2)}) collective-permute-start(bf16[320,2048]{1,0:T(8,128)(2,1)S(1)} %get-tuple-element.76), channel_id=1, source_target_pairs={{8,0},{24,8},{16,24},{0,16},{9,1},{25,9},{17,25},{1,17},{10,2},{26... | collective-permute-start | bytes 3932168 | tf_op jit(solution)/shard_map/ppermute | solution.py:381
  463.9 271.2 %reduce-scatter.11.cloned.1.call-start = ((), (), s32[]{:S(2)}) async-start(), calls=%async_computation.10 | async-start | bytes 4718592 | tf_op jit(solution)/shard_map/reduce_scatter | solution.py:698
  465.4 87.0 %collective-permute-start.22 = (bf16[1024,512]{1,0:T(8,128)(2,1)S(1)}, bf16[1024,512]{1,0:T(8,128)(2,1)S(1)}, u32[]{:S(2)}, u32[]{:S(2)}) collective-permute-start(bf16[1024,512]{1,0:T(8,128)(2,1)S(1)} %slice.197), channel_id=1, source_target_pairs={{0,8},{8,24},{24,16},{16,0},{1,9},{9,25},{25,17},{17,1},{2,10},{10... | collective-permute-start | bytes 3145736 | tf_op jit(solution)/shard_map/ppermute | solution.py:352
  468.0 85.3 %collective-permute-start.23 = (bf16[1024,512]{1,0:T(8,128)(2,1)S(1)}, bf16[1024,512]{1,0:T(8,128)(2,1)S(1)}, u32[]{:S(2)}, u32[]{:S(2)}) collective-permute-start(bf16[1024,512]{1,0:T(8,128)(2,1)S(1)} %slice.198), channel_id=1, source_target_pairs={{8,0},{24,8},{16,24},{0,16},{9,1},{25,9},{17,25},{1,17},{10,2},{26... | collective-permute-start | bytes 3145736 | tf_op jit(solution)/shard_map/ppermute | solution.py:353
  469.0 81.2 %collective-permute-start.16 = (bf16[640,256]{1,0:T(8,128)(2,1)S(1)}, bf16[640,256]{1,0:T(8,128)(2,1)S(1)}, u32[]{:S(2)}, u32[]{:S(2)}) collective-permute-start(bf16[640,256]{1,0:T(8,128)(2,1)S(1)} %bitcast.126), channel_id=1, source_target_pairs={{0,8},{8,24},{24,16},{16,0},{1,9},{9,25},{25,17},{17,1},{2,10},{10... | collective-permute-start | bytes 983048 | tf_op jit(solution)/shard_map/ppermute | solution.py:401
  470.3 80.6 %collective-permute-start.18 = (bf16[640,256]{1,0:T(8,128)(2,1)S(1)}, bf16[640,256]{1,0:T(8,128)(2,1)S(1)}, u32[]{:S(2)}, u32[]{:S(2)}) collective-permute-start(bf16[640,256]{1,0:T(8,128)(2,1)S(1)} %bitcast.125), channel_id=1, source_target_pairs={{0,16},{8,0},{24,8},{16,24},{1,17},{9,1},{25,9},{17,25},{2,18},{10... | collective-permute-start | bytes 983048 | tf_op jit(solution)/shard_map/ppermute | solution.py:401
  471.0 80.6 %collective-permute-start.20 = (bf16[640,256]{1,0:T(8,128)(2,1)S(1)}, bf16[640,256]{1,0:T(8,128)(2,1)S(1)}, u32[]{:S(2)}, u32[]{:S(2)}) collective-permute-start(bf16[640,256]{1,0:T(8,128)(2,1)S(1)} %bitcast.124), channel_id=1, source_target_pairs={{0,24},{8,16},{24,0},{16,8},{1,25},{9,17},{25,1},{17,9},{2,26},{10... | collective-permute-start | bytes 983048 | tf_op jit(solution)/shard_map/ppermute | solution.py:401
  579.2 43.7 %collective-permute-start.21 = (bf16[640,256]{1,0:T(8,128)(2,1)}, bf16[640,256]{1,0:T(8,128)(2,1)}, u32[]{:S(2)}, u32[]{:S(2)}) collective-permute-start(bf16[640,256]{1,0:T(8,128)(2,1)} %bitcast.25), channel_id=1, source_target_pairs={{0,24},{8,16},{24,0},{16,8},{1,25},{9,17},{25,1},{17,9},{2,26},{10... | collective-permute-start | bytes 983048 | tf_op jit(solution)/shard_map/ppermute | solution.py:401
  610.9 44.5 %collective-permute-start.26 = (bf16[320,2048]{1,0:T(8,128)(2,1)}, bf16[320,2048]{1,0:T(8,128)(2,1)S(1)}, u32[]{:S(2)}, u32[]{:S(2)}) collective-permute-start(bf16[320,2048]{1,0:T(8,128)(2,1)} %add_convert_fusion.2), channel_id=1, source_target_pairs={{0,8},{8,24},{24,16},{16,0},{1,9},{9,25},{25,17},{17,1},{2,10},{10... | collective-permute-start | bytes 3932168 | tf_op jit(solution)/shard_map/ppermute | solution.py:374
  620.9 49.8 %collective-permute-start.28 = (bf16[160,2048]{1,0:T(8,128)(2,1)}, bf16[160,2048]{1,0:T(8,128)(2,1)}, u32[]{:S(2)}, u32[]{:S(2)}) collective-permute-start(bf16[160,2048]{1,0:T(8,128)(2,1)} %get-tuple-element.171), channel_id=1, source_target_pairs={{0,8},{8,24},{24,16},{16,0},{1,9},{9,25},{25,17},{17,1},{2,10},{10... | collective-permute-start | bytes 1966088 | tf_op jit(solution)/shard_map/ppermute | solution.py:380
  621.9 48.8 %collective-permute-start.30 = (bf16[160,2048]{1,0:T(8,128)(2,1)}, bf16[160,2048]{1,0:T(8,128)(2,1)}, u32[]{:S(2)}, u32[]{:S(2)}) collective-permute-start(bf16[160,2048]{1,0:T(8,128)(2,1)} %get-tuple-element.169), channel_id=1, source_target_pairs={{8,0},{24,8},{16,24},{0,16},{9,1},{25,9},{17,25},{1,17},{10,2},{26... | collective-permute-start | bytes 1966088 | tf_op jit(solution)/shard_map/ppermute | solution.py:381
  (69 other events, 963.6 us)
Sparse Core Ops, SparseCore 0:
  9.6 84.7 all-gather.3
  96.0 81.0 all-gather.5
  179.2 80.2 all-gather.7
  290.8 88.8 reduce-scatter.4
  381.9 87.9 reduce-scatter.6
  472.1 48.3 reduce-scatter.8
  687.5 47.5 reduce-scatter.10

commit v6 on v5

--- a/solution.py
+++ b/solution.py
@@ -30,8 +30,8 @@
 
 def attention_kernel(where_ref, *refs, chunk, chunks, full_chunks, blk, group, scale):
     per = chunk // blk
-    q_in, k_in, v_in, g_in = (refs[n * per : (n + 1) * per] for n in range(4))
-    cos_ref, up_ref, down_ref, att_hbm, grad_hbm = refs[4 * per : 4 * per + 5]
+    qkv_in, g_in = refs[:per], refs[per : 2 * per]
+    cos_ref, up_ref, down_ref, att_hbm, grad_hbm = refs[2 * per : 2 * per + 5]
     (
         keys,
         values,
@@ -49,7 +49,7 @@
         value_stage,
         row_sem,
         col_sem,
-    ) = refs[4 * per + 5 :]
+    ) = refs[2 * per + 5 :]
     i = pl.program_id(0)
     slot = lax.rem(i, 2)
     half = LANES // 2
@@ -115,13 +115,14 @@
 
     here = pl.ds(pl.multiple_of(i * chunk, chunk), chunk)
     tab = tables(here)
-    query = (turned(load(q_in).astype(WIDE), tab, 1.0) * scale).astype(LOW)
-    key_new = turned(load(k_in).astype(WIDE), tab, 1.0)
-    value_new = load(v_in)
+    qkv = load(qkv_in)
+    query = (turned(qkv[:, :lanes].astype(WIDE), tab, 1.0) * scale).astype(LOW)
+    key_new = turned(qkv[:, lanes : 2 * lanes].astype(WIDE), tab, 1.0)
+    value_new = qkv[:, 2 * lanes :]
     grad = load(g_in)
     keys[here] = key_new.astype(LOW)
     values[here] = value_new
-    values_t[:, here] = value_new.astype(WIDE).T.astype(LOW)
+    values_t[:, here] = value_new.T
     key_sum[here] = jnp.zeros((chunk, lanes), WIDE)
     value_sum[here] = jnp.zeros((chunk, lanes), WIDE)
     top_ref[...] = jnp.full(top_ref.shape, -1e30, WIDE)
@@ -199,9 +200,9 @@
     attended = jnp.concatenate(
         [mix_ref[head_rows(h)] * inverse[h] for h in range(heads)], axis=0
     )
-    shared = grad.astype(WIDE).T * attended
+    shared = grad.T.astype(WIDE) * attended
     inner = [jnp.sum(shared[head_rows(h)], axis=0, keepdims=True) for h in range(heads)]
-    att_stage[slot] = attended.T.astype(LOW)
+    att_stage[slot] = attended.astype(LOW).T
     for copy in row_copies(0, slot):
         copy.start()
 
@@ -265,13 +266,12 @@
     qkv_blocks = qkv.reshape(blocks, blk, qkv.shape[1])
     grad_blocks = grad.reshape(blocks, blk, grad.shape[1])
 
-    def spec(column, r):
-        return pl.BlockSpec((1, blk, lanes), lambda i, at: (at[i * per + r], 0, column))
-
-    in_specs = [spec(3 * which + part, r) for part in range(3) for r in range(per)]
-    in_specs += [spec(which, r) for r in range(per)]
+    def spec(columns, r):
+        return pl.BlockSpec((1, blk, columns), lambda i, at: (at[i * per + r], 0, which))
+
+    in_specs = [spec(3 * lanes, r) for r in range(per)] + [spec(lanes, r) for r in range(per)]
     in_specs += [pl.BlockSpec((rows, LANES), lambda i, at: (0, 0), pipeline_mode=pl.Buffered(1))] * 3
-    operands = [qkv_blocks] * (3 * per) + [grad_blocks] * per + list(tabs)
+    operands = [qkv_blocks] * per + [grad_blocks] * per + list(tabs)
     kernel = functools.partial(
         attention_kernel,
         chunk=chunk,
@@ -358,27 +358,35 @@
 def ring_reduce(part, axis, cuts=1, chained=False):
     count = lax.axis_size(axis)
     _, ahead, behind = ring_of(count)
-    far = part(count - 1)
-    half = far.shape[0] // 2
 
     def plus(a, b):
         return (a.astype(WIDE) + b.astype(WIDE)).astype(LOW)
 
-    up, down = lax.ppermute(far[:half], axis, ahead), lax.ppermute(far[half:], axis, behind)
+    def cut_rows(term, sizes):
+        if isinstance(term, (list, tuple)):
+            return term
+        ends = [sum(sizes[: n + 1]) for n in range(len(sizes))]
+        return [term[end - size : end] for end, size in zip(ends, sizes)]
+
+    far = part(count - 1)
+    half = sum(a.shape[0] for a in far) // 2 if isinstance(far, (list, tuple)) else far.shape[0] // 2
+    far = cut_rows(far, [half, half])
+    up, down = lax.ppermute(far[0], axis, ahead), lax.ppermute(far[1], axis, behind)
     hops = [(up, down)]
     if count == 2:
         return [(0, up), (half, down)], hops
-    to_ahead, to_behind = part(count - 2), part(count - 3)
+    pieces = [half // cuts] * cuts
+    to_ahead = cut_rows(part(count - 2), [half] + pieces)
+    to_behind = cut_rows(part(count - 3), pieces + [half])
     got_up, got_down = {}, {}
-
-    got_up[0] = lax.ppermute(plus(to_ahead[:half], up), axis, ahead)
-    got_down[half] = lax.ppermute(plus(to_behind[half:], down), axis, behind)
+    got_up[0] = lax.ppermute(plus(to_ahead[0], up), axis, ahead)
+    got_down[half] = lax.ppermute(plus(to_behind[-1], down), axis, behind)
     hops.append((got_up[0], got_down[half]))
-    for at in range(0, half, half // cuts):
-        span, there = slice(at, at + half // cuts), slice(half + at, half + at + half // cuts)
+    for n in range(cuts):
         gate = hops[-1] if chained else ()
-        got_up[half + at] = lax.ppermute(after(to_ahead[there], *gate), axis, ahead)
-        got_down[at] = lax.ppermute(after(to_behind[span], *gate), axis, behind)
+        at = n * (half // cuts)
+        got_up[half + at] = lax.ppermute(after(to_ahead[1 + n], *gate), axis, ahead)
+        got_down[at] = lax.ppermute(after(to_behind[n], *gate), axis, behind)
         hops.append((got_up[half + at], got_down[at]))
     if count == 4:
         return sorted(got_up.items()) + sorted(got_down.items()), hops
@@ -461,19 +469,23 @@
 def input_grad_kernel(*refs, terms, ranks):
     grads, weights = refs[: terms * ranks], refs[terms * ranks : terms * ranks + terms]
     rest = refs[terms * (ranks + 1) :]
-    normed_refs, out_refs, sums_ref = rest[:ranks], rest[ranks : 2 * ranks], rest[2 * ranks]
+    normed_refs, out_refs, sums_ref = rest[:ranks], list(rest[ranks:-1]), rest[-1]
     plain = weighted = 0.0
     for n in range(ranks):
         mine = grads[n * terms : (n + 1) * terms]
         total = sum(dot(g[...], w[...], NT) for g, w in zip(mine, weights))
-        out_refs[n][...] = total.astype(LOW)
+        at = 0
+        while at < total.shape[0]:
+            out_ref = out_refs.pop(0)
+            out_ref[...] = total[at : at + out_ref.shape[0]].astype(LOW)
+            at += out_ref.shape[0]
         plain += jnp.sum(total, axis=0, keepdims=True)
         weighted += jnp.sum(total * normed_refs[n][...].astype(WIDE), axis=0, keepdims=True)
     sums_ref[0:1] = plain
     sums_ref[1:2] = weighted
 
 
-def input_grad(grads, weights, normed, ranks, rows):
+def input_grad(grads, weights, normed, ranks, rows, cuts, cost):
     width = normed.shape[1]
     cols = 512
     keep = pl.Buffered(1)
@@ -487,21 +499,22 @@
         for g, (_, at) in zip(grads, weights)
     ]
     in_specs += [pl.BlockSpec((rows, cols), lambda i, rank=rank: (rank, i)) for rank in ranks]
+    sizes = [size for cut in cuts for size in cut]
     *parts, sums = pl.pallas_call(
         functools.partial(input_grad_kernel, terms=len(grads), ranks=len(ranks)),
-        out_shape=[jax.ShapeDtypeStruct((rows, width), LOW)] * len(ranks)
+        out_shape=[jax.ShapeDtypeStruct((size, width), LOW) for size in sizes]
         + [jax.ShapeDtypeStruct((2, width), WIDE)],
         grid=(width // cols,),
         in_specs=in_specs,
-        out_specs=[pl.BlockSpec((rows, cols), lambda i: (0, i))] * len(ranks)
+        out_specs=[pl.BlockSpec((size, cols), lambda i: (0, i)) for size in sizes]
         + [pl.BlockSpec((2, cols), lambda i: (0, i))],
         compiler_params=pltpu.CompilerParams(
             dimension_semantics=("arbitrary",), vmem_limit_bytes=58 << 20
         ),
-        cost_estimate=LITTLE,
+        cost_estimate=cost,
         name="input_grad",
     )(*grads * len(ranks), *[w for w, _ in weights], *[normed] * len(ranks))
-    return parts, sums
+    return [[parts.pop(0) for _ in cut] for cut in cuts], sums
 
 
 def place_kernel(*refs, starts, count, groups):
@@ -551,7 +564,7 @@
         compiler_params=pltpu.CompilerParams(
             dimension_semantics=("arbitrary",), vmem_limit_bytes=48 << 20
         ),
-        cost_estimate=MUCH,
+        cost_estimate=LITTLE,
         name="place_output",
     )(*pieces, *dense_pieces, tokens, bias, own, *[term for _, term in terms])
 
@@ -596,7 +609,7 @@
         compiler_params=pltpu.CompilerParams(
             dimension_semantics=("arbitrary",), vmem_limit_bytes=48 << 20
         ),
-        cost_estimate=MUCH,
+        cost_estimate=LITTLE,
         name="token_grad",
     )(tokens, grad, own, gain[None], *[term for _, term in terms])
 
@@ -759,26 +772,35 @@
     early_swaps = [piece for pieces in swapped for piece in pieces]
     turn = after(expanded_grad, d_fc1, *dense_pieces[-2:], *early_swaps, *attended)
     swapped.append(ring_exchange(lambda rank: of_rank(attended[-1], rank), "ctx"))
-    far_part, far_sums = input_grad(qkv_grads + [turn], weights, normed, [count - 1], local_rows)
+    half = local_rows // 2
+    whole, far_cut, ahead_cut, behind_cut = [local_rows], [half, half], [half], [half]
+    if count > 2:
+        ahead_cut, behind_cut = [half, half // 2, half // 2], [half // 2, half // 2, half]
+    cut_of = {0: whole, count - 2: ahead_cut, count - 3: behind_cut, count - 1: far_cut}
+
+    def some_ranks(ranks, turn, cost=LITTLE):
+        cuts = [cut_of.get(rank, whole) for rank in ranks]
+        return input_grad(qkv_grads + [turn], weights, normed, ranks, local_rows, cuts, cost)
+
+    far_part, far_sums = some_ranks([count - 1], turn)
     middle = list(range(count - 2, 0, -1))
     middle_sums, parts = 0.0, {count - 1: far_part[0]}
-    turn = after(turn, *far_part)
+    turn = after(turn, *far_part[0])
     for n in range(0, len(middle), 2):
-        some, some_sums = input_grad(
-            qkv_grads + [turn], weights, normed, middle[n : n + 2], local_rows
-        )
-        turn = after(turn, *some)
+        some, some_sums = some_ranks(middle[n : n + 2], turn)
+        turn = after(turn, *[piece for pieces in some for piece in pieces])
         middle_sums = middle_sums + some_sums
         parts.update(zip(middle[n : n + 2], some))
+    for rank, pieces in parts.items():
+        if len(pieces) == 1:
+            parts[rank] = pieces[0]
 
     grad_terms, hops = ring_reduce(lambda rank: parts[rank], "ctx", cuts=2)
     covers = hops[1:] if len(hops) == 4 else [()] * 3
     gated = after(normed, turn, *hops[0], *swapped[-1], *d_attention)
     d_part = pair_grad(gated, grads, qkv_grads[-1], attended[-1])
     d_attention.append(scatter_rows(d_part))
-    own_part, own_sums = input_grad(
-        qkv_grads + [after(turn, d_part)], weights, normed, [0], local_rows
-    )
+    [own_part], own_sums = some_ranks([0], after(turn, d_part), MUCH)
     attended_own = [swapped[which][rank] for rank in range(count) for which in range(groups)]
     output = place_output(
         attended_own,

time: 755 us -> 733 us (0.971)
  waiting for transfers between devices: 110 us -> 79.5 us
    reduce_scatter x4, waiting for transfers between devices: 30 us -> 0.01 us  [scatter_rows(): return lax.psum_scatter(whole, 'fsdp', scatter_dimension=0, tiled=True)]
    unnamed x112 -> x122, local copies, waits for them, and re-layouts: 42.1 us -> 47.3 us
  transfers between devices with their start and end apart: 44 -> 44, of which waited for: 12 -> 9; matrix products, arithmetic and copies ran while one was open for 34% -> 36% of each run, Pallas kernels for 41% -> 42%
where the time goes in v6:
time: 733 us; the launch traced here: 726 us
  Pallas kernels  302 us (41%)
  matrix products  148 us (20%)
  local copies, waits for them, and re-layouts  92.5 us (13%)
  waiting for transfers between devices  79.5 us (11%)
  other arithmetic  44.9 us (6%)
  starting transfers between devices  43.3 us (6%)
  between operations  15.3 us (2%)
    pallas_call x2, Pallas kernels, attention(): pl.pallas_call(kernel, out_shape=(jax.ShapeDtypeStruct((blocks, blk, lane...  153 us
    dot_general x6, matrix products, dot(): return lax.dot_general(left, right, dims, preferred_element_type=WIDE)  148 us
    ppermute x3, waiting for transfers between devices, ring_pieces(): from_behind = lax.ppermute(from_behind, axis, ahead)  63.3 us
    pallas_call x3, Pallas kernels, input_grad(): pl.pallas_call(functools.partial(input_grad_kernel, terms=len(grads), ran...  57.4 us
    unnamed x122, local copies, waits for them, and re-layouts  47.3 us
    pallas_call x1, Pallas kernels, expand(): pl.pallas_call(functools.partial(expand_kernel, cols=min(512, hidden)), o...  38.8 us
    pallas_call x2, Pallas kernels, pair_grad(): pl.pallas_call(pair_grad_kernel, out_shape=jax.ShapeDtypeStruct((width, c...  34 us
  transfers between devices with their start and end apart: 44, of which 9 were waited for; matrix products, arithmetic and copies ran while one was open for 36% of the time, Pallas kernels for 42%

profile of v6, /device:TPU:0, one launch (start us, length us, event | category | flops | bytes accessed | tf_op | source)
XLA Modules:
  0.0 725.5 jit_solution(14385087141160195402)
XLA Ops:
  17.9 57.0 %collective-permute-done = bf16[640,2048]{1,0:T(8,128)(2,1)} collective-permute-done((bf16[640,2048]{1,0:T(8,128)(2,1)S(1)}, bf16[640,2048]{1,0:T(8,128)(2,1)}, u32[]{:S(2)}, u32[]{:S(2)}) %collective-permute-start) | collective-permute-done | bytes 2621472 | tf_op jit(solution)/shard_map/ppermute | solution.py:346
  77.7 6.2 fusion.7
  100.4 6.0 concatenate.36.refs_9_
  109.3 4.8 pad_maximum_fusion.refs_10_
  131.1 38.8 %expand.1 = (bf16[2560,2048]{1,0:T(8,128)(2,1)}, bf16[2560,2048]{1,0:T(8,128)(2,1)}) custom-call(bf16[2560,2048]{1,0:T(8,128)(2,1)} %constant_dynamic-update-slice_fusion.x_ref.refs_6_.refs_9_.refs_10_, bf16[2048,2048]{1,0:T(8,128)(2,1)} %all-gather.4.cloned.1.call-done.w_ref.refs_5_.refs_8_, f32[1,2048]{1,0:T(1,128)S(1)} %bitcast.67), custom_call_target="tpu_custom_call" | custom-call | flops 21474836480 | bytes 39845888 | tf_op jit(solution)/shard_map/expand/pallas_call | solution.py:447
  169.9 6.3 collective-permute-done.4
  183.3 27.7 %convolution_convert_fusion.refs_15_ = bf16[2560,2048]{1,0:T(8,128)(2,1)S(1)} fusion(bf16[2560,2048]{1,0:T(8,128)(2,1)} %get-tuple-element.62, bf16[2048,2048]{0,1:T(8,128)(2,1)} %all-gather.6.cloned.1.call-done), kind=kOutput, calls=%fused_computation.3 | convolution fusion | flops 21480079360 | bytes 29360128 | tf_op jit(solution)/shard_map/dot_general | solution.py:28
  212.8 5.6 constant_dynamic-update-slice_fusion.8
  231.3 29.6 %convert_reduce_fusion = (f32[2048]{0:T(1024)}, bf16[2560,2048]{1,0:T(8,128)(2,1)}) fusion(bf16[2560,2048]{1,0:T(8,128)(2,1)} %get-tuple-element.72, bf16[2560,2048]{1,0:T(8,128)(2,1)} %constant_dynamic-update-slice_fusion.5.y_ref, bf16[2048,2048]{0,1:T(8,128)(2,1)} %all-gather.6.cloned.1.call-done), kind=kOutput, calls=%fused_computation | convolution fusion | flops 21501048832 | bytes 39854080 | tf_op jit(solution)/shard_map/dot_general | solution.py:28
  260.9 28.9 %convolution_convert_fusion.2 = bf16[2048,2048]{1,0:T(8,128)(2,1)} fusion(bf16[2560,2048]{1,0:T(8,128)(2,1)} %constant_dynamic-update-slice_fusion.5.y_ref, bf16[2560,2048]{1,0:T(8,128)(2,1)} %get-tuple-element.62), kind=kOutput, calls=%fused_computation.7 | convolution fusion | flops 21479030784 | bytes 29360128 | tf_op jit(solution)/shard_map/dot_general | solution.py:28
  297.0 22.3 %add_convert_fusion = bf16[2560,1536]{1,0:T(8,128)(2,1)} fusion(bf16[2560,2048]{1,0:T(8,128)(2,1)} %constant_dynamic-update-slice_fusion.x_ref.refs_6_.refs_9_.refs_10_, f32[1536]{0:T(1024)S(1)} %reshape.255, bf16[2048,2048]{1,0:T(8,128)(2,1)} %all-gather.8.cloned.1.call-done.refs_3_.refs_4_.refs_6_.refs_7_), kind=kOutput, calls=%fused_computation.2 | convolution fusion | flops 16113991680 | bytes 24647680 | tf_op jit(solution)/shard_map/dot_general | solution.py:28
  320.7 10.5 %convolution_convert_fusion.3 = bf16[2560,512]{1,0:T(8,128)(2,1)} fusion(bf16[2560,2048]{1,0:T(8,128)(2,1)} %constant_dynamic-update-slice_fusion.5.y_ref, bf16[2048,2048]{1,0:T(8,128)(2,1)} %all-gather.8.cloned.1.call-done.refs_3_.refs_4_.refs_6_.refs_7_), kind=kOutput, calls=%fused_computation.18 | convolution fusion | flops 5370019840 | bytes 15204352 | tf_op jit(solution)/shard_map/dot_general | solution.py:28
  331.2 28.9 %convolution_convert_fusion.1 = bf16[2048,2048]{1,0:T(8,128)(2,1)} fusion(bf16[2560,2048]{1,0:T(8,128)(2,1)} %constant_dynamic-update-slice_fusion.x_ref.refs_6_.refs_9_.refs_10_, bf16[2560,2048]{1,0:T(8,128)(2,1)} %get-tuple-element.100.refs_2_.refs_5_), kind=kOutput, calls=%fused_computation.6 | convolution fusion | flops 21479030784 | bytes 29360128 | tf_op jit(solution)/shard_map/dot_general | solution.py:28
  366.6 76.2 %attention.2 = (bf16[40,64,256]{2,1,0:T(8,128)(2,1)}, bf16[40,64,768]{2,1,0:T(8,128)(2,1)}) custom-call(s32[40]{0:T(128)} %select_reduce_fusion.where_ref, bf16[40,64,1536]{2,1,0:T(8,128)(2,1)} %bitcast.68, bf16[40,64,1536]{2,1,0:T(8,128)(2,1)} %bitcast.69, bf16[40,64,1536]{2,1,0:T(8,128)(2,1)} %bitcast.70, bf16[40,64,1536]{2,1,0:T(8,128)(2,1)} %bitcast.71, ...), custom_call_target="tpu_custom_call" | custom-call | flops 1000000 | bytes 1000000 | tf_op jit(solution)/shard_map/attention/pallas_call | solution.py:284
  445.2 16.9 %pair_grad.2 = bf16[2048,1024]{1,0:T(8,128)(2,1)} custom-call(bf16[2560,2048]{1,0:T(8,128)(2,1)} %constant_dynamic-update-slice_fusion.x_ref.refs_6_.refs_9_.refs_10_, bf16[2560,2048]{1,0:T(8,128)(2,1)} %constant_dynamic-update-slice_fusion.5.y_ref, bf16[2560,768]{1,0:T(8,128)(2,1)} %bitcast.84, bf16[2560,256]{1,0:T(8,128)(2,1)} %bitcast.101), custom_call_target="tpu_custom_call" | custom-call | flops 1000000 | bytes 1000000 | tf_op jit(solution)/shard_map/pair_grad/pallas_call | solution.py:628
  470.5 76.4 %attention.3 = (bf16[40,64,256]{2,1,0:T(8,128)(2,1)}, bf16[40,64,768]{2,1,0:T(8,128)(2,1)}) custom-call(s32[40]{0:T(128)} %select_reduce_fusion.where_ref, bf16[40,64,1536]{2,1,0:T(8,128)(2,1)} %bitcast.72, bf16[40,64,1536]{2,1,0:T(8,128)(2,1)} %bitcast.73, bf16[40,64,1536]{2,1,0:T(8,128)(2,1)} %bitcast.74, bf16[40,64,1536]{2,1,0:T(8,128)(2,1)} %bitcast.75, ...), custom_call_target="tpu_custom_call" | custom-call | flops 1000000 | bytes 1000000 | tf_op jit(solution)/shard_map/attention/pallas_call | solution.py:284
  551.1 15.4 %input_grad.3 = (bf16[320,2048]{1,0:T(8,128)(2,1)}, bf16[320,2048]{1,0:T(8,128)(2,1)}, f32[2,2048]{1,0:T(2,128)}) custom-call(bf16[2560,768]{1,0:T(8,128)(2,1)} %bitcast.85, bf16[2560,768]{1,0:T(8,128)(2,1)} %bitcast.89, bf16[2560,2048]{1,0:T(8,128)(2,1)} %get-tuple-element.100.refs_2_.refs_5_, ...), custom_call_target="tpu_custom_call" | custom-call | flops 1000000 | bytes 1000000 | tf_op jit(solution)/shard_map/input_grad/pallas_call | solution.py:503
  579.2 26.6 %input_grad.4 = (bf16[320,2048]{1,0:T(8,128)(2,1)}, bf16[160,2048]{1,0:T(8,128)(2,1)}, bf16[160,2048]{1,0:T(8,128)(2,1)}, bf16[160,2048]{1,0:T(8,128)(2,1)}, bf1...) custom-call(bf16[2560,768]{1,0:T(8,128)(2,1)} %bitcast.86, bf16[2560,768]{1,0:T(8,128)(2,1)} %bitcast.90, ...), custom_call_target="tpu_custom_call" | custom-call | flops 1000000 | bytes 1000000 | tf_op jit(solution)/shard_map/input_grad/pallas_call | solution.py:503
  617.6 17.1 %pair_grad.3 = bf16[2048,1024]{1,0:T(8,128)(2,1)} custom-call(bf16[2560,2048]{1,0:T(8,128)(2,1)} %constant_dynamic-update-slice_fusion.x_ref.refs_6_.refs_9_.refs_10_, bf16[2560,2048]{1,0:T(8,128)(2,1)} %constant_dynamic-update-slice_fusion.5.y_ref, bf16[2560,768]{1,0:T(8,128)(2,1)} %bitcast.92, bf16[2560,256]{1,0:T(8,128)(2,1)} %bitcast.100), custom_call_target="tpu_custom_call" | custom-call | flops 1000000 | bytes 1000000 | tf_op jit(solution)/shard_map/pair_grad/pallas_call | solution.py:628
  634.7 15.4 %input_grad.5 = (bf16[640,2048]{1,0:T(8,128)(2,1)}, f32[2,2048]{1,0:T(2,128)}) custom-call(bf16[2560,768]{1,0:T(8,128)(2,1)} %bitcast.88, bf16[2560,768]{1,0:T(8,128)(2,1)} %bitcast.93, bf16[2560,2048]{1,0:T(8,128)(2,1)} %get-tuple-element.100.refs_2_.refs_5_, bf16[2048,2048]{1,0:T(8,128)(2,1)} %all-gather.8.cloned.1.call-done.refs_3_.refs_4_.refs_6_.refs_7_, ...), custom_call_target="tpu_custom_call" | custom-call | flops 99999997952 | bytes 1000000 | tf_op jit(solution)/shard_map/input_grad/pallas_call | solution.py:503
  656.4 10.9 %place_output.1 = bf16[640,2048]{1,0:T(8,128)(2,1)} custom-call(bf16[640,256]{1,0:T(8,128)(2,1)S(1)} %bitcast.63, bf16[640,256]{1,0:T(8,128)(2,1)S(1)} %bitcast.64, bf16[640,256]{1,0:T(8,128)(2,1)S(1)} %copy-done.9, bf16[640,256]{1,0:T(8,128)(2,1)S(1)} %copy-done.15, bf16[640,256]{1,0:T(8,128)(2,1)S(1)} %copy-done.11, bf16[640,256]{1,0:T(8,128)(2,1)S(1)} %copy-done.17, ...), custom_call_target="tpu_custom_call" | custom-call | flops 1000000 | bytes 1000000 | tf_op jit(solution)/shard_map/place_output/pallas_call | solution.py:555
  671.3 5.7 collective-permute-done.33
  682.5 4.4 collective-permute-done.34
  700.5 8.4 %token_grad.1 = bf16[640,2048]{1,0:T(8,128)(2,1)} custom-call(bf16[640,2048]{1,0:T(8,128)(2,1)} %bitcast.95, bf16[640,2048]{1,0:T(8,128)(2,1)} %bitcast.96, bf16[640,2048]{1,0:T(8,128)(2,1)} %get-tuple-element.101.own_ref, f32[1,2048]{1,0:T(1,128)S(1)} %bitcast.65, bf16[320,2048]{1,0:T(8,128)(2,1)S(1)} %collective-permute-done.26.refs_0_, ...), custom_call_target="tpu_custom_call" | custom-call | flops 1000000 | bytes 1000000 | tf_op jit(solution)/shard_map/token_grad/pallas_call | solution.py:599
  (283 shorter events, 164.2 us)
Async XLA Ops:
  7.2 123.9 %all-gather.4.cloned.1.call-start = ((), (), s32[]{:S(2)}) async-start(), calls=%async_computation.4 | async-start | bytes 9437184 | tf_op jit(solution)/shard_map/all_gather | solution.py:708
  7.9 175.4 %all-gather.6.cloned.1.call-start = ((), (), s32[]{:S(2)}) async-start(), calls=%async_computation.5 | async-start | bytes 9437184 | tf_op jit(solution)/shard_map/all_gather | solution.py:708
  14.9 59.9 %collective-permute-start = (bf16[640,2048]{1,0:T(8,128)(2,1)S(1)}, bf16[640,2048]{1,0:T(8,128)(2,1)}, u32[]{:S(2)}, u32[]{:S(2)}) collective-permute-start(bf16[640,2048]{1,0:T(8,128)(2,1)S(1)} %get-tuple-element.171), channel_id=1, source_target_pairs={{0,8},{8,24},{24,16},{16,0},{1,9},{9,25},{25,17},{17,1},{2,10},{10... | collective-permute-start | bytes 7864328 | tf_op jit(solution)/shard_map/ppermute | solution.py:346
  17.8 58.4 %collective-permute-start.1 = (bf16[640,2048]{1,0:T(8,128)(2,1)S(1)}, bf16[640,2048]{1,0:T(8,128)(2,1)}, u32[]{:S(2)}, u32[]{:S(2)}) collective-permute-start(bf16[640,2048]{1,0:T(8,128)(2,1)S(1)} %get-tuple-element.171), channel_id=1, source_target_pairs={{8,0},{24,8},{16,24},{0,16},{9,1},{25,9},{17,25},{1,17},{10,2},{26... | collective-permute-start | bytes 7864328 | tf_op jit(solution)/shard_map/ppermute | solution.py:347
  76.3 220.7 %all-gather.8.cloned.1.call-start = ((), (), s32[]{:S(2)}) async-start(), calls=%async_computation.6 | async-start | bytes 9437184 | tf_op jit(solution)/shard_map/all_gather | solution.py:708
  119.9 56.3 %collective-permute-start.4 = (bf16[640,2048]{1,0:T(8,128)(2,1)S(1)}, bf16[640,2048]{1,0:T(8,128)(2,1)}, u32[]{:S(2)}, u32[]{:S(2)}) collective-permute-start(bf16[640,2048]{1,0:T(8,128)(2,1)S(1)} %bitcast.97), channel_id=1, source_target_pairs={{0,8},{8,24},{24,16},{16,0},{1,9},{9,25},{25,17},{17,1},{2,10},{10... | collective-permute-start | bytes 7864328 | tf_op jit(solution)/shard_map/ppermute | solution.py:346
  120.5 59.0 %collective-permute-start.5 = (bf16[640,2048]{1,0:T(8,128)(2,1)S(1)}, bf16[640,2048]{1,0:T(8,128)(2,1)}, u32[]{:S(2)}, u32[]{:S(2)}) collective-permute-start(bf16[640,2048]{1,0:T(8,128)(2,1)S(1)} %bitcast.98), channel_id=1, source_target_pairs={{8,0},{24,8},{16,24},{0,16},{9,1},{25,9},{17,25},{1,17},{10,2},{26... | collective-permute-start | bytes 7864328 | tf_op jit(solution)/shard_map/ppermute | solution.py:347
  130.6 314.6 %reduce-scatter.5.cloned.1.call-start = ((), (), s32[]{:S(2)}) async-start(), calls=%async_computation.7 | async-start | bytes 9437184 | tf_op jit(solution)/shard_map/reduce_scatter | solution.py:711
  289.8 261.3 %reduce-scatter.7.cloned.1.call-start = ((), (), s32[]{:S(2)}) async-start(), calls=%async_computation.8 | async-start | bytes 9437184 | tf_op jit(solution)/shard_map/reduce_scatter | solution.py:711
  360.2 257.4 %reduce-scatter.9.cloned.1.call-start = ((), (), s32[]{:S(2)}) async-start(), calls=%async_computation.9 | async-start | bytes 4718592 | tf_op jit(solution)/shard_map/reduce_scatter | solution.py:711
  362.1 80.8 %collective-permute-start.14 = (bf16[2048,512]{1,0:T(8,128)(2,1)S(1)}, bf16[2048,512]{1,0:T(8,128)(2,1)S(1)}, u32[]{:S(2)}, u32[]{:S(2)}) collective-permute-start(bf16[2048,512]{1,0:T(8,128)(2,1)S(1)} %slice.162.refs_8_), channel_id=1, source_target_pairs={{0,8},{8,24},{24,16},{16,0},{1,9},{9,25},{25,17},{17,1},{2,10},{10... | collective-permute-start | bytes 6291464 | tf_op jit(solution)/shard_map/ppermute | solution.py:346
  363.4 81.8 %collective-permute-start.15 = (bf16[2048,512]{1,0:T(8,128)(2,1)S(1)}, bf16[2048,512]{1,0:T(8,128)(2,1)}, u32[]{:S(2)}, u32[]{:S(2)}) collective-permute-start(bf16[2048,512]{1,0:T(8,128)(2,1)S(1)} %slice.162.refs_8_), channel_id=1, source_target_pairs={{8,0},{24,8},{16,24},{0,16},{9,1},{25,9},{17,25},{1,17},{10,2},{26... | collective-permute-start | bytes 6291464 | tf_op jit(solution)/shard_map/ppermute | solution.py:347
  364.2 78.6 %collective-permute-start.12 = (bf16[320,2048]{1,0:T(8,128)(2,1)}, bf16[320,2048]{1,0:T(8,128)(2,1)S(1)}, u32[]{:S(2)}, u32[]{:S(2)}) collective-permute-start(bf16[320,2048]{1,0:T(8,128)(2,1)} %get-tuple-element.80), channel_id=1, source_target_pairs={{0,8},{8,24},{24,16},{16,0},{1,9},{9,25},{25,17},{17,1},{2,10},{10... | collective-permute-start | bytes 3932168 | tf_op jit(solution)/shard_map/ppermute | solution.py:388
  365.4 77.4 %collective-permute-start.13 = (bf16[320,2048]{1,0:T(8,128)(2,1)S(1)}, bf16[320,2048]{1,0:T(8,128)(2,1)S(1)}, u32[]{:S(2)}, u32[]{:S(2)}) collective-permute-start(bf16[320,2048]{1,0:T(8,128)(2,1)S(1)} %copy-done.30), channel_id=1, source_target_pairs={{8,0},{24,8},{16,24},{0,16},{9,1},{25,9},{17,25},{1,17},{10,2},{26... | collective-permute-start | bytes 3932168 | tf_op jit(solution)/shard_map/ppermute | solution.py:389
  462.1 249.6 %reduce-scatter.11.cloned.1.call-start = ((), (), s32[]{:S(2)}) async-start(), calls=%async_computation.10 | async-start | bytes 4718592 | tf_op jit(solution)/shard_map/reduce_scatter | solution.py:711
  463.6 85.5 %collective-permute-start.22 = (bf16[1024,512]{1,0:T(8,128)(2,1)S(1)}, bf16[1024,512]{1,0:T(8,128)(2,1)S(1)}, u32[]{:S(2)}, u32[]{:S(2)}) collective-permute-start(bf16[1024,512]{1,0:T(8,128)(2,1)S(1)} %slice.165), channel_id=1, source_target_pairs={{0,8},{8,24},{24,16},{16,0},{1,9},{9,25},{25,17},{17,1},{2,10},{10... | collective-permute-start | bytes 3145736 | tf_op jit(solution)/shard_map/ppermute | solution.py:352
  466.2 83.9 %collective-permute-start.23 = (bf16[1024,512]{1,0:T(8,128)(2,1)S(1)}, bf16[1024,512]{1,0:T(8,128)(2,1)S(1)}, u32[]{:S(2)}, u32[]{:S(2)}) collective-permute-start(bf16[1024,512]{1,0:T(8,128)(2,1)S(1)} %slice.166), channel_id=1, source_target_pairs={{8,0},{24,8},{16,24},{0,16},{9,1},{25,9},{17,25},{1,17},{10,2},{26... | collective-permute-start | bytes 3145736 | tf_op jit(solution)/shard_map/ppermute | solution.py:353
  467.1 79.7 %collective-permute-start.16 = (bf16[640,256]{1,0:T(8,128)(2,1)S(1)}, bf16[640,256]{1,0:T(8,128)(2,1)S(1)}, u32[]{:S(2)}, u32[]{:S(2)}) collective-permute-start(bf16[640,256]{1,0:T(8,128)(2,1)S(1)} %bitcast.114), channel_id=1, source_target_pairs={{0,8},{8,24},{24,16},{16,0},{1,9},{9,25},{25,17},{17,1},{2,10},{10... | collective-permute-start | bytes 983048 | tf_op jit(solution)/shard_map/ppermute | solution.py:409
  468.4 79.2 %collective-permute-start.18 = (bf16[640,256]{1,0:T(8,128)(2,1)S(1)}, bf16[640,256]{1,0:T(8,128)(2,1)S(1)}, u32[]{:S(2)}, u32[]{:S(2)}) collective-permute-start(bf16[640,256]{1,0:T(8,128)(2,1)S(1)} %bitcast.113), channel_id=1, source_target_pairs={{0,16},{8,0},{24,8},{16,24},{1,17},{9,1},{25,9},{17,25},{2,18},{10... | collective-permute-start | bytes 983048 | tf_op jit(solution)/shard_map/ppermute | solution.py:409
  469.2 79.2 %collective-permute-start.20 = (bf16[640,256]{1,0:T(8,128)(2,1)S(1)}, bf16[640,256]{1,0:T(8,128)(2,1)S(1)}, u32[]{:S(2)}, u32[]{:S(2)}) collective-permute-start(bf16[640,256]{1,0:T(8,128)(2,1)S(1)} %bitcast.112), channel_id=1, source_target_pairs={{0,24},{8,16},{24,0},{16,8},{1,25},{9,17},{25,1},{17,9},{2,26},{10... | collective-permute-start | bytes 983048 | tf_op jit(solution)/shard_map/ppermute | solution.py:409
  568.4 42.0 %collective-permute-start.25 = (bf16[320,2048]{1,0:T(8,128)(2,1)}, bf16[320,2048]{1,0:T(8,128)(2,1)}, u32[]{:S(2)}, u32[]{:S(2)}) collective-permute-start(bf16[320,2048]{1,0:T(8,128)(2,1)} %get-tuple-element.90), channel_id=1, source_target_pairs={{8,0},{24,8},{16,24},{0,16},{9,1},{25,9},{17,25},{1,17},{10,2},{26... | collective-permute-start | bytes 3932168 | tf_op jit(solution)/shard_map/ppermute | solution.py:374
  574.7 42.9 %collective-permute-start.21 = (bf16[640,256]{1,0:T(8,128)(2,1)}, bf16[640,256]{1,0:T(8,128)(2,1)}, u32[]{:S(2)}, u32[]{:S(2)}) collective-permute-start(bf16[640,256]{1,0:T(8,128)(2,1)} %bitcast.25), channel_id=1, source_target_pairs={{0,24},{8,16},{24,0},{16,8},{1,25},{9,17},{25,1},{17,9},{2,26},{10... | collective-permute-start | bytes 983048 | tf_op jit(solution)/shard_map/ppermute | solution.py:409
  605.8 61.5 %collective-permute-start.28 = (bf16[160,2048]{1,0:T(8,128)(2,1)}, bf16[160,2048]{1,0:T(8,128)(2,1)}, u32[]{:S(2)}, u32[]{:S(2)}) collective-permute-start(bf16[160,2048]{1,0:T(8,128)(2,1)} %get-tuple-element.93), channel_id=1, source_target_pairs={{0,8},{8,24},{24,16},{16,0},{1,9},{9,25},{25,17},{17,1},{2,10},{10... | collective-permute-start | bytes 1966088 | tf_op jit(solution)/shard_map/ppermute | solution.py:388
  610.4 56.9 %collective-permute-start.30 = (bf16[160,2048]{1,0:T(8,128)(2,1)}, bf16[160,2048]{1,0:T(8,128)(2,1)}, u32[]{:S(2)}, u32[]{:S(2)}) collective-permute-start(bf16[160,2048]{1,0:T(8,128)(2,1)} %get-tuple-element.95), channel_id=1, source_target_pairs={{8,0},{24,8},{16,24},{0,16},{9,1},{25,9},{17,25},{1,17},{10,2},{26... | collective-permute-start | bytes 1966088 | tf_op jit(solution)/shard_map/ppermute | solution.py:389
  (74 other events, 1021.2 us)
Sparse Core Ops, SparseCore 0:
  9.6 84.7 all-gather.3
  96.0 81.0 all-gather.5
  178.7 80.2 all-gather.7
  289.9 89.2 reduce-scatter.4
  381.4 87.9 reduce-scatter.6
  471.5 48.3 reduce-scatter.8
  634.8 53.6 reduce-scatter.10

commit v7 on v6

--- a/solution.py
+++ b/solution.py
@@ -31,7 +31,7 @@
 def attention_kernel(where_ref, *refs, chunk, chunks, full_chunks, blk, group, scale):
     per = chunk // blk
     qkv_in, g_in = refs[:per], refs[per : 2 * per]
-    cos_ref, up_ref, down_ref, att_hbm, grad_hbm = refs[2 * per : 2 * per + 5]
+    cos_ref, up_ref, down_ref, att_hbm, grad_hbm, sums_ref = refs[2 * per : 2 * per + 6]
     (
         keys,
         values,
@@ -49,7 +49,7 @@
         value_stage,
         row_sem,
         col_sem,
-    ) = refs[2 * per + 5 :]
+    ) = refs[2 * per + 6 :]
     i = pl.program_id(0)
     slot = lax.rem(i, 2)
     half = LANES // 2
@@ -231,7 +231,17 @@
             )
 
     sweep(back)
-    query_stage[slot] = turned(back_ref[...] * scale, tab, -1.0).astype(LOW)
+    query_grad = turned(back_ref[...] * scale, tab, -1.0)
+    query_stage[slot] = query_grad.astype(LOW)
+
+    def column_sums(x):
+        return jnp.sum(x.reshape(chunk // 8, 8, lanes), axis=0)
+
+    @pl.when(i == 0)
+    def _():
+        sums_ref[...] = jnp.zeros(sums_ref.shape, WIDE)
+
+    sums_ref[:, :lanes] += column_sums(query_grad)
     for copy in row_copies(1, slot):
         copy.start()
 
@@ -240,8 +250,11 @@
         @pl.loop(0, chunks)
         def _(n):
             rows = pl.ds(pl.multiple_of(n * chunk, chunk), chunk)
-            key_stage[rows] = turned(key_sum[rows], tables(rows), -1.0).astype(LOW)
+            key_grad = turned(key_sum[rows], tables(rows), -1.0)
+            key_stage[rows] = key_grad.astype(LOW)
             value_stage[rows] = value_sum[rows].astype(LOW)
+            sums_ref[:, lanes : 2 * lanes] += column_sums(key_grad)
+            sums_ref[:, 2 * lanes :] += column_sums(value_sum[rows])
             for r in range(per):
                 for copy in col_copies(n * per + r):
                     copy.start()
@@ -281,17 +294,19 @@
         group=group,
         scale=1.0 / math.sqrt(head_dim),
     )
-    attended, grads = pl.pallas_call(
+    attended, grads, sums = pl.pallas_call(
         kernel,
         out_shape=(
             jax.ShapeDtypeStruct((blocks, blk, lanes), LOW),
             jax.ShapeDtypeStruct((blocks, blk, 3 * lanes), LOW),
+            jax.ShapeDtypeStruct((8, 3 * lanes), WIDE),
         ),
         grid_spec=pltpu.PrefetchScalarGridSpec(
             num_scalar_prefetch=1,
             grid=(chunks,),
             in_specs=in_specs,
-            out_specs=[pl.BlockSpec(memory_space=pl.ANY)] * 2,
+            out_specs=[pl.BlockSpec(memory_space=pl.ANY)] * 2
+            + [pl.BlockSpec((8, 3 * lanes), lambda i, at: (0, 0))],
             scratch_shapes=[
                 pltpu.VMEM((rows, lanes), LOW),
                 pltpu.VMEM((rows, lanes), LOW),
@@ -317,7 +332,7 @@
         cost_estimate=LITTLE,
         name="attention",
     )(where, *operands)
-    return attended.reshape(rows, lanes), grads.reshape(rows, 3 * lanes)
+    return attended.reshape(rows, lanes), grads.reshape(rows, 3 * lanes), jnp.sum(sums, axis=0)
 
 
 def after(value, *others):
@@ -410,11 +425,13 @@
     return got
 
 
-def sum_everywhere(values, axes):
+def sum_everywhere(values, axes, gate=()):
     for axis in axes:
         count, span = lax.axis_size(axis), 1
         while span < count:
             pairs = [(n, n ^ span) for n in range(count)]
+            if axis == axes[-1] and 2 * span >= count:
+                values = after(values, *gate)
             values = values + lax.ppermute(values, axis, pairs)
             span *= 2
     return values
@@ -463,7 +480,7 @@
             transcendentals=rows * hidden,
         ),
         name="expand",
-    )(x, w, b.astype(WIDE)[None])
+    )(x, w, b[None])
 
 
 def input_grad_kernel(*refs, terms, ranks):
@@ -562,7 +579,7 @@
         out_specs=by_column(rows),
         scratch_shapes=[pltpu.VMEM((rows, cols), WIDE)],
         compiler_params=pltpu.CompilerParams(
-            dimension_semantics=("arbitrary",), vmem_limit_bytes=48 << 20
+            dimension_semantics=("arbitrary",), vmem_limit_bytes=58 << 20
         ),
         cost_estimate=LITTLE,
         name="place_output",
@@ -645,15 +662,19 @@
 
 
 def rope_tables(rows):
-    place = jnp.arange(rows, dtype=jnp.int32)
+    place = lax.broadcasted_iota(jnp.int32, (rows, LANES), 0)
+    lane = lax.broadcasted_iota(jnp.int32, (rows, LANES), 1)
     pos = jnp.where(place < PROMPT, place, PROMPT + (place - PROMPT) % CLEN)
     half = ROT // 2
     freq = 10000.0 ** (-2.0 * jnp.arange(half, dtype=WIDE) / ROT)
-    angle = pos.astype(WIDE)[:, None] * freq[None, :]
+    angle = pos.astype(WIDE) * jnp.tile(freq, LANES // half)[None, :]
+    dim = lane % (LANES // 2)
     cosine, sine = jnp.cos(angle), jnp.sin(angle)
-    zero, one = jnp.zeros_like(cosine), jnp.ones_like(cosine)
-    tabs = ((cosine, cosine, one, one), (zero, sine, zero, zero), (-sine, zero, zero, zero))
-    return [jnp.concatenate(tab * (LANES // (4 * half)), axis=1) for tab in tabs]
+    return [
+        jnp.where(dim < ROT, cosine, 1.0),
+        jnp.where((dim >= half) & (dim < ROT), sine, 0.0),
+        jnp.where(dim < half, -sine, 0.0),
+    ]
 
 
 def shards(
@@ -717,19 +738,18 @@
         cut = values.reshape(-1, 3, groups, lanes)
         return jnp.swapaxes(cut, 1, 2).reshape(-1, 3 * each)
 
+    tabs = rope_tables(rows)
+    own_grad_sum = jnp.sum(own_grad.astype(WIDE), axis=0)
+    fc1_bias = lax.dynamic_slice_in_dim(b_fc1, me * hidden, hidden, 0).astype(WIDE)
+    early = (where, own_grad_sum, fc1_bias, *tabs)
     normed_pieces = ring_pieces(normed_own, "ctx")
-    normed = jnp.concatenate(normed_pieces, axis=0)
+    normed = after(jnp.concatenate(normed_pieces, axis=0), *early)
     attention_shard = jnp.concatenate([by_group(w_qkv), w_dense.T], axis=1)
     fc1_weight = gather_rows(w_fc1)
     fc2_turned = gather_rows(after(w_fc2.T, *normed_pieces[1:-2]))
     attention_weight = gather_rows(after(attention_shard, *normed_pieces[-2:]))
     qkv_weight, dense_turned = attention_weight[:, : 3 * each], attention_weight[:, 3 * each :]
 
-    tabs = rope_tables(rows)
-    own_grad_sum = jnp.sum(own_grad.astype(WIDE), axis=0)
-    normed = after(normed, where, own_grad_sum, *tabs)
-
-    fc1_bias = lax.dynamic_slice_in_dim(b_fc1, me * hidden, hidden, 0)
     qkv_bias = lax.dynamic_slice_in_dim(b_qkv.reshape(3, width), me * each, each, 1)
     activated, slope = expand(normed, fc1_weight, fc1_bias)
 
@@ -753,14 +773,15 @@
 
     dense_pieces = ring_pieces(after(dense_turned, *second), "ctx")
 
-    attended, qkv_grads, d_attention, swapped = [], [], [], []
+    attended, qkv_grads, qkv_sums, d_attention, swapped = [], [], [], [], []
     ordered = (d_fc1_part,)
     for which in range(groups):
-        got, got_grads = attention(
+        got, got_grads, got_sums = attention(
             after(qkv, *ordered), attended_grad, where, tabs, lanes, which, head_dim
         )
         attended.append(got)
         qkv_grads.append(got_grads)
+        qkv_sums.append(got_sums)
         if which < groups - 1:
             swapped.append(ring_exchange(lambda rank, got=got: of_rank(got, rank), "ctx"))
             gated = after(normed, d_fc2, *last, *dense_pieces[1:-2]) if which == 0 else normed
@@ -813,16 +834,16 @@
         groups,
     )
     sums = after(far_sums + middle_sums + own_sums, output, *covers[1])
-    d_tokens = token_grad(tokens[0], own_grad, own_part[0], gain, grad_terms, local_rows // 4)
 
     d_qkv = jnp.concatenate(
         [part[:, : 3 * lanes].reshape(-1, 3, lanes) for part in d_attention], axis=2
     ).astype(WIDE)
     d_dense = jnp.concatenate([part[:, 3 * lanes :].T for part in d_attention], axis=0)
+    d_dense = d_dense.astype(WIDE)
     d_fc1, d_fc2 = d_fc1.astype(WIDE), d_fc2.T.astype(WIDE)
 
     qkv_bias_part = jnp.concatenate(
-        [jnp.sum(part.astype(WIDE), axis=0).reshape(3, lanes) for part in qkv_grads], axis=1
+        [part.reshape(3, lanes) for part in qkv_sums], axis=1
     )
     fc1_bias_part = jnp.sum(expanded_grad.astype(WIDE), axis=0)
     qkv_bias_wide = lax.dynamic_update_slice_in_dim(
@@ -842,7 +863,12 @@
         ),
         ("fsdp",),
     )
-    small = sum_everywhere(after(small, d_fc1, d_fc2, *covers[2]), ("ctx",))
+    small = after(small, d_fc1, d_fc2)
+    d_tokens = token_grad(
+        after(tokens[0], small), own_grad, own_part[0], gain, grad_terms, local_rows // 4
+    )
+    small = sum_everywhere(small, ("ctx",), gate=(d_tokens,))
+    small = after(small, d_qkv, d_dense)
     d_shift, with_normed, d_b_qkv, d_b_out, d_b_fc1 = jnp.split(
         small, [width, 2 * width, 5 * width, 6 * width]
     )
@@ -854,7 +880,7 @@
         d_shift,
         d_qkv,
         d_b_qkv,
-        d_dense.astype(WIDE),
+        d_dense,
         d_b_out,
         d_fc1,
         d_b_fc1,

time: 733 us -> 722 us (0.985)
  local copies, waits for them, and re-layouts: 92.5 us -> 56.7 us
  waiting for transfers between devices: 79.5 us -> 107 us
  other arithmetic: 44.9 us -> 32.5 us
  starting transfers between devices: 43.3 us -> 53 us
    unnamed x122 -> x88, local copies, waits for them, and re-layouts: 47.3 us -> 32.7 us
    ppermute x3, waiting for transfers between devices: 0.01 us -> 13.4 us  [ring_pieces(): lax.ppermute(from_behind[:half], axis, ahead)]
    concatenate x4 -> x1, local copies, waits for them, and re-layouts: 13.4 us -> 1.19 us  [shards(): normed = after(jnp.concatenate(normed_pieces, axis=0), *early)]
    ppermute x3, starting transfers between devices: 2.51 us -> 14 us  [ring_pieces(): lax.ppermute(from_ahead[half:], axis, behind)]
    select_n x0 -> x1, other arithmetic: none -> 7.67 us  [rope_tables(): jnp.where(dim < half, -sine, 0.0)]
  transfers between devices with their start and end apart: 44 -> 44, of which waited for: 9 -> 14; matrix products, arithmetic and copies ran while one was open for 36% -> 31% of each run, Pallas kernels for 42% -> 43%
where the time goes in v7:
time: 722 us; the launch traced here: 717 us
  Pallas kernels  307 us (43%)
  matrix products  147 us (20%)
  waiting for transfers between devices  107 us (15%)
  local copies, waits for them, and re-layouts  56.7 us (8%)
  starting transfers between devices  53 us (7%)
  other arithmetic  32.5 us (5%)
  between operations  15 us (2%)
    pallas_call x2, Pallas kernels, attention(): pl.pallas_call(kernel, out_shape=(jax.ShapeDtypeStruct((blocks, blk, lane...  154 us
    dot_general x6, matrix products, dot(): return lax.dot_general(left, right, dims, preferred_element_type=WIDE)  147 us
    ppermute x3, waiting for transfers between devices, ring_pieces(): from_behind = lax.ppermute(from_behind, axis, ahead)  66.3 us
    pallas_call x3, Pallas kernels, input_grad(): pl.pallas_call(functools.partial(input_grad_kernel, terms=len(grads), ran...  57.4 us
    pallas_call x1, Pallas kernels, expand(): pl.pallas_call(functools.partial(expand_kernel, cols=min(512, hidden)), o...  38.7 us
    pallas_call x2, Pallas kernels, pair_grad(): pl.pallas_call(pair_grad_kernel, out_shape=jax.ShapeDtypeStruct((width, c...  34.6 us
    unnamed x88, local copies, waits for them, and re-layouts  32.7 us
  transfers between devices with their start and end apart: 44, of which 14 were waited for; matrix products, arithmetic and copies ran while one was open for 31% of the time, Pallas kernels for 43%

profile of v7, /device:TPU:0, one launch (start us, length us, event | category | flops | bytes accessed | tf_op | source)
XLA Modules:
  0.0 717.4 jit_solution(4178456991126060536)
XLA Ops:
  17.9 57.0 %collective-permute-done = bf16[640,2048]{1,0:T(8,128)(2,1)} collective-permute-done((bf16[640,2048]{1,0:T(8,128)(2,1)S(1)}, bf16[640,2048]{1,0:T(8,128)(2,1)}, u32[]{:S(2)}, u32[]{:S(2)}) %collective-permute-start) | collective-permute-done | bytes 2621472 | tf_op jit(solution)/shard_map/ppermute | solution.py:361
  88.3 7.7 %negate_select_fusion = (f32[2560,128]{1,0:T(8,128)}, f32[2560,128]{1,0:T(8,128)}, f32[2560,128]{1,0:T(8,128)}) fusion(f32[128]{0:T(128)S(1)} %mul.108, s32[2560]{0:T(1024)S(1)} %get-tuple-element.190, s32[2560]{0:T(1024)S(1)} %get-tuple-element.191, s32[128]{0:T(128)S(1)} %get-tuple-element.194, s32[128]{0:T(128)S(1)} %get-tuple-element.195, ...), kind=kLoop, calls=%fused_computation.27 | loop fusion | flops 4587520 | bytes 3959424 | tf_op jit(solution)/shard_map/jit(_where)/select_n | solution.py:676
  99.6 13.4 %collective-permute-done.2 = bf16[320,2048]{1,0:T(8,128)(2,1)S(1)} collective-permute-done((bf16[320,2048]{1,0:T(8,128)(2,1)S(1)}, bf16[320,2048]{1,0:T(8,128)(2,1)S(1)}, u32[]{:S(2)}, u32[]{:S(2)}) %collective-permute-start.2) | collective-permute-done | bytes 1310752 | tf_op jit(solution)/shard_map/ppermute | solution.py:367
  124.0 38.7 %expand.1 = (bf16[2560,2048]{1,0:T(8,128)(2,1)}, bf16[2560,2048]{1,0:T(8,128)(2,1)}) custom-call(bf16[2560,2048]{1,0:T(8,128)(2,1)} %constant_dynamic-update-slice_fusion.x_ref.refs_6_.refs_9_.refs_10_, bf16[2048,2048]{1,0:T(8,128)(2,1)} %all-gather.4.cloned.1.call-done.w_ref.refs_5_.refs_8_, f32[1,2048]{1,0:T(1,128)S(1)} %bitcast.64), custom_call_target="tpu_custom_call" | custom-call | flops 21474836480 | bytes 39845888 | tf_op jit(solution)/shard_map/expand/pallas_call | solution.py:464
  162.7 9.4 %collective-permute-done.4 = bf16[640,2048]{1,0:T(8,128)(2,1)} collective-permute-done((bf16[640,2048]{1,0:T(8,128)(2,1)S(1)}, bf16[640,2048]{1,0:T(8,128)(2,1)}, u32[]{:S(2)}, u32[]{:S(2)}) %collective-permute-start.4) | collective-permute-done | bytes 2621472 | tf_op jit(solution)/shard_map/ppermute | solution.py:361
  178.0 12.6 %collective-permute-start.7 = (bf16[320,2048]{1,0:T(8,128)(2,1)}, bf16[320,2048]{1,0:T(8,128)(2,1)}, u32[]{:S(2)}, u32[]{:S(2)}) collective-permute-start(bf16[320,2048]{1,0:T(8,128)(2,1)} %slice.114), channel_id=1, source_target_pairs={{8,0},{24,8},{16,24},{0,16},{9,1},{25,9},{17,25},{1,17},{10,2},{26... | collective-permute-start | bytes 3932168 | tf_op jit(solution)/shard_map/ppermute | solution.py:368
  190.6 26.6 %convolution_convert_fusion.refs_15_ = bf16[2560,2048]{1,0:T(8,128)(2,1)S(1)} fusion(bf16[2560,2048]{1,0:T(8,128)(2,1)} %get-tuple-element.67, bf16[2048,2048]{0,1:T(8,128)(2,1)} %all-gather.6.cloned.1.call-done), kind=kOutput, calls=%fused_computation.3 | convolution fusion | flops 21480079360 | bytes 29360128 | tf_op jit(solution)/shard_map/dot_general | solution.py:28
  219.1 5.6 constant_dynamic-update-slice_fusion.8
  237.4 29.6 %convert_reduce_fusion = (f32[2048]{0:T(1024)}, bf16[2560,2048]{1,0:T(8,128)(2,1)}) fusion(bf16[2560,2048]{1,0:T(8,128)(2,1)} %get-tuple-element.77, bf16[2560,2048]{1,0:T(8,128)(2,1)} %constant_dynamic-update-slice_fusion.5.y_ref, bf16[2048,2048]{0,1:T(8,128)(2,1)} %all-gather.6.cloned.1.call-done), kind=kOutput, calls=%fused_computation | convolution fusion | flops 21501048832 | bytes 39854080 | tf_op jit(solution)/shard_map/dot_general | solution.py:28
  267.1 28.8 %convolution_convert_fusion.2 = bf16[2048,2048]{1,0:T(8,128)(2,1)} fusion(bf16[2560,2048]{1,0:T(8,128)(2,1)} %constant_dynamic-update-slice_fusion.5.y_ref, bf16[2560,2048]{1,0:T(8,128)(2,1)} %get-tuple-element.67), kind=kOutput, calls=%fused_computation.5 | convolution fusion | flops 21479030784 | bytes 29360128 | tf_op jit(solution)/shard_map/dot_general | solution.py:28
  296.7 4.2 add_convert_fusion.3
  303.3 22.3 %add_convert_fusion = bf16[2560,1536]{1,0:T(8,128)(2,1)} fusion(bf16[2560,2048]{1,0:T(8,128)(2,1)} %constant_dynamic-update-slice_fusion.x_ref.refs_6_.refs_9_.refs_10_, f32[1536]{0:T(1024)S(1)} %reshape.234, bf16[2048,2048]{1,0:T(8,128)(2,1)} %all-gather.8.cloned.1.call-done.refs_3_.refs_4_.refs_6_.refs_7_), kind=kOutput, calls=%fused_computation.2 | convolution fusion | flops 16113991680 | bytes 24647680 | tf_op jit(solution)/shard_map/dot_general | solution.py:28
  328.7 10.5 %convolution_convert_fusion.3 = bf16[2560,512]{1,0:T(8,128)(2,1)} fusion(bf16[2560,2048]{1,0:T(8,128)(2,1)} %constant_dynamic-update-slice_fusion.5.y_ref, bf16[2048,2048]{1,0:T(8,128)(2,1)} %all-gather.8.cloned.1.call-done.refs_3_.refs_4_.refs_6_.refs_7_), kind=kOutput, calls=%fused_computation.16 | convolution fusion | flops 5370019840 | bytes 15204352 | tf_op jit(solution)/shard_map/dot_general | solution.py:28
  339.2 29.0 %convolution_convert_fusion.1 = bf16[2048,2048]{1,0:T(8,128)(2,1)} fusion(bf16[2560,2048]{1,0:T(8,128)(2,1)} %constant_dynamic-update-slice_fusion.x_ref.refs_6_.refs_9_.refs_10_, bf16[2560,2048]{1,0:T(8,128)(2,1)} %get-tuple-element.105.refs_2_.refs_5_), kind=kOutput, calls=%fused_computation.4 | convolution fusion | flops 21479030784 | bytes 29360128 | tf_op jit(solution)/shard_map/dot_general | solution.py:28
  374.4 77.1 %attention.2 = (bf16[40,64,256]{2,1,0:T(8,128)(2,1)}, bf16[40,64,768]{2,1,0:T(8,128)(2,1)}, f32[8,768]{1,0:T(8,128)}) custom-call(s32[40]{0:T(128)} %select_reduce_fusion.where_ref, bf16[40,64,1536]{2,1,0:T(8,128)(2,1)} %bitcast.65, bf16[40,64,1536]{2,1,0:T(8,128)(2,1)} %bitcast.66, bf16[40,64,1536]{2,1,0:T(8,128)(2,1)} %bitcast.67, ...), custom_call_target="tpu_custom_call" | custom-call | flops 1000000 | bytes 1000000 | tf_op jit(solution)/shard_map/attention/pallas_call | solution.py:297
  453.1 17.6 %pair_grad.2 = bf16[2048,1024]{1,0:T(8,128)(2,1)} custom-call(bf16[2560,2048]{1,0:T(8,128)(2,1)} %constant_dynamic-update-slice_fusion.x_ref.refs_6_.refs_9_.refs_10_, bf16[2560,2048]{1,0:T(8,128)(2,1)} %constant_dynamic-update-slice_fusion.5.y_ref, bf16[2560,768]{1,0:T(8,128)(2,1)} %bitcast.83, bf16[2560,256]{1,0:T(8,128)(2,1)} %bitcast.98), custom_call_target="tpu_custom_call" | custom-call | flops 1000000 | bytes 1000000 | tf_op jit(solution)/shard_map/pair_grad/pallas_call | solution.py:645
  478.3 77.1 %attention.3 = (bf16[40,64,256]{2,1,0:T(8,128)(2,1)}, bf16[40,64,768]{2,1,0:T(8,128)(2,1)}, f32[8,768]{1,0:T(8,128)}) custom-call(s32[40]{0:T(128)} %select_reduce_fusion.where_ref, bf16[40,64,1536]{2,1,0:T(8,128)(2,1)} %bitcast.69, bf16[40,64,1536]{2,1,0:T(8,128)(2,1)} %bitcast.70, bf16[40,64,1536]{2,1,0:T(8,128)(2,1)} %bitcast.71, ...), custom_call_target="tpu_custom_call" | custom-call | flops 1000000 | bytes 1000000 | tf_op jit(solution)/shard_map/attention/pallas_call | solution.py:297
  556.4 15.6 %input_grad.3 = (bf16[320,2048]{1,0:T(8,128)(2,1)}, bf16[320,2048]{1,0:T(8,128)(2,1)}, f32[2,2048]{1,0:T(2,128)}) custom-call(bf16[2560,768]{1,0:T(8,128)(2,1)} %bitcast.84, bf16[2560,768]{1,0:T(8,128)(2,1)} %bitcast.88, bf16[2560,2048]{1,0:T(8,128)(2,1)} %get-tuple-element.105.refs_2_.refs_5_, ...), custom_call_target="tpu_custom_call" | custom-call | flops 1000000 | bytes 1000000 | tf_op jit(solution)/shard_map/input_grad/pallas_call | solution.py:520
  579.8 26.6 %input_grad.4 = (bf16[320,2048]{1,0:T(8,128)(2,1)}, bf16[160,2048]{1,0:T(8,128)(2,1)}, bf16[160,2048]{1,0:T(8,128)(2,1)}, bf16[160,2048]{1,0:T(8,128)(2,1)}, bf1...) custom-call(bf16[2560,768]{1,0:T(8,128)(2,1)} %bitcast.85, bf16[2560,768]{1,0:T(8,128)(2,1)} %bitcast.89, ...), custom_call_target="tpu_custom_call" | custom-call | flops 1000000 | bytes 1000000 | tf_op jit(solution)/shard_map/input_grad/pallas_call | solution.py:520
  619.0 17.0 %pair_grad.3 = bf16[2048,1024]{1,0:T(8,128)(2,1)} custom-call(bf16[2560,2048]{1,0:T(8,128)(2,1)} %constant_dynamic-update-slice_fusion.x_ref.refs_6_.refs_9_.refs_10_, bf16[2560,2048]{1,0:T(8,128)(2,1)} %constant_dynamic-update-slice_fusion.5.y_ref, bf16[2560,768]{1,0:T(8,128)(2,1)} %bitcast.91, bf16[2560,256]{1,0:T(8,128)(2,1)} %bitcast.97), custom_call_target="tpu_custom_call" | custom-call | flops 1000000 | bytes 1000000 | tf_op jit(solution)/shard_map/pair_grad/pallas_call | solution.py:645
  636.1 15.3 %input_grad.5 = (bf16[640,2048]{1,0:T(8,128)(2,1)}, f32[2,2048]{1,0:T(2,128)}) custom-call(bf16[2560,768]{1,0:T(8,128)(2,1)} %bitcast.87, bf16[2560,768]{1,0:T(8,128)(2,1)} %bitcast.92, bf16[2560,2048]{1,0:T(8,128)(2,1)} %get-tuple-element.105.refs_2_.refs_5_, bf16[2048,2048]{1,0:T(8,128)(2,1)} %all-gather.8.cloned.1.call-done.refs_3_.refs_4_.refs_6_.refs_7_, ...), custom_call_target="tpu_custom_call" | custom-call | flops 99999997952 | bytes 1000000 | tf_op jit(solution)/shard_map/input_grad/pallas_call | solution.py:520
  652.4 13.1 %place_output.1 = bf16[640,2048]{1,0:T(8,128)(2,1)} custom-call(bf16[640,256]{1,0:T(8,128)(2,1)} %bitcast.105, bf16[640,256]{1,0:T(8,128)(2,1)} %bitcast.106, bf16[640,256]{1,0:T(8,128)(2,1)} %copy-done.19, bf16[640,256]{1,0:T(8,128)(2,1)} %collective-permute-done.17.refs_3_, bf16[640,256]{1,0:T(8,128)(2,1)} %copy-done.20, ...), custom_call_target="tpu_custom_call" | custom-call | flops 1000000 | bytes 1000000 | tf_op jit(solution)/shard_map/place_output/pallas_call | solution.py:572
  679.4 5.9 collective-permute-done.32
  689.7 8.7 %token_grad.1 = bf16[640,2048]{1,0:T(8,128)(2,1)} custom-call(bf16[640,2048]{1,0:T(8,128)(2,1)} %bitcast.82, bf16[640,2048]{1,0:T(8,128)(2,1)} %bitcast.93, bf16[640,2048]{1,0:T(8,128)(2,1)} %get-tuple-element.106.own_ref, f32[1,2048]{1,0:T(1,128)S(1)} %bitcast.63, bf16[320,2048]{1,0:T(8,128)(2,1)S(1)} %collective-permute-done.26.refs_0_, ...), custom_call_target="tpu_custom_call" | custom-call | flops 1000000 | bytes 1000000 | tf_op jit(solution)/shard_map/token_grad/pallas_call | solution.py:616
  (247 shorter events, 133.1 us)
Async XLA Ops:
  7.2 116.8 %all-gather.4.cloned.1.call-start = ((), (), s32[]{:S(2)}) async-start(), calls=%async_computation.4 | async-start | bytes 9437184 | tf_op jit(solution)/shard_map/all_gather | solution.py:729
  7.9 182.7 %all-gather.6.cloned.1.call-start = ((), (), s32[]{:S(2)}) async-start(), calls=%async_computation.5 | async-start | bytes 9437184 | tf_op jit(solution)/shard_map/all_gather | solution.py:729
  14.9 59.9 %collective-permute-start = (bf16[640,2048]{1,0:T(8,128)(2,1)S(1)}, bf16[640,2048]{1,0:T(8,128)(2,1)}, u32[]{:S(2)}, u32[]{:S(2)}) collective-permute-start(bf16[640,2048]{1,0:T(8,128)(2,1)S(1)} %get-tuple-element.169), channel_id=1, source_target_pairs={{0,8},{8,24},{24,16},{16,0},{1,9},{9,25},{25,17},{17,1},{2,10},{10... | collective-permute-start | bytes 7864328 | tf_op jit(solution)/shard_map/ppermute | solution.py:361
  17.8 58.4 %collective-permute-start.1 = (bf16[640,2048]{1,0:T(8,128)(2,1)S(1)}, bf16[640,2048]{1,0:T(8,128)(2,1)}, u32[]{:S(2)}, u32[]{:S(2)}) collective-permute-start(bf16[640,2048]{1,0:T(8,128)(2,1)S(1)} %get-tuple-element.169), channel_id=1, source_target_pairs={{8,0},{24,8},{16,24},{0,16},{9,1},{25,9},{17,25},{1,17},{10,2},{26... | collective-permute-start | bytes 7864328 | tf_op jit(solution)/shard_map/ppermute | solution.py:362
  76.3 227.0 %all-gather.8.cloned.1.call-start = ((), (), s32[]{:S(2)}) async-start(), calls=%async_computation.6 | async-start | bytes 9437184 | tf_op jit(solution)/shard_map/all_gather | solution.py:729
  115.7 56.4 %collective-permute-start.4 = (bf16[640,2048]{1,0:T(8,128)(2,1)S(1)}, bf16[640,2048]{1,0:T(8,128)(2,1)}, u32[]{:S(2)}, u32[]{:S(2)}) collective-permute-start(bf16[640,2048]{1,0:T(8,128)(2,1)S(1)} %bitcast.94), channel_id=1, source_target_pairs={{0,8},{8,24},{24,16},{16,0},{1,9},{9,25},{25,17},{17,1},{2,10},{10... | collective-permute-start | bytes 7864328 | tf_op jit(solution)/shard_map/ppermute | solution.py:361
  116.3 59.0 %collective-permute-start.5 = (bf16[640,2048]{1,0:T(8,128)(2,1)S(1)}, bf16[640,2048]{1,0:T(8,128)(2,1)}, u32[]{:S(2)}, u32[]{:S(2)}) collective-permute-start(bf16[640,2048]{1,0:T(8,128)(2,1)S(1)} %bitcast.95), channel_id=1, source_target_pairs={{8,0},{24,8},{16,24},{0,16},{9,1},{25,9},{17,25},{1,17},{10,2},{26... | collective-permute-start | bytes 7864328 | tf_op jit(solution)/shard_map/ppermute | solution.py:362
  123.9 329.2 %reduce-scatter.5.cloned.1.call-start = ((), (), s32[]{:S(2)}) async-start(), calls=%async_computation.7 | async-start | bytes 9437184 | tf_op jit(solution)/shard_map/reduce_scatter | solution.py:732
  174.6 42.7 %collective-permute-start.6 = (bf16[320,2048]{1,0:T(8,128)(2,1)}, bf16[320,2048]{1,0:T(8,128)(2,1)}, u32[]{:S(2)}, u32[]{:S(2)}) collective-permute-start(bf16[320,2048]{1,0:T(8,128)(2,1)} %slice.113), channel_id=1, source_target_pairs={{0,8},{8,24},{24,16},{16,0},{1,9},{9,25},{25,17},{17,1},{2,10},{10... | collective-permute-start | bytes 3932168 | tf_op jit(solution)/shard_map/ppermute | solution.py:367
  296.0 260.4 %reduce-scatter.7.cloned.1.call-start = ((), (), s32[]{:S(2)}) async-start(), calls=%async_computation.8 | async-start | bytes 9437184 | tf_op jit(solution)/shard_map/reduce_scatter | solution.py:732
  368.3 250.8 %reduce-scatter.9.cloned.1.call-start = ((), (), s32[]{:S(2)}) async-start(), calls=%async_computation.9 | async-start | bytes 4718592 | tf_op jit(solution)/shard_map/reduce_scatter | solution.py:732
  370.2 81.5 %collective-permute-start.14 = (bf16[2048,512]{1,0:T(8,128)(2,1)S(1)}, bf16[2048,512]{1,0:T(8,128)(2,1)S(1)}, u32[]{:S(2)}, u32[]{:S(2)}) collective-permute-start(bf16[2048,512]{1,0:T(8,128)(2,1)S(1)} %slice.162.refs_8_), channel_id=1, source_target_pairs={{0,8},{8,24},{24,16},{16,0},{1,9},{9,25},{25,17},{17,1},{2,10},{10... | collective-permute-start | bytes 6291464 | tf_op jit(solution)/shard_map/ppermute | solution.py:361
  371.4 81.7 %collective-permute-start.15 = (bf16[2048,512]{1,0:T(8,128)(2,1)S(1)}, bf16[2048,512]{1,0:T(8,128)(2,1)}, u32[]{:S(2)}, u32[]{:S(2)}) collective-permute-start(bf16[2048,512]{1,0:T(8,128)(2,1)S(1)} %slice.162.refs_8_), channel_id=1, source_target_pairs={{8,0},{24,8},{16,24},{0,16},{9,1},{25,9},{17,25},{1,17},{10,2},{26... | collective-permute-start | bytes 6291464 | tf_op jit(solution)/shard_map/ppermute | solution.py:362
  372.2 79.3 %collective-permute-start.12 = (bf16[320,2048]{1,0:T(8,128)(2,1)}, bf16[320,2048]{1,0:T(8,128)(2,1)S(1)}, u32[]{:S(2)}, u32[]{:S(2)}) collective-permute-start(bf16[320,2048]{1,0:T(8,128)(2,1)} %get-tuple-element.85), channel_id=1, source_target_pairs={{0,8},{8,24},{24,16},{16,0},{1,9},{9,25},{25,17},{17,1},{2,10},{10... | collective-permute-start | bytes 3932168 | tf_op jit(solution)/shard_map/ppermute | solution.py:403
  373.4 78.2 %collective-permute-start.13 = (bf16[320,2048]{1,0:T(8,128)(2,1)S(1)}, bf16[320,2048]{1,0:T(8,128)(2,1)S(1)}, u32[]{:S(2)}, u32[]{:S(2)}) collective-permute-start(bf16[320,2048]{1,0:T(8,128)(2,1)S(1)} %copy-done.13), channel_id=1, source_target_pairs={{8,0},{24,8},{16,24},{0,16},{9,1},{25,9},{17,25},{1,17},{10,2},{26... | collective-permute-start | bytes 3932168 | tf_op jit(solution)/shard_map/ppermute | solution.py:404
  470.7 232.2 %reduce-scatter.11.cloned.1.call-start = ((), (), s32[]{:S(2)}) async-start(), calls=%async_computation.10 | async-start | bytes 4718592 | tf_op jit(solution)/shard_map/reduce_scatter | solution.py:732
  470.9 84.6 %collective-permute-start.22 = (bf16[1024,512]{1,0:T(8,128)(2,1)S(1)}, bf16[1024,512]{1,0:T(8,128)(2,1)}, u32[]{:S(2)}, u32[]{:S(2)}) collective-permute-start(bf16[1024,512]{1,0:T(8,128)(2,1)S(1)} %slice.165), channel_id=1, source_target_pairs={{0,8},{8,24},{24,16},{16,0},{1,9},{9,25},{25,17},{17,1},{2,10},{10... | collective-permute-start | bytes 3145736 | tf_op jit(solution)/shard_map/ppermute | solution.py:367
  473.4 82.9 %collective-permute-start.23 = (bf16[1024,512]{1,0:T(8,128)(2,1)S(1)}, bf16[1024,512]{1,0:T(8,128)(2,1)}, u32[]{:S(2)}, u32[]{:S(2)}) collective-permute-start(bf16[1024,512]{1,0:T(8,128)(2,1)S(1)} %slice.166), channel_id=1, source_target_pairs={{8,0},{24,8},{16,24},{0,16},{9,1},{25,9},{17,25},{1,17},{10,2},{26... | collective-permute-start | bytes 3145736 | tf_op jit(solution)/shard_map/ppermute | solution.py:368
  475.1 80.2 %collective-permute-start.16 = (bf16[640,256]{1,0:T(8,128)(2,1)S(1)}, bf16[640,256]{1,0:T(8,128)(2,1)S(1)}, u32[]{:S(2)}, u32[]{:S(2)}) collective-permute-start(bf16[640,256]{1,0:T(8,128)(2,1)S(1)} %bitcast.113), channel_id=1, source_target_pairs={{0,8},{8,24},{24,16},{16,0},{1,9},{9,25},{25,17},{17,1},{2,10},{10... | collective-permute-start | bytes 983048 | tf_op jit(solution)/shard_map/ppermute | solution.py:424
  476.3 79.1 %collective-permute-start.18 = (bf16[640,256]{1,0:T(8,128)(2,1)S(1)}, bf16[640,256]{1,0:T(8,128)(2,1)S(1)}, u32[]{:S(2)}, u32[]{:S(2)}) collective-permute-start(bf16[640,256]{1,0:T(8,128)(2,1)S(1)} %bitcast.112), channel_id=1, source_target_pairs={{0,16},{8,0},{24,8},{16,24},{1,17},{9,1},{25,9},{17,25},{2,18},{10... | collective-permute-start | bytes 983048 | tf_op jit(solution)/shard_map/ppermute | solution.py:424
  477.1 78.3 %collective-permute-start.20 = (bf16[640,256]{1,0:T(8,128)(2,1)S(1)}, bf16[640,256]{1,0:T(8,128)(2,1)S(1)}, u32[]{:S(2)}, u32[]{:S(2)}) collective-permute-start(bf16[640,256]{1,0:T(8,128)(2,1)S(1)} %bitcast.111), channel_id=1, source_target_pairs={{0,24},{8,16},{24,0},{16,8},{1,25},{9,17},{25,1},{17,9},{2,26},{10... | collective-permute-start | bytes 983048 | tf_op jit(solution)/shard_map/ppermute | solution.py:424
  577.9 41.1 %collective-permute-start.21 = (bf16[640,256]{1,0:T(8,128)(2,1)}, bf16[640,256]{1,0:T(8,128)(2,1)}, u32[]{:S(2)}, u32[]{:S(2)}) collective-permute-start(bf16[640,256]{1,0:T(8,128)(2,1)} %bitcast.25), channel_id=1, source_target_pairs={{0,24},{8,16},{24,0},{16,8},{1,25},{9,17},{25,1},{17,9},{2,26},{10... | collective-permute-start | bytes 983048 | tf_op jit(solution)/shard_map/ppermute | solution.py:424
  606.4 59.2 %collective-permute-start.28 = (bf16[160,2048]{1,0:T(8,128)(2,1)}, bf16[160,2048]{1,0:T(8,128)(2,1)S(1)}, u32[]{:S(2)}, u32[]{:S(2)}) collective-permute-start(bf16[160,2048]{1,0:T(8,128)(2,1)} %get-tuple-element.98), channel_id=1, source_target_pairs={{0,8},{8,24},{24,16},{16,0},{1,9},{9,25},{25,17},{17,1},{2,10},{10... | collective-permute-start | bytes 1966088 | tf_op jit(solution)/shard_map/ppermute | solution.py:403
  611.0 54.6 %collective-permute-start.29 = (bf16[160,2048]{1,0:T(8,128)(2,1)}, bf16[160,2048]{1,0:T(8,128)(2,1)}, u32[]{:S(2)}, u32[]{:S(2)}) collective-permute-start(bf16[160,2048]{1,0:T(8,128)(2,1)} %get-tuple-element.100), channel_id=1, source_target_pairs={{8,0},{24,8},{16,24},{0,16},{9,1},{25,9},{17,25},{1,17},{10,2},{26... | collective-permute-start | bytes 1966088 | tf_op jit(solution)/shard_map/ppermute | solution.py:404
  (57 other events, 973.3 us)
Sparse Core Ops, SparseCore 0:
  9.6 84.7 all-gather.3
  96.0 81.0 all-gather.5
  178.7 80.2 all-gather.7
  296.1 89.2 reduce-scatter.4
  387.5 87.9 reduce-scatter.6
  477.7 48.5 reduce-scatter.8
  636.2 53.0 reduce-scatter.10

commit v8 on v7

--- a/solution.py
+++ b/solution.py
@@ -425,13 +425,13 @@
     return got
 
 
-def sum_everywhere(values, axes, gate=()):
+def sum_everywhere(values, axes, gates=()):
+    gates = list(gates)
     for axis in axes:
         count, span = lax.axis_size(axis), 1
         while span < count:
             pairs = [(n, n ^ span) for n in range(count)]
-            if axis == axes[-1] and 2 * span >= count:
-                values = after(values, *gate)
+            values = after(values, *(gates.pop(0) if gates else ()))
             values = values + lax.ppermute(values, axis, pairs)
             span *= 2
     return values
@@ -481,6 +481,71 @@
         ),
         name="expand",
     )(x, w, b[None])
+
+
+def slope_grad_kernel(*refs, spans, cols):
+    pieces = refs[: len(spans)]
+    w_ref, slope_ref, out_ref, whole_ref, sums_ref = refs[len(spans) :]
+    i = pl.program_id(0)
+    for (first, span), piece in zip(spans, pieces):
+
+        @pl.when((i >= first) & (i < first + span))
+        def _(piece=piece):
+            whole_ref[...] = piece[...]
+
+    @pl.when(i == 0)
+    def _():
+        sums_ref[...] = jnp.zeros(sums_ref.shape, WIDE)
+
+    x = whole_ref[...]
+    for n in range(w_ref.shape[1] // cols):
+        at = slice(n * cols, (n + 1) * cols)
+        value = dot(x, w_ref[:, at], NN) * slope_ref[:, at].astype(WIDE)
+        out_ref[:, at] = value.astype(LOW)
+        sums_ref[:, at] += jnp.sum(value.reshape(value.shape[0] // 8, 8, cols), axis=0)
+
+
+def slope_grad(pieces, w, slope):
+    width, hidden = w.shape
+    tile = pieces[-1].shape[0]
+    spans, first = [], 0
+    for piece in pieces:
+        spans.append((first, piece.shape[0] // tile))
+        first += piece.shape[0] // tile
+    by_row = pl.BlockSpec((tile, hidden), lambda i: (i, 0))
+
+    def piece_spec(first, span):
+        return pl.BlockSpec((tile, width), lambda i: (jnp.clip(i - first, 0, span - 1), 0))
+
+    grad, whole, sums = pl.pallas_call(
+        functools.partial(slope_grad_kernel, spans=tuple(spans), cols=min(512, hidden)),
+        out_shape=(
+            jax.ShapeDtypeStruct((first * tile, hidden), LOW),
+            jax.ShapeDtypeStruct((first * tile, width), LOW),
+            jax.ShapeDtypeStruct((8, hidden), WIDE),
+        ),
+        grid=(first,),
+        in_specs=[piece_spec(*span) for span in spans]
+        + [
+            pl.BlockSpec((width, hidden), lambda i: (0, 0), pipeline_mode=pl.Buffered(1)),
+            by_row,
+        ],
+        out_specs=[
+            by_row,
+            pl.BlockSpec((tile, width), lambda i: (i, 0)),
+            pl.BlockSpec((8, hidden), lambda i: (0, 0)),
+        ],
+        compiler_params=pltpu.CompilerParams(
+            dimension_semantics=("arbitrary",), vmem_limit_bytes=48 << 20
+        ),
+        cost_estimate=pl.CostEstimate(
+            flops=2 * first * tile * width * hidden,
+            bytes_accessed=2 * first * tile * (2 * width + 2 * hidden),
+            transcendentals=0,
+        ),
+        name="slope_grad",
+    )(*pieces, w, slope)
+    return grad, whole, jnp.sum(sums, axis=0)
 
 
 def input_grad_kernel(*refs, terms, ranks):
@@ -756,12 +821,11 @@
     sent_grad = after(own_grad, *normed_pieces[-2:])
     grad_pieces = ring_pieces(sent_grad, "ctx", gate=(activated,))
     ff_part = dot(activated, fc2_turned, NT).astype(LOW)
-    grads = jnp.concatenate([after(piece, ff_part) for piece in grad_pieces], axis=0)
     ff_terms, ff_hops = ring_reduce(lambda rank: of_rank(ff_part, rank), "ctx", chained=True)
     first, second, last = ff_hops[0], ff_hops[min(1, len(ff_hops) - 1)], ff_hops[-1]
 
-    gated = after(grads, ff_part)
-    expanded_grad = (dot(gated, fc2_turned, NN) * slope.astype(WIDE)).astype(LOW)
+    gated = [after(piece, ff_part) for piece in grad_pieces]
+    expanded_grad, grads, fc1_bias_part = slope_grad(gated, fc2_turned, slope)
     d_fc2_part = dot(after(grads, expanded_grad, *first), activated, TN).astype(LOW)
     d_fc2 = scatter_rows(d_fc2_part)
     qkv = dot(after(normed, d_fc2_part), qkv_weight, NN)
@@ -796,7 +860,7 @@
     half = local_rows // 2
     whole, far_cut, ahead_cut, behind_cut = [local_rows], [half, half], [half], [half]
     if count > 2:
-        ahead_cut, behind_cut = [half, half // 2, half // 2], [half // 2, half // 2, half]
+        ahead_cut, behind_cut = [half, half], [half, half]
     cut_of = {0: whole, count - 2: ahead_cut, count - 3: behind_cut, count - 1: far_cut}
 
     def some_ranks(ranks, turn, cost=LITTLE):
@@ -816,8 +880,8 @@
         if len(pieces) == 1:
             parts[rank] = pieces[0]
 
-    grad_terms, hops = ring_reduce(lambda rank: parts[rank], "ctx", cuts=2)
-    covers = hops[1:] if len(hops) == 4 else [()] * 3
+    grad_terms, hops = ring_reduce(lambda rank: parts[rank], "ctx")
+    last_hops = [piece for hop in hops[1:3] for piece in hop]
     gated = after(normed, turn, *hops[0], *swapped[-1], *d_attention)
     d_part = pair_grad(gated, grads, qkv_grads[-1], attended[-1])
     d_attention.append(scatter_rows(d_part))
@@ -826,14 +890,14 @@
     output = place_output(
         attended_own,
         dense_pieces,
-        after(tokens[0], *own_part, *covers[0]),
+        after(tokens[0], *own_part),
         (b_dense.astype(WIDE) + b_fc2.astype(WIDE))[None],
         ff_part,
         ff_terms,
         count,
         groups,
     )
-    sums = after(far_sums + middle_sums + own_sums, output, *covers[1])
+    sums = after(far_sums + middle_sums + own_sums, output, *last_hops)
 
     d_qkv = jnp.concatenate(
         [part[:, : 3 * lanes].reshape(-1, 3, lanes) for part in d_attention], axis=2
@@ -845,14 +909,13 @@
     qkv_bias_part = jnp.concatenate(
         [part.reshape(3, lanes) for part in qkv_sums], axis=1
     )
-    fc1_bias_part = jnp.sum(expanded_grad.astype(WIDE), axis=0)
     qkv_bias_wide = lax.dynamic_update_slice_in_dim(
         jnp.zeros((3, width), WIDE), qkv_bias_part, me * each, 1
     ).reshape(-1)
     fc1_bias_wide = lax.dynamic_update_slice_in_dim(
         jnp.zeros((b_fc1.shape[0],), WIDE), fc1_bias_part, me * hidden, 0
     )
-    small = sum_everywhere(
+    small = (
         jnp.concatenate(
             [
                 sums.reshape(-1),
@@ -860,15 +923,13 @@
                 own_grad_sum,
                 fc1_bias_wide,
             ]
-        ),
-        ("fsdp",),
-    )
-    small = after(small, d_fc1, d_fc2)
+        )
+    )
     d_tokens = token_grad(
         after(tokens[0], small), own_grad, own_part[0], gain, grad_terms, local_rows // 4
     )
-    small = sum_everywhere(small, ("ctx",), gate=(d_tokens,))
-    small = after(small, d_qkv, d_dense)
+    gates = [(), (d_tokens,), (d_fc1, d_fc2), (), (d_qkv, d_dense)]
+    small = sum_everywhere(small, ("fsdp", "ctx"), gates)
     d_shift, with_normed, d_b_qkv, d_b_out, d_b_fc1 = jnp.split(
         small, [width, 2 * width, 5 * width, 6 * width]
     )

time: 722 us -> 718 us (level)
  Pallas kernels: 307 us -> 338 us
  matrix products: 147 us -> 117 us
  starting transfers between devices: 53 us -> 39.2 us
    ppermute x3, waiting for transfers between devices: 66.3 us -> 2.06 us  [ring_pieces(): from_behind = lax.ppermute(from_behind, axis, ahead)]
    ppermute x3, waiting for transfers between devices: 1.44 us -> 63.3 us  [ring_pieces(): from_ahead = lax.ppermute(from_ahead, axis, behind)]
    pallas_call x0 -> x1, Pallas kernels: none -> 30.9 us  [slope_grad(): pl.pallas_call(functools.partial(slope_grad_kernel, spans=tuple(spans), c...]
    dot_general x6 -> x5, matrix products: 147 us -> 117 us  [dot(): return lax.dot_general(left, right, dims, preferred_element_type=WIDE)]
    ppermute x3, waiting for transfers between devices: 2.75 us -> 19.4 us  [ring_pieces(): lax.ppermute(from_ahead[half:], axis, behind)]
    ppermute x3, starting transfers between devices: 14 us -> 3.88 us  [ring_pieces(): lax.ppermute(from_ahead[half:], axis, behind)]
    ppermute x3, waiting for transfers between devices: 13.4 us -> 3.74 us  [ring_pieces(): lax.ppermute(from_behind[:half], axis, ahead)]
    unnamed x88 -> x99, local copies, waits for them, and re-layouts: 32.7 us -> 27.1 us
  transfers between devices with their start and end apart: 44 -> 42, of which waited for: 14 -> 12; matrix products, arithmetic and copies ran while one was open for 31% -> 27% of each run, Pallas kernels for 43% -> 48%
where the time goes in v8:
time: 718 us; the launch traced here: 710 us
  Pallas kernels  338 us (47%)
  matrix products  117 us (16%)
  waiting for transfers between devices  109 us (15%)
  local copies, waits for them, and re-layouts  51.7 us (7%)
  starting transfers between devices  39.2 us (5%)
  other arithmetic  38.6 us (5%)
  between operations  15.1 us (2%)
    pallas_call x2, Pallas kernels, attention(): pl.pallas_call(kernel, out_shape=(jax.ShapeDtypeStruct((blocks, blk, lane...  154 us
    dot_general x5, matrix products, dot(): return lax.dot_general(left, right, dims, preferred_element_type=WIDE)  117 us
    ppermute x3, waiting for transfers between devices, ring_pieces(): from_ahead = lax.ppermute(from_ahead, axis, behind)  63.3 us
    pallas_call x3, Pallas kernels, input_grad(): pl.pallas_call(functools.partial(input_grad_kernel, terms=len(grads), ran...  57.3 us
    pallas_call x1, Pallas kernels, expand(): pl.pallas_call(functools.partial(expand_kernel, cols=min(512, hidden)), o...  38.8 us
    pallas_call x2, Pallas kernels, pair_grad(): pl.pallas_call(pair_grad_kernel, out_shape=jax.ShapeDtypeStruct((width, c...  34.5 us
    pallas_call x1, Pallas kernels, slope_grad(): pl.pallas_call(functools.partial(slope_grad_kernel, spans=tuple(spans), c...  30.9 us
    unnamed x99, local copies, waits for them, and re-layouts  27.1 us
  transfers between devices with their start and end apart: 42, of which 12 were waited for; matrix products, arithmetic and copies ran while one was open for 27% of the time, Pallas kernels for 48%

profile of v8, /device:TPU:0, one launch (start us, length us, event | category | flops | bytes accessed | tf_op | source)
XLA Modules:
  0.0 709.6 jit_solution(15623866709601002517)
XLA Ops:
  21.1 54.7 %collective-permute-done.1 = bf16[640,2048]{1,0:T(8,128)(2,1)S(1)} collective-permute-done((bf16[640,2048]{1,0:T(8,128)(2,1)}, bf16[640,2048]{1,0:T(8,128)(2,1)S(1)}, u32[]{:S(2)}, u32[]{:S(2)}) %collective-permute-start.1) | collective-permute-done | bytes 2621472 | tf_op jit(solution)/shard_map/ppermute | solution.py:362
  88.8 19.4 %collective-permute-done.3 = bf16[320,2048]{1,0:T(8,128)(2,1)} collective-permute-done((bf16[320,2048]{1,0:T(8,128)(2,1)}, bf16[320,2048]{1,0:T(8,128)(2,1)}, u32[]{:S(2)}, u32[]{:S(2)}) %collective-permute-start.3) | collective-permute-done | bytes 1310752 | tf_op jit(solution)/shard_map/ppermute | solution.py:368
  115.9 7.9 %negate_select_fusion = (f32[2560,128]{1,0:T(8,128)}, f32[2560,128]{1,0:T(8,128)}, f32[2560,128]{1,0:T(8,128)}) fusion(f32[128]{0:T(128)S(1)} %mul.105, s32[2560]{0:T(1024)S(1)} %get-tuple-element.188, s32[2560]{0:T(1024)S(1)} %get-tuple-element.189, s32[128]{0:T(128)S(1)} %get-tuple-element.192, s32[128]{0:T(128)S(1)} %get-tuple-element.193, ...), kind=kLoop, calls=%fused_computation.25 | loop fusion | flops 4587520 | bytes 3959424 | tf_op jit(solution)/shard_map/jit(_where)/select_n | solution.py:741
  136.4 38.8 %expand.1 = (bf16[2560,2048]{1,0:T(8,128)(2,1)}, bf16[2560,2048]{1,0:T(8,128)(2,1)}) custom-call(bf16[2560,2048]{1,0:T(8,128)(2,1)} %constant_dynamic-update-slice_fusion.x_ref.refs_6_.refs_9_.refs_10_, bf16[2048,2048]{1,0:T(8,128)(2,1)} %all-gather.4.cloned.1.call-done.w_ref.refs_5_.refs_8_, f32[1,2048]{1,0:T(1,128)S(1)} %bitcast.66), custom_call_target="tpu_custom_call" | custom-call | flops 21474836480 | bytes 39845888 | tf_op jit(solution)/shard_map/expand/pallas_call | solution.py:464
  175.2 8.6 %collective-permute-done.5.refs_2_ = bf16[640,2048]{1,0:T(8,128)(2,1)} collective-permute-done((bf16[640,2048]{1,0:T(8,128)(2,1)S(1)}, bf16[640,2048]{1,0:T(8,128)(2,1)}, u32[]{:S(2)}, u32[]{:S(2)}) %collective-permute-start.5) | collective-permute-done | bytes 2621472 | tf_op jit(solution)/shard_map/ppermute | solution.py:362
  191.7 26.7 %convolution_convert_fusion.refs_15_ = bf16[2560,2048]{1,0:T(8,128)(2,1)S(1)} fusion(bf16[2560,2048]{1,0:T(8,128)(2,1)} %get-tuple-element.67, bf16[2048,2048]{1,0:T(8,128)(2,1)} %all-gather.6.cloned.1.call-done.refs_5_), kind=kOutput, calls=%fused_computation.1 | convolution fusion | flops 21480079360 | bytes 29360128 | tf_op jit(solution)/shard_map/dot_general | solution.py:28
  225.3 30.9 %slope_grad.1 = (bf16[2560,2048]{1,0:T(8,128)(2,1)}, bf16[2560,2048]{1,0:T(8,128)(2,1)}, f32[8,2048]{1,0:T(8,128)S(1)}) custom-call(bf16[640,2048]{1,0:T(8,128)(2,1)S(1)} %bitcast.64, bf16[640,2048]{1,0:T(8,128)(2,1)} %collective-permute-done.4.refs_1_, bf16[640,2048]{1,0:T(8,128)(2,1)} %collective-permute-done.5.refs_2_, ...), custom_call_target="tpu_custom_call" | custom-call | flops 21474836480 | bytes 41943040 | tf_op jit(solution)/shard_map/slope_grad/pallas_call | solution.py:520
  258.3 28.8 %convolution_convert_fusion.2 = bf16[2048,2048]{1,0:T(8,128)(2,1)} fusion(bf16[2560,2048]{1,0:T(8,128)(2,1)} %get-tuple-element.82.y_ref, bf16[2560,2048]{1,0:T(8,128)(2,1)} %get-tuple-element.67), kind=kOutput, calls=%fused_computation.3 | convolution fusion | flops 21479030784 | bytes 29360128 | tf_op jit(solution)/shard_map/dot_general | solution.py:28
  288.9 4.2 add_convert_fusion.3
  295.5 22.3 %add_convert_fusion = bf16[2560,1536]{1,0:T(8,128)(2,1)} fusion(bf16[2560,2048]{1,0:T(8,128)(2,1)} %constant_dynamic-update-slice_fusion.x_ref.refs_6_.refs_9_.refs_10_, f32[1536]{0:T(1024)S(1)} %reshape.234, bf16[2048,2048]{1,0:T(8,128)(2,1)} %all-gather.8.cloned.1.call-done.refs_3_.refs_4_.refs_6_.refs_7_), kind=kOutput, calls=%fused_computation | convolution fusion | flops 16113991680 | bytes 24647680 | tf_op jit(solution)/shard_map/dot_general | solution.py:28
  320.7 10.5 %convolution_convert_fusion.3 = bf16[2560,512]{1,0:T(8,128)(2,1)} fusion(bf16[2560,2048]{1,0:T(8,128)(2,1)} %get-tuple-element.82.y_ref, bf16[2048,2048]{1,0:T(8,128)(2,1)} %all-gather.8.cloned.1.call-done.refs_3_.refs_4_.refs_6_.refs_7_), kind=kOutput, calls=%fused_computation.14 | convolution fusion | flops 5370019840 | bytes 15204352 | tf_op jit(solution)/shard_map/dot_general | solution.py:28
  331.2 29.1 %convolution_convert_fusion.1 = bf16[2048,2048]{1,0:T(8,128)(2,1)} fusion(bf16[2560,2048]{1,0:T(8,128)(2,1)} %constant_dynamic-update-slice_fusion.x_ref.refs_6_.refs_9_.refs_10_, bf16[2560,2048]{1,0:T(8,128)(2,1)} %get-tuple-element.104.refs_2_.refs_5_), kind=kOutput, calls=%fused_computation.2 | convolution fusion | flops 21479030784 | bytes 29360128 | tf_op jit(solution)/shard_map/dot_general | solution.py:28
  366.5 77.2 %attention.2 = (bf16[40,64,256]{2,1,0:T(8,128)(2,1)}, bf16[40,64,768]{2,1,0:T(8,128)(2,1)}, f32[8,768]{1,0:T(8,128)}) custom-call(s32[40]{0:T(128)} %select_reduce_fusion.where_ref, bf16[40,64,1536]{2,1,0:T(8,128)(2,1)} %bitcast.67, bf16[40,64,1536]{2,1,0:T(8,128)(2,1)} %bitcast.68, bf16[40,64,1536]{2,1,0:T(8,128)(2,1)} %bitcast.69, ...), custom_call_target="tpu_custom_call" | custom-call | flops 1000000 | bytes 1000000 | tf_op jit(solution)/shard_map/attention/pallas_call | solution.py:297
  444.9 17.6 %pair_grad.2 = bf16[2048,1024]{1,0:T(8,128)(2,1)} custom-call(bf16[2560,2048]{1,0:T(8,128)(2,1)} %constant_dynamic-update-slice_fusion.x_ref.refs_6_.refs_9_.refs_10_, bf16[2560,2048]{1,0:T(8,128)(2,1)} %get-tuple-element.82.y_ref, bf16[2560,768]{1,0:T(8,128)(2,1)} %bitcast.85, bf16[2560,256]{1,0:T(8,128)(2,1)} %bitcast.96), custom_call_target="tpu_custom_call" | custom-call | flops 1000000 | bytes 1000000 | tf_op jit(solution)/shard_map/pair_grad/pallas_call | solution.py:710
  470.2 77.3 %attention.3 = (bf16[40,64,256]{2,1,0:T(8,128)(2,1)}, bf16[40,64,768]{2,1,0:T(8,128)(2,1)}, f32[8,768]{1,0:T(8,128)}) custom-call(s32[40]{0:T(128)} %select_reduce_fusion.where_ref, bf16[40,64,1536]{2,1,0:T(8,128)(2,1)} %bitcast.71, bf16[40,64,1536]{2,1,0:T(8,128)(2,1)} %bitcast.72, bf16[40,64,1536]{2,1,0:T(8,128)(2,1)} %bitcast.73, ...), custom_call_target="tpu_custom_call" | custom-call | flops 1000000 | bytes 1000000 | tf_op jit(solution)/shard_map/attention/pallas_call | solution.py:297
  548.6 15.6 %input_grad.3 = (bf16[320,2048]{1,0:T(8,128)(2,1)}, bf16[320,2048]{1,0:T(8,128)(2,1)}, f32[2,2048]{1,0:T(2,128)}) custom-call(bf16[2560,768]{1,0:T(8,128)(2,1)} %bitcast.86, bf16[2560,768]{1,0:T(8,128)(2,1)} %bitcast.90, bf16[2560,2048]{1,0:T(8,128)(2,1)} %get-tuple-element.104.refs_2_.refs_5_, ...), custom_call_target="tpu_custom_call" | custom-call | flops 1000000 | bytes 1000000 | tf_op jit(solution)/shard_map/input_grad/pallas_call | solution.py:585
  571.8 26.4 %input_grad.4 = (bf16[320,2048]{1,0:T(8,128)(2,1)}, bf16[320,2048]{1,0:T(8,128)(2,1)}, bf16[320,2048]{1,0:T(8,128)(2,1)}, bf16[320,2048]{1,0:T(8,128)(2,1)}, f32[2,2048]{1,0:T(2,128)}) custom-call(bf16[2560,768]{1,0:T(8,128)(2,1)} %bitcast.87, bf16[2560,768]{1,0:T(8,128)(2,1)} %bitcast.91, bf16[2560,2048]{1,0:T(8,128)(2,1)} %get-tuple-element.104.refs_2_.refs_5_, ...), custom_call_target="tpu_custom_call" | custom-call | flops 1000000 | bytes 1000000 | tf_op jit(solution)/shard_map/input_grad/pallas_call | solution.py:585
  609.1 16.9 %pair_grad.3 = bf16[2048,1024]{1,0:T(8,128)(2,1)} custom-call(bf16[2560,2048]{1,0:T(8,128)(2,1)} %constant_dynamic-update-slice_fusion.x_ref.refs_6_.refs_9_.refs_10_, bf16[2560,2048]{1,0:T(8,128)(2,1)} %get-tuple-element.82.y_ref, bf16[2560,768]{1,0:T(8,128)(2,1)} %bitcast.93, bf16[2560,256]{1,0:T(8,128)(2,1)} %bitcast.95), custom_call_target="tpu_custom_call" | custom-call | flops 1000000 | bytes 1000000 | tf_op jit(solution)/shard_map/pair_grad/pallas_call | solution.py:710
  626.0 15.3 %input_grad.5 = (bf16[640,2048]{1,0:T(8,128)(2,1)}, f32[2,2048]{1,0:T(2,128)}) custom-call(bf16[2560,768]{1,0:T(8,128)(2,1)} %bitcast.89, bf16[2560,768]{1,0:T(8,128)(2,1)} %bitcast.94, bf16[2560,2048]{1,0:T(8,128)(2,1)} %get-tuple-element.104.refs_2_.refs_5_, bf16[2048,2048]{1,0:T(8,128)(2,1)} %all-gather.8.cloned.1.call-done.refs_3_.refs_4_.refs_6_.refs_7_, ...), custom_call_target="tpu_custom_call" | custom-call | flops 99999997952 | bytes 1000000 | tf_op jit(solution)/shard_map/input_grad/pallas_call | solution.py:585
  641.4 13.1 %place_output.1 = bf16[640,2048]{1,0:T(8,128)(2,1)} custom-call(bf16[640,256]{1,0:T(8,128)(2,1)} %bitcast.104, bf16[640,256]{1,0:T(8,128)(2,1)} %bitcast.105, bf16[640,256]{1,0:T(8,128)(2,1)} %copy-done.27, bf16[640,256]{1,0:T(8,128)(2,1)} %collective-permute-done.17.refs_3_, bf16[640,256]{1,0:T(8,128)(2,1)} %copy-done.25, bf16[640,256]{1,0:T(8,128)(2,1)} %copy-done.28, ...), custom_call_target="tpu_custom_call" | custom-call | flops 1000000 | bytes 1000000 | tf_op jit(solution)/shard_map/place_output/pallas_call | solution.py:637
  654.5 3.8 collective-permute-done.27.refs_3_
  658.4 9.0 %token_grad.1 = bf16[640,2048]{1,0:T(8,128)(2,1)} custom-call(bf16[640,2048]{1,0:T(8,128)(2,1)} %bitcast.84, bf16[640,2048]{1,0:T(8,128)(2,1)} %bitcast.61, bf16[640,2048]{1,0:T(8,128)(2,1)} %get-tuple-element.105.own_ref, f32[1,2048]{1,0:T(1,128)S(1)} %bitcast.65, bf16[320,2048]{1,0:T(8,128)(2,1)} %collective-permute-done.26.refs_0_, ...), custom_call_target="tpu_custom_call" | custom-call | flops 1000000 | bytes 1000000 | tf_op jit(solution)/shard_map/token_grad/pallas_call | solution.py:681
  670.7 4.3 collective-permute-done.31
  676.7 5.3 collective-permute-done.32
  (255 shorter events, 130.7 us)
Async XLA Ops:
  7.2 129.2 %all-gather.4.cloned.1.call-start = ((), (), s32[]{:S(2)}) async-start(), calls=%async_computation.4 | async-start | bytes 9437184 | tf_op jit(solution)/shard_map/all_gather | solution.py:794
  7.9 183.8 %all-gather.6.cloned.1.call-start = ((), (), s32[]{:S(2)}) async-start(), calls=%async_computation.5 | async-start | bytes 9437184 | tf_op jit(solution)/shard_map/all_gather | solution.py:794
  15.8 60.0 %collective-permute-start.1 = (bf16[640,2048]{1,0:T(8,128)(2,1)}, bf16[640,2048]{1,0:T(8,128)(2,1)S(1)}, u32[]{:S(2)}, u32[]{:S(2)}) collective-permute-start(bf16[640,2048]{1,0:T(8,128)(2,1)} %get-tuple-element.169), channel_id=1, source_target_pairs={{8,0},{24,8},{16,24},{0,16},{9,1},{25,9},{17,25},{1,17},{10,2},{26... | collective-permute-start | bytes 7864328 | tf_op jit(solution)/shard_map/ppermute | solution.py:362
  18.7 58.6 %collective-permute-start = (bf16[640,2048]{1,0:T(8,128)(2,1)}, bf16[640,2048]{1,0:T(8,128)(2,1)}, u32[]{:S(2)}, u32[]{:S(2)}) collective-permute-start(bf16[640,2048]{1,0:T(8,128)(2,1)} %get-tuple-element.169), channel_id=1, source_target_pairs={{0,8},{8,24},{24,16},{16,0},{1,9},{9,25},{25,17},{17,1},{2,10},{10... | collective-permute-start | bytes 7864328 | tf_op jit(solution)/shard_map/ppermute | solution.py:361
  77.4 218.1 %all-gather.8.cloned.1.call-start = ((), (), s32[]{:S(2)}) async-start(), calls=%async_computation.6 | async-start | bytes 9437184 | tf_op jit(solution)/shard_map/all_gather | solution.py:794
  112.0 332.9 %reduce-scatter.5.cloned.1.call-start = ((), (), s32[]{:S(2)}) async-start(), calls=%async_computation.7 | async-start | bytes 9437184 | tf_op jit(solution)/shard_map/reduce_scatter | solution.py:797
  127.5 56.3 %collective-permute-start.5 = (bf16[640,2048]{1,0:T(8,128)(2,1)S(1)}, bf16[640,2048]{1,0:T(8,128)(2,1)}, u32[]{:S(2)}, u32[]{:S(2)}) collective-permute-start(bf16[640,2048]{1,0:T(8,128)(2,1)S(1)} %bitcast.62), channel_id=1, source_target_pairs={{8,0},{24,8},{16,24},{0,16},{9,1},{25,9},{17,25},{1,17},{10,2},{26... | collective-permute-start | bytes 7864328 | tf_op jit(solution)/shard_map/ppermute | solution.py:362
  128.1 56.2 %collective-permute-start.4 = (bf16[640,2048]{1,0:T(8,128)(2,1)S(1)}, bf16[640,2048]{1,0:T(8,128)(2,1)}, u32[]{:S(2)}, u32[]{:S(2)}) collective-permute-start(bf16[640,2048]{1,0:T(8,128)(2,1)S(1)} %bitcast.63), channel_id=1, source_target_pairs={{0,8},{8,24},{24,16},{16,0},{1,9},{9,25},{25,17},{17,1},{2,10},{10... | collective-permute-start | bytes 7864328 | tf_op jit(solution)/shard_map/ppermute | solution.py:361
  287.2 261.3 %reduce-scatter.7.cloned.1.call-start = ((), (), s32[]{:S(2)}) async-start(), calls=%async_computation.8 | async-start | bytes 9437184 | tf_op jit(solution)/shard_map/reduce_scatter | solution.py:797
  360.3 248.8 %reduce-scatter.9.cloned.1.call-start = ((), (), s32[]{:S(2)}) async-start(), calls=%async_computation.9 | async-start | bytes 4718592 | tf_op jit(solution)/shard_map/reduce_scatter | solution.py:797
  362.2 81.5 %collective-permute-start.15 = (bf16[2048,512]{1,0:T(8,128)(2,1)S(1)}, bf16[2048,512]{1,0:T(8,128)(2,1)S(1)}, u32[]{:S(2)}, u32[]{:S(2)}) collective-permute-start(bf16[2048,512]{1,0:T(8,128)(2,1)S(1)} %slice.162.refs_8_), channel_id=1, source_target_pairs={{8,0},{24,8},{16,24},{0,16},{9,1},{25,9},{17,25},{1,17},{10,2},{26... | collective-permute-start | bytes 6291464 | tf_op jit(solution)/shard_map/ppermute | solution.py:362
  363.3 81.6 %collective-permute-start.14 = (bf16[2048,512]{1,0:T(8,128)(2,1)S(1)}, bf16[2048,512]{1,0:T(8,128)(2,1)}, u32[]{:S(2)}, u32[]{:S(2)}) collective-permute-start(bf16[2048,512]{1,0:T(8,128)(2,1)S(1)} %slice.162.refs_8_), channel_id=1, source_target_pairs={{0,8},{8,24},{24,16},{16,0},{1,9},{9,25},{25,17},{17,1},{2,10},{10... | collective-permute-start | bytes 6291464 | tf_op jit(solution)/shard_map/ppermute | solution.py:361
  364.3 79.4 %collective-permute-start.12 = (bf16[320,2048]{1,0:T(8,128)(2,1)}, bf16[320,2048]{1,0:T(8,128)(2,1)S(1)}, u32[]{:S(2)}, u32[]{:S(2)}) collective-permute-start(bf16[320,2048]{1,0:T(8,128)(2,1)} %get-tuple-element.86), channel_id=1, source_target_pairs={{0,8},{8,24},{24,16},{16,0},{1,9},{9,25},{25,17},{17,1},{2,10},{10... | collective-permute-start | bytes 3932168 | tf_op jit(solution)/shard_map/ppermute | solution.py:403
  364.9 78.9 %collective-permute-start.13 = (bf16[320,2048]{1,0:T(8,128)(2,1)S(1)}, bf16[320,2048]{1,0:T(8,128)(2,1)S(1)}, u32[]{:S(2)}, u32[]{:S(2)}) collective-permute-start(bf16[320,2048]{1,0:T(8,128)(2,1)S(1)} %copy-done.16), channel_id=1, source_target_pairs={{8,0},{24,8},{16,24},{0,16},{9,1},{25,9},{17,25},{1,17},{10,2},{26... | collective-permute-start | bytes 3932168 | tf_op jit(solution)/shard_map/ppermute | solution.py:404
  462.5 226.5 %reduce-scatter.11.cloned.1.call-start = ((), (), s32[]{:S(2)}) async-start(), calls=%async_computation.10 | async-start | bytes 4718592 | tf_op jit(solution)/shard_map/reduce_scatter | solution.py:797
  462.7 84.9 %collective-permute-start.23 = (bf16[1024,512]{1,0:T(8,128)(2,1)S(1)}, bf16[1024,512]{1,0:T(8,128)(2,1)}, u32[]{:S(2)}, u32[]{:S(2)}) collective-permute-start(bf16[1024,512]{1,0:T(8,128)(2,1)S(1)} %slice.166), channel_id=1, source_target_pairs={{8,0},{24,8},{16,24},{0,16},{9,1},{25,9},{17,25},{1,17},{10,2},{26... | collective-permute-start | bytes 3145736 | tf_op jit(solution)/shard_map/ppermute | solution.py:368
  465.1 83.5 %collective-permute-start.22 = (bf16[1024,512]{1,0:T(8,128)(2,1)S(1)}, bf16[1024,512]{1,0:T(8,128)(2,1)}, u32[]{:S(2)}, u32[]{:S(2)}) collective-permute-start(bf16[1024,512]{1,0:T(8,128)(2,1)S(1)} %slice.165), channel_id=1, source_target_pairs={{0,8},{8,24},{24,16},{16,0},{1,9},{9,25},{25,17},{17,1},{2,10},{10... | collective-permute-start | bytes 3145736 | tf_op jit(solution)/shard_map/ppermute | solution.py:367
  466.9 80.6 %collective-permute-start.18 = (bf16[640,256]{1,0:T(8,128)(2,1)S(1)}, bf16[640,256]{1,0:T(8,128)(2,1)S(1)}, u32[]{:S(2)}, u32[]{:S(2)}) collective-permute-start(bf16[640,256]{1,0:T(8,128)(2,1)S(1)} %bitcast.112), channel_id=1, source_target_pairs={{0,16},{8,0},{24,8},{16,24},{1,17},{9,1},{25,9},{17,25},{2,18},{10... | collective-permute-start | bytes 983048 | tf_op jit(solution)/shard_map/ppermute | solution.py:424
  467.9 79.6 %collective-permute-start.20 = (bf16[640,256]{1,0:T(8,128)(2,1)S(1)}, bf16[640,256]{1,0:T(8,128)(2,1)S(1)}, u32[]{:S(2)}, u32[]{:S(2)}) collective-permute-start(bf16[640,256]{1,0:T(8,128)(2,1)S(1)} %bitcast.111), channel_id=1, source_target_pairs={{0,24},{8,16},{24,0},{16,8},{1,25},{9,17},{25,1},{17,9},{2,26},{10... | collective-permute-start | bytes 983048 | tf_op jit(solution)/shard_map/ppermute | solution.py:424
  468.9 78.6 %collective-permute-start.16 = (bf16[640,256]{1,0:T(8,128)(2,1)S(1)}, bf16[640,256]{1,0:T(8,128)(2,1)S(1)}, u32[]{:S(2)}, u32[]{:S(2)}) collective-permute-start(bf16[640,256]{1,0:T(8,128)(2,1)S(1)} %bitcast.110), channel_id=1, source_target_pairs={{0,8},{8,24},{24,16},{16,0},{1,9},{9,25},{25,17},{17,1},{2,10},{10... | collective-permute-start | bytes 983048 | tf_op jit(solution)/shard_map/ppermute | solution.py:424
  598.2 56.3 %collective-permute-start.28 = (bf16[320,2048]{1,0:T(8,128)(2,1)}, bf16[320,2048]{1,0:T(8,128)(2,1)S(1)}, u32[]{:S(2)}, u32[]{:S(2)}) collective-permute-start(bf16[320,2048]{1,0:T(8,128)(2,1)} %get-tuple-element.99), channel_id=1, source_target_pairs={{0,8},{8,24},{24,16},{16,0},{1,9},{9,25},{25,17},{17,1},{2,10},{10... | collective-permute-start | bytes 3932168 | tf_op jit(solution)/shard_map/ppermute | solution.py:403
  601.7 52.8 %collective-permute-start.29 = (bf16[320,2048]{1,0:T(8,128)(2,1)}, bf16[320,2048]{1,0:T(8,128)(2,1)S(1)}, u32[]{:S(2)}, u32[]{:S(2)}) collective-permute-start(bf16[320,2048]{1,0:T(8,128)(2,1)} %get-tuple-element.100), channel_id=1, source_target_pairs={{8,0},{24,8},{16,24},{0,16},{9,1},{25,9},{17,25},{1,17},{10,2},{26... | collective-permute-start | bytes 3932168 | tf_op jit(solution)/shard_map/ppermute | solution.py:404
  606.0 52.3 %collective-permute-start.27 = (bf16[320,2048]{1,0:T(8,128)(2,1)}, bf16[320,2048]{1,0:T(8,128)(2,1)}, u32[]{:S(2)}, u32[]{:S(2)}) collective-permute-start(bf16[320,2048]{1,0:T(8,128)(2,1)} %add_convert_fusion.1), channel_id=1, source_target_pairs={{8,0},{24,8},{16,24},{0,16},{9,1},{25,9},{17,25},{1,17},{10,2},{26... | collective-permute-start | bytes 3932168 | tf_op jit(solution)/shard_map/ppermute | solution.py:398
  607.1 51.2 %collective-permute-start.26 = (bf16[320,2048]{1,0:T(8,128)(2,1)}, bf16[320,2048]{1,0:T(8,128)(2,1)}, u32[]{:S(2)}, u32[]{:S(2)}) collective-permute-start(bf16[320,2048]{1,0:T(8,128)(2,1)} %add_convert_fusion.2), channel_id=1, source_target_pairs={{0,8},{8,24},{24,16},{16,0},{1,9},{9,25},{25,17},{17,1},{2,10},{10... | collective-permute-start | bytes 3932168 | tf_op jit(solution)/shard_map/ppermute | solution.py:397
  (63 other events, 992.2 us)
Sparse Core Ops, SparseCore 0:
  9.6 84.7 all-gather.3
  96.6 80.5 all-gather.5
  178.8 80.5 all-gather.7
  287.3 89.7 reduce-scatter.4
  379.2 87.9 reduce-scatter.6
  469.4 48.3 reduce-scatter.8
  626.2 52.9 reduce-scatter.10

commit v9 on v8

--- a/solution.py
+++ b/solution.py
@@ -363,6 +363,8 @@
         pieces += [from_behind, from_ahead]
     if gate:
         from_behind, from_ahead = after(from_behind, *gate), after(from_ahead, *gate)
+        if count > 2:
+            pieces[-2:] = [from_behind, from_ahead]
     far = [
         lax.ppermute(from_behind[:half], axis, ahead),
         lax.ppermute(from_ahead[half:], axis, behind),
@@ -425,15 +427,19 @@
     return got
 
 
-def sum_everywhere(values, axes, gates=()):
-    gates = list(gates)
+def exchange_steps(axes):
+    steps = []
     for axis in axes:
         count, span = lax.axis_size(axis), 1
         while span < count:
-            pairs = [(n, n ^ span) for n in range(count)]
-            values = after(values, *(gates.pop(0) if gates else ()))
-            values = values + lax.ppermute(values, axis, pairs)
+            steps.append((axis, [(n, n ^ span) for n in range(count)]))
             span *= 2
+    return steps
+
+
+def exchange(values, steps):
+    for axis, pairs in steps:
+        values = values + lax.ppermute(values, axis, pairs)
     return values
 
 
@@ -447,8 +453,32 @@
     return (h * rise).astype(LOW), (rise + (half - half * t * t) * bend).astype(LOW)
 
 
-def expand_kernel(x_ref, w_ref, b_ref, act_ref, slope_ref, *, cols):
-    x = x_ref[...]
+def join_piece(pieces, spans, whole_ref):
+    i = pl.program_id(0)
+    for (first, span), piece in zip(spans, pieces):
+
+        @pl.when((i >= first) & (i < first + span))
+        def _(piece=piece):
+            whole_ref[...] = piece[...]
+
+
+def piece_blocks(pieces):
+    tile, width = pieces[-1].shape
+    spans, first = [], 0
+    for piece in pieces:
+        spans.append((first, piece.shape[0] // tile))
+        first += piece.shape[0] // tile
+
+    def spec(first, span):
+        return pl.BlockSpec((tile, width), lambda i: (jnp.clip(i - first, 0, span - 1), 0))
+
+    return tile, tuple(spans), [spec(*span) for span in spans]
+
+
+def expand_kernel(*refs, spans, cols):
+    w_ref, b_ref, act_ref, slope_ref, whole_ref = refs[len(spans) :]
+    join_piece(refs[: len(spans)], spans, whole_ref)
+    x = whole_ref[...]
     for n in range(w_ref.shape[1] // cols):
         at = slice(n * cols, (n + 1) * cols)
         act, slope = gelu_and_slope(dot(x, w_ref[:, at], NN) + b_ref[:, at])
@@ -456,44 +486,40 @@
         slope_ref[:, at] = slope
 
 
-def expand(x, w, b):
-    rows, width = x.shape
-    hidden = w.shape[1]
-    tile = 320
+def expand(pieces, w, b):
+    width, hidden = w.shape
+    tile, spans, specs = piece_blocks(pieces)
+    rows = sum(piece.shape[0] for piece in pieces)
+    by_row = pl.BlockSpec((tile, hidden), lambda i: (i, 0))
     out = jax.ShapeDtypeStruct((rows, hidden), LOW)
     return pl.pallas_call(
-        functools.partial(expand_kernel, cols=min(512, hidden)),
-        out_shape=(out, out),
+        functools.partial(expand_kernel, spans=spans, cols=min(512, hidden)),
+        out_shape=(out, out, jax.ShapeDtypeStruct((rows, width), LOW)),
         grid=(rows // tile,),
-        in_specs=[
-            pl.BlockSpec((tile, width), lambda i: (i, 0)),
+        in_specs=specs
+        + [
             pl.BlockSpec((width, hidden), lambda i: (0, 0), pipeline_mode=pl.Buffered(1)),
             pl.BlockSpec((1, hidden), lambda i: (0, 0)),
         ],
-        out_specs=[pl.BlockSpec((tile, hidden), lambda i: (i, 0))] * 2,
+        out_specs=[by_row, by_row, pl.BlockSpec((tile, width), lambda i: (i, 0))],
         compiler_params=pltpu.CompilerParams(
             dimension_semantics=("arbitrary",), vmem_limit_bytes=48 << 20
         ),
         cost_estimate=pl.CostEstimate(
             flops=2 * rows * width * hidden,
-            bytes_accessed=2 * (rows * width + width * hidden + 2 * rows * hidden),
+            bytes_accessed=2 * rows * (2 * width + 2 * hidden),
             transcendentals=rows * hidden,
         ),
         name="expand",
-    )(x, w, b[None])
+    )(*pieces, w, b[None])
 
 
 def slope_grad_kernel(*refs, spans, cols):
     pieces = refs[: len(spans)]
     w_ref, slope_ref, out_ref, whole_ref, sums_ref = refs[len(spans) :]
-    i = pl.program_id(0)
-    for (first, span), piece in zip(spans, pieces):
-
-        @pl.when((i >= first) & (i < first + span))
-        def _(piece=piece):
-            whole_ref[...] = piece[...]
-
-    @pl.when(i == 0)
+    join_piece(pieces, spans, whole_ref)
+
+    @pl.when(pl.program_id(0) == 0)
     def _():
         sums_ref[...] = jnp.zeros(sums_ref.shape, WIDE)
 
@@ -507,25 +533,18 @@
 
 def slope_grad(pieces, w, slope):
     width, hidden = w.shape
-    tile = pieces[-1].shape[0]
-    spans, first = [], 0
-    for piece in pieces:
-        spans.append((first, piece.shape[0] // tile))
-        first += piece.shape[0] // tile
+    tile, spans, specs = piece_blocks(pieces)
+    first = sum(span for _, span in spans)
     by_row = pl.BlockSpec((tile, hidden), lambda i: (i, 0))
-
-    def piece_spec(first, span):
-        return pl.BlockSpec((tile, width), lambda i: (jnp.clip(i - first, 0, span - 1), 0))
-
     grad, whole, sums = pl.pallas_call(
-        functools.partial(slope_grad_kernel, spans=tuple(spans), cols=min(512, hidden)),
+        functools.partial(slope_grad_kernel, spans=spans, cols=min(512, hidden)),
         out_shape=(
             jax.ShapeDtypeStruct((first * tile, hidden), LOW),
             jax.ShapeDtypeStruct((first * tile, width), LOW),
             jax.ShapeDtypeStruct((8, hidden), WIDE),
         ),
         grid=(first,),
-        in_specs=[piece_spec(*span) for span in spans]
+        in_specs=specs
         + [
             pl.BlockSpec((width, hidden), lambda i: (0, 0), pipeline_mode=pl.Buffered(1)),
             by_row,
@@ -608,16 +627,14 @@
     acc[...] = token_ref[...].astype(WIDE) + bias_ref[...] + own_ref[...].astype(WIDE)
     for start, term in zip(starts, terms):
         acc[start : start + term.shape[0]] += term[...].astype(WIDE)
-    lanes = pieces[0].shape[1]
     steps = pl.num_programs(0)
     low_half = pl.program_id(0) * 2 < steps
     far = jnp.where(low_half, dense[count - 1][...], dense[count][...])
     total = acc[...]
     for rank in range(count):
         weight = dense[rank][...] if rank < count - 1 else far
-        for n in range(groups):
-            part = weight[:, n * lanes : (n + 1) * lanes]
-            total += dot(pieces[rank * groups + n][...], part, NT)
+        mine = [piece[...] for piece in pieces[rank * groups : (rank + 1) * groups]]
+        total += dot(jnp.concatenate(mine, axis=1), weight, NT)
     out_ref[...] = total.astype(LOW)
 
 
@@ -807,8 +824,7 @@
     own_grad_sum = jnp.sum(own_grad.astype(WIDE), axis=0)
     fc1_bias = lax.dynamic_slice_in_dim(b_fc1, me * hidden, hidden, 0).astype(WIDE)
     early = (where, own_grad_sum, fc1_bias, *tabs)
-    normed_pieces = ring_pieces(normed_own, "ctx")
-    normed = after(jnp.concatenate(normed_pieces, axis=0), *early)
+    normed_pieces = ring_pieces(normed_own, "ctx", gate=early)
     attention_shard = jnp.concatenate([by_group(w_qkv), w_dense.T], axis=1)
     fc1_weight = gather_rows(w_fc1)
     fc2_turned = gather_rows(after(w_fc2.T, *normed_pieces[1:-2]))
@@ -816,7 +832,7 @@
     qkv_weight, dense_turned = attention_weight[:, : 3 * each], attention_weight[:, 3 * each :]
 
     qkv_bias = lax.dynamic_slice_in_dim(b_qkv.reshape(3, width), me * each, each, 1)
-    activated, slope = expand(normed, fc1_weight, fc1_bias)
+    activated, slope, normed = expand(normed_pieces, fc1_weight, fc1_bias)
 
     sent_grad = after(own_grad, *normed_pieces[-2:])
     grad_pieces = ring_pieces(sent_grad, "ctx", gate=(activated,))
@@ -886,50 +902,50 @@
     d_part = pair_grad(gated, grads, qkv_grads[-1], attended[-1])
     d_attention.append(scatter_rows(d_part))
     [own_part], own_sums = some_ranks([0], after(turn, d_part), MUCH)
-    attended_own = [swapped[which][rank] for rank in range(count) for which in range(groups)]
+    d_qkv = jnp.concatenate(
+        [part[:, : 3 * lanes].reshape(-1, 3, lanes) for part in d_attention], axis=2
+    ).astype(WIDE)
+    d_dense = jnp.concatenate([part[:, 3 * lanes :].T for part in d_attention], axis=0)
+    d_dense = d_dense.astype(WIDE)
+
+    qkv_bias_part = jnp.concatenate(
+        [part.reshape(3, lanes) for part in qkv_sums], axis=1
+    )
+    qkv_bias_wide = lax.dynamic_update_slice_in_dim(
+        jnp.zeros((3, width), WIDE), qkv_bias_part, me * each, 1
+    ).reshape(-1)
+    fc1_bias_wide = lax.dynamic_update_slice_in_dim(
+        jnp.zeros((b_fc1.shape[0],), WIDE), fc1_bias_part, me * hidden, 0
+    )
+    small = jnp.concatenate(
+        [
+            (far_sums + middle_sums + own_sums).reshape(-1),
+            qkv_bias_wide,
+            own_grad_sum,
+            fc1_bias_wide,
+        ]
+    )
+    steps = exchange_steps(("fsdp", "ctx"))
+    small = exchange(small, steps[:1])
+    small = exchange(after(small, *last_hops), steps[1:2])
+    d_fc1, d_fc2 = d_fc1.astype(WIDE), d_fc2.T.astype(WIDE)
     output = place_output(
-        attended_own,
+        [swapped[which][rank] for rank in range(count) for which in range(groups)],
         dense_pieces,
-        after(tokens[0], *own_part),
+        after(tokens[0], small, d_fc1, d_fc2, *own_part),
         (b_dense.astype(WIDE) + b_fc2.astype(WIDE))[None],
         ff_part,
         ff_terms,
         count,
         groups,
     )
-    sums = after(far_sums + middle_sums + own_sums, output, *last_hops)
-
-    d_qkv = jnp.concatenate(
-        [part[:, : 3 * lanes].reshape(-1, 3, lanes) for part in d_attention], axis=2
-    ).astype(WIDE)
-    d_dense = jnp.concatenate([part[:, 3 * lanes :].T for part in d_attention], axis=0)
-    d_dense = d_dense.astype(WIDE)
-    d_fc1, d_fc2 = d_fc1.astype(WIDE), d_fc2.T.astype(WIDE)
-
-    qkv_bias_part = jnp.concatenate(
-        [part.reshape(3, lanes) for part in qkv_sums], axis=1
-    )
-    qkv_bias_wide = lax.dynamic_update_slice_in_dim(
-        jnp.zeros((3, width), WIDE), qkv_bias_part, me * each, 1
-    ).reshape(-1)
-    fc1_bias_wide = lax.dynamic_update_slice_in_dim(
-        jnp.zeros((b_fc1.shape[0],), WIDE), fc1_bias_part, me * hidden, 0
-    )
-    small = (
-        jnp.concatenate(
-            [
-                sums.reshape(-1),
-                qkv_bias_wide,
-                own_grad_sum,
-                fc1_bias_wide,
-            ]
-        )
-    )
+    small = exchange(small, steps[2:-2])
     d_tokens = token_grad(
-        after(tokens[0], small), own_grad, own_part[0], gain, grad_terms, local_rows // 4
-    )
-    gates = [(), (d_tokens,), (d_fc1, d_fc2), (), (d_qkv, d_dense)]
-    small = sum_everywhere(small, ("fsdp", "ctx"), gates)
+        after(tokens[0], output), own_grad, own_part[0], gain, grad_terms, local_rows // 4
+    )
+    small = exchange(after(small, output), steps[-2:-1])
+    small = exchange(after(small, d_tokens), steps[-1:])
+    small = after(small, d_qkv, d_dense)
     d_shift, with_normed, d_b_qkv, d_b_out, d_b_fc1 = jnp.split(
         small, [width, 2 * width, 5 * width, 6 * width]
     )

time: 718 us -> 716 us (level)
  waiting for transfers between devices: 109 us -> 118 us
  local copies, waits for them, and re-layouts: 51.7 us -> 44 us
    ppermute x2, waiting for transfers between devices: 5.14 us -> 20.8 us  [ring_reduce(): got_down[half] = lax.ppermute(plus(to_behind[-1], down), axis, behind)]
    ppermute x3, waiting for transfers between devices: 63.3 us -> 55.5 us  [ring_pieces(): from_ahead = lax.ppermute(from_ahead, axis, behind)]
    unnamed x99 -> x92, local copies, waits for them, and re-layouts: 27.1 us -> 19.5 us
  transfers between devices with their start and end apart: 42 -> 42, of which waited for: 12 -> 13; matrix products, arithmetic and copies ran while one was open for 27% -> 26% of each run, Pallas kernels for 48% -> 48%
where the time goes in v9:
time: 716 us; the launch traced here: 708 us
  Pallas kernels  341 us (48%)
  waiting for transfers between devices  118 us (16%)
  matrix products  117 us (16%)
  local copies, waits for them, and re-layouts  44 us (6%)
  other arithmetic  37.2 us (5%)
  starting transfers between devices  35.3 us (5%)
  between operations  15.3 us (2%)
    pallas_call x2, Pallas kernels, attention(): pl.pallas_call(kernel, out_shape=(jax.ShapeDtypeStruct((blocks, blk, lane...  154 us
    dot_general x5, matrix products, dot(): return lax.dot_general(left, right, dims, preferred_element_type=WIDE)  117 us
    pallas_call x3, Pallas kernels, input_grad(): pl.pallas_call(functools.partial(input_grad_kernel, terms=len(grads), ran...  57.3 us
    ppermute x3, waiting for transfers between devices, ring_pieces(): from_ahead = lax.ppermute(from_ahead, axis, behind)  55.5 us
    pallas_call x1, Pallas kernels, expand(): pl.pallas_call(functools.partial(expand_kernel, spans=spans, cols=min(512...  42.1 us
    pallas_call x2, Pallas kernels, pair_grad(): pl.pallas_call(pair_grad_kernel, out_shape=jax.ShapeDtypeStruct((width, c...  34.7 us
    pallas_call x1, Pallas kernels, slope_grad(): pl.pallas_call(functools.partial(slope_grad_kernel, spans=spans, cols=min...  30.9 us
    ppermute x2, waiting for transfers between devices, ring_reduce(): got_down[half] = lax.ppermute(plus(to_behind[-1], down), axis, behind)  20.8 us
  transfers between devices with their start and end apart: 42, of which 13 were waited for; matrix products, arithmetic and copies ran while one was open for 26% of the time, Pallas kernels for 48%

profile of v9, /device:TPU:0, one launch (start us, length us, event | category | flops | bytes accessed | tf_op | source)
XLA Modules:
  0.0 708.1 jit_solution(4356035297674341617)
XLA Ops:
  24.2 7.7 %negate_select_fusion = (f32[2560,128]{1,0:T(8,128)}, f32[2560,128]{1,0:T(8,128)}, f32[2560,128]{1,0:T(8,128)}) fusion(f32[128]{0:T(128)S(1)} %mul.123, s32[2560]{0:T(1024)S(1)} %get-tuple-element.190, s32[2560]{0:T(1024)S(1)} %get-tuple-element.191, s32[128]{0:T(128)S(1)} %get-tuple-element.194, s32[128]{0:T(128)S(1)} %get-tuple-element.195, ...), kind=kLoop, calls=%fused_computation.25 | loop fusion | flops 4587520 | bytes 3959424 | tf_op jit(solution)/shard_map/jit(_where)/select_n | solution.py:758
  31.9 43.3 %collective-permute-done.1.refs_2_ = bf16[640,2048]{1,0:T(8,128)(2,1)} collective-permute-done((bf16[640,2048]{1,0:T(8,128)(2,1)}, bf16[640,2048]{1,0:T(8,128)(2,1)}, u32[]{:S(2)}, u32[]{:S(2)}) %collective-permute-start.1) | collective-permute-done | bytes 2621472 | tf_op jit(solution)/shard_map/ppermute | solution.py:362
  91.6 19.9 %collective-permute-done.3.refs_4_ = bf16[320,2048]{1,0:T(8,128)(2,1)} collective-permute-done((bf16[320,2048]{1,0:T(8,128)(2,1)}, bf16[320,2048]{1,0:T(8,128)(2,1)}, u32[]{:S(2)}, u32[]{:S(2)}) %collective-permute-start.3) | collective-permute-done | bytes 1310752 | tf_op jit(solution)/shard_map/ppermute | solution.py:370
  114.9 42.1 %expand.1 = (bf16[2560,2048]{1,0:T(8,128)(2,1)}, bf16[2560,2048]{1,0:T(8,128)(2,1)}, bf16[2560,2048]{1,0:T(8,128)(2,1)}) custom-call(bf16[640,2048]{1,0:T(8,128)(2,1)} %fusion.6.refs_0_, bf16[640,2048]{1,0:T(8,128)(2,1)} %collective-permute-done.refs_1_, bf16[640,2048]{1,0:T(8,128)(2,1)} %collective-permute-done.1.refs_2_, ...), custom_call_target="tpu_custom_call" | custom-call | flops 21474836480 | bytes 41943040 | tf_op jit(solution)/shard_map/expand/pallas_call | solution.py:495
  157.0 12.2 %collective-permute-done.5.refs_2_ = bf16[640,2048]{1,0:T(8,128)(2,1)} collective-permute-done((bf16[640,2048]{1,0:T(8,128)(2,1)S(1)}, bf16[640,2048]{1,0:T(8,128)(2,1)}, u32[]{:S(2)}, u32[]{:S(2)}) %collective-permute-start.5) | collective-permute-done | bytes 2621472 | tf_op jit(solution)/shard_map/ppermute | solution.py:362
  176.9 26.6 %convolution_convert_fusion.refs_15_ = bf16[2560,2048]{1,0:T(8,128)(2,1)S(1)} fusion(bf16[2560,2048]{1,0:T(8,128)(2,1)} %get-tuple-element.71, bf16[2048,2048]{1,0:T(8,128)(2,1)} %all-gather.6.cloned.1.call-done.refs_5_), kind=kOutput, calls=%fused_computation.1 | convolution fusion | flops 21480079360 | bytes 29360128 | tf_op jit(solution)/shard_map/dot_general | solution.py:28
  210.5 30.9 %slope_grad.1 = (bf16[2560,2048]{1,0:T(8,128)(2,1)}, bf16[2560,2048]{1,0:T(8,128)(2,1)}, f32[8,2048]{1,0:T(8,128)S(1)}) custom-call(bf16[640,2048]{1,0:T(8,128)(2,1)S(1)} %bitcast.64, bf16[640,2048]{1,0:T(8,128)(2,1)} %collective-permute-done.4.refs_1_, bf16[640,2048]{1,0:T(8,128)(2,1)} %collective-permute-done.5.refs_2_, ...), custom_call_target="tpu_custom_call" | custom-call | flops 21474836480 | bytes 41943040 | tf_op jit(solution)/shard_map/slope_grad/pallas_call | solution.py:539
  243.5 28.9 %convolution_convert_fusion.2 = bf16[2048,2048]{1,0:T(8,128)(2,1)} fusion(bf16[2560,2048]{1,0:T(8,128)(2,1)} %get-tuple-element.86.y_ref, bf16[2560,2048]{1,0:T(8,128)(2,1)} %get-tuple-element.71), kind=kOutput, calls=%fused_computation.3 | convolution fusion | flops 21479030784 | bytes 29360128 | tf_op jit(solution)/shard_map/dot_general | solution.py:28
  280.6 22.3 %add_convert_fusion = bf16[2560,1536]{1,0:T(8,128)(2,1)} fusion(bf16[2560,2048]{1,0:T(8,128)(2,1)} %get-tuple-element.109.x_ref.refs_6_.refs_9_.refs_10_, f32[1536]{0:T(1024)S(1)} %reshape.234, bf16[2048,2048]{1,0:T(8,128)(2,1)} %all-gather.8.cloned.1.call-done.refs_3_.refs_4_.refs_6_.refs_7_), kind=kOutput, calls=%fused_computation | convolution fusion | flops 16113991680 | bytes 24647680 | tf_op jit(solution)/shard_map/dot_general | solution.py:28
  302.8 5.8 collective-permute-done.11.refs_19_
  310.1 10.5 %convolution_convert_fusion.3 = bf16[2560,512]{1,0:T(8,128)(2,1)} fusion(bf16[2560,2048]{1,0:T(8,128)(2,1)} %get-tuple-element.86.y_ref, bf16[2048,2048]{1,0:T(8,128)(2,1)} %all-gather.8.cloned.1.call-done.refs_3_.refs_4_.refs_6_.refs_7_), kind=kOutput, calls=%fused_computation.14 | convolution fusion | flops 5370019840 | bytes 15204352 | tf_op jit(solution)/shard_map/dot_general | solution.py:28
  320.6 28.9 %convolution_convert_fusion.1 = bf16[2048,2048]{1,0:T(8,128)(2,1)} fusion(bf16[2560,2048]{1,0:T(8,128)(2,1)} %get-tuple-element.109.x_ref.refs_6_.refs_9_.refs_10_, bf16[2560,2048]{1,0:T(8,128)(2,1)} %get-tuple-element.110.refs_2_.refs_5_), kind=kOutput, calls=%fused_computation.2 | convolution fusion | flops 21479030784 | bytes 29360128 | tf_op jit(solution)/shard_map/dot_general | solution.py:28
  356.0 77.1 %attention.2 = (bf16[40,64,256]{2,1,0:T(8,128)(2,1)}, bf16[40,64,768]{2,1,0:T(8,128)(2,1)}, f32[8,768]{1,0:T(8,128)}) custom-call(s32[40]{0:T(128)} %select_reduce_fusion.where_ref, bf16[40,64,1536]{2,1,0:T(8,128)(2,1)} %bitcast.67, bf16[40,64,1536]{2,1,0:T(8,128)(2,1)} %bitcast.68, bf16[40,64,1536]{2,1,0:T(8,128)(2,1)} %bitcast.69, ...), custom_call_target="tpu_custom_call" | custom-call | flops 1000000 | bytes 1000000 | tf_op jit(solution)/shard_map/attention/pallas_call | solution.py:297
  434.2 17.7 %pair_grad.2 = bf16[2048,1024]{1,0:T(8,128)(2,1)} custom-call(bf16[2560,2048]{1,0:T(8,128)(2,1)} %get-tuple-element.109.x_ref.refs_6_.refs_9_.refs_10_, bf16[2560,2048]{1,0:T(8,128)(2,1)} %get-tuple-element.86.y_ref, bf16[2560,768]{1,0:T(8,128)(2,1)} %bitcast.85, bf16[2560,256]{1,0:T(8,128)(2,1)} %bitcast.96), custom_call_target="tpu_custom_call" | custom-call | flops 1000000 | bytes 1000000 | tf_op jit(solution)/shard_map/pair_grad/pallas_call | solution.py:727
  459.8 77.1 %attention.3 = (bf16[40,64,256]{2,1,0:T(8,128)(2,1)}, bf16[40,64,768]{2,1,0:T(8,128)(2,1)}, f32[8,768]{1,0:T(8,128)}) custom-call(s32[40]{0:T(128)} %select_reduce_fusion.where_ref, bf16[40,64,1536]{2,1,0:T(8,128)(2,1)} %bitcast.71, bf16[40,64,1536]{2,1,0:T(8,128)(2,1)} %bitcast.72, bf16[40,64,1536]{2,1,0:T(8,128)(2,1)} %bitcast.73, ...), custom_call_target="tpu_custom_call" | custom-call | flops 1000000 | bytes 1000000 | tf_op jit(solution)/shard_map/attention/pallas_call | solution.py:297
  537.9 15.5 %input_grad.3 = (bf16[320,2048]{1,0:T(8,128)(2,1)}, bf16[320,2048]{1,0:T(8,128)(2,1)}, f32[2,2048]{1,0:T(2,128)}) custom-call(bf16[2560,768]{1,0:T(8,128)(2,1)} %bitcast.86, bf16[2560,768]{1,0:T(8,128)(2,1)} %bitcast.90, bf16[2560,2048]{1,0:T(8,128)(2,1)} %get-tuple-element.110.refs_2_.refs_5_, ...), custom_call_target="tpu_custom_call" | custom-call | flops 1000000 | bytes 1000000 | tf_op jit(solution)/shard_map/input_grad/pallas_call | solution.py:604
  560.2 26.5 %input_grad.4 = (bf16[320,2048]{1,0:T(8,128)(2,1)}, bf16[320,2048]{1,0:T(8,128)(2,1)}, bf16[320,2048]{1,0:T(8,128)(2,1)}, bf16[320,2048]{1,0:T(8,128)(2,1)}, f32[2,2048]{1,0:T(2,128)}) custom-call(bf16[2560,768]{1,0:T(8,128)(2,1)} %bitcast.87, bf16[2560,768]{1,0:T(8,128)(2,1)} %bitcast.91, bf16[2560,2048]{1,0:T(8,128)(2,1)} %get-tuple-element.110.refs_2_.refs_5_, ...), custom_call_target="tpu_custom_call" | custom-call | flops 1000000 | bytes 1000000 | tf_op jit(solution)/shard_map/input_grad/pallas_call | solution.py:604
  586.7 5.6 collective-permute-done.24
  602.1 17.0 %pair_grad.3 = bf16[2048,1024]{1,0:T(8,128)(2,1)} custom-call(bf16[2560,2048]{1,0:T(8,128)(2,1)} %get-tuple-element.109.x_ref.refs_6_.refs_9_.refs_10_, bf16[2560,2048]{1,0:T(8,128)(2,1)} %get-tuple-element.86.y_ref, bf16[2560,768]{1,0:T(8,128)(2,1)} %bitcast.93, bf16[2560,256]{1,0:T(8,128)(2,1)} %bitcast.95), custom_call_target="tpu_custom_call" | custom-call | flops 1000000 | bytes 1000000 | tf_op jit(solution)/shard_map/pair_grad/pallas_call | solution.py:727
  619.2 15.3 %input_grad.5 = (bf16[640,2048]{1,0:T(8,128)(2,1)}, f32[2,2048]{1,0:T(2,128)}) custom-call(bf16[2560,768]{1,0:T(8,128)(2,1)} %bitcast.89, bf16[2560,768]{1,0:T(8,128)(2,1)} %bitcast.94, bf16[2560,2048]{1,0:T(8,128)(2,1)} %get-tuple-element.110.refs_2_.refs_5_, bf16[2048,2048]{1,0:T(8,128)(2,1)} %all-gather.8.cloned.1.call-done.refs_3_.refs_4_.refs_6_.refs_7_, ...), custom_call_target="tpu_custom_call" | custom-call | flops 99999997952 | bytes 1000000 | tf_op jit(solution)/shard_map/input_grad/pallas_call | solution.py:604
  636.8 15.0 %collective-permute-done.28.refs_3_ = bf16[320,2048]{1,0:T(8,128)(2,1)} collective-permute-done((bf16[320,2048]{1,0:T(8,128)(2,1)}, bf16[320,2048]{1,0:T(8,128)(2,1)}, u32[]{:S(2)}, u32[]{:S(2)}) %collective-permute-start.28) | collective-permute-done | bytes 1310752 | tf_op jit(solution)/shard_map/ppermute | solution.py:400
  652.5 6.1 collective-permute-done.31
  662.3 12.9 %place_output.1 = bf16[640,2048]{1,0:T(8,128)(2,1)} custom-call(bf16[640,256]{1,0:T(8,128)(2,1)} %bitcast.104, bf16[640,256]{1,0:T(8,128)(2,1)} %bitcast.105, bf16[640,256]{1,0:T(8,128)(2,1)} %copy-done.26, bf16[640,256]{1,0:T(8,128)(2,1)} %collective-permute-done.17.refs_3_, bf16[640,256]{1,0:T(8,128)(2,1)} %copy-done.24, bf16[640,256]{1,0:T(8,128)(2,1)} %copy-done.27, ...), custom_call_target="tpu_custom_call" | custom-call | flops 1000000 | bytes 1000000 | tf_op jit(solution)/shard_map/place_output/pallas_call | solution.py:654
  679.0 8.9 %token_grad.1 = bf16[640,2048]{1,0:T(8,128)(2,1)} custom-call(bf16[640,2048]{1,0:T(8,128)(2,1)} %bitcast.84, bf16[640,2048]{1,0:T(8,128)(2,1)} %bitcast.61, bf16[640,2048]{1,0:T(8,128)(2,1)} %get-tuple-element.116.own_ref, f32[1,2048]{1,0:T(1,128)S(1)} %bitcast.65, bf16[320,2048]{1,0:T(8,128)(2,1)} %collective-permute-done.27.refs_0_, ...), custom_call_target="tpu_custom_call" | custom-call | flops 1000000 | bytes 1000000 | tf_op jit(solution)/shard_map/token_grad/pallas_call | solution.py:698
  (247 shorter events, 118.9 us)
Async XLA Ops:
  7.2 107.7 %all-gather.4.cloned.1.call-start = ((), (), s32[]{:S(2)}) async-start(), calls=%async_computation.4 | async-start | bytes 9437184 | tf_op jit(solution)/shard_map/all_gather | solution.py:811
  7.9 169.0 %all-gather.6.cloned.1.call-start = ((), (), s32[]{:S(2)}) async-start(), calls=%async_computation.5 | async-start | bytes 9437184 | tf_op jit(solution)/shard_map/all_gather | solution.py:811
  15.1 60.1 %collective-permute-start.1 = (bf16[640,2048]{1,0:T(8,128)(2,1)}, bf16[640,2048]{1,0:T(8,128)(2,1)}, u32[]{:S(2)}, u32[]{:S(2)}) collective-permute-start(bf16[640,2048]{1,0:T(8,128)(2,1)} %fusion.6.refs_0_), channel_id=1, source_target_pairs={{8,0},{24,8},{16,24},{0,16},{9,1},{25,9},{17,25},{1,17},{10,2},{26... | collective-permute-start | bytes 7864328 | tf_op jit(solution)/shard_map/ppermute | solution.py:362
  18.0 58.6 %collective-permute-start = (bf16[640,2048]{1,0:T(8,128)(2,1)}, bf16[640,2048]{1,0:T(8,128)(2,1)}, u32[]{:S(2)}, u32[]{:S(2)}) collective-permute-start(bf16[640,2048]{1,0:T(8,128)(2,1)} %fusion.6.refs_0_), channel_id=1, source_target_pairs={{0,8},{8,24},{24,16},{16,0},{1,9},{9,25},{25,17},{17,1},{2,10},{10... | collective-permute-start | bytes 7864328 | tf_op jit(solution)/shard_map/ppermute | solution.py:361
  76.7 203.8 %all-gather.8.cloned.1.call-start = ((), (), s32[]{:S(2)}) async-start(), calls=%async_computation.6 | async-start | bytes 9437184 | tf_op jit(solution)/shard_map/all_gather | solution.py:811
  112.8 321.4 %reduce-scatter.5.cloned.1.call-start = ((), (), s32[]{:S(2)}) async-start(), calls=%async_computation.7 | async-start | bytes 9437184 | tf_op jit(solution)/shard_map/reduce_scatter | solution.py:814
  112.8 56.4 %collective-permute-start.5 = (bf16[640,2048]{1,0:T(8,128)(2,1)S(1)}, bf16[640,2048]{1,0:T(8,128)(2,1)}, u32[]{:S(2)}, u32[]{:S(2)}) collective-permute-start(bf16[640,2048]{1,0:T(8,128)(2,1)S(1)} %bitcast.62), channel_id=1, source_target_pairs={{8,0},{24,8},{16,24},{0,16},{9,1},{25,9},{17,25},{1,17},{10,2},{26... | collective-permute-start | bytes 7864328 | tf_op jit(solution)/shard_map/ppermute | solution.py:362
  113.5 56.2 %collective-permute-start.4 = (bf16[640,2048]{1,0:T(8,128)(2,1)S(1)}, bf16[640,2048]{1,0:T(8,128)(2,1)}, u32[]{:S(2)}, u32[]{:S(2)}) collective-permute-start(bf16[640,2048]{1,0:T(8,128)(2,1)S(1)} %bitcast.63), channel_id=1, source_target_pairs={{0,8},{8,24},{24,16},{16,0},{1,9},{9,25},{25,17},{17,1},{2,10},{10... | collective-permute-start | bytes 7864328 | tf_op jit(solution)/shard_map/ppermute | solution.py:361
  272.4 265.5 %reduce-scatter.7.cloned.1.call-start = ((), (), s32[]{:S(2)}) async-start(), calls=%async_computation.8 | async-start | bytes 9437184 | tf_op jit(solution)/shard_map/reduce_scatter | solution.py:814
  349.6 252.5 %reduce-scatter.9.cloned.1.call-start = ((), (), s32[]{:S(2)}) async-start(), calls=%async_computation.9 | async-start | bytes 4718592 | tf_op jit(solution)/shard_map/reduce_scatter | solution.py:814
  351.5 81.6 %collective-permute-start.15 = (bf16[2048,512]{1,0:T(8,128)(2,1)S(1)}, bf16[2048,512]{1,0:T(8,128)(2,1)S(1)}, u32[]{:S(2)}, u32[]{:S(2)}) collective-permute-start(bf16[2048,512]{1,0:T(8,128)(2,1)S(1)} %slice.160.refs_8_), channel_id=1, source_target_pairs={{8,0},{24,8},{16,24},{0,16},{9,1},{25,9},{17,25},{1,17},{10,2},{26... | collective-permute-start | bytes 6291464 | tf_op jit(solution)/shard_map/ppermute | solution.py:362
  353.0 81.2 %collective-permute-start.14 = (bf16[2048,512]{1,0:T(8,128)(2,1)S(1)}, bf16[2048,512]{1,0:T(8,128)(2,1)}, u32[]{:S(2)}, u32[]{:S(2)}) collective-permute-start(bf16[2048,512]{1,0:T(8,128)(2,1)S(1)} %slice.160.refs_8_), channel_id=1, source_target_pairs={{0,8},{8,24},{24,16},{16,0},{1,9},{9,25},{25,17},{17,1},{2,10},{10... | collective-permute-start | bytes 6291464 | tf_op jit(solution)/shard_map/ppermute | solution.py:361
  353.6 79.5 %collective-permute-start.12 = (bf16[320,2048]{1,0:T(8,128)(2,1)}, bf16[320,2048]{1,0:T(8,128)(2,1)S(1)}, u32[]{:S(2)}, u32[]{:S(2)}) collective-permute-start(bf16[320,2048]{1,0:T(8,128)(2,1)} %get-tuple-element.90), channel_id=1, source_target_pairs={{0,8},{8,24},{24,16},{16,0},{1,9},{9,25},{25,17},{17,1},{2,10},{10... | collective-permute-start | bytes 3932168 | tf_op jit(solution)/shard_map/ppermute | solution.py:405
  354.2 78.9 %collective-permute-start.13 = (bf16[320,2048]{1,0:T(8,128)(2,1)S(1)}, bf16[320,2048]{1,0:T(8,128)(2,1)S(1)}, u32[]{:S(2)}, u32[]{:S(2)}) collective-permute-start(bf16[320,2048]{1,0:T(8,128)(2,1)S(1)} %copy-done.15), channel_id=1, source_target_pairs={{8,0},{24,8},{16,24},{0,16},{9,1},{25,9},{17,25},{1,17},{10,2},{26... | collective-permute-start | bytes 3932168 | tf_op jit(solution)/shard_map/ppermute | solution.py:406
  451.9 241.5 %reduce-scatter.11.cloned.1.call-start = ((), (), s32[]{:S(2)}) async-start(), calls=%async_computation.10 | async-start | bytes 4718592 | tf_op jit(solution)/shard_map/reduce_scatter | solution.py:814
  452.1 84.9 %collective-permute-start.23 = (bf16[1024,512]{1,0:T(8,128)(2,1)S(1)}, bf16[1024,512]{1,0:T(8,128)(2,1)}, u32[]{:S(2)}, u32[]{:S(2)}) collective-permute-start(bf16[1024,512]{1,0:T(8,128)(2,1)S(1)} %slice.164), channel_id=1, source_target_pairs={{8,0},{24,8},{16,24},{0,16},{9,1},{25,9},{17,25},{1,17},{10,2},{26... | collective-permute-start | bytes 3145736 | tf_op jit(solution)/shard_map/ppermute | solution.py:370
  454.9 83.0 %collective-permute-start.22 = (bf16[1024,512]{1,0:T(8,128)(2,1)S(1)}, bf16[1024,512]{1,0:T(8,128)(2,1)}, u32[]{:S(2)}, u32[]{:S(2)}) collective-permute-start(bf16[1024,512]{1,0:T(8,128)(2,1)S(1)} %slice.163), channel_id=1, source_target_pairs={{0,8},{8,24},{24,16},{16,0},{1,9},{9,25},{25,17},{17,1},{2,10},{10... | collective-permute-start | bytes 3145736 | tf_op jit(solution)/shard_map/ppermute | solution.py:369
  456.3 80.6 %collective-permute-start.18 = (bf16[640,256]{1,0:T(8,128)(2,1)S(1)}, bf16[640,256]{1,0:T(8,128)(2,1)S(1)}, u32[]{:S(2)}, u32[]{:S(2)}) collective-permute-start(bf16[640,256]{1,0:T(8,128)(2,1)S(1)} %bitcast.112), channel_id=1, source_target_pairs={{0,16},{8,0},{24,8},{16,24},{1,17},{9,1},{25,9},{17,25},{2,18},{10... | collective-permute-start | bytes 983048 | tf_op jit(solution)/shard_map/ppermute | solution.py:426
  457.8 79.2 %collective-permute-start.20 = (bf16[640,256]{1,0:T(8,128)(2,1)S(1)}, bf16[640,256]{1,0:T(8,128)(2,1)S(1)}, u32[]{:S(2)}, u32[]{:S(2)}) collective-permute-start(bf16[640,256]{1,0:T(8,128)(2,1)S(1)} %bitcast.111), channel_id=1, source_target_pairs={{0,24},{8,16},{24,0},{16,8},{1,25},{9,17},{25,1},{17,9},{2,26},{10... | collective-permute-start | bytes 983048 | tf_op jit(solution)/shard_map/ppermute | solution.py:426
  458.4 78.6 %collective-permute-start.16 = (bf16[640,256]{1,0:T(8,128)(2,1)S(1)}, bf16[640,256]{1,0:T(8,128)(2,1)S(1)}, u32[]{:S(2)}, u32[]{:S(2)}) collective-permute-start(bf16[640,256]{1,0:T(8,128)(2,1)S(1)} %bitcast.110), channel_id=1, source_target_pairs={{0,8},{8,24},{24,16},{16,0},{1,9},{9,25},{25,17},{17,1},{2,10},{10... | collective-permute-start | bytes 983048 | tf_op jit(solution)/shard_map/ppermute | solution.py:426
  556.8 43.3 %collective-permute-start.19 = (bf16[640,256]{1,0:T(8,128)(2,1)S(1)}, bf16[640,256]{1,0:T(8,128)(2,1)S(1)}, u32[]{:S(2)}, u32[]{:S(2)}) collective-permute-start(bf16[640,256]{1,0:T(8,128)(2,1)S(1)} %bitcast.109), channel_id=1, source_target_pairs={{0,16},{8,0},{24,8},{16,24},{1,17},{9,1},{25,9},{17,25},{2,18},{10... | collective-permute-start | bytes 983048 | tf_op jit(solution)/shard_map/ppermute | solution.py:426
  592.3 44.5 %collective-permute-start.29 = (bf16[320,2048]{1,0:T(8,128)(2,1)}, bf16[320,2048]{1,0:T(8,128)(2,1)S(1)}, u32[]{:S(2)}, u32[]{:S(2)}) collective-permute-start(bf16[320,2048]{1,0:T(8,128)(2,1)} %get-tuple-element.105), channel_id=1, source_target_pairs={{0,8},{8,24},{24,16},{16,0},{1,9},{9,25},{25,17},{17,1},{2,10},{10... | collective-permute-start | bytes 3932168 | tf_op jit(solution)/shard_map/ppermute | solution.py:405
  600.0 51.8 %collective-permute-start.28 = (bf16[320,2048]{1,0:T(8,128)(2,1)}, bf16[320,2048]{1,0:T(8,128)(2,1)}, u32[]{:S(2)}, u32[]{:S(2)}) collective-permute-start(bf16[320,2048]{1,0:T(8,128)(2,1)} %add_convert_fusion.1), channel_id=1, source_target_pairs={{8,0},{24,8},{16,24},{0,16},{9,1},{25,9},{17,25},{1,17},{10,2},{26... | collective-permute-start | bytes 3932168 | tf_op jit(solution)/shard_map/ppermute | solution.py:400
  600.1 51.8 %collective-permute-start.27 = (bf16[320,2048]{1,0:T(8,128)(2,1)}, bf16[320,2048]{1,0:T(8,128)(2,1)}, u32[]{:S(2)}, u32[]{:S(2)}) collective-permute-start(bf16[320,2048]{1,0:T(8,128)(2,1)} %add_convert_fusion.2), channel_id=1, source_target_pairs={{0,8},{8,24},{24,16},{16,0},{1,9},{9,25},{25,17},{17,1},{2,10},{10... | collective-permute-start | bytes 3932168 | tf_op jit(solution)/shard_map/ppermute | solution.py:399
  (61 other events, 1016.1 us)
Sparse Core Ops, SparseCore 0:
  9.6 84.7 all-gather.3
  96.0 80.5 all-gather.5
  178.2 80.5 all-gather.7
  272.5 89.7 reduce-scatter.4
  364.4 87.9 reduce-scatter.6
  454.6 48.3 reduce-scatter.8
  619.3 51.5 reduce-scatter.10

commit v10 on v9

--- a/solution.py
+++ b/solution.py
@@ -927,24 +927,23 @@
     )
     steps = exchange_steps(("fsdp", "ctx"))
     small = exchange(small, steps[:1])
-    small = exchange(after(small, *last_hops), steps[1:2])
     d_fc1, d_fc2 = d_fc1.astype(WIDE), d_fc2.T.astype(WIDE)
     output = place_output(
         [swapped[which][rank] for rank in range(count) for which in range(groups)],
         dense_pieces,
-        after(tokens[0], small, d_fc1, d_fc2, *own_part),
+        after(tokens[0], *own_part),
         (b_dense.astype(WIDE) + b_fc2.astype(WIDE))[None],
         ff_part,
         ff_terms,
         count,
         groups,
     )
-    small = exchange(small, steps[2:-2])
+    small = exchange(after(small, output, *last_hops), steps[1:2])
     d_tokens = token_grad(
         after(tokens[0], output), own_grad, own_part[0], gain, grad_terms, local_rows // 4
     )
-    small = exchange(after(small, output), steps[-2:-1])
-    small = exchange(after(small, d_tokens), steps[-1:])
+    small = exchange(after(small, d_tokens), steps[2:-1])
+    small = exchange(after(small, d_fc1, d_fc2), steps[-1:])
     small = after(small, d_qkv, d_dense)
     d_shift, with_normed, d_b_qkv, d_b_out, d_b_fc1 = jnp.split(
         small, [width, 2 * width, 5 * width, 6 * width]

time: 716 us -> 702 us (0.980)
  waiting for transfers between devices: 118 us -> 106 us
    ppermute x2, waiting for transfers between devices: 20.8 us -> 8.68 us  [ring_reduce(): got_down[half] = lax.ppermute(plus(to_behind[-1], down), axis, behind)]
  transfers between devices with their start and end apart: 42 -> 42, of which waited for: 13 -> 13; matrix products, arithmetic and copies ran while one was open for 26% -> 26% of each run, Pallas kernels for 48% -> 49%
where the time goes in v10:
time: 702 us; the launch traced here: 694 us
  Pallas kernels  341 us (49%)
  matrix products  117 us (17%)
  waiting for transfers between devices  106 us (15%)
  local copies, waits for them, and re-layouts  42.7 us (6%)
  starting transfers between devices  37.7 us (5%)
  other arithmetic  34.2 us (5%)
  between operations  15.3 us (2%)
    pallas_call x2, Pallas kernels, attention(): pl.pallas_call(kernel, out_shape=(jax.ShapeDtypeStruct((blocks, blk, lane...  154 us
    dot_general x5, matrix products, dot(): return lax.dot_general(left, right, dims, preferred_element_type=WIDE)  117 us
    pallas_call x3, Pallas kernels, input_grad(): pl.pallas_call(functools.partial(input_grad_kernel, terms=len(grads), ran...  57.3 us
    ppermute x3, waiting for transfers between devices, ring_pieces(): from_ahead = lax.ppermute(from_ahead, axis, behind)  55.6 us
    pallas_call x1, Pallas kernels, expand(): pl.pallas_call(functools.partial(expand_kernel, spans=spans, cols=min(512...  42 us
    pallas_call x2, Pallas kernels, pair_grad(): pl.pallas_call(pair_grad_kernel, out_shape=jax.ShapeDtypeStruct((width, c...  34.7 us
    pallas_call x1, Pallas kernels, slope_grad(): pl.pallas_call(functools.partial(slope_grad_kernel, spans=spans, cols=min...  30.9 us
    ppermute x3, waiting for transfers between devices, ring_pieces(): lax.ppermute(from_ahead[half:], axis, behind)  19.9 us
  transfers between devices with their start and end apart: 42, of which 13 were waited for; matrix products, arithmetic and copies ran while one was open for 26% of the time, Pallas kernels for 49%

profile of v10, /device:TPU:0, one launch (start us, length us, event | category | flops | bytes accessed | tf_op | source)
XLA Modules:
  0.0 693.9 jit_solution(15461811361409808342)
XLA Ops:
  24.2 7.7 %negate_select_fusion = (f32[2560,128]{1,0:T(8,128)}, f32[2560,128]{1,0:T(8,128)}, f32[2560,128]{1,0:T(8,128)}) fusion(f32[128]{0:T(128)S(1)} %mul.123, s32[2560]{0:T(1024)S(1)} %get-tuple-element.190, s32[2560]{0:T(1024)S(1)} %get-tuple-element.191, s32[128]{0:T(128)S(1)} %get-tuple-element.194, s32[128]{0:T(128)S(1)} %get-tuple-element.195, ...), kind=kLoop, calls=%fused_computation.25 | loop fusion | flops 4587520 | bytes 3959424 | tf_op jit(solution)/shard_map/jit(_where)/select_n | solution.py:758
  31.8 43.3 %collective-permute-done.1.refs_2_ = bf16[640,2048]{1,0:T(8,128)(2,1)} collective-permute-done((bf16[640,2048]{1,0:T(8,128)(2,1)}, bf16[640,2048]{1,0:T(8,128)(2,1)}, u32[]{:S(2)}, u32[]{:S(2)}) %collective-permute-start.1) | collective-permute-done | bytes 2621472 | tf_op jit(solution)/shard_map/ppermute | solution.py:362
  91.6 19.9 %collective-permute-done.3.refs_4_ = bf16[320,2048]{1,0:T(8,128)(2,1)} collective-permute-done((bf16[320,2048]{1,0:T(8,128)(2,1)}, bf16[320,2048]{1,0:T(8,128)(2,1)}, u32[]{:S(2)}, u32[]{:S(2)}) %collective-permute-start.3) | collective-permute-done | bytes 1310752 | tf_op jit(solution)/shard_map/ppermute | solution.py:370
  114.9 42.0 %expand.1 = (bf16[2560,2048]{1,0:T(8,128)(2,1)}, bf16[2560,2048]{1,0:T(8,128)(2,1)}, bf16[2560,2048]{1,0:T(8,128)(2,1)}) custom-call(bf16[640,2048]{1,0:T(8,128)(2,1)} %fusion.6.refs_0_, bf16[640,2048]{1,0:T(8,128)(2,1)} %collective-permute-done.refs_1_, bf16[640,2048]{1,0:T(8,128)(2,1)} %collective-permute-done.1.refs_2_, ...), custom_call_target="tpu_custom_call" | custom-call | flops 21474836480 | bytes 41943040 | tf_op jit(solution)/shard_map/expand/pallas_call | solution.py:495
  156.9 12.3 %collective-permute-done.5.refs_2_ = bf16[640,2048]{1,0:T(8,128)(2,1)} collective-permute-done((bf16[640,2048]{1,0:T(8,128)(2,1)S(1)}, bf16[640,2048]{1,0:T(8,128)(2,1)}, u32[]{:S(2)}, u32[]{:S(2)}) %collective-permute-start.5) | collective-permute-done | bytes 2621472 | tf_op jit(solution)/shard_map/ppermute | solution.py:362
  177.2 26.6 %convolution_convert_fusion.refs_15_ = bf16[2560,2048]{1,0:T(8,128)(2,1)S(1)} fusion(bf16[2560,2048]{1,0:T(8,128)(2,1)} %get-tuple-element.71, bf16[2048,2048]{1,0:T(8,128)(2,1)} %all-gather.6.cloned.1.call-done.refs_5_), kind=kOutput, calls=%fused_computation.1 | convolution fusion | flops 21480079360 | bytes 29360128 | tf_op jit(solution)/shard_map/dot_general | solution.py:28
  210.5 30.9 %slope_grad.1 = (bf16[2560,2048]{1,0:T(8,128)(2,1)}, bf16[2560,2048]{1,0:T(8,128)(2,1)}, f32[8,2048]{1,0:T(8,128)S(1)}) custom-call(bf16[640,2048]{1,0:T(8,128)(2,1)S(1)} %bitcast.64, bf16[640,2048]{1,0:T(8,128)(2,1)} %collective-permute-done.4.refs_1_, bf16[640,2048]{1,0:T(8,128)(2,1)} %collective-permute-done.5.refs_2_, ...), custom_call_target="tpu_custom_call" | custom-call | flops 21474836480 | bytes 41943040 | tf_op jit(solution)/shard_map/slope_grad/pallas_call | solution.py:539
  243.6 28.9 %convolution_convert_fusion.2 = bf16[2048,2048]{1,0:T(8,128)(2,1)} fusion(bf16[2560,2048]{1,0:T(8,128)(2,1)} %get-tuple-element.86.y_ref, bf16[2560,2048]{1,0:T(8,128)(2,1)} %get-tuple-element.71), kind=kOutput, calls=%fused_computation.3 | convolution fusion | flops 21479030784 | bytes 29360128 | tf_op jit(solution)/shard_map/dot_general | solution.py:28
  274.2 4.2 add_convert_fusion.3
  280.6 22.3 %add_convert_fusion = bf16[2560,1536]{1,0:T(8,128)(2,1)} fusion(bf16[2560,2048]{1,0:T(8,128)(2,1)} %get-tuple-element.107.x_ref.refs_6_.refs_9_.refs_10_, f32[1536]{0:T(1024)S(1)} %reshape.234, bf16[2048,2048]{1,0:T(8,128)(2,1)} %all-gather.8.cloned.1.call-done.refs_3_.refs_4_.refs_6_.refs_7_), kind=kOutput, calls=%fused_computation | convolution fusion | flops 16113991680 | bytes 24647680 | tf_op jit(solution)/shard_map/dot_general | solution.py:28
  302.9 6.1 collective-permute-done.11.refs_19_
  310.4 10.5 %convolution_convert_fusion.3 = bf16[2560,512]{1,0:T(8,128)(2,1)} fusion(bf16[2560,2048]{1,0:T(8,128)(2,1)} %get-tuple-element.86.y_ref, bf16[2048,2048]{1,0:T(8,128)(2,1)} %all-gather.8.cloned.1.call-done.refs_3_.refs_4_.refs_6_.refs_7_), kind=kOutput, calls=%fused_computation.14 | convolution fusion | flops 5370019840 | bytes 15204352 | tf_op jit(solution)/shard_map/dot_general | solution.py:28
  320.9 28.9 %convolution_convert_fusion.1 = bf16[2048,2048]{1,0:T(8,128)(2,1)} fusion(bf16[2560,2048]{1,0:T(8,128)(2,1)} %get-tuple-element.107.x_ref.refs_6_.refs_9_.refs_10_, bf16[2560,2048]{1,0:T(8,128)(2,1)} %get-tuple-element.108.refs_2_.refs_5_), kind=kOutput, calls=%fused_computation.2 | convolution fusion | flops 21479030784 | bytes 29360128 | tf_op jit(solution)/shard_map/dot_general | solution.py:28
  356.3 77.1 %attention.2 = (bf16[40,64,256]{2,1,0:T(8,128)(2,1)}, bf16[40,64,768]{2,1,0:T(8,128)(2,1)}, f32[8,768]{1,0:T(8,128)}) custom-call(s32[40]{0:T(128)} %select_reduce_fusion.where_ref, bf16[40,64,1536]{2,1,0:T(8,128)(2,1)} %bitcast.67, bf16[40,64,1536]{2,1,0:T(8,128)(2,1)} %bitcast.68, bf16[40,64,1536]{2,1,0:T(8,128)(2,1)} %bitcast.69, ...), custom_call_target="tpu_custom_call" | custom-call | flops 1000000 | bytes 1000000 | tf_op jit(solution)/shard_map/attention/pallas_call | solution.py:297
  434.6 17.7 %pair_grad.2 = bf16[2048,1024]{1,0:T(8,128)(2,1)} custom-call(bf16[2560,2048]{1,0:T(8,128)(2,1)} %get-tuple-element.107.x_ref.refs_6_.refs_9_.refs_10_, bf16[2560,2048]{1,0:T(8,128)(2,1)} %get-tuple-element.86.y_ref, bf16[2560,768]{1,0:T(8,128)(2,1)} %bitcast.85, bf16[2560,256]{1,0:T(8,128)(2,1)} %bitcast.96), custom_call_target="tpu_custom_call" | custom-call | flops 1000000 | bytes 1000000 | tf_op jit(solution)/shard_map/pair_grad/pallas_call | solution.py:727
  460.2 77.1 %attention.3 = (bf16[40,64,256]{2,1,0:T(8,128)(2,1)}, bf16[40,64,768]{2,1,0:T(8,128)(2,1)}, f32[8,768]{1,0:T(8,128)}) custom-call(s32[40]{0:T(128)} %select_reduce_fusion.where_ref, bf16[40,64,1536]{2,1,0:T(8,128)(2,1)} %bitcast.71, bf16[40,64,1536]{2,1,0:T(8,128)(2,1)} %bitcast.72, bf16[40,64,1536]{2,1,0:T(8,128)(2,1)} %bitcast.73, ...), custom_call_target="tpu_custom_call" | custom-call | flops 1000000 | bytes 1000000 | tf_op jit(solution)/shard_map/attention/pallas_call | solution.py:297
  538.3 15.5 %input_grad.3 = (bf16[320,2048]{1,0:T(8,128)(2,1)}, bf16[320,2048]{1,0:T(8,128)(2,1)}, f32[2,2048]{1,0:T(2,128)}) custom-call(bf16[2560,768]{1,0:T(8,128)(2,1)} %bitcast.86, bf16[2560,768]{1,0:T(8,128)(2,1)} %bitcast.90, bf16[2560,2048]{1,0:T(8,128)(2,1)} %get-tuple-element.108.refs_2_.refs_5_, ...), custom_call_target="tpu_custom_call" | custom-call | flops 1000000 | bytes 1000000 | tf_op jit(solution)/shard_map/input_grad/pallas_call | solution.py:604
  560.5 26.5 %input_grad.4 = (bf16[320,2048]{1,0:T(8,128)(2,1)}, bf16[320,2048]{1,0:T(8,128)(2,1)}, bf16[320,2048]{1,0:T(8,128)(2,1)}, bf16[320,2048]{1,0:T(8,128)(2,1)}, f32[2,2048]{1,0:T(2,128)}) custom-call(bf16[2560,768]{1,0:T(8,128)(2,1)} %bitcast.87, bf16[2560,768]{1,0:T(8,128)(2,1)} %bitcast.91, bf16[2560,2048]{1,0:T(8,128)(2,1)} %get-tuple-element.108.refs_2_.refs_5_, ...), custom_call_target="tpu_custom_call" | custom-call | flops 1000000 | bytes 1000000 | tf_op jit(solution)/shard_map/input_grad/pallas_call | solution.py:604
  587.1 5.7 collective-permute-done.24
  602.5 17.0 %pair_grad.3 = bf16[2048,1024]{1,0:T(8,128)(2,1)} custom-call(bf16[2560,2048]{1,0:T(8,128)(2,1)} %get-tuple-element.107.x_ref.refs_6_.refs_9_.refs_10_, bf16[2560,2048]{1,0:T(8,128)(2,1)} %get-tuple-element.86.y_ref, bf16[2560,768]{1,0:T(8,128)(2,1)} %bitcast.93, bf16[2560,256]{1,0:T(8,128)(2,1)} %bitcast.95), custom_call_target="tpu_custom_call" | custom-call | flops 1000000 | bytes 1000000 | tf_op jit(solution)/shard_map/pair_grad/pallas_call | solution.py:727
  619.7 15.3 %input_grad.5 = (bf16[640,2048]{1,0:T(8,128)(2,1)}, f32[2,2048]{1,0:T(2,128)}) custom-call(bf16[2560,768]{1,0:T(8,128)(2,1)} %bitcast.89, bf16[2560,768]{1,0:T(8,128)(2,1)} %bitcast.94, bf16[2560,2048]{1,0:T(8,128)(2,1)} %get-tuple-element.108.refs_2_.refs_5_, bf16[2048,2048]{1,0:T(8,128)(2,1)} %all-gather.8.cloned.1.call-done.refs_3_.refs_4_.refs_6_.refs_7_, ...), custom_call_target="tpu_custom_call" | custom-call | flops 99999997952 | bytes 1000000 | tf_op jit(solution)/shard_map/input_grad/pallas_call | solution.py:604
  636.5 13.2 %place_output.1 = bf16[640,2048]{1,0:T(8,128)(2,1)} custom-call(bf16[640,256]{1,0:T(8,128)(2,1)} %bitcast.104, bf16[640,256]{1,0:T(8,128)(2,1)} %bitcast.105, bf16[640,256]{1,0:T(8,128)(2,1)} %copy-done.26, bf16[640,256]{1,0:T(8,128)(2,1)} %collective-permute-done.17.refs_3_, bf16[640,256]{1,0:T(8,128)(2,1)} %copy-done.24, bf16[640,256]{1,0:T(8,128)(2,1)} %copy-done.27, ...), custom_call_target="tpu_custom_call" | custom-call | flops 1000000 | bytes 1000000 | tf_op jit(solution)/shard_map/place_output/pallas_call | solution.py:654
  652.3 9.0 %token_grad.1 = bf16[640,2048]{1,0:T(8,128)(2,1)} custom-call(bf16[640,2048]{1,0:T(8,128)(2,1)} %bitcast.84, bf16[640,2048]{1,0:T(8,128)(2,1)} %bitcast.61, bf16[640,2048]{1,0:T(8,128)(2,1)} %get-tuple-element.109.own_ref, f32[1,2048]{1,0:T(1,128)S(1)} %bitcast.65, bf16[320,2048]{1,0:T(8,128)(2,1)} %collective-permute-done.26.refs_0_, ...), custom_call_target="tpu_custom_call" | custom-call | flops 1000000 | bytes 1000000 | tf_op jit(solution)/shard_map/token_grad/pallas_call | solution.py:698
  662.2 7.0 %collective-permute-done.32 = f32[20480]{0:T(1024)S(1)} collective-permute-done((f32[20480]{0:T(1024)S(1)}, f32[20480]{0:T(1024)S(1)}, u32[]{:S(2)}, u32[]{:S(2)}) %collective-permute-start.32) | collective-permute-done | bytes 81952 | tf_op jit(solution)/shard_map/ppermute | solution.py:442
  (247 shorter events, 113.8 us)
Async XLA Ops:
  7.2 107.7 %all-gather.4.cloned.1.call-start = ((), (), s32[]{:S(2)}) async-start(), calls=%async_computation.4 | async-start | bytes 9437184 | tf_op jit(solution)/shard_map/all_gather | solution.py:811
  7.9 169.3 %all-gather.6.cloned.1.call-start = ((), (), s32[]{:S(2)}) async-start(), calls=%async_computation.5 | async-start | bytes 9437184 | tf_op jit(solution)/shard_map/all_gather | solution.py:811
  15.1 60.1 %collective-permute-start.1 = (bf16[640,2048]{1,0:T(8,128)(2,1)}, bf16[640,2048]{1,0:T(8,128)(2,1)}, u32[]{:S(2)}, u32[]{:S(2)}) collective-permute-start(bf16[640,2048]{1,0:T(8,128)(2,1)} %fusion.6.refs_0_), channel_id=1, source_target_pairs={{8,0},{24,8},{16,24},{0,16},{9,1},{25,9},{17,25},{1,17},{10,2},{26... | collective-permute-start | bytes 7864328 | tf_op jit(solution)/shard_map/ppermute | solution.py:362
  18.0 58.6 %collective-permute-start = (bf16[640,2048]{1,0:T(8,128)(2,1)}, bf16[640,2048]{1,0:T(8,128)(2,1)}, u32[]{:S(2)}, u32[]{:S(2)}) collective-permute-start(bf16[640,2048]{1,0:T(8,128)(2,1)} %fusion.6.refs_0_), channel_id=1, source_target_pairs={{0,8},{8,24},{24,16},{16,0},{1,9},{9,25},{25,17},{17,1},{2,10},{10... | collective-permute-start | bytes 7864328 | tf_op jit(solution)/shard_map/ppermute | solution.py:361
  76.7 203.9 %all-gather.8.cloned.1.call-start = ((), (), s32[]{:S(2)}) async-start(), calls=%async_computation.6 | async-start | bytes 9437184 | tf_op jit(solution)/shard_map/all_gather | solution.py:811
  112.8 321.8 %reduce-scatter.5.cloned.1.call-start = ((), (), s32[]{:S(2)}) async-start(), calls=%async_computation.7 | async-start | bytes 9437184 | tf_op jit(solution)/shard_map/reduce_scatter | solution.py:814
  112.8 56.4 %collective-permute-start.5 = (bf16[640,2048]{1,0:T(8,128)(2,1)S(1)}, bf16[640,2048]{1,0:T(8,128)(2,1)}, u32[]{:S(2)}, u32[]{:S(2)}) collective-permute-start(bf16[640,2048]{1,0:T(8,128)(2,1)S(1)} %bitcast.62), channel_id=1, source_target_pairs={{8,0},{24,8},{16,24},{0,16},{9,1},{25,9},{17,25},{1,17},{10,2},{26... | collective-permute-start | bytes 7864328 | tf_op jit(solution)/shard_map/ppermute | solution.py:362
  113.5 56.2 %collective-permute-start.4 = (bf16[640,2048]{1,0:T(8,128)(2,1)S(1)}, bf16[640,2048]{1,0:T(8,128)(2,1)}, u32[]{:S(2)}, u32[]{:S(2)}) collective-permute-start(bf16[640,2048]{1,0:T(8,128)(2,1)S(1)} %bitcast.63), channel_id=1, source_target_pairs={{0,8},{8,24},{24,16},{16,0},{1,9},{9,25},{25,17},{17,1},{2,10},{10... | collective-permute-start | bytes 7864328 | tf_op jit(solution)/shard_map/ppermute | solution.py:361
  272.5 265.8 %reduce-scatter.7.cloned.1.call-start = ((), (), s32[]{:S(2)}) async-start(), calls=%async_computation.8 | async-start | bytes 9437184 | tf_op jit(solution)/shard_map/reduce_scatter | solution.py:814
  349.9 252.6 %reduce-scatter.9.cloned.1.call-start = ((), (), s32[]{:S(2)}) async-start(), calls=%async_computation.9 | async-start | bytes 4718592 | tf_op jit(solution)/shard_map/reduce_scatter | solution.py:814
  351.8 81.6 %collective-permute-start.15 = (bf16[2048,512]{1,0:T(8,128)(2,1)S(1)}, bf16[2048,512]{1,0:T(8,128)(2,1)S(1)}, u32[]{:S(2)}, u32[]{:S(2)}) collective-permute-start(bf16[2048,512]{1,0:T(8,128)(2,1)S(1)} %slice.160.refs_8_), channel_id=1, source_target_pairs={{8,0},{24,8},{16,24},{0,16},{9,1},{25,9},{17,25},{1,17},{10,2},{26... | collective-permute-start | bytes 6291464 | tf_op jit(solution)/shard_map/ppermute | solution.py:362
  353.3 81.2 %collective-permute-start.14 = (bf16[2048,512]{1,0:T(8,128)(2,1)S(1)}, bf16[2048,512]{1,0:T(8,128)(2,1)}, u32[]{:S(2)}, u32[]{:S(2)}) collective-permute-start(bf16[2048,512]{1,0:T(8,128)(2,1)S(1)} %slice.160.refs_8_), channel_id=1, source_target_pairs={{0,8},{8,24},{24,16},{16,0},{1,9},{9,25},{25,17},{17,1},{2,10},{10... | collective-permute-start | bytes 6291464 | tf_op jit(solution)/shard_map/ppermute | solution.py:361
  353.9 79.5 %collective-permute-start.12 = (bf16[320,2048]{1,0:T(8,128)(2,1)}, bf16[320,2048]{1,0:T(8,128)(2,1)S(1)}, u32[]{:S(2)}, u32[]{:S(2)}) collective-permute-start(bf16[320,2048]{1,0:T(8,128)(2,1)} %get-tuple-element.90), channel_id=1, source_target_pairs={{0,8},{8,24},{24,16},{16,0},{1,9},{9,25},{25,17},{17,1},{2,10},{10... | collective-permute-start | bytes 3932168 | tf_op jit(solution)/shard_map/ppermute | solution.py:405
  354.4 79.0 %collective-permute-start.13 = (bf16[320,2048]{1,0:T(8,128)(2,1)S(1)}, bf16[320,2048]{1,0:T(8,128)(2,1)S(1)}, u32[]{:S(2)}, u32[]{:S(2)}) collective-permute-start(bf16[320,2048]{1,0:T(8,128)(2,1)S(1)} %copy-done.15), channel_id=1, source_target_pairs={{8,0},{24,8},{16,24},{0,16},{9,1},{25,9},{17,25},{1,17},{10,2},{26... | collective-permute-start | bytes 3932168 | tf_op jit(solution)/shard_map/ppermute | solution.py:406
  452.3 226.9 %reduce-scatter.11.cloned.1.call-start = ((), (), s32[]{:S(2)}) async-start(), calls=%async_computation.10 | async-start | bytes 4718592 | tf_op jit(solution)/shard_map/reduce_scatter | solution.py:814
  452.4 84.9 %collective-permute-start.23 = (bf16[1024,512]{1,0:T(8,128)(2,1)S(1)}, bf16[1024,512]{1,0:T(8,128)(2,1)}, u32[]{:S(2)}, u32[]{:S(2)}) collective-permute-start(bf16[1024,512]{1,0:T(8,128)(2,1)S(1)} %slice.164), channel_id=1, source_target_pairs={{8,0},{24,8},{16,24},{0,16},{9,1},{25,9},{17,25},{1,17},{10,2},{26... | collective-permute-start | bytes 3145736 | tf_op jit(solution)/shard_map/ppermute | solution.py:370
  455.3 83.0 %collective-permute-start.22 = (bf16[1024,512]{1,0:T(8,128)(2,1)S(1)}, bf16[1024,512]{1,0:T(8,128)(2,1)}, u32[]{:S(2)}, u32[]{:S(2)}) collective-permute-start(bf16[1024,512]{1,0:T(8,128)(2,1)S(1)} %slice.163), channel_id=1, source_target_pairs={{0,8},{8,24},{24,16},{16,0},{1,9},{9,25},{25,17},{17,1},{2,10},{10... | collective-permute-start | bytes 3145736 | tf_op jit(solution)/shard_map/ppermute | solution.py:369
  456.7 80.6 %collective-permute-start.18 = (bf16[640,256]{1,0:T(8,128)(2,1)S(1)}, bf16[640,256]{1,0:T(8,128)(2,1)S(1)}, u32[]{:S(2)}, u32[]{:S(2)}) collective-permute-start(bf16[640,256]{1,0:T(8,128)(2,1)S(1)} %bitcast.112), channel_id=1, source_target_pairs={{0,16},{8,0},{24,8},{16,24},{1,17},{9,1},{25,9},{17,25},{2,18},{10... | collective-permute-start | bytes 983048 | tf_op jit(solution)/shard_map/ppermute | solution.py:426
  458.2 79.2 %collective-permute-start.20 = (bf16[640,256]{1,0:T(8,128)(2,1)S(1)}, bf16[640,256]{1,0:T(8,128)(2,1)S(1)}, u32[]{:S(2)}, u32[]{:S(2)}) collective-permute-start(bf16[640,256]{1,0:T(8,128)(2,1)S(1)} %bitcast.111), channel_id=1, source_target_pairs={{0,24},{8,16},{24,0},{16,8},{1,25},{9,17},{25,1},{17,9},{2,26},{10... | collective-permute-start | bytes 983048 | tf_op jit(solution)/shard_map/ppermute | solution.py:426
  458.7 78.6 %collective-permute-start.16 = (bf16[640,256]{1,0:T(8,128)(2,1)S(1)}, bf16[640,256]{1,0:T(8,128)(2,1)S(1)}, u32[]{:S(2)}, u32[]{:S(2)}) collective-permute-start(bf16[640,256]{1,0:T(8,128)(2,1)S(1)} %bitcast.110), channel_id=1, source_target_pairs={{0,8},{8,24},{24,16},{16,0},{1,9},{9,25},{25,17},{17,1},{2,10},{10... | collective-permute-start | bytes 983048 | tf_op jit(solution)/shard_map/ppermute | solution.py:426
  592.7 57.0 %collective-permute-start.27 = (bf16[320,2048]{1,0:T(8,128)(2,1)}, bf16[320,2048]{1,0:T(8,128)(2,1)S(1)}, u32[]{:S(2)}, u32[]{:S(2)}) collective-permute-start(bf16[320,2048]{1,0:T(8,128)(2,1)} %get-tuple-element.103), channel_id=1, source_target_pairs={{0,8},{8,24},{24,16},{16,0},{1,9},{9,25},{25,17},{17,1},{2,10},{10... | collective-permute-start | bytes 3932168 | tf_op jit(solution)/shard_map/ppermute | solution.py:405
  595.6 54.1 %collective-permute-start.28 = (bf16[320,2048]{1,0:T(8,128)(2,1)}, bf16[320,2048]{1,0:T(8,128)(2,1)S(1)}, u32[]{:S(2)}, u32[]{:S(2)}) collective-permute-start(bf16[320,2048]{1,0:T(8,128)(2,1)} %get-tuple-element.104), channel_id=1, source_target_pairs={{8,0},{24,8},{16,24},{0,16},{9,1},{25,9},{17,25},{1,17},{10,2},{26... | collective-permute-start | bytes 3932168 | tf_op jit(solution)/shard_map/ppermute | solution.py:406
  600.5 51.8 %collective-permute-start.29 = (bf16[320,2048]{1,0:T(8,128)(2,1)}, bf16[320,2048]{1,0:T(8,128)(2,1)}, u32[]{:S(2)}, u32[]{:S(2)}) collective-permute-start(bf16[320,2048]{1,0:T(8,128)(2,1)} %add_convert_fusion.1), channel_id=1, source_target_pairs={{8,0},{24,8},{16,24},{0,16},{9,1},{25,9},{17,25},{1,17},{10,2},{26... | collective-permute-start | bytes 3932168 | tf_op jit(solution)/shard_map/ppermute | solution.py:400
  600.5 51.8 %collective-permute-start.26 = (bf16[320,2048]{1,0:T(8,128)(2,1)}, bf16[320,2048]{1,0:T(8,128)(2,1)}, u32[]{:S(2)}, u32[]{:S(2)}) collective-permute-start(bf16[320,2048]{1,0:T(8,128)(2,1)} %add_convert_fusion.2), channel_id=1, source_target_pairs={{0,8},{8,24},{24,16},{16,0},{1,9},{9,25},{25,17},{17,1},{2,10},{10... | collective-permute-start | bytes 3932168 | tf_op jit(solution)/shard_map/ppermute | solution.py:399
  (61 other events, 935.6 us)
Sparse Core Ops, SparseCore 0:
  9.6 84.7 all-gather.3
  96.6 80.5 all-gather.5
  178.8 80.5 all-gather.7
  272.6 89.5 reduce-scatter.4
  364.3 87.9 reduce-scatter.6
  454.4 48.3 reduce-scatter.8
  619.7 51.3 reduce-scatter.10

commit v11 on v10

--- a/solution.py
+++ b/solution.py
@@ -886,9 +886,9 @@
     far_part, far_sums = some_ranks([count - 1], turn)
     middle = list(range(count - 2, 0, -1))
     middle_sums, parts = 0.0, {count - 1: far_part[0]}
-    turn = after(turn, *far_part[0])
+    turn = after(turn, *far_part[0], *swapped[-1])
     for n in range(0, len(middle), 2):
-        some, some_sums = some_ranks(middle[n : n + 2], turn)
+        some, some_sums = some_ranks(middle[n : n + 2], turn, MUCH)
         turn = after(turn, *[piece for pieces in some for piece in pieces])
         middle_sums = middle_sums + some_sums
         parts.update(zip(middle[n : n + 2], some))
@@ -898,7 +898,7 @@
 
     grad_terms, hops = ring_reduce(lambda rank: parts[rank], "ctx")
     last_hops = [piece for hop in hops[1:3] for piece in hop]
-    gated = after(normed, turn, *hops[0], *swapped[-1], *d_attention)
+    gated = after(normed, turn, *hops[0], *d_attention)
     d_part = pair_grad(gated, grads, qkv_grads[-1], attended[-1])
     d_attention.append(scatter_rows(d_part))
     [own_part], own_sums = some_ranks([0], after(turn, d_part), MUCH)
@@ -925,7 +925,8 @@
             fc1_bias_wide,
         ]
     )
-    steps = exchange_steps(("fsdp", "ctx"))
+    near, across = exchange_steps(("fsdp",)), exchange_steps(("ctx",))
+    steps = near[:1] + across + near[1:]
     small = exchange(small, steps[:1])
     d_fc1, d_fc2 = d_fc1.astype(WIDE), d_fc2.T.astype(WIDE)
     output = place_output(
@@ -943,8 +944,9 @@
         after(tokens[0], output), own_grad, own_part[0], gain, grad_terms, local_rows // 4
     )
     small = exchange(after(small, d_tokens), steps[2:-1])
-    small = exchange(after(small, d_fc1, d_fc2), steps[-1:])
-    small = after(small, d_qkv, d_dense)
+    small = after(small, d_fc1, d_fc2)
+    axis, pairs = steps[-1]
+    small = after(small, d_qkv, d_dense) + lax.ppermute(small, axis, pairs)
     d_shift, with_normed, d_b_qkv, d_b_out, d_b_fc1 = jnp.split(
         small, [width, 2 * width, 5 * width, 6 * width]
     )

time: 702 us -> 738 us (1.051)
  waiting for transfers between devices: 106 us -> 138 us
    ppermute x3, waiting for transfers between devices: 55.6 us -> 100 us  [ring_pieces(): from_ahead = lax.ppermute(from_ahead, axis, behind)]
  transfers between devices with their start and end apart: 42 -> 42, of which waited for: 13 -> 11; matrix products, arithmetic and copies ran while one was open for 26% -> 26% of each run, Pallas kernels for 49% -> 47%
where the time goes in v11:
time: 738 us; the launch traced here: 730 us
  Pallas kernels  342 us (46%)
  waiting for transfers between devices  138 us (19%)
  matrix products  117 us (16%)
  local copies, waits for them, and re-layouts  47.3 us (6%)
  starting transfers between devices  35.8 us (5%)
  other arithmetic  34.4 us (5%)
  between operations  15.1 us (2%)
    pallas_call x2, Pallas kernels, attention(): pl.pallas_call(kernel, out_shape=(jax.ShapeDtypeStruct((blocks, blk, lane...  155 us
    dot_general x5, matrix products, dot(): return lax.dot_general(left, right, dims, preferred_element_type=WIDE)  117 us
    ppermute x3, waiting for transfers between devices, ring_pieces(): from_ahead = lax.ppermute(from_ahead, axis, behind)  100 us
    pallas_call x3, Pallas kernels, input_grad(): pl.pallas_call(functools.partial(input_grad_kernel, terms=len(grads), ran...  58.3 us
    pallas_call x1, Pallas kernels, expand(): pl.pallas_call(functools.partial(expand_kernel, spans=spans, cols=min(512...  42 us
    pallas_call x2, Pallas kernels, pair_grad(): pl.pallas_call(pair_grad_kernel, out_shape=jax.ShapeDtypeStruct((width, c...  33.7 us
    pallas_call x1, Pallas kernels, slope_grad(): pl.pallas_call(functools.partial(slope_grad_kernel, spans=spans, cols=min...  30.9 us
    ppermute x3, waiting for transfers between devices, ring_pieces(): lax.ppermute(from_ahead[half:], axis, behind)  20 us
  transfers between devices with their start and end apart: 42, of which 11 were waited for; matrix products, arithmetic and copies ran while one was open for 26% of the time, Pallas kernels for 47%

profile of v11, /device:TPU:0, one launch (start us, length us, event | category | flops | bytes accessed | tf_op | source)
XLA Modules:
  0.0 729.8 jit_solution(9465447420527836562)
XLA Ops:
  24.2 7.7 %negate_select_fusion = (f32[2560,128]{1,0:T(8,128)}, f32[2560,128]{1,0:T(8,128)}, f32[2560,128]{1,0:T(8,128)}) fusion(f32[128]{0:T(128)S(1)} %mul.123, s32[2560]{0:T(1024)S(1)} %get-tuple-element.190, s32[2560]{0:T(1024)S(1)} %get-tuple-element.191, s32[128]{0:T(128)S(1)} %get-tuple-element.194, s32[128]{0:T(128)S(1)} %get-tuple-element.195, ...), kind=kLoop, calls=%fused_computation.25 | loop fusion | flops 4587520 | bytes 3959424 | tf_op jit(solution)/shard_map/jit(_where)/select_n | solution.py:758
  31.9 43.3 %collective-permute-done.1.refs_2_ = bf16[640,2048]{1,0:T(8,128)(2,1)} collective-permute-done((bf16[640,2048]{1,0:T(8,128)(2,1)}, bf16[640,2048]{1,0:T(8,128)(2,1)}, u32[]{:S(2)}, u32[]{:S(2)}) %collective-permute-start.1) | collective-permute-done | bytes 2621472 | tf_op jit(solution)/shard_map/ppermute | solution.py:362
  91.5 20.0 %collective-permute-done.3.refs_4_ = bf16[320,2048]{1,0:T(8,128)(2,1)} collective-permute-done((bf16[320,2048]{1,0:T(8,128)(2,1)}, bf16[320,2048]{1,0:T(8,128)(2,1)}, u32[]{:S(2)}, u32[]{:S(2)}) %collective-permute-start.3) | collective-permute-done | bytes 1310752 | tf_op jit(solution)/shard_map/ppermute | solution.py:370
  114.9 42.0 %expand.1 = (bf16[2560,2048]{1,0:T(8,128)(2,1)}, bf16[2560,2048]{1,0:T(8,128)(2,1)}, bf16[2560,2048]{1,0:T(8,128)(2,1)}) custom-call(bf16[640,2048]{1,0:T(8,128)(2,1)} %fusion.6.refs_0_, bf16[640,2048]{1,0:T(8,128)(2,1)} %collective-permute-done.refs_1_, bf16[640,2048]{1,0:T(8,128)(2,1)} %collective-permute-done.1.refs_2_, ...), custom_call_target="tpu_custom_call" | custom-call | flops 21474836480 | bytes 41943040 | tf_op jit(solution)/shard_map/expand/pallas_call | solution.py:495
  156.9 12.3 %collective-permute-done.5.refs_2_ = bf16[640,2048]{1,0:T(8,128)(2,1)} collective-permute-done((bf16[640,2048]{1,0:T(8,128)(2,1)S(1)}, bf16[640,2048]{1,0:T(8,128)(2,1)}, u32[]{:S(2)}, u32[]{:S(2)}) %collective-permute-start.5) | collective-permute-done | bytes 2621472 | tf_op jit(solution)/shard_map/ppermute | solution.py:362
  177.2 26.6 %convolution_convert_fusion.refs_15_ = bf16[2560,2048]{1,0:T(8,128)(2,1)S(1)} fusion(bf16[2560,2048]{1,0:T(8,128)(2,1)} %get-tuple-element.71, bf16[2048,2048]{1,0:T(8,128)(2,1)} %all-gather.6.cloned.1.call-done.refs_5_), kind=kOutput, calls=%fused_computation.1 | convolution fusion | flops 21480079360 | bytes 29360128 | tf_op jit(solution)/shard_map/dot_general | solution.py:28
  210.6 30.9 %slope_grad.1 = (bf16[2560,2048]{1,0:T(8,128)(2,1)}, bf16[2560,2048]{1,0:T(8,128)(2,1)}, f32[8,2048]{1,0:T(8,128)S(1)}) custom-call(bf16[640,2048]{1,0:T(8,128)(2,1)S(1)} %bitcast.64, bf16[640,2048]{1,0:T(8,128)(2,1)} %collective-permute-done.4.refs_1_, bf16[640,2048]{1,0:T(8,128)(2,1)} %collective-permute-done.5.refs_2_, ...), custom_call_target="tpu_custom_call" | custom-call | flops 21474836480 | bytes 41943040 | tf_op jit(solution)/shard_map/slope_grad/pallas_call | solution.py:539
  243.6 28.9 %convolution_convert_fusion.2 = bf16[2048,2048]{1,0:T(8,128)(2,1)} fusion(bf16[2560,2048]{1,0:T(8,128)(2,1)} %get-tuple-element.86.y_ref, bf16[2560,2048]{1,0:T(8,128)(2,1)} %get-tuple-element.71), kind=kOutput, calls=%fused_computation.3 | convolution fusion | flops 21479030784 | bytes 29360128 | tf_op jit(solution)/shard_map/dot_general | solution.py:28
  274.2 4.2 add_convert_fusion.3
  280.6 22.3 %add_convert_fusion = bf16[2560,1536]{1,0:T(8,128)(2,1)} fusion(bf16[2560,2048]{1,0:T(8,128)(2,1)} %get-tuple-element.107.x_ref.refs_6_.refs_9_.refs_10_, f32[1536]{0:T(1024)S(1)} %reshape.234, bf16[2048,2048]{1,0:T(8,128)(2,1)} %all-gather.8.cloned.1.call-done.refs_3_.refs_4_.refs_6_.refs_7_), kind=kOutput, calls=%fused_computation | convolution fusion | flops 16113991680 | bytes 24647680 | tf_op jit(solution)/shard_map/dot_general | solution.py:28
  302.9 6.1 collective-permute-done.11.refs_19_
  310.4 10.5 %convolution_convert_fusion.3 = bf16[2560,512]{1,0:T(8,128)(2,1)} fusion(bf16[2560,2048]{1,0:T(8,128)(2,1)} %get-tuple-element.86.y_ref, bf16[2048,2048]{1,0:T(8,128)(2,1)} %all-gather.8.cloned.1.call-done.refs_3_.refs_4_.refs_6_.refs_7_), kind=kOutput, calls=%fused_computation.14 | convolution fusion | flops 5370019840 | bytes 15204352 | tf_op jit(solution)/shard_map/dot_general | solution.py:28
  320.9 28.9 %convolution_convert_fusion.1 = bf16[2048,2048]{1,0:T(8,128)(2,1)} fusion(bf16[2560,2048]{1,0:T(8,128)(2,1)} %get-tuple-element.107.x_ref.refs_6_.refs_9_.refs_10_, bf16[2560,2048]{1,0:T(8,128)(2,1)} %get-tuple-element.108.refs_2_.refs_5_), kind=kOutput, calls=%fused_computation.2 | convolution fusion | flops 21479030784 | bytes 29360128 | tf_op jit(solution)/shard_map/dot_general | solution.py:28
  356.0 44.5 %collective-permute-done.15.refs_10_ = bf16[2048,512]{1,0:T(8,128)(2,1)S(1)} collective-permute-done((bf16[2048,512]{1,0:T(8,128)(2,1)S(1)}, bf16[2048,512]{1,0:T(8,128)(2,1)S(1)}, u32[]{:S(2)}, u32[]{:S(2)}) %collective-permute-start.15) | collective-permute-done | bytes 2097184 | tf_op jit(solution)/shard_map/ppermute | solution.py:362
  405.5 77.2 %attention.2 = (bf16[40,64,256]{2,1,0:T(8,128)(2,1)}, bf16[40,64,768]{2,1,0:T(8,128)(2,1)}, f32[8,768]{1,0:T(8,128)}) custom-call(s32[40]{0:T(128)} %select_reduce_fusion.where_ref, bf16[40,64,1536]{2,1,0:T(8,128)(2,1)} %bitcast.67, bf16[40,64,1536]{2,1,0:T(8,128)(2,1)} %bitcast.68, bf16[40,64,1536]{2,1,0:T(8,128)(2,1)} %bitcast.69, ...), custom_call_target="tpu_custom_call" | custom-call | flops 1000000 | bytes 1000000 | tf_op jit(solution)/shard_map/attention/pallas_call | solution.py:297
  488.4 16.8 %pair_grad.2 = bf16[2048,1024]{1,0:T(8,128)(2,1)} custom-call(bf16[2560,2048]{1,0:T(8,128)(2,1)} %get-tuple-element.107.x_ref.refs_6_.refs_9_.refs_10_, bf16[2560,2048]{1,0:T(8,128)(2,1)} %get-tuple-element.86.y_ref, bf16[2560,768]{1,0:T(8,128)(2,1)} %bitcast.85, bf16[2560,256]{1,0:T(8,128)(2,1)} %bitcast.96), custom_call_target="tpu_custom_call" | custom-call | flops 1000000 | bytes 1000000 | tf_op jit(solution)/shard_map/pair_grad/pallas_call | solution.py:727
  505.1 77.5 %attention.3 = (bf16[40,64,256]{2,1,0:T(8,128)(2,1)}, bf16[40,64,768]{2,1,0:T(8,128)(2,1)}, f32[8,768]{1,0:T(8,128)}) custom-call(s32[40]{0:T(128)} %select_reduce_fusion.where_ref, bf16[40,64,1536]{2,1,0:T(8,128)(2,1)} %bitcast.71, bf16[40,64,1536]{2,1,0:T(8,128)(2,1)} %bitcast.72, bf16[40,64,1536]{2,1,0:T(8,128)(2,1)} %bitcast.73, ...), custom_call_target="tpu_custom_call" | custom-call | flops 1000000 | bytes 1000000 | tf_op jit(solution)/shard_map/attention/pallas_call | solution.py:297
  591.2 15.7 %input_grad.3 = (bf16[320,2048]{1,0:T(8,128)(2,1)}, bf16[320,2048]{1,0:T(8,128)(2,1)}, f32[2,2048]{1,0:T(2,128)}) custom-call(bf16[2560,768]{1,0:T(8,128)(2,1)} %bitcast.86, bf16[2560,768]{1,0:T(8,128)(2,1)} %bitcast.90, bf16[2560,2048]{1,0:T(8,128)(2,1)} %get-tuple-element.108.refs_2_.refs_5_, ...), custom_call_target="tpu_custom_call" | custom-call | flops 1000000 | bytes 1000000 | tf_op jit(solution)/shard_map/input_grad/pallas_call | solution.py:604
  609.1 26.9 %input_grad.4 = (bf16[320,2048]{1,0:T(8,128)(2,1)}, bf16[320,2048]{1,0:T(8,128)(2,1)}, bf16[320,2048]{1,0:T(8,128)(2,1)}, bf16[320,2048]{1,0:T(8,128)(2,1)}, f32[2,2048]{1,0:T(2,128)}) custom-call(bf16[2560,768]{1,0:T(8,128)(2,1)} %bitcast.87, bf16[2560,768]{1,0:T(8,128)(2,1)} %bitcast.91, bf16[2560,2048]{1,0:T(8,128)(2,1)} %get-tuple-element.108.refs_2_.refs_5_, ...), custom_call_target="tpu_custom_call" | custom-call | flops 99999997952 | bytes 1000000 | tf_op jit(solution)/shard_map/input_grad/pallas_call | solution.py:604
  644.7 17.0 %pair_grad.3 = bf16[2048,1024]{1,0:T(8,128)(2,1)} custom-call(bf16[2560,2048]{1,0:T(8,128)(2,1)} %get-tuple-element.107.x_ref.refs_6_.refs_9_.refs_10_, bf16[2560,2048]{1,0:T(8,128)(2,1)} %get-tuple-element.86.y_ref, bf16[2560,768]{1,0:T(8,128)(2,1)} %bitcast.93, bf16[2560,256]{1,0:T(8,128)(2,1)} %bitcast.95), custom_call_target="tpu_custom_call" | custom-call | flops 1000000 | bytes 1000000 | tf_op jit(solution)/shard_map/pair_grad/pallas_call | solution.py:727
  661.8 15.6 %input_grad.5 = (bf16[640,2048]{1,0:T(8,128)(2,1)}, f32[2,2048]{1,0:T(2,128)}) custom-call(bf16[2560,768]{1,0:T(8,128)(2,1)} %bitcast.89, bf16[2560,768]{1,0:T(8,128)(2,1)} %bitcast.94, bf16[2560,2048]{1,0:T(8,128)(2,1)} %get-tuple-element.108.refs_2_.refs_5_, bf16[2048,2048]{1,0:T(8,128)(2,1)} %all-gather.8.cloned.1.call-done.refs_3_.refs_4_.refs_6_.refs_7_, ...), custom_call_target="tpu_custom_call" | custom-call | flops 99999997952 | bytes 1000000 | tf_op jit(solution)/shard_map/input_grad/pallas_call | solution.py:604
  679.6 13.0 %place_output.1 = bf16[640,2048]{1,0:T(8,128)(2,1)} custom-call(bf16[640,256]{1,0:T(8,128)(2,1)} %bitcast.104, bf16[640,256]{1,0:T(8,128)(2,1)} %bitcast.105, bf16[640,256]{1,0:T(8,128)(2,1)} %copy-done.24, bf16[640,256]{1,0:T(8,128)(2,1)} %copy-done.27, bf16[640,256]{1,0:T(8,128)(2,1)} %copy-done.22, bf16[640,256]{1,0:T(8,128)(2,1)} %copy-done.25, ...), custom_call_target="tpu_custom_call" | custom-call | flops 1000000 | bytes 1000000 | tf_op jit(solution)/shard_map/place_output/pallas_call | solution.py:654
  693.5 9.0 %token_grad.1 = bf16[640,2048]{1,0:T(8,128)(2,1)} custom-call(bf16[640,2048]{1,0:T(8,128)(2,1)} %bitcast.84, bf16[640,2048]{1,0:T(8,128)(2,1)} %bitcast.61, bf16[640,2048]{1,0:T(8,128)(2,1)} %get-tuple-element.109.own_ref, f32[1,2048]{1,0:T(1,128)S(1)} %bitcast.65, bf16[320,2048]{1,0:T(8,128)(2,1)} %collective-permute-done.26.refs_0_, ...), custom_call_target="tpu_custom_call" | custom-call | flops 1000000 | bytes 1000000 | tf_op jit(solution)/shard_map/token_grad/pallas_call | solution.py:698
  707.9 4.3 collective-permute-done.33
  (247 shorter events, 113.5 us)
Async XLA Ops:
  7.2 107.7 %all-gather.4.cloned.1.call-start = ((), (), s32[]{:S(2)}) async-start(), calls=%async_computation.4 | async-start | bytes 9437184 | tf_op jit(solution)/shard_map/all_gather | solution.py:811
  7.9 169.3 %all-gather.6.cloned.1.call-start = ((), (), s32[]{:S(2)}) async-start(), calls=%async_computation.5 | async-start | bytes 9437184 | tf_op jit(solution)/shard_map/all_gather | solution.py:811
  15.1 60.1 %collective-permute-start.1 = (bf16[640,2048]{1,0:T(8,128)(2,1)}, bf16[640,2048]{1,0:T(8,128)(2,1)}, u32[]{:S(2)}, u32[]{:S(2)}) collective-permute-start(bf16[640,2048]{1,0:T(8,128)(2,1)} %fusion.6.refs_0_), channel_id=1, source_target_pairs={{8,0},{24,8},{16,24},{0,16},{9,1},{25,9},{17,25},{1,17},{10,2},{26... | collective-permute-start | bytes 7864328 | tf_op jit(solution)/shard_map/ppermute | solution.py:362
  18.0 58.6 %collective-permute-start = (bf16[640,2048]{1,0:T(8,128)(2,1)}, bf16[640,2048]{1,0:T(8,128)(2,1)}, u32[]{:S(2)}, u32[]{:S(2)}) collective-permute-start(bf16[640,2048]{1,0:T(8,128)(2,1)} %fusion.6.refs_0_), channel_id=1, source_target_pairs={{0,8},{8,24},{24,16},{16,0},{1,9},{9,25},{25,17},{17,1},{2,10},{10... | collective-permute-start | bytes 7864328 | tf_op jit(solution)/shard_map/ppermute | solution.py:361
  76.7 203.9 %all-gather.8.cloned.1.call-start = ((), (), s32[]{:S(2)}) async-start(), calls=%async_computation.6 | async-start | bytes 9437184 | tf_op jit(solution)/shard_map/all_gather | solution.py:811
  112.8 375.6 %reduce-scatter.5.cloned.1.call-start = ((), (), s32[]{:S(2)}) async-start(), calls=%async_computation.7 | async-start | bytes 9437184 | tf_op jit(solution)/shard_map/reduce_scatter | solution.py:814
  112.8 56.4 %collective-permute-start.5 = (bf16[640,2048]{1,0:T(8,128)(2,1)S(1)}, bf16[640,2048]{1,0:T(8,128)(2,1)}, u32[]{:S(2)}, u32[]{:S(2)}) collective-permute-start(bf16[640,2048]{1,0:T(8,128)(2,1)S(1)} %bitcast.62), channel_id=1, source_target_pairs={{8,0},{24,8},{16,24},{0,16},{9,1},{25,9},{17,25},{1,17},{10,2},{26... | collective-permute-start | bytes 7864328 | tf_op jit(solution)/shard_map/ppermute | solution.py:362
  113.5 56.2 %collective-permute-start.4 = (bf16[640,2048]{1,0:T(8,128)(2,1)S(1)}, bf16[640,2048]{1,0:T(8,128)(2,1)}, u32[]{:S(2)}, u32[]{:S(2)}) collective-permute-start(bf16[640,2048]{1,0:T(8,128)(2,1)S(1)} %bitcast.63), channel_id=1, source_target_pairs={{0,8},{8,24},{24,16},{16,0},{1,9},{9,25},{25,17},{17,1},{2,10},{10... | collective-permute-start | bytes 7864328 | tf_op jit(solution)/shard_map/ppermute | solution.py:361
  272.5 318.7 %reduce-scatter.7.cloned.1.call-start = ((), (), s32[]{:S(2)}) async-start(), calls=%async_computation.8 | async-start | bytes 9437184 | tf_op jit(solution)/shard_map/reduce_scatter | solution.py:814
  349.9 294.7 %reduce-scatter.9.cloned.1.call-start = ((), (), s32[]{:S(2)}) async-start(), calls=%async_computation.9 | async-start | bytes 4718592 | tf_op jit(solution)/shard_map/reduce_scatter | solution.py:814
  351.9 48.6 %collective-permute-start.15 = (bf16[2048,512]{1,0:T(8,128)(2,1)S(1)}, bf16[2048,512]{1,0:T(8,128)(2,1)S(1)}, u32[]{:S(2)}, u32[]{:S(2)}) collective-permute-start(bf16[2048,512]{1,0:T(8,128)(2,1)S(1)} %slice.160.refs_8_), channel_id=1, source_target_pairs={{8,0},{24,8},{16,24},{0,16},{9,1},{25,9},{17,25},{1,17},{10,2},{26... | collective-permute-start | bytes 6291464 | tf_op jit(solution)/shard_map/ppermute | solution.py:362
  353.4 49.7 %collective-permute-start.14 = (bf16[2048,512]{1,0:T(8,128)(2,1)S(1)}, bf16[2048,512]{1,0:T(8,128)(2,1)S(1)}, u32[]{:S(2)}, u32[]{:S(2)}) collective-permute-start(bf16[2048,512]{1,0:T(8,128)(2,1)S(1)} %slice.160.refs_8_), channel_id=1, source_target_pairs={{0,8},{8,24},{24,16},{16,0},{1,9},{9,25},{25,17},{17,1},{2,10},{10... | collective-permute-start | bytes 6291464 | tf_op jit(solution)/shard_map/ppermute | solution.py:361
  354.0 132.4 %collective-permute-start.12 = (bf16[320,2048]{1,0:T(8,128)(2,1)S(1)}, bf16[320,2048]{1,0:T(8,128)(2,1)}, u32[]{:S(2)}, u32[]{:S(2)}) collective-permute-start(bf16[320,2048]{1,0:T(8,128)(2,1)S(1)} %copy-done.13), channel_id=1, source_target_pairs={{0,8},{8,24},{24,16},{16,0},{1,9},{9,25},{25,17},{17,1},{2,10},{10... | collective-permute-start | bytes 3932168 | tf_op jit(solution)/shard_map/ppermute | solution.py:405
  355.3 131.7 %collective-permute-start.13 = (bf16[320,2048]{1,0:T(8,128)(2,1)S(1)}, bf16[320,2048]{1,0:T(8,128)(2,1)}, u32[]{:S(2)}, u32[]{:S(2)}) collective-permute-start(bf16[320,2048]{1,0:T(8,128)(2,1)S(1)} %copy-done.12), channel_id=1, source_target_pairs={{8,0},{24,8},{16,24},{0,16},{9,1},{25,9},{17,25},{1,17},{10,2},{26... | collective-permute-start | bytes 3932168 | tf_op jit(solution)/shard_map/ppermute | solution.py:406
  401.6 189.6 %collective-permute-start.23 = (bf16[1024,512]{1,0:T(8,128)(2,1)}, bf16[1024,512]{1,0:T(8,128)(2,1)}, u32[]{:S(2)}, u32[]{:S(2)}) collective-permute-start(bf16[1024,512]{1,0:T(8,128)(2,1)} %slice.164), channel_id=1, source_target_pairs={{8,0},{24,8},{16,24},{0,16},{9,1},{25,9},{17,25},{1,17},{10,2},{26... | collective-permute-start | bytes 3145736 | tf_op jit(solution)/shard_map/ppermute | solution.py:370
  404.8 186.5 %collective-permute-start.22 = (bf16[1024,512]{1,0:T(8,128)(2,1)}, bf16[1024,512]{1,0:T(8,128)(2,1)}, u32[]{:S(2)}, u32[]{:S(2)}) collective-permute-start(bf16[1024,512]{1,0:T(8,128)(2,1)} %slice.163), channel_id=1, source_target_pairs={{0,8},{8,24},{24,16},{16,0},{1,9},{9,25},{25,17},{17,1},{2,10},{10... | collective-permute-start | bytes 3145736 | tf_op jit(solution)/shard_map/ppermute | solution.py:369
  484.9 99.9 %collective-permute-start.18 = (bf16[640,256]{1,0:T(8,128)(2,1)}, bf16[640,256]{1,0:T(8,128)(2,1)S(1)}, u32[]{:S(2)}, u32[]{:S(2)}) collective-permute-start(bf16[640,256]{1,0:T(8,128)(2,1)} %bitcast.22), channel_id=1, source_target_pairs={{0,16},{8,0},{24,8},{16,24},{1,17},{9,1},{25,9},{17,25},{2,18},{10... | collective-permute-start | bytes 983048 | tf_op jit(solution)/shard_map/ppermute | solution.py:426
  486.4 99.1 %collective-permute-start.20 = (bf16[640,256]{1,0:T(8,128)(2,1)}, bf16[640,256]{1,0:T(8,128)(2,1)S(1)}, u32[]{:S(2)}, u32[]{:S(2)}) collective-permute-start(bf16[640,256]{1,0:T(8,128)(2,1)} %bitcast.24), channel_id=1, source_target_pairs={{0,24},{8,16},{24,0},{16,8},{1,25},{9,17},{25,1},{17,9},{2,26},{10... | collective-permute-start | bytes 983048 | tf_op jit(solution)/shard_map/ppermute | solution.py:426
  486.9 100.9 %collective-permute-start.16 = (bf16[640,256]{1,0:T(8,128)(2,1)S(1)}, bf16[640,256]{1,0:T(8,128)(2,1)S(1)}, u32[]{:S(2)}, u32[]{:S(2)}) collective-permute-start(bf16[640,256]{1,0:T(8,128)(2,1)S(1)} %bitcast.110), channel_id=1, source_target_pairs={{0,8},{8,24},{24,16},{16,0},{1,9},{9,25},{25,17},{17,1},{2,10},{10... | collective-permute-start | bytes 983048 | tf_op jit(solution)/shard_map/ppermute | solution.py:426
  590.5 122.5 %reduce-scatter.11.cloned.1.call-start = ((), (), s32[]{:S(2)}) async-start(), calls=%async_computation.10 | async-start | bytes 4718592 | tf_op jit(solution)/shard_map/reduce_scatter | solution.py:814
  636.1 57.3 %collective-permute-start.27 = (bf16[320,2048]{1,0:T(8,128)(2,1)}, bf16[320,2048]{1,0:T(8,128)(2,1)S(1)}, u32[]{:S(2)}, u32[]{:S(2)}) collective-permute-start(bf16[320,2048]{1,0:T(8,128)(2,1)} %get-tuple-element.103), channel_id=1, source_target_pairs={{0,8},{8,24},{24,16},{16,0},{1,9},{9,25},{25,17},{17,1},{2,10},{10... | collective-permute-start | bytes 3932168 | tf_op jit(solution)/shard_map/ppermute | solution.py:405
  636.3 57.1 %collective-permute-start.28 = (bf16[320,2048]{1,0:T(8,128)(2,1)}, bf16[320,2048]{1,0:T(8,128)(2,1)S(1)}, u32[]{:S(2)}, u32[]{:S(2)}) collective-permute-start(bf16[320,2048]{1,0:T(8,128)(2,1)} %get-tuple-element.104), channel_id=1, source_target_pairs={{8,0},{24,8},{16,24},{0,16},{9,1},{25,9},{17,25},{1,17},{10,2},{26... | collective-permute-start | bytes 3932168 | tf_op jit(solution)/shard_map/ppermute | solution.py:406
  641.1 52.3 %collective-permute-start.29 = (bf16[320,2048]{1,0:T(8,128)(2,1)}, bf16[320,2048]{1,0:T(8,128)(2,1)}, u32[]{:S(2)}, u32[]{:S(2)}) collective-permute-start(bf16[320,2048]{1,0:T(8,128)(2,1)} %add_convert_fusion.1), channel_id=1, source_target_pairs={{8,0},{24,8},{16,24},{0,16},{9,1},{25,9},{17,25},{1,17},{10,2},{26... | collective-permute-start | bytes 3932168 | tf_op jit(solution)/shard_map/ppermute | solution.py:400
  644.1 49.3 %collective-permute-start.26 = (bf16[320,2048]{1,0:T(8,128)(2,1)}, bf16[320,2048]{1,0:T(8,128)(2,1)}, u32[]{:S(2)}, u32[]{:S(2)}) collective-permute-start(bf16[320,2048]{1,0:T(8,128)(2,1)} %add_convert_fusion.2), channel_id=1, source_target_pairs={{0,8},{8,24},{24,16},{16,0},{1,9},{9,25},{25,17},{17,1},{2,10},{10... | collective-permute-start | bytes 3932168 | tf_op jit(solution)/shard_map/ppermute | solution.py:399
  (61 other events, 819.3 us)
Sparse Core Ops, SparseCore 0:
  9.6 84.7 all-gather.3
  96.6 80.5 all-gather.5
  178.8 80.5 all-gather.7
  272.6 89.7 reduce-scatter.4
  364.6 87.9 reduce-scatter.6
  590.6 47.5 reduce-scatter.8
  661.8 47.2 reduce-scatter.10

commit v12 on v11

--- a/solution.py
+++ b/solution.py
@@ -851,7 +851,6 @@
     d_fc1_part = dot(gated, expanded_grad, TN).astype(LOW)
     d_fc1 = scatter_rows(d_fc1_part)
 
-    dense_pieces = ring_pieces(after(dense_turned, *second), "ctx")
 
     attended, qkv_grads, qkv_sums, d_attention, swapped = [], [], [], [], []
     ordered = (d_fc1_part,)
@@ -859,6 +858,8 @@
         got, got_grads, got_sums = attention(
             after(qkv, *ordered), attended_grad, where, tabs, lanes, which, head_dim
         )
+        if which == 0:
+            dense_pieces = ring_pieces(after(dense_turned, *second), "ctx", gate=(got,))
         attended.append(got)
         qkv_grads.append(got_grads)
         qkv_sums.append(got_sums)

time: 738 us -> 691 us (0.936)
  waiting for transfers between devices: 138 us -> 92.8 us
    ppermute x3, waiting for transfers between devices: 100 us -> 55.6 us  [ring_pieces(): from_ahead = lax.ppermute(from_ahead, axis, behind)]
    unnamed x92 -> x90, local copies, waits for them, and re-layouts: 16.8 us -> 16.2 us
  transfers between devices with their start and end apart: 42 -> 42, of which waited for: 11 -> 11; matrix products, arithmetic and copies ran while one was open for 26% -> 27% of each run, Pallas kernels for 47% -> 50%
where the time goes in v12:
time: 691 us; the launch traced here: 682 us
  Pallas kernels  341 us (49%)
  matrix products  117 us (17%)
  waiting for transfers between devices  92.8 us (13%)
  local copies, waits for them, and re-layouts  45.4 us (7%)
  starting transfers between devices  36 us (5%)
  other arithmetic  34.5 us (5%)
  between operations  15 us (2%)
    pallas_call x2, Pallas kernels, attention(): pl.pallas_call(kernel, out_shape=(jax.ShapeDtypeStruct((blocks, blk, lane...  154 us
    dot_general x5, matrix products, dot(): return lax.dot_general(left, right, dims, preferred_element_type=WIDE)  117 us
    pallas_call x3, Pallas kernels, input_grad(): pl.pallas_call(functools.partial(input_grad_kernel, terms=len(grads), ran...  58.5 us
    ppermute x3, waiting for transfers between devices, ring_pieces(): from_ahead = lax.ppermute(from_ahead, axis, behind)  55.6 us
    pallas_call x1, Pallas kernels, expand(): pl.pallas_call(functools.partial(expand_kernel, spans=spans, cols=min(512...  42 us
    pallas_call x2, Pallas kernels, pair_grad(): pl.pallas_call(pair_grad_kernel, out_shape=jax.ShapeDtypeStruct((width, c...  33.8 us
    pallas_call x1, Pallas kernels, slope_grad(): pl.pallas_call(functools.partial(slope_grad_kernel, spans=spans, cols=min...  30.9 us
    ppermute x3, waiting for transfers between devices, ring_pieces(): lax.ppermute(from_ahead[half:], axis, behind)  20 us
  transfers between devices with their start and end apart: 42, of which 11 were waited for; matrix products, arithmetic and copies ran while one was open for 27% of the time, Pallas kernels for 50%

profile of v12, /device:TPU:0, one launch (start us, length us, event | category | flops | bytes accessed | tf_op | source)
XLA Modules:
  0.0 682.4 jit_solution(1431781809530933622)
XLA Ops:
  15.1 3.0 collective-permute-start.1
  24.2 7.7 %negate_select_fusion = (f32[2560,128]{1,0:T(8,128)}, f32[2560,128]{1,0:T(8,128)}, f32[2560,128]{1,0:T(8,128)}) fusion(f32[128]{0:T(128)S(1)} %mul.123, s32[2560]{0:T(1024)S(1)} %get-tuple-element.194, s32[2560]{0:T(1024)S(1)} %get-tuple-element.195, s32[128]{0:T(128)S(1)} %get-tuple-element.198, s32[128]{0:T(128)S(1)} %get-tuple-element.199, ...), kind=kLoop, calls=%fused_computation.25 | loop fusion | flops 4587520 | bytes 3959424 | tf_op jit(solution)/shard_map/jit(_where)/select_n | solution.py:758
  31.9 43.3 %collective-permute-done.1.refs_2_ = bf16[640,2048]{1,0:T(8,128)(2,1)} collective-permute-done((bf16[640,2048]{1,0:T(8,128)(2,1)}, bf16[640,2048]{1,0:T(8,128)(2,1)}, u32[]{:S(2)}, u32[]{:S(2)}) %collective-permute-start.1) | collective-permute-done | bytes 2621472 | tf_op jit(solution)/shard_map/ppermute | solution.py:362
  91.6 20.0 %collective-permute-done.3.refs_4_ = bf16[320,2048]{1,0:T(8,128)(2,1)} collective-permute-done((bf16[320,2048]{1,0:T(8,128)(2,1)}, bf16[320,2048]{1,0:T(8,128)(2,1)}, u32[]{:S(2)}, u32[]{:S(2)}) %collective-permute-start.3) | collective-permute-done | bytes 1310752 | tf_op jit(solution)/shard_map/ppermute | solution.py:370
  114.9 42.0 %expand.1 = (bf16[2560,2048]{1,0:T(8,128)(2,1)}, bf16[2560,2048]{1,0:T(8,128)(2,1)}, bf16[2560,2048]{1,0:T(8,128)(2,1)}) custom-call(bf16[640,2048]{1,0:T(8,128)(2,1)} %fusion.6.refs_0_, bf16[640,2048]{1,0:T(8,128)(2,1)} %collective-permute-done.refs_1_, bf16[640,2048]{1,0:T(8,128)(2,1)} %collective-permute-done.1.refs_2_, ...), custom_call_target="tpu_custom_call" | custom-call | flops 21474836480 | bytes 41943040 | tf_op jit(solution)/shard_map/expand/pallas_call | solution.py:495
  156.9 12.3 %collective-permute-done.5.refs_2_ = bf16[640,2048]{1,0:T(8,128)(2,1)} collective-permute-done((bf16[640,2048]{1,0:T(8,128)(2,1)S(1)}, bf16[640,2048]{1,0:T(8,128)(2,1)}, u32[]{:S(2)}, u32[]{:S(2)}) %collective-permute-start.5) | collective-permute-done | bytes 2621472 | tf_op jit(solution)/shard_map/ppermute | solution.py:362
  176.9 26.6 %convolution_convert_fusion.refs_15_ = bf16[2560,2048]{1,0:T(8,128)(2,1)S(1)} fusion(bf16[2560,2048]{1,0:T(8,128)(2,1)} %get-tuple-element.73, bf16[2048,2048]{1,0:T(8,128)(2,1)} %all-gather.6.cloned.1.call-done.refs_5_), kind=kOutput, calls=%fused_computation.1 | convolution fusion | flops 21480079360 | bytes 29360128 | tf_op jit(solution)/shard_map/dot_general | solution.py:28
  210.3 30.9 %slope_grad.1 = (bf16[2560,2048]{1,0:T(8,128)(2,1)}, bf16[2560,2048]{1,0:T(8,128)(2,1)}, f32[8,2048]{1,0:T(8,128)S(1)}) custom-call(bf16[640,2048]{1,0:T(8,128)(2,1)S(1)} %bitcast.64, bf16[640,2048]{1,0:T(8,128)(2,1)} %collective-permute-done.4.refs_1_, bf16[640,2048]{1,0:T(8,128)(2,1)} %collective-permute-done.5.refs_2_, ...), custom_call_target="tpu_custom_call" | custom-call | flops 21474836480 | bytes 41943040 | tf_op jit(solution)/shard_map/slope_grad/pallas_call | solution.py:539
  243.2 28.8 %convolution_convert_fusion.2 = bf16[2048,2048]{1,0:T(8,128)(2,1)} fusion(bf16[2560,2048]{1,0:T(8,128)(2,1)} %get-tuple-element.88.y_ref, bf16[2560,2048]{1,0:T(8,128)(2,1)} %get-tuple-element.73), kind=kOutput, calls=%fused_computation.3 | convolution fusion | flops 21479030784 | bytes 29360128 | tf_op jit(solution)/shard_map/dot_general | solution.py:28
  273.8 4.2 add_convert_fusion.3
  280.4 22.3 %add_convert_fusion = bf16[2560,1536]{1,0:T(8,128)(2,1)} fusion(bf16[2560,2048]{1,0:T(8,128)(2,1)} %get-tuple-element.111.x_ref.refs_6_.refs_9_.refs_10_, f32[1536]{0:T(1024)S(1)} %reshape.234, bf16[2048,2048]{1,0:T(8,128)(2,1)} %all-gather.8.cloned.1.call-done.refs_3_.refs_4_.refs_6_.refs_7_), kind=kOutput, calls=%fused_computation | convolution fusion | flops 16113991680 | bytes 24647680 | tf_op jit(solution)/shard_map/dot_general | solution.py:28
  302.7 5.6 collective-permute-done.11.refs_19_
  310.0 10.5 %convolution_convert_fusion.3 = bf16[2560,512]{1,0:T(8,128)(2,1)} fusion(bf16[2560,2048]{1,0:T(8,128)(2,1)} %get-tuple-element.88.y_ref, bf16[2048,2048]{1,0:T(8,128)(2,1)} %all-gather.8.cloned.1.call-done.refs_3_.refs_4_.refs_6_.refs_7_), kind=kOutput, calls=%fused_computation.14 | convolution fusion | flops 5370019840 | bytes 15204352 | tf_op jit(solution)/shard_map/dot_general | solution.py:28
  320.5 29.0 %convolution_convert_fusion.1 = bf16[2048,2048]{1,0:T(8,128)(2,1)} fusion(bf16[2560,2048]{1,0:T(8,128)(2,1)} %get-tuple-element.111.x_ref.refs_6_.refs_9_.refs_10_, bf16[2560,2048]{1,0:T(8,128)(2,1)} %get-tuple-element.112.refs_2_.refs_5_), kind=kOutput, calls=%fused_computation.2 | convolution fusion | flops 21479030784 | bytes 29360128 | tf_op jit(solution)/shard_map/dot_general | solution.py:28
  355.5 77.1 %attention.2 = (bf16[40,64,256]{2,1,0:T(8,128)(2,1)}, bf16[40,64,768]{2,1,0:T(8,128)(2,1)}, f32[8,768]{1,0:T(8,128)}) custom-call(s32[40]{0:T(128)} %select_reduce_fusion.where_ref, bf16[40,64,1536]{2,1,0:T(8,128)(2,1)} %bitcast.67, bf16[40,64,1536]{2,1,0:T(8,128)(2,1)} %bitcast.68, bf16[40,64,1536]{2,1,0:T(8,128)(2,1)} %bitcast.69, ...), custom_call_target="tpu_custom_call" | custom-call | flops 1000000 | bytes 1000000 | tf_op jit(solution)/shard_map/attention/pallas_call | solution.py:297
  441.8 16.9 %pair_grad.2 = bf16[2048,1024]{1,0:T(8,128)(2,1)} custom-call(bf16[2560,2048]{1,0:T(8,128)(2,1)} %get-tuple-element.111.x_ref.refs_6_.refs_9_.refs_10_, bf16[2560,2048]{1,0:T(8,128)(2,1)} %get-tuple-element.88.y_ref, bf16[2560,768]{1,0:T(8,128)(2,1)} %bitcast.85, bf16[2560,256]{1,0:T(8,128)(2,1)} %bitcast.96), custom_call_target="tpu_custom_call" | custom-call | flops 1000000 | bytes 1000000 | tf_op jit(solution)/shard_map/pair_grad/pallas_call | solution.py:727
  458.6 77.1 %attention.3 = (bf16[40,64,256]{2,1,0:T(8,128)(2,1)}, bf16[40,64,768]{2,1,0:T(8,128)(2,1)}, f32[8,768]{1,0:T(8,128)}) custom-call(s32[40]{0:T(128)} %select_reduce_fusion.where_ref, bf16[40,64,1536]{2,1,0:T(8,128)(2,1)} %bitcast.71, bf16[40,64,1536]{2,1,0:T(8,128)(2,1)} %bitcast.72, bf16[40,64,1536]{2,1,0:T(8,128)(2,1)} %bitcast.73, ...), custom_call_target="tpu_custom_call" | custom-call | flops 1000000 | bytes 1000000 | tf_op jit(solution)/shard_map/attention/pallas_call | solution.py:297
  544.4 16.0 %input_grad.3 = (bf16[320,2048]{1,0:T(8,128)(2,1)}, bf16[320,2048]{1,0:T(8,128)(2,1)}, f32[2,2048]{1,0:T(2,128)}) custom-call(bf16[2560,768]{1,0:T(8,128)(2,1)} %bitcast.86, bf16[2560,768]{1,0:T(8,128)(2,1)} %bitcast.90, bf16[2560,2048]{1,0:T(8,128)(2,1)} %get-tuple-element.112.refs_2_.refs_5_, ...), custom_call_target="tpu_custom_call" | custom-call | flops 1000000 | bytes 1000000 | tf_op jit(solution)/shard_map/input_grad/pallas_call | solution.py:604
  562.5 26.9 %input_grad.4 = (bf16[320,2048]{1,0:T(8,128)(2,1)}, bf16[320,2048]{1,0:T(8,128)(2,1)}, bf16[320,2048]{1,0:T(8,128)(2,1)}, bf16[320,2048]{1,0:T(8,128)(2,1)}, f32[2,2048]{1,0:T(2,128)}) custom-call(bf16[2560,768]{1,0:T(8,128)(2,1)} %bitcast.87, bf16[2560,768]{1,0:T(8,128)(2,1)} %bitcast.91, bf16[2560,2048]{1,0:T(8,128)(2,1)} %get-tuple-element.112.refs_2_.refs_5_, ...), custom_call_target="tpu_custom_call" | custom-call | flops 99999997952 | bytes 1000000 | tf_op jit(solution)/shard_map/input_grad/pallas_call | solution.py:604
  598.1 16.9 %pair_grad.3 = bf16[2048,1024]{1,0:T(8,128)(2,1)} custom-call(bf16[2560,2048]{1,0:T(8,128)(2,1)} %get-tuple-element.111.x_ref.refs_6_.refs_9_.refs_10_, bf16[2560,2048]{1,0:T(8,128)(2,1)} %get-tuple-element.88.y_ref, bf16[2560,768]{1,0:T(8,128)(2,1)} %bitcast.93, bf16[2560,256]{1,0:T(8,128)(2,1)} %bitcast.95), custom_call_target="tpu_custom_call" | custom-call | flops 1000000 | bytes 1000000 | tf_op jit(solution)/shard_map/pair_grad/pallas_call | solution.py:727
  615.1 15.6 %input_grad.5 = (bf16[640,2048]{1,0:T(8,128)(2,1)}, f32[2,2048]{1,0:T(2,128)}) custom-call(bf16[2560,768]{1,0:T(8,128)(2,1)} %bitcast.89, bf16[2560,768]{1,0:T(8,128)(2,1)} %bitcast.94, bf16[2560,2048]{1,0:T(8,128)(2,1)} %get-tuple-element.112.refs_2_.refs_5_, bf16[2048,2048]{1,0:T(8,128)(2,1)} %all-gather.8.cloned.1.call-done.refs_3_.refs_4_.refs_6_.refs_7_, ...), custom_call_target="tpu_custom_call" | custom-call | flops 99999997952 | bytes 1000000 | tf_op jit(solution)/shard_map/input_grad/pallas_call | solution.py:604
  632.9 13.0 %place_output.1 = bf16[640,2048]{1,0:T(8,128)(2,1)} custom-call(bf16[640,256]{1,0:T(8,128)(2,1)} %bitcast.104, bf16[640,256]{1,0:T(8,128)(2,1)} %bitcast.105, bf16[640,256]{1,0:T(8,128)(2,1)} %copy-done.23, bf16[640,256]{1,0:T(8,128)(2,1)} %copy-done.26, bf16[640,256]{1,0:T(8,128)(2,1)} %copy-done.21, bf16[640,256]{1,0:T(8,128)(2,1)} %copy-done.24, ...), custom_call_target="tpu_custom_call" | custom-call | flops 1000000 | bytes 1000000 | tf_op jit(solution)/shard_map/place_output/pallas_call | solution.py:654
  646.9 9.0 %token_grad.1 = bf16[640,2048]{1,0:T(8,128)(2,1)} custom-call(bf16[640,2048]{1,0:T(8,128)(2,1)} %bitcast.84, bf16[640,2048]{1,0:T(8,128)(2,1)} %bitcast.61, bf16[640,2048]{1,0:T(8,128)(2,1)} %get-tuple-element.113.own_ref, f32[1,2048]{1,0:T(1,128)S(1)} %bitcast.65, bf16[320,2048]{1,0:T(8,128)(2,1)} %collective-permute-done.26.refs_0_, ...), custom_call_target="tpu_custom_call" | custom-call | flops 1000000 | bytes 1000000 | tf_op jit(solution)/shard_map/token_grad/pallas_call | solution.py:698
  661.1 4.2 collective-permute-done.33
  (245 shorter events, 108.5 us)
Async XLA Ops:
  7.2 107.7 %all-gather.4.cloned.1.call-start = ((), (), s32[]{:S(2)}) async-start(), calls=%async_computation.4 | async-start | bytes 9437184 | tf_op jit(solution)/shard_map/all_gather | solution.py:811
  7.9 169.0 %all-gather.6.cloned.1.call-start = ((), (), s32[]{:S(2)}) async-start(), calls=%async_computation.5 | async-start | bytes 9437184 | tf_op jit(solution)/shard_map/all_gather | solution.py:811
  15.1 60.1 %collective-permute-start.1 = (bf16[640,2048]{1,0:T(8,128)(2,1)}, bf16[640,2048]{1,0:T(8,128)(2,1)}, u32[]{:S(2)}, u32[]{:S(2)}) collective-permute-start(bf16[640,2048]{1,0:T(8,128)(2,1)} %fusion.6.refs_0_), channel_id=1, source_target_pairs={{8,0},{24,8},{16,24},{0,16},{9,1},{25,9},{17,25},{1,17},{10,2},{26... | collective-permute-start | bytes 7864328 | tf_op jit(solution)/shard_map/ppermute | solution.py:362
  18.0 58.6 %collective-permute-start = (bf16[640,2048]{1,0:T(8,128)(2,1)}, bf16[640,2048]{1,0:T(8,128)(2,1)}, u32[]{:S(2)}, u32[]{:S(2)}) collective-permute-start(bf16[640,2048]{1,0:T(8,128)(2,1)} %fusion.6.refs_0_), channel_id=1, source_target_pairs={{0,8},{8,24},{24,16},{16,0},{1,9},{9,25},{25,17},{17,1},{2,10},{10... | collective-permute-start | bytes 7864328 | tf_op jit(solution)/shard_map/ppermute | solution.py:361
  76.7 203.7 %all-gather.8.cloned.1.call-start = ((), (), s32[]{:S(2)}) async-start(), calls=%async_computation.6 | async-start | bytes 9437184 | tf_op jit(solution)/shard_map/all_gather | solution.py:811
  112.8 329.0 %reduce-scatter.5.cloned.1.call-start = ((), (), s32[]{:S(2)}) async-start(), calls=%async_computation.7 | async-start | bytes 9437184 | tf_op jit(solution)/shard_map/reduce_scatter | solution.py:814
  112.8 56.4 %collective-permute-start.5 = (bf16[640,2048]{1,0:T(8,128)(2,1)S(1)}, bf16[640,2048]{1,0:T(8,128)(2,1)}, u32[]{:S(2)}, u32[]{:S(2)}) collective-permute-start(bf16[640,2048]{1,0:T(8,128)(2,1)S(1)} %bitcast.62), channel_id=1, source_target_pairs={{8,0},{24,8},{16,24},{0,16},{9,1},{25,9},{17,25},{1,17},{10,2},{26... | collective-permute-start | bytes 7864328 | tf_op jit(solution)/shard_map/ppermute | solution.py:362
  113.5 56.2 %collective-permute-start.4 = (bf16[640,2048]{1,0:T(8,128)(2,1)S(1)}, bf16[640,2048]{1,0:T(8,128)(2,1)}, u32[]{:S(2)}, u32[]{:S(2)}) collective-permute-start(bf16[640,2048]{1,0:T(8,128)(2,1)S(1)} %bitcast.63), channel_id=1, source_target_pairs={{0,8},{8,24},{24,16},{16,0},{1,9},{9,25},{25,17},{17,1},{2,10},{10... | collective-permute-start | bytes 7864328 | tf_op jit(solution)/shard_map/ppermute | solution.py:361
  272.1 272.3 %reduce-scatter.7.cloned.1.call-start = ((), (), s32[]{:S(2)}) async-start(), calls=%async_computation.8 | async-start | bytes 9437184 | tf_op jit(solution)/shard_map/reduce_scatter | solution.py:814
  349.5 248.6 %reduce-scatter.9.cloned.1.call-start = ((), (), s32[]{:S(2)}) async-start(), calls=%async_computation.9 | async-start | bytes 4718592 | tf_op jit(solution)/shard_map/reduce_scatter | solution.py:814
  351.3 81.4 %collective-permute-start.15 = (bf16[2048,512]{1,0:T(8,128)(2,1)S(1)}, bf16[2048,512]{1,0:T(8,128)(2,1)S(1)}, u32[]{:S(2)}, u32[]{:S(2)}) collective-permute-start(bf16[2048,512]{1,0:T(8,128)(2,1)S(1)} %slice.160.refs_8_), channel_id=1, source_target_pairs={{8,0},{24,8},{16,24},{0,16},{9,1},{25,9},{17,25},{1,17},{10,2},{26... | collective-permute-start | bytes 6291464 | tf_op jit(solution)/shard_map/ppermute | solution.py:362
  352.8 79.9 %collective-permute-start.14 = (bf16[2048,512]{1,0:T(8,128)(2,1)S(1)}, bf16[2048,512]{1,0:T(8,128)(2,1)S(1)}, u32[]{:S(2)}, u32[]{:S(2)}) collective-permute-start(bf16[2048,512]{1,0:T(8,128)(2,1)S(1)} %slice.160.refs_8_), channel_id=1, source_target_pairs={{0,8},{8,24},{24,16},{16,0},{1,9},{9,25},{25,17},{17,1},{2,10},{10... | collective-permute-start | bytes 6291464 | tf_op jit(solution)/shard_map/ppermute | solution.py:361
  353.4 86.1 %collective-permute-start.12 = (bf16[320,2048]{1,0:T(8,128)(2,1)}, bf16[320,2048]{1,0:T(8,128)(2,1)}, u32[]{:S(2)}, u32[]{:S(2)}) collective-permute-start(bf16[320,2048]{1,0:T(8,128)(2,1)} %get-tuple-element.92), channel_id=1, source_target_pairs={{0,8},{8,24},{24,16},{16,0},{1,9},{9,25},{25,17},{17,1},{2,10},{10... | collective-permute-start | bytes 3932168 | tf_op jit(solution)/shard_map/ppermute | solution.py:405
  353.9 86.2 %collective-permute-start.13 = (bf16[320,2048]{1,0:T(8,128)(2,1)}, bf16[320,2048]{1,0:T(8,128)(2,1)}, u32[]{:S(2)}, u32[]{:S(2)}) collective-permute-start(bf16[320,2048]{1,0:T(8,128)(2,1)} %get-tuple-element.93), channel_id=1, source_target_pairs={{8,0},{24,8},{16,24},{0,16},{9,1},{25,9},{17,25},{1,17},{10,2},{26... | collective-permute-start | bytes 3932168 | tf_op jit(solution)/shard_map/ppermute | solution.py:406
  434.9 109.5 %collective-permute-start.23 = (bf16[1024,512]{1,0:T(8,128)(2,1)}, bf16[1024,512]{1,0:T(8,128)(2,1)}, u32[]{:S(2)}, u32[]{:S(2)}) collective-permute-start(bf16[1024,512]{1,0:T(8,128)(2,1)} %slice.140), channel_id=1, source_target_pairs={{8,0},{24,8},{16,24},{0,16},{9,1},{25,9},{17,25},{1,17},{10,2},{26... | collective-permute-start | bytes 3145736 | tf_op jit(solution)/shard_map/ppermute | solution.py:370
  436.3 108.1 %collective-permute-start.22 = (bf16[1024,512]{1,0:T(8,128)(2,1)}, bf16[1024,512]{1,0:T(8,128)(2,1)}, u32[]{:S(2)}, u32[]{:S(2)}) collective-permute-start(bf16[1024,512]{1,0:T(8,128)(2,1)} %slice.139), channel_id=1, source_target_pairs={{0,8},{8,24},{24,16},{16,0},{1,9},{9,25},{25,17},{17,1},{2,10},{10... | collective-permute-start | bytes 3145736 | tf_op jit(solution)/shard_map/ppermute | solution.py:369
  438.0 99.8 %collective-permute-start.18 = (bf16[640,256]{1,0:T(8,128)(2,1)}, bf16[640,256]{1,0:T(8,128)(2,1)S(1)}, u32[]{:S(2)}, u32[]{:S(2)}) collective-permute-start(bf16[640,256]{1,0:T(8,128)(2,1)} %bitcast.22), channel_id=1, source_target_pairs={{0,16},{8,0},{24,8},{16,24},{1,17},{9,1},{25,9},{17,25},{2,18},{10... | collective-permute-start | bytes 983048 | tf_op jit(solution)/shard_map/ppermute | solution.py:426
  439.5 99.2 %collective-permute-start.20 = (bf16[640,256]{1,0:T(8,128)(2,1)}, bf16[640,256]{1,0:T(8,128)(2,1)S(1)}, u32[]{:S(2)}, u32[]{:S(2)}) collective-permute-start(bf16[640,256]{1,0:T(8,128)(2,1)} %bitcast.24), channel_id=1, source_target_pairs={{0,24},{8,16},{24,0},{16,8},{1,25},{9,17},{25,1},{17,9},{2,26},{10... | collective-permute-start | bytes 983048 | tf_op jit(solution)/shard_map/ppermute | solution.py:426
  440.1 100.7 %collective-permute-start.16 = (bf16[640,256]{1,0:T(8,128)(2,1)}, bf16[640,256]{1,0:T(8,128)(2,1)S(1)}, u32[]{:S(2)}, u32[]{:S(2)}) collective-permute-start(bf16[640,256]{1,0:T(8,128)(2,1)} %bitcast.20), channel_id=1, source_target_pairs={{0,8},{8,24},{24,16},{16,0},{1,9},{9,25},{25,17},{17,1},{2,10},{10... | collective-permute-start | bytes 983048 | tf_op jit(solution)/shard_map/ppermute | solution.py:426
  543.6 122.6 %reduce-scatter.11.cloned.1.call-start = ((), (), s32[]{:S(2)}) async-start(), calls=%async_computation.10 | async-start | bytes 4718592 | tf_op jit(solution)/shard_map/reduce_scatter | solution.py:814
  589.5 57.3 %collective-permute-start.27 = (bf16[320,2048]{1,0:T(8,128)(2,1)}, bf16[320,2048]{1,0:T(8,128)(2,1)S(1)}, u32[]{:S(2)}, u32[]{:S(2)}) collective-permute-start(bf16[320,2048]{1,0:T(8,128)(2,1)} %get-tuple-element.107), channel_id=1, source_target_pairs={{0,8},{8,24},{24,16},{16,0},{1,9},{9,25},{25,17},{17,1},{2,10},{10... | collective-permute-start | bytes 3932168 | tf_op jit(solution)/shard_map/ppermute | solution.py:405
  589.8 56.9 %collective-permute-start.28 = (bf16[320,2048]{1,0:T(8,128)(2,1)}, bf16[320,2048]{1,0:T(8,128)(2,1)S(1)}, u32[]{:S(2)}, u32[]{:S(2)}) collective-permute-start(bf16[320,2048]{1,0:T(8,128)(2,1)} %get-tuple-element.108), channel_id=1, source_target_pairs={{8,0},{24,8},{16,24},{0,16},{9,1},{25,9},{17,25},{1,17},{10,2},{26... | collective-permute-start | bytes 3932168 | tf_op jit(solution)/shard_map/ppermute | solution.py:406
  594.5 52.3 %collective-permute-start.29 = (bf16[320,2048]{1,0:T(8,128)(2,1)}, bf16[320,2048]{1,0:T(8,128)(2,1)}, u32[]{:S(2)}, u32[]{:S(2)}) collective-permute-start(bf16[320,2048]{1,0:T(8,128)(2,1)} %add_convert_fusion.1), channel_id=1, source_target_pairs={{8,0},{24,8},{16,24},{0,16},{9,1},{25,9},{17,25},{1,17},{10,2},{26... | collective-permute-start | bytes 3932168 | tf_op jit(solution)/shard_map/ppermute | solution.py:400
  597.4 49.4 %collective-permute-start.26 = (bf16[320,2048]{1,0:T(8,128)(2,1)}, bf16[320,2048]{1,0:T(8,128)(2,1)}, u32[]{:S(2)}, u32[]{:S(2)}) collective-permute-start(bf16[320,2048]{1,0:T(8,128)(2,1)} %add_convert_fusion.2), channel_id=1, source_target_pairs={{0,8},{8,24},{24,16},{16,0},{1,9},{9,25},{25,17},{17,1},{2,10},{10... | collective-permute-start | bytes 3932168 | tf_op jit(solution)/shard_map/ppermute | solution.py:399
  (60 other events, 899.7 us)
Sparse Core Ops, SparseCore 0:
  9.6 84.7 all-gather.3
  96.0 80.5 all-gather.5
  178.8 80.5 all-gather.7
  272.2 89.9 reduce-scatter.4
  364.3 87.9 reduce-scatter.6
  543.8 47.6 reduce-scatter.8
  615.2 47.2 reduce-scatter.10

commit v13 on v12

--- a/solution.py
+++ b/solution.py
@@ -427,20 +427,21 @@
     return got
 
 
-def exchange_steps(axes):
-    steps = []
-    for axis in axes:
-        count, span = lax.axis_size(axis), 1
-        while span < count:
-            steps.append((axis, [(n, n ^ span) for n in range(count)]))
-            span *= 2
+def exchange_steps(axis, spans):
+    steps, count = [], lax.axis_size(axis)
+    spans = [span for span in spans if span < count]
+    while spans:
+        step, spans = spans[:2], spans[2:]
+        steps.append((axis, step + [step[0] + step[1]] if len(step) == 2 else step))
     return steps
 
 
-def exchange(values, steps):
-    for axis, pairs in steps:
-        values = values + lax.ppermute(values, axis, pairs)
-    return values
+def exchange(values, step, gate=()):
+    axis, flips = step
+    count = lax.axis_size(axis)
+    got = [lax.ppermute(values, axis, [(n, n ^ flip) for n in range(count)]) for flip in flips]
+    total = after(values, *gate) + got[0]
+    return total + (got[1] + got[2]) if len(got) == 3 else total
 
 
 def gelu_and_slope(h):
@@ -926,9 +927,10 @@
             fc1_bias_wide,
         ]
     )
-    near, across = exchange_steps(("fsdp",)), exchange_steps(("ctx",))
-    steps = near[:1] + across + near[1:]
-    small = exchange(small, steps[:1])
+    doubled = [2**n for n in range(1, 30)]
+    steps = exchange_steps("fsdp", [1]) + exchange_steps("ctx", [1] + doubled)
+    steps += exchange_steps("fsdp", doubled)
+    small = exchange(small, steps[0])
     d_fc1, d_fc2 = d_fc1.astype(WIDE), d_fc2.T.astype(WIDE)
     output = place_output(
         [swapped[which][rank] for rank in range(count) for which in range(groups)],
@@ -940,14 +942,13 @@
         count,
         groups,
     )
-    small = exchange(after(small, output, *last_hops), steps[1:2])
+    small = exchange(after(small, output, *last_hops), steps[1])
     d_tokens = token_grad(
         after(tokens[0], output), own_grad, own_part[0], gain, grad_terms, local_rows // 4
     )
-    small = exchange(after(small, d_tokens), steps[2:-1])
-    small = after(small, d_fc1, d_fc2)
-    axis, pairs = steps[-1]
-    small = after(small, d_qkv, d_dense) + lax.ppermute(small, axis, pairs)
+    for step in steps[2:-1]:
+        small = exchange(small, step)
+    small = exchange(after(small, d_tokens), steps[-1], (d_fc1, d_fc2, d_qkv, d_dense))
     d_shift, with_normed, d_b_qkv, d_b_out, d_b_fc1 = jnp.split(
         small, [width, 2 * width, 5 * width, 6 * width]
     )

time: 691 us -> 697 us (level)
    unnamed x90 -> x88, local copies, waits for them, and re-layouts: 16.2 us -> 17.2 us
  transfers between devices with their start and end apart: 42 -> 44, of which waited for: 11 -> 9; matrix products, arithmetic and copies ran while one was open for 27% -> 28% of each run, Pallas kernels for 50% -> 50%
where the time goes in v13:
time: 697 us; the launch traced here: 688 us
  Pallas kernels  341 us (49%)
  matrix products  117 us (17%)
  waiting for transfers between devices  87.5 us (13%)
  local copies, waits for them, and re-layouts  46.5 us (7%)
  starting transfers between devices  41.7 us (6%)
  other arithmetic  38.7 us (6%)
  between operations  15 us (2%)
    pallas_call x2, Pallas kernels, attention(): pl.pallas_call(kernel, out_shape=(jax.ShapeDtypeStruct((blocks, blk, lane...  154 us
    dot_general x5, matrix products, dot(): return lax.dot_general(left, right, dims, preferred_element_type=WIDE)  117 us
    pallas_call x3, Pallas kernels, input_grad(): pl.pallas_call(functools.partial(input_grad_kernel, terms=len(grads), ran...  58.5 us
    ppermute x3, waiting for transfers between devices, ring_pieces(): from_ahead = lax.ppermute(from_ahead, axis, behind)  55.6 us
    pallas_call x1, Pallas kernels, expand(): pl.pallas_call(functools.partial(expand_kernel, spans=spans, cols=min(512...  42 us
    pallas_call x2, Pallas kernels, pair_grad(): pl.pallas_call(pair_grad_kernel, out_shape=jax.ShapeDtypeStruct((width, c...  33.8 us
    pallas_call x1, Pallas kernels, slope_grad(): pl.pallas_call(functools.partial(slope_grad_kernel, spans=spans, cols=min...  30.9 us
    ppermute x3, waiting for transfers between devices, ring_pieces(): lax.ppermute(from_ahead[half:], axis, behind)  19.9 us
  transfers between devices with their start and end apart: 44, of which 9 were waited for; matrix products, arithmetic and copies ran while one was open for 28% of the time, Pallas kernels for 50%

profile of v13, /device:TPU:0, one launch (start us, length us, event | category | flops | bytes accessed | tf_op | source)
XLA Modules:
  0.0 688.1 jit_solution(2728914742812295528)
XLA Ops:
  15.1 3.0 collective-permute-start.1
  24.2 7.7 %negate_select_fusion = (f32[2560,128]{1,0:T(8,128)}, f32[2560,128]{1,0:T(8,128)}, f32[2560,128]{1,0:T(8,128)}) fusion(f32[128]{0:T(128)S(1)} %mul.123, s32[2560]{0:T(1024)S(1)} %get-tuple-element.192, s32[2560]{0:T(1024)S(1)} %get-tuple-element.193, s32[128]{0:T(128)S(1)} %get-tuple-element.196, s32[128]{0:T(128)S(1)} %get-tuple-element.197, ...), kind=kLoop, calls=%fused_computation.25 | loop fusion | flops 4587520 | bytes 3959424 | tf_op jit(solution)/shard_map/jit(_where)/select_n | solution.py:759
  31.9 43.3 %collective-permute-done.1.refs_2_ = bf16[640,2048]{1,0:T(8,128)(2,1)} collective-permute-done((bf16[640,2048]{1,0:T(8,128)(2,1)}, bf16[640,2048]{1,0:T(8,128)(2,1)}, u32[]{:S(2)}, u32[]{:S(2)}) %collective-permute-start.1) | collective-permute-done | bytes 2621472 | tf_op jit(solution)/shard_map/ppermute | solution.py:362
  91.6 19.9 %collective-permute-done.3.refs_4_ = bf16[320,2048]{1,0:T(8,128)(2,1)} collective-permute-done((bf16[320,2048]{1,0:T(8,128)(2,1)}, bf16[320,2048]{1,0:T(8,128)(2,1)}, u32[]{:S(2)}, u32[]{:S(2)}) %collective-permute-start.3) | collective-permute-done | bytes 1310752 | tf_op jit(solution)/shard_map/ppermute | solution.py:370
  114.9 42.0 %expand.1 = (bf16[2560,2048]{1,0:T(8,128)(2,1)}, bf16[2560,2048]{1,0:T(8,128)(2,1)}, bf16[2560,2048]{1,0:T(8,128)(2,1)}) custom-call(bf16[640,2048]{1,0:T(8,128)(2,1)} %fusion.6.refs_0_, bf16[640,2048]{1,0:T(8,128)(2,1)} %collective-permute-done.refs_1_, bf16[640,2048]{1,0:T(8,128)(2,1)} %collective-permute-done.1.refs_2_, ...), custom_call_target="tpu_custom_call" | custom-call | flops 21474836480 | bytes 41943040 | tf_op jit(solution)/shard_map/expand/pallas_call | solution.py:496
  156.9 12.2 %collective-permute-done.5.refs_2_ = bf16[640,2048]{1,0:T(8,128)(2,1)} collective-permute-done((bf16[640,2048]{1,0:T(8,128)(2,1)S(1)}, bf16[640,2048]{1,0:T(8,128)(2,1)}, u32[]{:S(2)}, u32[]{:S(2)}) %collective-permute-start.5) | collective-permute-done | bytes 2621472 | tf_op jit(solution)/shard_map/ppermute | solution.py:362
  176.9 26.6 %convolution_convert_fusion.refs_15_ = bf16[2560,2048]{1,0:T(8,128)(2,1)S(1)} fusion(bf16[2560,2048]{1,0:T(8,128)(2,1)} %get-tuple-element.72, bf16[2048,2048]{1,0:T(8,128)(2,1)} %all-gather.6.cloned.1.call-done.refs_5_), kind=kOutput, calls=%fused_computation.1 | convolution fusion | flops 21480079360 | bytes 29360128 | tf_op jit(solution)/shard_map/dot_general | solution.py:28
  210.3 30.9 %slope_grad.1 = (bf16[2560,2048]{1,0:T(8,128)(2,1)}, bf16[2560,2048]{1,0:T(8,128)(2,1)}, f32[8,2048]{1,0:T(8,128)S(1)}) custom-call(bf16[640,2048]{1,0:T(8,128)(2,1)S(1)} %bitcast.64, bf16[640,2048]{1,0:T(8,128)(2,1)} %collective-permute-done.4.refs_1_, bf16[640,2048]{1,0:T(8,128)(2,1)} %collective-permute-done.5.refs_2_, ...), custom_call_target="tpu_custom_call" | custom-call | flops 21474836480 | bytes 41943040 | tf_op jit(solution)/shard_map/slope_grad/pallas_call | solution.py:540
  243.3 28.9 %convolution_convert_fusion.2 = bf16[2048,2048]{1,0:T(8,128)(2,1)} fusion(bf16[2560,2048]{1,0:T(8,128)(2,1)} %get-tuple-element.87.y_ref, bf16[2560,2048]{1,0:T(8,128)(2,1)} %get-tuple-element.72), kind=kOutput, calls=%fused_computation.3 | convolution fusion | flops 21479030784 | bytes 29360128 | tf_op jit(solution)/shard_map/dot_general | solution.py:28
  273.9 4.2 add_convert_fusion.3
  280.6 22.3 %add_convert_fusion = bf16[2560,1536]{1,0:T(8,128)(2,1)} fusion(bf16[2560,2048]{1,0:T(8,128)(2,1)} %get-tuple-element.110.x_ref.refs_6_.refs_9_.refs_10_, f32[1536]{0:T(1024)S(1)} %reshape.234, bf16[2048,2048]{1,0:T(8,128)(2,1)} %all-gather.8.cloned.1.call-done.refs_3_.refs_4_.refs_6_.refs_7_), kind=kOutput, calls=%fused_computation | convolution fusion | flops 16113991680 | bytes 24647680 | tf_op jit(solution)/shard_map/dot_general | solution.py:28
  302.9 5.6 collective-permute-done.11.refs_19_
  310.1 10.5 %convolution_convert_fusion.3 = bf16[2560,512]{1,0:T(8,128)(2,1)} fusion(bf16[2560,2048]{1,0:T(8,128)(2,1)} %get-tuple-element.87.y_ref, bf16[2048,2048]{1,0:T(8,128)(2,1)} %all-gather.8.cloned.1.call-done.refs_3_.refs_4_.refs_6_.refs_7_), kind=kOutput, calls=%fused_computation.14 | convolution fusion | flops 5370019840 | bytes 15204352 | tf_op jit(solution)/shard_map/dot_general | solution.py:28
  320.6 28.9 %convolution_convert_fusion.1 = bf16[2048,2048]{1,0:T(8,128)(2,1)} fusion(bf16[2560,2048]{1,0:T(8,128)(2,1)} %get-tuple-element.110.x_ref.refs_6_.refs_9_.refs_10_, bf16[2560,2048]{1,0:T(8,128)(2,1)} %get-tuple-element.111.refs_2_.refs_5_), kind=kOutput, calls=%fused_computation.2 | convolution fusion | flops 21479030784 | bytes 29360128 | tf_op jit(solution)/shard_map/dot_general | solution.py:28
  355.6 77.1 %attention.2 = (bf16[40,64,256]{2,1,0:T(8,128)(2,1)}, bf16[40,64,768]{2,1,0:T(8,128)(2,1)}, f32[8,768]{1,0:T(8,128)}) custom-call(s32[40]{0:T(128)} %select_reduce_fusion.where_ref, bf16[40,64,1536]{2,1,0:T(8,128)(2,1)} %bitcast.67, bf16[40,64,1536]{2,1,0:T(8,128)(2,1)} %bitcast.68, bf16[40,64,1536]{2,1,0:T(8,128)(2,1)} %bitcast.69, ...), custom_call_target="tpu_custom_call" | custom-call | flops 1000000 | bytes 1000000 | tf_op jit(solution)/shard_map/attention/pallas_call | solution.py:297
  441.8 16.8 %pair_grad.2 = bf16[2048,1024]{1,0:T(8,128)(2,1)} custom-call(bf16[2560,2048]{1,0:T(8,128)(2,1)} %get-tuple-element.110.x_ref.refs_6_.refs_9_.refs_10_, bf16[2560,2048]{1,0:T(8,128)(2,1)} %get-tuple-element.87.y_ref, bf16[2560,768]{1,0:T(8,128)(2,1)} %bitcast.85, bf16[2560,256]{1,0:T(8,128)(2,1)} %bitcast.96), custom_call_target="tpu_custom_call" | custom-call | flops 1000000 | bytes 1000000 | tf_op jit(solution)/shard_map/pair_grad/pallas_call | solution.py:728
  458.7 77.1 %attention.3 = (bf16[40,64,256]{2,1,0:T(8,128)(2,1)}, bf16[40,64,768]{2,1,0:T(8,128)(2,1)}, f32[8,768]{1,0:T(8,128)}) custom-call(s32[40]{0:T(128)} %select_reduce_fusion.where_ref, bf16[40,64,1536]{2,1,0:T(8,128)(2,1)} %bitcast.71, bf16[40,64,1536]{2,1,0:T(8,128)(2,1)} %bitcast.72, bf16[40,64,1536]{2,1,0:T(8,128)(2,1)} %bitcast.73, ...), custom_call_target="tpu_custom_call" | custom-call | flops 1000000 | bytes 1000000 | tf_op jit(solution)/shard_map/attention/pallas_call | solution.py:297
  545.0 16.0 %input_grad.3 = (bf16[320,2048]{1,0:T(8,128)(2,1)}, bf16[320,2048]{1,0:T(8,128)(2,1)}, f32[2,2048]{1,0:T(2,128)}) custom-call(bf16[2560,768]{1,0:T(8,128)(2,1)} %bitcast.86, bf16[2560,768]{1,0:T(8,128)(2,1)} %bitcast.90, bf16[2560,2048]{1,0:T(8,128)(2,1)} %get-tuple-element.111.refs_2_.refs_5_, ...), custom_call_target="tpu_custom_call" | custom-call | flops 1000000 | bytes 1000000 | tf_op jit(solution)/shard_map/input_grad/pallas_call | solution.py:605
  563.1 26.9 %input_grad.4 = (bf16[320,2048]{1,0:T(8,128)(2,1)}, bf16[320,2048]{1,0:T(8,128)(2,1)}, bf16[320,2048]{1,0:T(8,128)(2,1)}, bf16[320,2048]{1,0:T(8,128)(2,1)}, f32[2,2048]{1,0:T(2,128)}) custom-call(bf16[2560,768]{1,0:T(8,128)(2,1)} %bitcast.87, bf16[2560,768]{1,0:T(8,128)(2,1)} %bitcast.91, bf16[2560,2048]{1,0:T(8,128)(2,1)} %get-tuple-element.111.refs_2_.refs_5_, ...), custom_call_target="tpu_custom_call" | custom-call | flops 99999997952 | bytes 1000000 | tf_op jit(solution)/shard_map/input_grad/pallas_call | solution.py:605
  598.6 16.9 %pair_grad.3 = bf16[2048,1024]{1,0:T(8,128)(2,1)} custom-call(bf16[2560,2048]{1,0:T(8,128)(2,1)} %get-tuple-element.110.x_ref.refs_6_.refs_9_.refs_10_, bf16[2560,2048]{1,0:T(8,128)(2,1)} %get-tuple-element.87.y_ref, bf16[2560,768]{1,0:T(8,128)(2,1)} %bitcast.93, bf16[2560,256]{1,0:T(8,128)(2,1)} %bitcast.95), custom_call_target="tpu_custom_call" | custom-call | flops 1000000 | bytes 1000000 | tf_op jit(solution)/shard_map/pair_grad/pallas_call | solution.py:728
  615.6 15.7 %input_grad.5 = (bf16[640,2048]{1,0:T(8,128)(2,1)}, f32[2,2048]{1,0:T(2,128)}) custom-call(bf16[2560,768]{1,0:T(8,128)(2,1)} %bitcast.89, bf16[2560,768]{1,0:T(8,128)(2,1)} %bitcast.94, bf16[2560,2048]{1,0:T(8,128)(2,1)} %get-tuple-element.111.refs_2_.refs_5_, bf16[2048,2048]{1,0:T(8,128)(2,1)} %all-gather.8.cloned.1.call-done.refs_3_.refs_4_.refs_6_.refs_7_, ...), custom_call_target="tpu_custom_call" | custom-call | flops 99999997952 | bytes 1000000 | tf_op jit(solution)/shard_map/input_grad/pallas_call | solution.py:605
  640.2 13.1 %place_output.1 = bf16[640,2048]{1,0:T(8,128)(2,1)} custom-call(bf16[640,256]{1,0:T(8,128)(2,1)} %bitcast.104, bf16[640,256]{1,0:T(8,128)(2,1)} %bitcast.105, bf16[640,256]{1,0:T(8,128)(2,1)} %copy-done.22, bf16[640,256]{1,0:T(8,128)(2,1)} %copy-done.25, bf16[640,256]{1,0:T(8,128)(2,1)} %copy-done.20, bf16[640,256]{1,0:T(8,128)(2,1)} %copy-done.23, ...), custom_call_target="tpu_custom_call" | custom-call | flops 1000000 | bytes 1000000 | tf_op jit(solution)/shard_map/place_output/pallas_call | solution.py:655
  658.5 8.9 %token_grad.1 = bf16[640,2048]{1,0:T(8,128)(2,1)} custom-call(bf16[640,2048]{1,0:T(8,128)(2,1)} %bitcast.84, bf16[640,2048]{1,0:T(8,128)(2,1)} %bitcast.61, bf16[640,2048]{1,0:T(8,128)(2,1)} %get-tuple-element.112.own_ref, f32[1,2048]{1,0:T(1,128)S(1)} %bitcast.65, bf16[320,2048]{1,0:T(8,128)(2,1)} %collective-permute-done.26.refs_0_, ...), custom_call_target="tpu_custom_call" | custom-call | flops 1000000 | bytes 1000000 | tf_op jit(solution)/shard_map/token_grad/pallas_call | solution.py:699
  668.6 4.2 collective-permute-start.34
  (244 shorter events, 114.2 us)
Async XLA Ops:
  7.2 107.7 %all-gather.4.cloned.1.call-start = ((), (), s32[]{:S(2)}) async-start(), calls=%async_computation.4 | async-start | bytes 9437184 | tf_op jit(solution)/shard_map/all_gather | solution.py:812
  7.9 169.0 %all-gather.6.cloned.1.call-start = ((), (), s32[]{:S(2)}) async-start(), calls=%async_computation.5 | async-start | bytes 9437184 | tf_op jit(solution)/shard_map/all_gather | solution.py:812
  15.1 60.1 %collective-permute-start.1 = (bf16[640,2048]{1,0:T(8,128)(2,1)}, bf16[640,2048]{1,0:T(8,128)(2,1)}, u32[]{:S(2)}, u32[]{:S(2)}) collective-permute-start(bf16[640,2048]{1,0:T(8,128)(2,1)} %fusion.6.refs_0_), channel_id=1, source_target_pairs={{8,0},{24,8},{16,24},{0,16},{9,1},{25,9},{17,25},{1,17},{10,2},{26... | collective-permute-start | bytes 7864328 | tf_op jit(solution)/shard_map/ppermute | solution.py:362
  18.0 58.6 %collective-permute-start = (bf16[640,2048]{1,0:T(8,128)(2,1)}, bf16[640,2048]{1,0:T(8,128)(2,1)}, u32[]{:S(2)}, u32[]{:S(2)}) collective-permute-start(bf16[640,2048]{1,0:T(8,128)(2,1)} %fusion.6.refs_0_), channel_id=1, source_target_pairs={{0,8},{8,24},{24,16},{16,0},{1,9},{9,25},{25,17},{17,1},{2,10},{10... | collective-permute-start | bytes 7864328 | tf_op jit(solution)/shard_map/ppermute | solution.py:361
  76.7 203.8 %all-gather.8.cloned.1.call-start = ((), (), s32[]{:S(2)}) async-start(), calls=%async_computation.6 | async-start | bytes 9437184 | tf_op jit(solution)/shard_map/all_gather | solution.py:812
  112.8 329.1 %reduce-scatter.5.cloned.1.call-start = ((), (), s32[]{:S(2)}) async-start(), calls=%async_computation.7 | async-start | bytes 9437184 | tf_op jit(solution)/shard_map/reduce_scatter | solution.py:815
  112.8 56.4 %collective-permute-start.5 = (bf16[640,2048]{1,0:T(8,128)(2,1)S(1)}, bf16[640,2048]{1,0:T(8,128)(2,1)}, u32[]{:S(2)}, u32[]{:S(2)}) collective-permute-start(bf16[640,2048]{1,0:T(8,128)(2,1)S(1)} %bitcast.62), channel_id=1, source_target_pairs={{8,0},{24,8},{16,24},{0,16},{9,1},{25,9},{17,25},{1,17},{10,2},{26... | collective-permute-start | bytes 7864328 | tf_op jit(solution)/shard_map/ppermute | solution.py:362
  113.5 56.2 %collective-permute-start.4 = (bf16[640,2048]{1,0:T(8,128)(2,1)S(1)}, bf16[640,2048]{1,0:T(8,128)(2,1)}, u32[]{:S(2)}, u32[]{:S(2)}) collective-permute-start(bf16[640,2048]{1,0:T(8,128)(2,1)S(1)} %bitcast.63), channel_id=1, source_target_pairs={{0,8},{8,24},{24,16},{16,0},{1,9},{9,25},{25,17},{17,1},{2,10},{10... | collective-permute-start | bytes 7864328 | tf_op jit(solution)/shard_map/ppermute | solution.py:361
  272.2 272.7 %reduce-scatter.7.cloned.1.call-start = ((), (), s32[]{:S(2)}) async-start(), calls=%async_computation.8 | async-start | bytes 9437184 | tf_op jit(solution)/shard_map/reduce_scatter | solution.py:815
  349.6 249.0 %reduce-scatter.9.cloned.1.call-start = ((), (), s32[]{:S(2)}) async-start(), calls=%async_computation.9 | async-start | bytes 4718592 | tf_op jit(solution)/shard_map/reduce_scatter | solution.py:815
  351.4 81.4 %collective-permute-start.15 = (bf16[2048,512]{1,0:T(8,128)(2,1)S(1)}, bf16[2048,512]{1,0:T(8,128)(2,1)S(1)}, u32[]{:S(2)}, u32[]{:S(2)}) collective-permute-start(bf16[2048,512]{1,0:T(8,128)(2,1)S(1)} %slice.160.refs_8_), channel_id=1, source_target_pairs={{8,0},{24,8},{16,24},{0,16},{9,1},{25,9},{17,25},{1,17},{10,2},{26... | collective-permute-start | bytes 6291464 | tf_op jit(solution)/shard_map/ppermute | solution.py:362
  352.9 79.9 %collective-permute-start.14 = (bf16[2048,512]{1,0:T(8,128)(2,1)S(1)}, bf16[2048,512]{1,0:T(8,128)(2,1)S(1)}, u32[]{:S(2)}, u32[]{:S(2)}) collective-permute-start(bf16[2048,512]{1,0:T(8,128)(2,1)S(1)} %slice.160.refs_8_), channel_id=1, source_target_pairs={{0,8},{8,24},{24,16},{16,0},{1,9},{9,25},{25,17},{17,1},{2,10},{10... | collective-permute-start | bytes 6291464 | tf_op jit(solution)/shard_map/ppermute | solution.py:361
  353.5 86.0 %collective-permute-start.12 = (bf16[320,2048]{1,0:T(8,128)(2,1)}, bf16[320,2048]{1,0:T(8,128)(2,1)}, u32[]{:S(2)}, u32[]{:S(2)}) collective-permute-start(bf16[320,2048]{1,0:T(8,128)(2,1)} %get-tuple-element.91), channel_id=1, source_target_pairs={{0,8},{8,24},{24,16},{16,0},{1,9},{9,25},{25,17},{17,1},{2,10},{10... | collective-permute-start | bytes 3932168 | tf_op jit(solution)/shard_map/ppermute | solution.py:405
  354.0 86.2 %collective-permute-start.13 = (bf16[320,2048]{1,0:T(8,128)(2,1)}, bf16[320,2048]{1,0:T(8,128)(2,1)}, u32[]{:S(2)}, u32[]{:S(2)}) collective-permute-start(bf16[320,2048]{1,0:T(8,128)(2,1)} %get-tuple-element.92), channel_id=1, source_target_pairs={{8,0},{24,8},{16,24},{0,16},{9,1},{25,9},{17,25},{1,17},{10,2},{26... | collective-permute-start | bytes 3932168 | tf_op jit(solution)/shard_map/ppermute | solution.py:406
  434.9 110.0 %collective-permute-start.23 = (bf16[1024,512]{1,0:T(8,128)(2,1)}, bf16[1024,512]{1,0:T(8,128)(2,1)}, u32[]{:S(2)}, u32[]{:S(2)}) collective-permute-start(bf16[1024,512]{1,0:T(8,128)(2,1)} %slice.140), channel_id=1, source_target_pairs={{8,0},{24,8},{16,24},{0,16},{9,1},{25,9},{17,25},{1,17},{10,2},{26... | collective-permute-start | bytes 3145736 | tf_op jit(solution)/shard_map/ppermute | solution.py:370
  436.4 108.6 %collective-permute-start.22 = (bf16[1024,512]{1,0:T(8,128)(2,1)}, bf16[1024,512]{1,0:T(8,128)(2,1)}, u32[]{:S(2)}, u32[]{:S(2)}) collective-permute-start(bf16[1024,512]{1,0:T(8,128)(2,1)} %slice.139), channel_id=1, source_target_pairs={{0,8},{8,24},{24,16},{16,0},{1,9},{9,25},{25,17},{17,1},{2,10},{10... | collective-permute-start | bytes 3145736 | tf_op jit(solution)/shard_map/ppermute | solution.py:369
  438.0 99.9 %collective-permute-start.18 = (bf16[640,256]{1,0:T(8,128)(2,1)}, bf16[640,256]{1,0:T(8,128)(2,1)S(1)}, u32[]{:S(2)}, u32[]{:S(2)}) collective-permute-start(bf16[640,256]{1,0:T(8,128)(2,1)} %bitcast.22), channel_id=1, source_target_pairs={{0,16},{8,0},{24,8},{16,24},{1,17},{9,1},{25,9},{17,25},{2,18},{10... | collective-permute-start | bytes 983048 | tf_op jit(solution)/shard_map/ppermute | solution.py:426
  439.5 99.1 %collective-permute-start.20 = (bf16[640,256]{1,0:T(8,128)(2,1)}, bf16[640,256]{1,0:T(8,128)(2,1)S(1)}, u32[]{:S(2)}, u32[]{:S(2)}) collective-permute-start(bf16[640,256]{1,0:T(8,128)(2,1)} %bitcast.24), channel_id=1, source_target_pairs={{0,24},{8,16},{24,0},{16,8},{1,25},{9,17},{25,1},{17,9},{2,26},{10... | collective-permute-start | bytes 983048 | tf_op jit(solution)/shard_map/ppermute | solution.py:426
  440.2 100.6 %collective-permute-start.16 = (bf16[640,256]{1,0:T(8,128)(2,1)}, bf16[640,256]{1,0:T(8,128)(2,1)S(1)}, u32[]{:S(2)}, u32[]{:S(2)}) collective-permute-start(bf16[640,256]{1,0:T(8,128)(2,1)} %bitcast.20), channel_id=1, source_target_pairs={{0,8},{8,24},{24,16},{16,0},{1,9},{9,25},{25,17},{17,1},{2,10},{10... | collective-permute-start | bytes 983048 | tf_op jit(solution)/shard_map/ppermute | solution.py:426
  544.2 128.7 %reduce-scatter.11.cloned.1.call-start = ((), (), s32[]{:S(2)}) async-start(), calls=%async_computation.10 | async-start | bytes 4718592 | tf_op jit(solution)/shard_map/reduce_scatter | solution.py:815
  590.0 64.7 %collective-permute-start.27 = (bf16[320,2048]{1,0:T(8,128)(2,1)}, bf16[320,2048]{1,0:T(8,128)(2,1)S(1)}, u32[]{:S(2)}, u32[]{:S(2)}) collective-permute-start(bf16[320,2048]{1,0:T(8,128)(2,1)} %get-tuple-element.106), channel_id=1, source_target_pairs={{0,8},{8,24},{24,16},{16,0},{1,9},{9,25},{25,17},{17,1},{2,10},{10... | collective-permute-start | bytes 3932168 | tf_op jit(solution)/shard_map/ppermute | solution.py:405
  590.3 64.3 %collective-permute-start.28 = (bf16[320,2048]{1,0:T(8,128)(2,1)}, bf16[320,2048]{1,0:T(8,128)(2,1)S(1)}, u32[]{:S(2)}, u32[]{:S(2)}) collective-permute-start(bf16[320,2048]{1,0:T(8,128)(2,1)} %get-tuple-element.107), channel_id=1, source_target_pairs={{8,0},{24,8},{16,24},{0,16},{9,1},{25,9},{17,25},{1,17},{10,2},{26... | collective-permute-start | bytes 3932168 | tf_op jit(solution)/shard_map/ppermute | solution.py:406
  595.0 59.6 %collective-permute-start.29 = (bf16[320,2048]{1,0:T(8,128)(2,1)}, bf16[320,2048]{1,0:T(8,128)(2,1)}, u32[]{:S(2)}, u32[]{:S(2)}) collective-permute-start(bf16[320,2048]{1,0:T(8,128)(2,1)} %add_convert_fusion.1), channel_id=1, source_target_pairs={{8,0},{24,8},{16,24},{0,16},{9,1},{25,9},{17,25},{1,17},{10,2},{26... | collective-permute-start | bytes 3932168 | tf_op jit(solution)/shard_map/ppermute | solution.py:400
  597.9 56.7 %collective-permute-start.26 = (bf16[320,2048]{1,0:T(8,128)(2,1)}, bf16[320,2048]{1,0:T(8,128)(2,1)}, u32[]{:S(2)}, u32[]{:S(2)}) collective-permute-start(bf16[320,2048]{1,0:T(8,128)(2,1)} %add_convert_fusion.2), channel_id=1, source_target_pairs={{0,8},{8,24},{24,16},{16,0},{1,9},{9,25},{25,17},{17,1},{2,10},{10... | collective-permute-start | bytes 3932168 | tf_op jit(solution)/shard_map/ppermute | solution.py:399
  (60 other events, 945.5 us)
Sparse Core Ops, SparseCore 0:
  9.6 84.7 all-gather.3
  96.0 80.5 all-gather.5
  178.2 80.5 all-gather.7
  272.4 89.7 reduce-scatter.4
  364.3 87.9 reduce-scatter.6
  544.3 47.7 reduce-scatter.8
  615.7 47.2 reduce-scatter.10

commit v14 on v13

--- a/solution.py
+++ b/solution.py
@@ -929,9 +929,9 @@
     )
     doubled = [2**n for n in range(1, 30)]
     steps = exchange_steps("fsdp", [1]) + exchange_steps("ctx", [1] + doubled)
-    steps += exchange_steps("fsdp", doubled)
+    for span in doubled:
+        steps += exchange_steps("fsdp", [span])
     small = exchange(small, steps[0])
-    d_fc1, d_fc2 = d_fc1.astype(WIDE), d_fc2.T.astype(WIDE)
     output = place_output(
         [swapped[which][rank] for rank in range(count) for which in range(groups)],
         dense_pieces,
@@ -946,9 +946,11 @@
     d_tokens = token_grad(
         after(tokens[0], output), own_grad, own_part[0], gain, grad_terms, local_rows // 4
     )
+    d_fc1, d_fc2 = after(d_fc1, small).astype(WIDE), after(d_fc2, small).T.astype(WIDE)
+    small = after(small, d_tokens)
     for step in steps[2:-1]:
         small = exchange(small, step)
-    small = exchange(after(small, d_tokens), steps[-1], (d_fc1, d_fc2, d_qkv, d_dense))
+    small = exchange(after(small, d_fc1, d_fc2), steps[-1], (d_qkv, d_dense))
     d_shift, with_normed, d_b_qkv, d_b_out, d_b_fc1 = jnp.split(
         small, [width, 2 * width, 5 * width, 6 * width]
     )

time: 697 us -> 691 us (level)
    unnamed x88 -> x90, local copies, waits for them, and re-layouts: 17.2 us -> 16.2 us
  transfers between devices with their start and end apart: 44 -> 43, of which waited for: 9 -> 10; matrix products, arithmetic and copies ran while one was open for 28% -> 28% of each run, Pallas kernels for 50% -> 50%
where the time goes in v14:
time: 691 us; the launch traced here: 683 us
  Pallas kernels  341 us (49%)
  matrix products  117 us (17%)
  waiting for transfers between devices  90.4 us (13%)
  local copies, waits for them, and re-layouts  45.4 us (7%)
  starting transfers between devices  37.5 us (5%)
  other arithmetic  36.1 us (5%)
  between operations  15 us (2%)
    pallas_call x2, Pallas kernels, attention(): pl.pallas_call(kernel, out_shape=(jax.ShapeDtypeStruct((blocks, blk, lane...  154 us
    dot_general x5, matrix products, dot(): return lax.dot_general(left, right, dims, preferred_element_type=WIDE)  117 us
    pallas_call x3, Pallas kernels, input_grad(): pl.pallas_call(functools.partial(input_grad_kernel, terms=len(grads), ran...  58.5 us
    ppermute x3, waiting for transfers between devices, ring_pieces(): from_ahead = lax.ppermute(from_ahead, axis, behind)  55.6 us
    pallas_call x1, Pallas kernels, expand(): pl.pallas_call(functools.partial(expand_kernel, spans=spans, cols=min(512...  42 us
    pallas_call x2, Pallas kernels, pair_grad(): pl.pallas_call(pair_grad_kernel, out_shape=jax.ShapeDtypeStruct((width, c...  33.8 us
    pallas_call x1, Pallas kernels, slope_grad(): pl.pallas_call(functools.partial(slope_grad_kernel, spans=spans, cols=min...  30.9 us
    ppermute x3, waiting for transfers between devices, ring_pieces(): lax.ppermute(from_ahead[half:], axis, behind)  20 us
  transfers between devices with their start and end apart: 43, of which 10 were waited for; matrix products, arithmetic and copies ran while one was open for 28% of the time, Pallas kernels for 50%

profile of v14, /device:TPU:0, one launch (start us, length us, event | category | flops | bytes accessed | tf_op | source)
XLA Modules:
  0.0 683.2 jit_solution(10066699108772217953)
XLA Ops:
  15.1 3.0 collective-permute-start.1
  24.2 7.7 %negate_select_fusion = (f32[2560,128]{1,0:T(8,128)}, f32[2560,128]{1,0:T(8,128)}, f32[2560,128]{1,0:T(8,128)}) fusion(f32[128]{0:T(128)S(1)} %mul.123, s32[2560]{0:T(1024)S(1)} %get-tuple-element.198, s32[2560]{0:T(1024)S(1)} %get-tuple-element.199, s32[128]{0:T(128)S(1)} %get-tuple-element.202, s32[128]{0:T(128)S(1)} %get-tuple-element.203, ...), kind=kLoop, calls=%fused_computation.25 | loop fusion | flops 4587520 | bytes 3959424 | tf_op jit(solution)/shard_map/jit(_where)/select_n | solution.py:759
  31.9 43.3 %collective-permute-done.1.refs_2_ = bf16[640,2048]{1,0:T(8,128)(2,1)} collective-permute-done((bf16[640,2048]{1,0:T(8,128)(2,1)}, bf16[640,2048]{1,0:T(8,128)(2,1)}, u32[]{:S(2)}, u32[]{:S(2)}) %collective-permute-start.1) | collective-permute-done | bytes 2621472 | tf_op jit(solution)/shard_map/ppermute | solution.py:362
  91.6 19.9 %collective-permute-done.3.refs_4_ = bf16[320,2048]{1,0:T(8,128)(2,1)} collective-permute-done((bf16[320,2048]{1,0:T(8,128)(2,1)}, bf16[320,2048]{1,0:T(8,128)(2,1)}, u32[]{:S(2)}, u32[]{:S(2)}) %collective-permute-start.3) | collective-permute-done | bytes 1310752 | tf_op jit(solution)/shard_map/ppermute | solution.py:370
  114.9 42.0 %expand.1 = (bf16[2560,2048]{1,0:T(8,128)(2,1)}, bf16[2560,2048]{1,0:T(8,128)(2,1)}, bf16[2560,2048]{1,0:T(8,128)(2,1)}) custom-call(bf16[640,2048]{1,0:T(8,128)(2,1)} %fusion.6.refs_0_, bf16[640,2048]{1,0:T(8,128)(2,1)} %collective-permute-done.refs_1_, bf16[640,2048]{1,0:T(8,128)(2,1)} %collective-permute-done.1.refs_2_, ...), custom_call_target="tpu_custom_call" | custom-call | flops 21474836480 | bytes 41943040 | tf_op jit(solution)/shard_map/expand/pallas_call | solution.py:496
  156.9 12.2 %collective-permute-done.5.refs_2_ = bf16[640,2048]{1,0:T(8,128)(2,1)} collective-permute-done((bf16[640,2048]{1,0:T(8,128)(2,1)S(1)}, bf16[640,2048]{1,0:T(8,128)(2,1)}, u32[]{:S(2)}, u32[]{:S(2)}) %collective-permute-start.5) | collective-permute-done | bytes 2621472 | tf_op jit(solution)/shard_map/ppermute | solution.py:362
  176.9 26.6 %convolution_convert_fusion.refs_15_ = bf16[2560,2048]{1,0:T(8,128)(2,1)S(1)} fusion(bf16[2560,2048]{1,0:T(8,128)(2,1)} %get-tuple-element.75, bf16[2048,2048]{1,0:T(8,128)(2,1)} %all-gather.6.cloned.1.call-done.refs_5_), kind=kOutput, calls=%fused_computation.1 | convolution fusion | flops 21480079360 | bytes 29360128 | tf_op jit(solution)/shard_map/dot_general | solution.py:28
  210.2 30.9 %slope_grad.1 = (bf16[2560,2048]{1,0:T(8,128)(2,1)}, bf16[2560,2048]{1,0:T(8,128)(2,1)}, f32[8,2048]{1,0:T(8,128)S(1)}) custom-call(bf16[640,2048]{1,0:T(8,128)(2,1)S(1)} %bitcast.64, bf16[640,2048]{1,0:T(8,128)(2,1)} %collective-permute-done.4.refs_1_, bf16[640,2048]{1,0:T(8,128)(2,1)} %collective-permute-done.5.refs_2_, ...), custom_call_target="tpu_custom_call" | custom-call | flops 21474836480 | bytes 41943040 | tf_op jit(solution)/shard_map/slope_grad/pallas_call | solution.py:540
  243.2 28.8 %convolution_convert_fusion.2 = bf16[2048,2048]{1,0:T(8,128)(2,1)} fusion(bf16[2560,2048]{1,0:T(8,128)(2,1)} %get-tuple-element.90.y_ref, bf16[2560,2048]{1,0:T(8,128)(2,1)} %get-tuple-element.75), kind=kOutput, calls=%fused_computation.3 | convolution fusion | flops 21479030784 | bytes 29360128 | tf_op jit(solution)/shard_map/dot_general | solution.py:28
  273.8 4.2 add_convert_fusion.3
  280.4 22.3 %add_convert_fusion = bf16[2560,1536]{1,0:T(8,128)(2,1)} fusion(bf16[2560,2048]{1,0:T(8,128)(2,1)} %get-tuple-element.113.x_ref.refs_6_.refs_9_.refs_10_, f32[1536]{0:T(1024)S(1)} %reshape.234, bf16[2048,2048]{1,0:T(8,128)(2,1)} %all-gather.8.cloned.1.call-done.refs_3_.refs_4_.refs_6_.refs_7_), kind=kOutput, calls=%fused_computation | convolution fusion | flops 16113991680 | bytes 24647680 | tf_op jit(solution)/shard_map/dot_general | solution.py:28
  302.7 5.6 collective-permute-done.11.refs_19_
  310.0 10.5 %convolution_convert_fusion.3 = bf16[2560,512]{1,0:T(8,128)(2,1)} fusion(bf16[2560,2048]{1,0:T(8,128)(2,1)} %get-tuple-element.90.y_ref, bf16[2048,2048]{1,0:T(8,128)(2,1)} %all-gather.8.cloned.1.call-done.refs_3_.refs_4_.refs_6_.refs_7_), kind=kOutput, calls=%fused_computation.14 | convolution fusion | flops 5370019840 | bytes 15204352 | tf_op jit(solution)/shard_map/dot_general | solution.py:28
  320.5 28.9 %convolution_convert_fusion.1 = bf16[2048,2048]{1,0:T(8,128)(2,1)} fusion(bf16[2560,2048]{1,0:T(8,128)(2,1)} %get-tuple-element.113.x_ref.refs_6_.refs_9_.refs_10_, bf16[2560,2048]{1,0:T(8,128)(2,1)} %get-tuple-element.114.refs_2_.refs_5_), kind=kOutput, calls=%fused_computation.2 | convolution fusion | flops 21479030784 | bytes 29360128 | tf_op jit(solution)/shard_map/dot_general | solution.py:28
  355.5 77.1 %attention.2 = (bf16[40,64,256]{2,1,0:T(8,128)(2,1)}, bf16[40,64,768]{2,1,0:T(8,128)(2,1)}, f32[8,768]{1,0:T(8,128)}) custom-call(s32[40]{0:T(128)} %select_reduce_fusion.where_ref, bf16[40,64,1536]{2,1,0:T(8,128)(2,1)} %bitcast.67, bf16[40,64,1536]{2,1,0:T(8,128)(2,1)} %bitcast.68, bf16[40,64,1536]{2,1,0:T(8,128)(2,1)} %bitcast.69, ...), custom_call_target="tpu_custom_call" | custom-call | flops 1000000 | bytes 1000000 | tf_op jit(solution)/shard_map/attention/pallas_call | solution.py:297
  441.7 16.8 %pair_grad.2 = bf16[2048,1024]{1,0:T(8,128)(2,1)} custom-call(bf16[2560,2048]{1,0:T(8,128)(2,1)} %get-tuple-element.113.x_ref.refs_6_.refs_9_.refs_10_, bf16[2560,2048]{1,0:T(8,128)(2,1)} %get-tuple-element.90.y_ref, bf16[2560,768]{1,0:T(8,128)(2,1)} %bitcast.85, bf16[2560,256]{1,0:T(8,128)(2,1)} %bitcast.96), custom_call_target="tpu_custom_call" | custom-call | flops 1000000 | bytes 1000000 | tf_op jit(solution)/shard_map/pair_grad/pallas_call | solution.py:728
  458.6 77.1 %attention.3 = (bf16[40,64,256]{2,1,0:T(8,128)(2,1)}, bf16[40,64,768]{2,1,0:T(8,128)(2,1)}, f32[8,768]{1,0:T(8,128)}) custom-call(s32[40]{0:T(128)} %select_reduce_fusion.where_ref, bf16[40,64,1536]{2,1,0:T(8,128)(2,1)} %bitcast.71, bf16[40,64,1536]{2,1,0:T(8,128)(2,1)} %bitcast.72, bf16[40,64,1536]{2,1,0:T(8,128)(2,1)} %bitcast.73, ...), custom_call_target="tpu_custom_call" | custom-call | flops 1000000 | bytes 1000000 | tf_op jit(solution)/shard_map/attention/pallas_call | solution.py:297
  544.3 16.0 %input_grad.3 = (bf16[320,2048]{1,0:T(8,128)(2,1)}, bf16[320,2048]{1,0:T(8,128)(2,1)}, f32[2,2048]{1,0:T(2,128)}) custom-call(bf16[2560,768]{1,0:T(8,128)(2,1)} %bitcast.86, bf16[2560,768]{1,0:T(8,128)(2,1)} %bitcast.90, bf16[2560,2048]{1,0:T(8,128)(2,1)} %get-tuple-element.114.refs_2_.refs_5_, ...), custom_call_target="tpu_custom_call" | custom-call | flops 1000000 | bytes 1000000 | tf_op jit(solution)/shard_map/input_grad/pallas_call | solution.py:605
  562.4 26.9 %input_grad.4 = (bf16[320,2048]{1,0:T(8,128)(2,1)}, bf16[320,2048]{1,0:T(8,128)(2,1)}, bf16[320,2048]{1,0:T(8,128)(2,1)}, bf16[320,2048]{1,0:T(8,128)(2,1)}, f32[2,2048]{1,0:T(2,128)}) custom-call(bf16[2560,768]{1,0:T(8,128)(2,1)} %bitcast.87, bf16[2560,768]{1,0:T(8,128)(2,1)} %bitcast.91, bf16[2560,2048]{1,0:T(8,128)(2,1)} %get-tuple-element.114.refs_2_.refs_5_, ...), custom_call_target="tpu_custom_call" | custom-call | flops 99999997952 | bytes 1000000 | tf_op jit(solution)/shard_map/input_grad/pallas_call | solution.py:605
  591.5 2.9 add_convert_fusion.1
  598.0 16.9 %pair_grad.3 = bf16[2048,1024]{1,0:T(8,128)(2,1)} custom-call(bf16[2560,2048]{1,0:T(8,128)(2,1)} %get-tuple-element.113.x_ref.refs_6_.refs_9_.refs_10_, bf16[2560,2048]{1,0:T(8,128)(2,1)} %get-tuple-element.90.y_ref, bf16[2560,768]{1,0:T(8,128)(2,1)} %bitcast.93, bf16[2560,256]{1,0:T(8,128)(2,1)} %bitcast.95), custom_call_target="tpu_custom_call" | custom-call | flops 1000000 | bytes 1000000 | tf_op jit(solution)/shard_map/pair_grad/pallas_call | solution.py:728
  615.0 15.6 %input_grad.5 = (bf16[640,2048]{1,0:T(8,128)(2,1)}, f32[2,2048]{1,0:T(2,128)}) custom-call(bf16[2560,768]{1,0:T(8,128)(2,1)} %bitcast.89, bf16[2560,768]{1,0:T(8,128)(2,1)} %bitcast.94, bf16[2560,2048]{1,0:T(8,128)(2,1)} %get-tuple-element.114.refs_2_.refs_5_, bf16[2048,2048]{1,0:T(8,128)(2,1)} %all-gather.8.cloned.1.call-done.refs_3_.refs_4_.refs_6_.refs_7_, ...), custom_call_target="tpu_custom_call" | custom-call | flops 99999997952 | bytes 1000000 | tf_op jit(solution)/shard_map/input_grad/pallas_call | solution.py:605
  632.8 13.1 %place_output.1 = bf16[640,2048]{1,0:T(8,128)(2,1)} custom-call(bf16[640,256]{1,0:T(8,128)(2,1)} %bitcast.104, bf16[640,256]{1,0:T(8,128)(2,1)} %bitcast.105, bf16[640,256]{1,0:T(8,128)(2,1)} %copy-done.23, bf16[640,256]{1,0:T(8,128)(2,1)} %copy-done.26, bf16[640,256]{1,0:T(8,128)(2,1)} %copy-done.21, bf16[640,256]{1,0:T(8,128)(2,1)} %copy-done.24, ...), custom_call_target="tpu_custom_call" | custom-call | flops 1000000 | bytes 1000000 | tf_op jit(solution)/shard_map/place_output/pallas_call | solution.py:655
  651.1 9.0 %token_grad.1 = bf16[640,2048]{1,0:T(8,128)(2,1)} custom-call(bf16[640,2048]{1,0:T(8,128)(2,1)} %bitcast.84, bf16[640,2048]{1,0:T(8,128)(2,1)} %bitcast.61, bf16[640,2048]{1,0:T(8,128)(2,1)} %get-tuple-element.115.own_ref, f32[1,2048]{1,0:T(1,128)S(1)} %bitcast.65, bf16[320,2048]{1,0:T(8,128)(2,1)} %collective-permute-done.26.refs_0_, ...), custom_call_target="tpu_custom_call" | custom-call | flops 1000000 | bytes 1000000 | tf_op jit(solution)/shard_map/token_grad/pallas_call | solution.py:699
  (245 shorter events, 110.6 us)
Async XLA Ops:
  7.2 107.7 %all-gather.4.cloned.1.call-start = ((), (), s32[]{:S(2)}) async-start(), calls=%async_computation.4 | async-start | bytes 9437184 | tf_op jit(solution)/shard_map/all_gather | solution.py:812
  7.9 169.0 %all-gather.6.cloned.1.call-start = ((), (), s32[]{:S(2)}) async-start(), calls=%async_computation.5 | async-start | bytes 9437184 | tf_op jit(solution)/shard_map/all_gather | solution.py:812
  15.1 60.1 %collective-permute-start.1 = (bf16[640,2048]{1,0:T(8,128)(2,1)}, bf16[640,2048]{1,0:T(8,128)(2,1)}, u32[]{:S(2)}, u32[]{:S(2)}) collective-permute-start(bf16[640,2048]{1,0:T(8,128)(2,1)} %fusion.6.refs_0_), channel_id=1, source_target_pairs={{8,0},{24,8},{16,24},{0,16},{9,1},{25,9},{17,25},{1,17},{10,2},{26... | collective-permute-start | bytes 7864328 | tf_op jit(solution)/shard_map/ppermute | solution.py:362
  18.0 58.6 %collective-permute-start = (bf16[640,2048]{1,0:T(8,128)(2,1)}, bf16[640,2048]{1,0:T(8,128)(2,1)}, u32[]{:S(2)}, u32[]{:S(2)}) collective-permute-start(bf16[640,2048]{1,0:T(8,128)(2,1)} %fusion.6.refs_0_), channel_id=1, source_target_pairs={{0,8},{8,24},{24,16},{16,0},{1,9},{9,25},{25,17},{17,1},{2,10},{10... | collective-permute-start | bytes 7864328 | tf_op jit(solution)/shard_map/ppermute | solution.py:361
  76.7 203.7 %all-gather.8.cloned.1.call-start = ((), (), s32[]{:S(2)}) async-start(), calls=%async_computation.6 | async-start | bytes 9437184 | tf_op jit(solution)/shard_map/all_gather | solution.py:812
  112.8 329.0 %reduce-scatter.5.cloned.1.call-start = ((), (), s32[]{:S(2)}) async-start(), calls=%async_computation.7 | async-start | bytes 9437184 | tf_op jit(solution)/shard_map/reduce_scatter | solution.py:815
  112.8 56.4 %collective-permute-start.5 = (bf16[640,2048]{1,0:T(8,128)(2,1)S(1)}, bf16[640,2048]{1,0:T(8,128)(2,1)}, u32[]{:S(2)}, u32[]{:S(2)}) collective-permute-start(bf16[640,2048]{1,0:T(8,128)(2,1)S(1)} %bitcast.62), channel_id=1, source_target_pairs={{8,0},{24,8},{16,24},{0,16},{9,1},{25,9},{17,25},{1,17},{10,2},{26... | collective-permute-start | bytes 7864328 | tf_op jit(solution)/shard_map/ppermute | solution.py:362
  113.5 56.2 %collective-permute-start.4 = (bf16[640,2048]{1,0:T(8,128)(2,1)S(1)}, bf16[640,2048]{1,0:T(8,128)(2,1)}, u32[]{:S(2)}, u32[]{:S(2)}) collective-permute-start(bf16[640,2048]{1,0:T(8,128)(2,1)S(1)} %bitcast.63), channel_id=1, source_target_pairs={{0,8},{8,24},{24,16},{16,0},{1,9},{9,25},{25,17},{17,1},{2,10},{10... | collective-permute-start | bytes 7864328 | tf_op jit(solution)/shard_map/ppermute | solution.py:361
  272.1 272.2 %reduce-scatter.7.cloned.1.call-start = ((), (), s32[]{:S(2)}) async-start(), calls=%async_computation.8 | async-start | bytes 9437184 | tf_op jit(solution)/shard_map/reduce_scatter | solution.py:815
  349.5 248.5 %reduce-scatter.9.cloned.1.call-start = ((), (), s32[]{:S(2)}) async-start(), calls=%async_computation.9 | async-start | bytes 4718592 | tf_op jit(solution)/shard_map/reduce_scatter | solution.py:815
  351.3 81.4 %collective-permute-start.15 = (bf16[2048,512]{1,0:T(8,128)(2,1)S(1)}, bf16[2048,512]{1,0:T(8,128)(2,1)S(1)}, u32[]{:S(2)}, u32[]{:S(2)}) collective-permute-start(bf16[2048,512]{1,0:T(8,128)(2,1)S(1)} %slice.160.refs_8_), channel_id=1, source_target_pairs={{8,0},{24,8},{16,24},{0,16},{9,1},{25,9},{17,25},{1,17},{10,2},{26... | collective-permute-start | bytes 6291464 | tf_op jit(solution)/shard_map/ppermute | solution.py:362
  352.8 79.8 %collective-permute-start.14 = (bf16[2048,512]{1,0:T(8,128)(2,1)S(1)}, bf16[2048,512]{1,0:T(8,128)(2,1)S(1)}, u32[]{:S(2)}, u32[]{:S(2)}) collective-permute-start(bf16[2048,512]{1,0:T(8,128)(2,1)S(1)} %slice.160.refs_8_), channel_id=1, source_target_pairs={{0,8},{8,24},{24,16},{16,0},{1,9},{9,25},{25,17},{17,1},{2,10},{10... | collective-permute-start | bytes 6291464 | tf_op jit(solution)/shard_map/ppermute | solution.py:361
  353.3 86.1 %collective-permute-start.12 = (bf16[320,2048]{1,0:T(8,128)(2,1)}, bf16[320,2048]{1,0:T(8,128)(2,1)}, u32[]{:S(2)}, u32[]{:S(2)}) collective-permute-start(bf16[320,2048]{1,0:T(8,128)(2,1)} %get-tuple-element.94), channel_id=1, source_target_pairs={{0,8},{8,24},{24,16},{16,0},{1,9},{9,25},{25,17},{17,1},{2,10},{10... | collective-permute-start | bytes 3932168 | tf_op jit(solution)/shard_map/ppermute | solution.py:405
  353.9 86.2 %collective-permute-start.13 = (bf16[320,2048]{1,0:T(8,128)(2,1)}, bf16[320,2048]{1,0:T(8,128)(2,1)}, u32[]{:S(2)}, u32[]{:S(2)}) collective-permute-start(bf16[320,2048]{1,0:T(8,128)(2,1)} %get-tuple-element.95), channel_id=1, source_target_pairs={{8,0},{24,8},{16,24},{0,16},{9,1},{25,9},{17,25},{1,17},{10,2},{26... | collective-permute-start | bytes 3932168 | tf_op jit(solution)/shard_map/ppermute | solution.py:406
  434.8 109.5 %collective-permute-start.23 = (bf16[1024,512]{1,0:T(8,128)(2,1)}, bf16[1024,512]{1,0:T(8,128)(2,1)}, u32[]{:S(2)}, u32[]{:S(2)}) collective-permute-start(bf16[1024,512]{1,0:T(8,128)(2,1)} %slice.140), channel_id=1, source_target_pairs={{8,0},{24,8},{16,24},{0,16},{9,1},{25,9},{17,25},{1,17},{10,2},{26... | collective-permute-start | bytes 3145736 | tf_op jit(solution)/shard_map/ppermute | solution.py:370
  436.3 108.0 %collective-permute-start.22 = (bf16[1024,512]{1,0:T(8,128)(2,1)}, bf16[1024,512]{1,0:T(8,128)(2,1)}, u32[]{:S(2)}, u32[]{:S(2)}) collective-permute-start(bf16[1024,512]{1,0:T(8,128)(2,1)} %slice.139), channel_id=1, source_target_pairs={{0,8},{8,24},{24,16},{16,0},{1,9},{9,25},{25,17},{17,1},{2,10},{10... | collective-permute-start | bytes 3145736 | tf_op jit(solution)/shard_map/ppermute | solution.py:369
  438.0 99.9 %collective-permute-start.18 = (bf16[640,256]{1,0:T(8,128)(2,1)}, bf16[640,256]{1,0:T(8,128)(2,1)S(1)}, u32[]{:S(2)}, u32[]{:S(2)}) collective-permute-start(bf16[640,256]{1,0:T(8,128)(2,1)} %bitcast.22), channel_id=1, source_target_pairs={{0,16},{8,0},{24,8},{16,24},{1,17},{9,1},{25,9},{17,25},{2,18},{10... | collective-permute-start | bytes 983048 | tf_op jit(solution)/shard_map/ppermute | solution.py:426
  439.5 99.1 %collective-permute-start.20 = (bf16[640,256]{1,0:T(8,128)(2,1)}, bf16[640,256]{1,0:T(8,128)(2,1)S(1)}, u32[]{:S(2)}, u32[]{:S(2)}) collective-permute-start(bf16[640,256]{1,0:T(8,128)(2,1)} %bitcast.24), channel_id=1, source_target_pairs={{0,24},{8,16},{24,0},{16,8},{1,25},{9,17},{25,1},{17,9},{2,26},{10... | collective-permute-start | bytes 983048 | tf_op jit(solution)/shard_map/ppermute | solution.py:426
  440.1 100.7 %collective-permute-start.16 = (bf16[640,256]{1,0:T(8,128)(2,1)}, bf16[640,256]{1,0:T(8,128)(2,1)S(1)}, u32[]{:S(2)}, u32[]{:S(2)}) collective-permute-start(bf16[640,256]{1,0:T(8,128)(2,1)} %bitcast.20), channel_id=1, source_target_pairs={{0,8},{8,24},{24,16},{16,0},{1,9},{9,25},{25,17},{17,1},{2,10},{10... | collective-permute-start | bytes 983048 | tf_op jit(solution)/shard_map/ppermute | solution.py:426
  543.6 122.4 %reduce-scatter.11.cloned.1.call-start = ((), (), s32[]{:S(2)}) async-start(), calls=%async_computation.10 | async-start | bytes 4718592 | tf_op jit(solution)/shard_map/reduce_scatter | solution.py:815
  589.4 57.9 %collective-permute-start.27 = (bf16[320,2048]{1,0:T(8,128)(2,1)}, bf16[320,2048]{1,0:T(8,128)(2,1)S(1)}, u32[]{:S(2)}, u32[]{:S(2)}) collective-permute-start(bf16[320,2048]{1,0:T(8,128)(2,1)} %get-tuple-element.109), channel_id=1, source_target_pairs={{0,8},{8,24},{24,16},{16,0},{1,9},{9,25},{25,17},{17,1},{2,10},{10... | collective-permute-start | bytes 3932168 | tf_op jit(solution)/shard_map/ppermute | solution.py:405
  589.7 57.6 %collective-permute-start.28 = (bf16[320,2048]{1,0:T(8,128)(2,1)}, bf16[320,2048]{1,0:T(8,128)(2,1)S(1)}, u32[]{:S(2)}, u32[]{:S(2)}) collective-permute-start(bf16[320,2048]{1,0:T(8,128)(2,1)} %get-tuple-element.110), channel_id=1, source_target_pairs={{8,0},{24,8},{16,24},{0,16},{9,1},{25,9},{17,25},{1,17},{10,2},{26... | collective-permute-start | bytes 3932168 | tf_op jit(solution)/shard_map/ppermute | solution.py:406
  594.4 52.9 %collective-permute-start.29 = (bf16[320,2048]{1,0:T(8,128)(2,1)}, bf16[320,2048]{1,0:T(8,128)(2,1)}, u32[]{:S(2)}, u32[]{:S(2)}) collective-permute-start(bf16[320,2048]{1,0:T(8,128)(2,1)} %add_convert_fusion.1), channel_id=1, source_target_pairs={{8,0},{24,8},{16,24},{0,16},{9,1},{25,9},{17,25},{1,17},{10,2},{26... | collective-permute-start | bytes 3932168 | tf_op jit(solution)/shard_map/ppermute | solution.py:400
  597.3 50.0 %collective-permute-start.26 = (bf16[320,2048]{1,0:T(8,128)(2,1)}, bf16[320,2048]{1,0:T(8,128)(2,1)}, u32[]{:S(2)}, u32[]{:S(2)}) collective-permute-start(bf16[320,2048]{1,0:T(8,128)(2,1)} %add_convert_fusion.2), channel_id=1, source_target_pairs={{0,8},{8,24},{24,16},{16,0},{1,9},{9,25},{25,17},{17,1},{2,10},{10... | collective-permute-start | bytes 3932168 | tf_op jit(solution)/shard_map/ppermute | solution.py:399
  (60 other events, 942.5 us)
Sparse Core Ops, SparseCore 0:
  9.6 84.7 all-gather.3
  96.0 80.5 all-gather.5
  178.8 80.5 all-gather.7
  272.2 89.9 reduce-scatter.4
  364.3 87.9 reduce-scatter.6
  543.7 47.7 reduce-scatter.8
  615.1 47.2 reduce-scatter.10
